TPU v7x, 32 devices: a whole 2x2x4 slice. The times are simulated.
32 devices in a mesh: fsdp: 8 (over z, core), expert: 4 (over y, x).
Axes of the slice: x: 2, y: 2, z: 4, core: 2. Of those that a mesh axis runs over, the one named last changes fastest.
Arguments:
- tokens: bfloat16 [4096, 1536], P(('fsdp', 'expert')), may hold values from -6 to 6
- lengths: int32 [32, 4], P(('fsdp', 'expert')), may hold values from 1 to 64, 128 in all within a row
- routes: int32 [2, 4096, 8], P(None, ('fsdp', 'expert')), may hold values from 0 to 19, all different within a row; in each aligned block of 128 rows (0 to 127, 128 to 255, ..., all dimensions but the last counted through in order) at most 80 rows name the same one
- gates: float32 [2, 4096, 8], P(None, ('fsdp', 'expert')), may hold values from 0.04 to 0.4
- cotangent: bfloat16 [4096, 1536], P(('fsdp', 'expert')), may hold values from -6 to 6
- norm_attn: bfloat16 [2, 1536], P(None, ('fsdp', 'expert')), may hold values from 0.5 to 1.5
- norm_ffn: bfloat16 [2, 1536], P(None, ('fsdp', 'expert')), may hold values from 0.5 to 1.5
- query: bfloat16 [2, 1536, 1536], P(None, ('fsdp', 'expert')), may hold values from -0.15625 to 0.15625
- key: bfloat16 [2, 1536, 512], P(None, ('fsdp', 'expert')), may hold values from -0.15625 to 0.15625
- value: bfloat16 [2, 1536, 512], P(None, ('fsdp', 'expert')), may hold values from -0.15625 to 0.15625
- output: bfloat16 [2, 1536, 1536], P(None, ('fsdp', 'expert')), may hold values from -0.625 to 0.625
- w_gate: bfloat16 [2, 1536, 20, 512], P(None, 'fsdp', 'expert'), may hold values from -0.15625 to 0.15625
- w_up: bfloat16 [2, 1536, 20, 512], P(None, 'fsdp', 'expert'), may hold values from -0.15625 to 0.15625
- w_down: bfloat16 [2, 1536, 20, 512], P(None, 'fsdp', 'expert'), may hold values from -0.75 to 0.75
Outputs:
- result: bfloat16 [4096, 1536], P(('fsdp', 'expert'))
- grad_tokens: float32 [4096, 1536], P(('fsdp', 'expert'))
- grad_norm_attn: float32 [2, 1536], P(None, ('fsdp', 'expert'))
- grad_norm_ffn: float32 [2, 1536], P(None, ('fsdp', 'expert'))
- grad_query: float32 [2, 1536, 1536], P(None, ('fsdp', 'expert'))
- grad_key: float32 [2, 1536, 512], P(None, ('fsdp', 'expert'))
- grad_value: float32 [2, 1536, 512], P(None, ('fsdp', 'expert'))
- grad_output: float32 [2, 1536, 1536], P(None, ('fsdp', 'expert'))
- grad_w_gate: float32 [2, 1536, 20, 512], P(None, 'fsdp', 'expert')
- grad_w_up: float32 [2, 1536, 20, 512], P(None, 'fsdp', 'expert')
- grad_w_down: float32 [2, 1536, 20, 512], P(None, 'fsdp', 'expert')
Inputs may be any that keep to these rules, and one draw needn't show every extreme that they name: `lengths`: every row sums to 128, and the largest entry of every row is 64. `routes`: the 8 experts of a token in a layer differ. Among the 128 rows of one device in one layer, no expert is named by more than 80 rows, and in every layer some expert is named by exactly 80 rows of some device.
All inputs are finite; a program needn't handle non-finite values.
Results may differ from a plain program's by a relative error of at most 0.025.
Values may be sent and summed in bfloat16 or wider, within the bound.
No kernel may reach another device: no remote copies, remote signals or barrier semaphores. Data moves between devices by JAX's collectives and lax.ppermute only.
A program may use at most 512 MiB of HBM per device.

v0:
```python
import math

import jax
import jax.numpy as jnp
from jax import lax
from jax.sharding import PartitionSpec as P

QUERY_HEADS = 24
KEY_VALUE_HEADS = 8
HEAD_DIMENSION = 64


NORM_EPS = 1e-06
MASKED = -1000000000.0


def positions(length_row, count_of_rows):
    ends = jnp.cumsum(length_row)
    token_order = jnp.arange(count_of_rows, dtype=jnp.int32)
    passed = token_order[:, None] >= ends[None, :]
    segment = jnp.sum(passed.astype(jnp.int32), axis=1)
    before = jnp.sum(jnp.where(passed, length_row[None, :], 0), axis=1)
    return (segment, token_order - before)


def rope_tables(seq_place, head_width):
    half_width = head_width // 2
    freq_table = jnp.exp(
        jnp.arange(half_width, dtype=jnp.float32) * (-2.0 * math.log(10000.0) / head_width)
    )
    angles = seq_place.astype(jnp.float32)[:, None] * freq_table[None, :]
    return (jnp.cos(angles), jnp.sin(angles))


def apply_rotation(vector, cosine_table, sine_table):
    half_width = vector.shape[-1] // 2
    former = vector[..., :half_width]
    latter = vector[..., half_width:]
    cos_wide = cosine_table[:, None, :]
    sin_wide = sine_table[:, None, :]
    return jnp.concatenate(
        [former * cos_wide - latter * sin_wide, latter * cos_wide + former * sin_wide], axis=-1
    )


def reverse_rotation(vector, cosine_table, sine_table):
    half_width = vector.shape[-1] // 2
    former = vector[..., :half_width]
    latter = vector[..., half_width:]
    cos_wide = cosine_table[:, None, :]
    sin_wide = sine_table[:, None, :]
    return jnp.concatenate(
        [former * cos_wide + latter * sin_wide, latter * cos_wide - former * sin_wide], axis=-1
    )


def rms_forward(residual, norm_gain):
    inverse = lax.rsqrt(jnp.mean(residual * residual, axis=-1, keepdims=True) + NORM_EPS)
    return (inverse, (residual * inverse * norm_gain).astype(jnp.bfloat16))


def rms_backward(residual, inverse, norm_gain, upstream):
    gain_grad = jnp.sum(upstream * residual * inverse, axis=0)
    scaled = upstream * norm_gain
    inner = jnp.mean(scaled * residual, axis=-1, keepdims=True)
    return (gain_grad, inverse * scaled - residual * inverse * inverse * inverse * inner)


def score_block(rotated_query, turned_k, allowed):
    scores = jnp.einsum(
        "qhgd,khd->hgqk", rotated_query, turned_k, preferred_element_type=jnp.float32
    ) * HEAD_DIMENSION ** (-0.5)
    return jnp.where(allowed, scores, MASKED)


def activate(gate_pre):
    gate_sig = jax.nn.sigmoid(gate_pre)
    return (gate_sig, gate_pre * gate_sig)


def attend_forward(residual, allowed, cosine_table, sine_table, attn_full):
    gain_attn, gain_ffn, w_query, key_matrix, value_matrix, w_output = attn_full
    count_of_rows = residual.shape[0]
    inverse, normalized_input = rms_forward(residual, gain_attn)
    query_unrotated = jnp.dot(
        normalized_input, w_query, preferred_element_type=jnp.float32
    ).reshape(count_of_rows, QUERY_HEADS, HEAD_DIMENSION)
    key_unrotated = jnp.dot(
        normalized_input, key_matrix, preferred_element_type=jnp.float32
    ).reshape(count_of_rows, KEY_VALUE_HEADS, HEAD_DIMENSION)
    value_rows = (
        jnp.dot(normalized_input, value_matrix, preferred_element_type=jnp.float32)
        .astype(jnp.bfloat16)
        .reshape(count_of_rows, KEY_VALUE_HEADS, HEAD_DIMENSION)
    )
    rotated_query = (
        apply_rotation(query_unrotated, cosine_table, sine_table)
        .astype(jnp.bfloat16)
        .reshape(count_of_rows, KEY_VALUE_HEADS, QUERY_HEADS // KEY_VALUE_HEADS, HEAD_DIMENSION)
    )
    turned_k = apply_rotation(key_unrotated, cosine_table, sine_table).astype(jnp.bfloat16)
    scores = score_block(rotated_query, turned_k, allowed)
    row_top = jnp.max(scores, axis=-1, keepdims=True)
    exp_scores = jnp.exp(scores - row_top)
    row_total = jnp.sum(exp_scores, axis=-1, keepdims=True)
    attn_probs = (exp_scores / row_total).astype(jnp.bfloat16)
    log_total = row_top + jnp.log(row_total)
    mixed_heads = jnp.einsum(
        "hgqk,khd->qhgd", attn_probs, value_rows, preferred_element_type=jnp.float32
    )
    mixed_heads = mixed_heads.astype(jnp.bfloat16).reshape(
        count_of_rows, QUERY_HEADS * HEAD_DIMENSION
    )
    attn_out = jnp.dot(mixed_heads, w_output, preferred_element_type=jnp.float32)
    return (
        residual + attn_out,
        (inverse, normalized_input, rotated_query, turned_k, value_rows, log_total, mixed_heads),
    )


def attend_backward(residual, allowed, cosine_table, sine_table, attn_full, stash, upstream):
    gain_attn, gain_ffn, w_query, key_matrix, value_matrix, w_output = attn_full
    inverse, normalized_input, rotated_query, turned_k, value_rows, log_total, mixed_heads = stash
    count_of_rows = residual.shape[0]
    branch_grad = upstream.astype(jnp.bfloat16)
    grad_wo = jnp.einsum("td,te->de", mixed_heads, branch_grad, preferred_element_type=jnp.float32)
    mixed_gradient = jnp.einsum(
        "te,de->td", branch_grad, w_output, preferred_element_type=jnp.float32
    )
    mixed_gradient = mixed_gradient.astype(jnp.bfloat16).reshape(
        count_of_rows, KEY_VALUE_HEADS, QUERY_HEADS // KEY_VALUE_HEADS, HEAD_DIMENSION
    )
    attn_probs = jnp.exp(score_block(rotated_query, turned_k, allowed) - log_total)
    value_rows_gradient = jnp.einsum(
        "hgqk,qhgd->khd",
        attn_probs.astype(jnp.bfloat16),
        mixed_gradient,
        preferred_element_type=jnp.float32,
    )
    value_rows_gradient = value_rows_gradient.astype(jnp.bfloat16).reshape(
        count_of_rows, KEY_VALUE_HEADS * HEAD_DIMENSION
    )
    grad_probs = jnp.einsum(
        "qhgd,khd->hgqk", mixed_gradient, value_rows, preferred_element_type=jnp.float32
    )
    grad_scores = attn_probs * (
        grad_probs - jnp.sum(attn_probs * grad_probs, axis=-1, keepdims=True)
    )
    grad_scores = grad_scores.astype(jnp.bfloat16)
    grad_tq = jnp.einsum(
        "hgqk,khd->qhgd", grad_scores, turned_k, preferred_element_type=jnp.float32
    ) * HEAD_DIMENSION ** (-0.5)
    turned_key_gradient = jnp.einsum(
        "hgqk,qhgd->khd", grad_scores, rotated_query, preferred_element_type=jnp.float32
    ) * HEAD_DIMENSION ** (-0.5)
    grad_query = reverse_rotation(
        grad_tq.reshape(count_of_rows, QUERY_HEADS, HEAD_DIMENSION), cosine_table, sine_table
    )
    grad_query = grad_query.astype(jnp.bfloat16).reshape(
        count_of_rows, QUERY_HEADS * HEAD_DIMENSION
    )
    grad_key = (
        reverse_rotation(turned_key_gradient, cosine_table, sine_table)
        .astype(jnp.bfloat16)
        .reshape(count_of_rows, KEY_VALUE_HEADS * HEAD_DIMENSION)
    )
    grad_wq = jnp.einsum(
        "td,te->de", normalized_input, grad_query, preferred_element_type=jnp.float32
    )
    grad_wk = jnp.einsum(
        "td,te->de", normalized_input, grad_key, preferred_element_type=jnp.float32
    )
    grad_wv = jnp.einsum(
        "td,te->de", normalized_input, value_rows_gradient, preferred_element_type=jnp.float32
    )
    grad_normed = jnp.einsum("te,de->td", grad_query, w_query, preferred_element_type=jnp.float32)
    grad_normed = grad_normed + jnp.einsum(
        "te,de->td", grad_key, key_matrix, preferred_element_type=jnp.float32
    )
    grad_normed = grad_normed + jnp.einsum(
        "te,de->td", value_rows_gradient, value_matrix, preferred_element_type=jnp.float32
    )
    gain_grad, residual_grad = rms_backward(residual, inverse, gain_attn, grad_normed)
    return (upstream + residual_grad, (gain_grad, grad_wq, grad_wk, grad_wv, grad_wo))


def route_places(choices, expert_count, capacity):
    flat_routes = choices.reshape(-1)
    onehot = (flat_routes[:, None] == jnp.arange(expert_count, dtype=jnp.int32)[None, :]).astype(
        jnp.int32
    )
    slot_index = jnp.sum(jnp.cumsum(onehot, axis=0) * onehot, axis=1) - 1
    places = flat_routes * capacity + slot_index
    token_ids = jnp.arange(flat_routes.shape[0], dtype=jnp.int32) // choices.shape[1]
    owners = (
        jnp.full((expert_count * capacity,), choices.shape[0], jnp.int32).at[places].set(token_ids)
    )
    return (places, owners)


def experts_forward(middle, gain_ffn, choices, gate_weights, expert_full, capacity, expert_count):
    w_gate_full, w_up_full, w_down_full = expert_full
    model_width = middle.shape[1]
    inverse, normalized_input = rms_forward(middle, gain_ffn)
    places, owners = route_places(choices, expert_count, capacity)
    outgoing = jnp.take(normalized_input, owners, axis=0, mode="fill", fill_value=0)
    outgoing = outgoing.reshape(-1, w_gate_full.shape[1], capacity, model_width)
    arriving = lax.all_to_all(outgoing, "expert", split_axis=0, concat_axis=0, tiled=True)
    gate_pre = jnp.einsum(
        "secd,def->secf", arriving, w_gate_full, preferred_element_type=jnp.float32
    )
    up_pre = jnp.einsum("secd,def->secf", arriving, w_up_full, preferred_element_type=jnp.float32)
    hidden = (activate(gate_pre)[1] * up_pre).astype(jnp.bfloat16)
    produced = jnp.einsum("secf,def->secd", hidden, w_down_full, preferred_element_type=jnp.float32)
    returned = lax.all_to_all(
        produced.astype(jnp.bfloat16), "expert", split_axis=0, concat_axis=0, tiled=True
    )
    returned, arriving, gate_pre, up_pre = (returned, arriving, gate_pre, up_pre)
    picked = jnp.take(returned.reshape(-1, model_width), places, axis=0)
    picked = picked.reshape(choices.shape[0], choices.shape[1], model_width)
    moe_out = jnp.einsum("tk,tkd->td", gate_weights, picked, preferred_element_type=jnp.float32)
    return (middle + moe_out, (inverse, places, owners, arriving, gate_pre, up_pre))


def experts_backward(middle, gain_ffn, choices, gate_weights, expert_full, stash, upstream):
    w_gate_full, w_up_full, w_down_full = expert_full
    inverse, places, owners, arriving, gate_pre, up_pre = stash
    model_width = middle.shape[1]
    slot_gate = jnp.zeros((owners.shape[0],), jnp.float32).at[places].set(gate_weights.reshape(-1))
    upstream_rows = jnp.take(upstream, owners, axis=0, mode="fill", fill_value=0.0)
    outgoing_grad = (
        (upstream_rows * slot_gate[:, None]).astype(jnp.bfloat16).reshape(arriving.shape)
    )
    arriving_grad = lax.all_to_all(outgoing_grad, "expert", split_axis=0, concat_axis=0, tiled=True)
    gate_sig, activated = activate(gate_pre)
    hidden = (activated * up_pre).astype(jnp.bfloat16)
    hidden_grad = jnp.einsum(
        "secd,def->secf", arriving_grad, w_down_full, preferred_element_type=jnp.float32
    )
    gate_grad = (hidden_grad * up_pre * gate_sig * (1.0 + gate_pre * (1.0 - gate_sig))).astype(
        jnp.bfloat16
    )
    up_grad = (hidden_grad * activated).astype(jnp.bfloat16)
    rows_grad = jnp.einsum(
        "secf,def->secd", gate_grad, w_gate_full, preferred_element_type=jnp.float32
    )
    rows_grad = rows_grad + jnp.einsum(
        "secf,def->secd", up_grad, w_up_full, preferred_element_type=jnp.float32
    )
    rows_grad = rows_grad.astype(jnp.bfloat16)
    expert_grads = lax.psum_scatter(
        jnp.stack(
            [
                jnp.einsum(
                    "secd,secf->def", arriving, gate_grad, preferred_element_type=jnp.float32
                ),
                jnp.einsum("secd,secf->def", arriving, up_grad, preferred_element_type=jnp.float32),
                jnp.einsum(
                    "secd,secf->def", arriving_grad, hidden, preferred_element_type=jnp.float32
                ),
            ],
            axis=1,
        ).astype(jnp.bfloat16),
        "fsdp",
        scatter_dimension=0,
        tiled=True,
    ).astype(jnp.float32)
    returned_grad = lax.all_to_all(rows_grad, "expert", split_axis=0, concat_axis=0, tiled=True)
    picked = jnp.take(returned_grad.reshape(-1, model_width), places, axis=0)
    picked = picked.reshape(choices.shape[0], choices.shape[1], model_width)
    normed_grad = jnp.sum(picked, axis=1, dtype=jnp.float32)
    gain_grad, middle_grad = rms_backward(middle, inverse, gain_ffn, normed_grad)
    return (upstream + middle_grad, gain_grad, expert_grads)


def attn_sums(terms):
    gain_a, gain_b, grad_wq, grad_wk, grad_wv, grad_wo = terms
    return (
        lax.psum_scatter(gain_a, ("fsdp", "expert"), scatter_dimension=0, tiled=True),
        lax.psum_scatter(gain_b, ("fsdp", "expert"), scatter_dimension=0, tiled=True),
        lax.psum_scatter(grad_wq, ("fsdp", "expert"), scatter_dimension=0, tiled=True),
        lax.psum_scatter(grad_wk, ("fsdp", "expert"), scatter_dimension=0, tiled=True),
        lax.psum_scatter(grad_wv, ("fsdp", "expert"), scatter_dimension=0, tiled=True),
        lax.psum_scatter(grad_wo, ("fsdp", "expert"), scatter_dimension=0, tiled=True),
    )


def shards(
    tokens,
    lengths,
    routes,
    gates,
    cotangent,
    norm_attn,
    norm_ffn,
    query,
    key,
    value,
    output,
    w_gate,
    w_up,
    w_down,
):
    token_rows = tokens.shape[0]
    layer_count = w_gate.shape[0]
    expert_count = w_gate.shape[2] * lax.axis_size("expert")
    capacity = 8 * max(1, token_rows * routes.shape[2] // (5 * expert_count))
    segment, seq_place = positions(lengths[0], token_rows)
    cosine_table, sine_table = rope_tables(seq_place, HEAD_DIMENSION)
    token_order = jnp.arange(token_rows, dtype=jnp.int32)
    allowed = (segment[:, None] == segment[None, :]) & (
        token_order[:, None] >= token_order[None, :]
    )
    residual = tokens.astype(jnp.float32)
    stored_weights = []
    stored_layers = []
    for layer_idx in range(layer_count):
        attn_full = (
            lax.all_gather(norm_attn[layer_idx], ("fsdp", "expert"), axis=0, tiled=True),
            lax.all_gather(norm_ffn[layer_idx], ("fsdp", "expert"), axis=0, tiled=True),
            lax.all_gather(query[layer_idx], ("fsdp", "expert"), axis=0, tiled=True),
            lax.all_gather(key[layer_idx], ("fsdp", "expert"), axis=0, tiled=True),
            lax.all_gather(value[layer_idx], ("fsdp", "expert"), axis=0, tiled=True),
            lax.all_gather(output[layer_idx], ("fsdp", "expert"), axis=0, tiled=True),
        )
        expert_full = (
            lax.all_gather(w_gate[layer_idx], "fsdp", axis=0, tiled=True),
            lax.all_gather(w_up[layer_idx], "fsdp", axis=0, tiled=True),
            lax.all_gather(w_down[layer_idx], "fsdp", axis=0, tiled=True),
        )
        layer_input = residual
        middle, attn_stash = attend_forward(
            layer_input, allowed, cosine_table, sine_table, attn_full
        )
        residual, moe_stash = experts_forward(
            middle,
            attn_full[1],
            routes[layer_idx],
            gates[layer_idx],
            expert_full,
            capacity,
            expert_count,
        )
        stored_layers.append((layer_input, middle, attn_stash, moe_stash))
        stored_weights.append(None)
    result = residual.astype(jnp.bfloat16)
    upstream = cotangent.astype(jnp.float32)
    attn_grad_list = [None] * layer_count
    expert_grad_list = [None] * layer_count
    for layer_idx in reversed(range(layer_count)):
        attn_full = (
            lax.all_gather(norm_attn[layer_idx], ("fsdp", "expert"), axis=0, tiled=True),
            lax.all_gather(norm_ffn[layer_idx], ("fsdp", "expert"), axis=0, tiled=True),
            lax.all_gather(query[layer_idx], ("fsdp", "expert"), axis=0, tiled=True),
            lax.all_gather(key[layer_idx], ("fsdp", "expert"), axis=0, tiled=True),
            lax.all_gather(value[layer_idx], ("fsdp", "expert"), axis=0, tiled=True),
            lax.all_gather(output[layer_idx], ("fsdp", "expert"), axis=0, tiled=True),
        )
        expert_full = (
            lax.all_gather(w_gate[layer_idx], "fsdp", axis=0, tiled=True),
            lax.all_gather(w_up[layer_idx], "fsdp", axis=0, tiled=True),
            lax.all_gather(w_down[layer_idx], "fsdp", axis=0, tiled=True),
        )
        layer_input, middle, attn_stash, moe_stash = stored_layers[layer_idx]
        upstream, gain_ffn_grad, expert_grads = experts_backward(
            middle,
            attn_full[1],
            routes[layer_idx],
            gates[layer_idx],
            expert_full,
            moe_stash,
            upstream,
        )
        upstream, attn_terms = attend_backward(
            layer_input, allowed, cosine_table, sine_table, attn_full, attn_stash, upstream
        )
        gain_attn_grad, grad_wq, grad_wk, grad_wv, grad_wo = attn_terms
        attn_grad_list[layer_idx] = attn_sums(
            (gain_attn_grad, gain_ffn_grad, grad_wq, grad_wk, grad_wv, grad_wo)
        )
        expert_grad_list[layer_idx] = expert_grads
    grad_norm_attn = jnp.stack([entry[0] for entry in attn_grad_list])
    grad_norm_ffn = jnp.stack([entry[1] for entry in attn_grad_list])
    grad_query = jnp.stack([entry[2] for entry in attn_grad_list])
    grad_key = jnp.stack([entry[3] for entry in attn_grad_list])
    grad_value = jnp.stack([entry[4] for entry in attn_grad_list])
    grad_output = jnp.stack([entry[5] for entry in attn_grad_list])
    grad_w_gate = jnp.stack([entry[:, 0] for entry in expert_grad_list])
    grad_w_up = jnp.stack([entry[:, 1] for entry in expert_grad_list])
    grad_w_down = jnp.stack([entry[:, 2] for entry in expert_grad_list])
    return (
        result,
        upstream,
        grad_norm_attn,
        grad_norm_ffn,
        grad_query,
        grad_key,
        grad_value,
        grad_output,
        grad_w_gate,
        grad_w_up,
        grad_w_down,
    )


def solution(mesh):
    in_specs = (
        P(("fsdp", "expert"), None),
        P(("fsdp", "expert"), None),
        P(None, ("fsdp", "expert"), None),
        P(None, ("fsdp", "expert"), None),
        P(("fsdp", "expert"), None),
        P(None, ("fsdp", "expert")),
        P(None, ("fsdp", "expert")),
        P(None, ("fsdp", "expert"), None),
        P(None, ("fsdp", "expert"), None),
        P(None, ("fsdp", "expert"), None),
        P(None, ("fsdp", "expert"), None),
        P(None, "fsdp", "expert", None),
        P(None, "fsdp", "expert", None),
        P(None, "fsdp", "expert", None),
    )
    out_specs = (
        P(("fsdp", "expert"), None),
        P(("fsdp", "expert"), None),
        P(None, ("fsdp", "expert")),
        P(None, ("fsdp", "expert")),
        P(None, ("fsdp", "expert"), None),
        P(None, ("fsdp", "expert"), None),
        P(None, ("fsdp", "expert"), None),
        P(None, ("fsdp", "expert"), None),
        P(None, "fsdp", "expert", None),
        P(None, "fsdp", "expert", None),
        P(None, "fsdp", "expert", None),
    )
    return jax.shard_map(shards, mesh=mesh, in_specs=in_specs, out_specs=out_specs, check_vma=False)
```

profile of v0, /device:TPU:0, one launch (start us, length us, event | category | flops | bytes accessed | tf_op | source)
XLA Modules:
  0.0 2782.5 jit_solution(11801197462531285664)
XLA Ops:
  36.5 42.3 %all-reduce.9 = (bf16[1536]{0:T(1024)(128)(2,1)S(1)}, bf16[1536]{0:T(1024)(128)(2,1)S(1)}, bf16[1536]{0:T(1024)(128)(2,1)S(1)}, bf16[1536]{0:T(1024)(128)(2,1)S(1)}) all-reduce(bf16[1536]{0:T(1024)(128)(2,1)S(1)} %dynamic-update-slice, bf16[1536]{0:T(1024)(128)(2,1)S(1)} %dynamic-update-slice.1, ...), channel_id=2, replica_groups=mesh['fsdp'=8,'expert'=4] {'fsdp','expert'}, use_global_device_ids=true, to_apply=%add | all-reduce | flops 6144 | bytes 24576
  81.8 44.5 %all-gather.33.cloned.1.call-done = bf16[1,1536,512]{2,1,0:T(8,128)(2,1)} async-done(((bf16[1,48,512]{2,1,0:T(8,128)(2,1)}), bf16[1,1536,512]{2,1,0:T(8,128)(2,1)}) %all-gather.33.cloned.1.call-update) | async-done | bytes 1572880 | tf_op jit(solution)/shard_map/all_gather | solution.py:323
  128.3 63.9 %all-gather.37.cloned.1.call-done = bf16[1,1536,1536]{2,1,0:T(8,128)(2,1)} async-done(((bf16[1,48,1536]{2,1,0:T(8,128)(2,1)}), bf16[1,1536,1536]{2,1,0:T(8,128)(2,1)}) %all-gather.37.cloned.1.call-update) | async-done | bytes 4718608 | tf_op jit(solution)/shard_map/all_gather | solution.py:321
  199.4 58.5 %all-gather.39.cloned.1.call-done = bf16[1,1536,1536]{2,1,0:T(8,128)(2,1)} async-done(((bf16[1,48,1536]{2,1,0:T(8,128)(2,1)}), bf16[1,1536,1536]{2,1,0:T(8,128)(2,1)}) %all-gather.39.cloned.1.call-update) | async-done | bytes 4718608 | tf_op jit(solution)/shard_map/all_gather | solution.py:324
  271.2 60.2 %all_to_all.40 = bf16[4,5,80,1536]{3,2,1,0:T(8,128)(2,1)} all-to-all(bf16[4,5,80,1536]{3,2,1,0:T(8,128)(2,1)S(1)} %bitcast.519), channel_id=1, replica_groups=mesh['fsdp'=8,'expert'=4] {'expert'}, dimensions={0} | all-to-all | bytes 9830400 | tf_op jit(solution)/shard_map/all_to_all | solution.py:208
  336.6 9.1 fusion.14
  345.7 69.2 %all-gather.43.cloned.1.call-done = bf16[1,1536,5,512]{3,1,2,0:T(8,128)(2,1)} async-done(((bf16[1,192,5,512]{3,1,2,0:T(8,128)(2,1)}), bf16[1,1536,5,512]{3,1,2,0:T(8,128)(2,1)}) %all-gather.43.cloned.1.call-update) | async-done | bytes 7864336 | tf_op jit(solution)/shard_map/all_gather | solution.py:328
  414.9 10.1 fusion.75
  425.0 68.4 %all-gather.45.cloned.1.call-done = bf16[1,1536,5,512]{3,1,2,0:T(8,128)(2,1)} async-done(((bf16[1,192,5,512]{3,1,2,0:T(8,128)(2,1)}), bf16[1,1536,5,512]{3,1,2,0:T(8,128)(2,1)}) %all-gather.45.cloned.1.call-update) | async-done | bytes 7864336 | tf_op jit(solution)/shard_map/all_gather | solution.py:329
  493.4 8.7 convert_bitcast_fusion.1
  523.3 46.6 %all-to-all-done.1 = bf16[4,5,80,1536]{3,2,1,0:T(8,128)(2,1)} async-done(((bf16[4,5,80,1536]{3,2,1,0:T(8,128)(2,1)}), bf16[4,5,80,1536]{3,2,1,0:T(8,128)(2,1)}, u32[]{:S(2)}, u32[]{:S(2)}) %all-to-all-start.1) | async-done | bytes 4915232 | tf_op jit(solution)/shard_map/all_to_all | solution.py:215
  569.9 10.3 gather_fusion.1
  586.2 38.0 %all-gather.49.cloned.1.call-done = bf16[1,1536,512]{2,1,0:T(8,128)(2,1)} async-done(((bf16[1,48,512]{2,1,0:T(8,128)(2,1)}), bf16[1,1536,512]{2,1,0:T(8,128)(2,1)}) %all-gather.49.cloned.1.call-update) | async-done | bytes 1572880 | tf_op jit(solution)/shard_map/all_gather | solution.py:322
  627.0 62.9 %all-gather.51.cloned.1.call-done = bf16[1,1536,1536]{2,1,0:T(8,128)(2,1)} async-done(((bf16[1,48,1536]{2,1,0:T(8,128)(2,1)}), bf16[1,1536,1536]{2,1,0:T(8,128)(2,1)}) %all-gather.51.cloned.1.call-update) | async-done | bytes 4718608 | tf_op jit(solution)/shard_map/all_gather | solution.py:321
  696.4 59.5 %all-gather.53.cloned.1.call-done = bf16[1,1536,1536]{2,1,0:T(8,128)(2,1)} async-done(((bf16[1,48,1536]{2,1,0:T(8,128)(2,1)}), bf16[1,1536,1536]{2,1,0:T(8,128)(2,1)}) %all-gather.53.cloned.1.call-update) | async-done | bytes 4718608 | tf_op jit(solution)/shard_map/all_gather | solution.py:324
  797.7 35.3 %all-to-all-done.2 = bf16[4,5,80,1536]{3,2,1,0:T(8,128)(2,1)} async-done(((bf16[4,5,80,1536]{3,2,1,0:T(8,128)(2,1)}), bf16[4,5,80,1536]{3,2,1,0:T(8,128)(2,1)}, u32[]{:S(2)}, u32[]{:S(2)}) %all-to-all-start.2) | async-done | bytes 4915232 | tf_op jit(solution)/shard_map/all_to_all | solution.py:208
  838.2 9.9 fusion.26
  848.1 63.7 %all-gather.57.cloned.1.call-done = bf16[1,1536,5,512]{3,1,2,0:T(8,128)(2,1)} async-done(((bf16[1,192,5,512]{3,1,2,0:T(8,128)(2,1)}), bf16[1,1536,5,512]{3,1,2,0:T(8,128)(2,1)}) %all-gather.57.cloned.1.call-update) | async-done | bytes 7864336 | tf_op jit(solution)/shard_map/all_gather | solution.py:328
  911.8 9.1 fusion.22
  920.9 68.7 %all-gather.59.cloned.1.call-done = bf16[1,1536,5,512]{3,1,2,0:T(8,128)(2,1)} async-done(((bf16[1,192,5,512]{3,1,2,0:T(8,128)(2,1)}), bf16[1,1536,5,512]{3,1,2,0:T(8,128)(2,1)}) %all-gather.59.cloned.1.call-update) | async-done | bytes 7864336 | tf_op jit(solution)/shard_map/all_gather | solution.py:329
  989.6 11.5 fusion.68
  1006.4 11.8 fusion.32
  1037.3 46.7 %all-to-all-done.5 = bf16[4,5,80,1536]{3,2,1,0:T(8,128)(2,1)} async-done(((bf16[4,5,80,1536]{3,2,1,0:T(8,128)(2,1)}), bf16[4,5,80,1536]{3,2,1,0:T(8,128)(2,1)}, u32[]{:S(2)}, u32[]{:S(2)}) %all-to-all-start.5) | async-done | bytes 4915232 | tf_op jit(solution)/shard_map/all_to_all | solution.py:268
  1096.2 10.5 gather_fusion.5
  1113.9 30.1 %all-to-all-done.3 = bf16[4,5,80,1536]{3,2,1,0:T(8,128)(2,1)} async-done(((bf16[4,5,80,1536]{3,2,1,0:T(8,128)(2,1)}), bf16[4,5,80,1536]{3,2,1,0:T(8,128)(2,1)}, u32[]{:S(2)}, u32[]{:S(2)}) %all-to-all-start.3) | async-done | bytes 4915232 | tf_op jit(solution)/shard_map/all_to_all | solution.py:215
  1144.0 10.4 gather_fusion.3
  1184.0 58.0 %all_to_all.41 = bf16[4,5,80,1536]{3,2,1,0:T(8,128)(2,1)S(1)} all-to-all(bf16[4,5,80,1536]{3,2,1,0:T(8,128)(2,1)S(1)} %bitcast.517), channel_id=1, replica_groups=mesh['fsdp'=8,'expert'=4] {'expert'}, dimensions={0} | all-to-all | bytes 9830400 | tf_op jit(solution)/shard_map/all_to_all | solution.py:234
  1242.0 10.5 fusion.64
  1257.8 11.5 fusion.33
  1282.4 50.4 %all-to-all-done.7 = bf16[4,5,80,1536]{3,2,1,0:T(8,128)(2,1)} async-done(((bf16[4,5,80,1536]{3,2,1,0:T(8,128)(2,1)}), bf16[4,5,80,1536]{3,2,1,0:T(8,128)(2,1)}, u32[]{:S(2)}, u32[]{:S(2)}) %all-to-all-start.7) | async-done | bytes 4915232 | tf_op jit(solution)/shard_map/all_to_all | solution.py:268
  1332.8 10.7 gather_fusion.7
  1401.0 9.0 fusion.6
  1410.1 8.9 fusion.7
  1418.9 17.0 pad_maximum_fusion.1
  1435.9 27.9 %copy.232 = bf16[1536,7680]{1,0:T(8,128)(2,1)} copy(bf16[1536,7680]{0,1:T(8,128)(2,1)} %bitcast.514) | data formatting | bytes 47185920
  1471.6 9.0 fusion.2
  1480.6 8.8 fusion.3
  1489.4 16.8 pad_maximum_fusion
  1506.3 29.5 %copy.230 = bf16[1536,7680]{1,0:T(8,128)(2,1)} copy(bf16[1536,7680]{0,1:T(8,128)(2,1)} %bitcast.515) | data formatting | bytes 47185920
  1541.7 41.3 %all-reduce.8 = (f32[1536]{0:T(1024)S(1)}, f32[1536]{0:T(1024)S(1)}, f32[1536]{0:T(1024)S(1)}, f32[1536]{0:T(1024)S(1)}) all-reduce(f32[1536]{0:T(1024)S(1)} %copy-done.101, f32[1536]{0:T(1024)S(1)} %get-tuple-element.64, f32[1536]{0:T(1024)S(1)} %copy-done.100, ...), channel_id=21, replica_groups=mesh['fsdp'=8,'expert'=4] {'fsdp','expert'}, use_global_device_ids=true, to_apply=%region_32.36.clone | all-reduce | flops 6144 | bytes 49152
  1587.0 12.1 reduce-scatter.21.cloned.1.call-done
  1599.1 106.3 %reduce-scatter.19.cloned.1.call-done = f32[48,512]{1,0:T(8,128)} async-done(((f32[1536,512]{1,0:T(8,128)}), f32[48,512]{1,0:T(8,128)}) %reduce-scatter.19.cloned.1.call-update) | async-done | bytes 98320 | tf_op jit(solution)/shard_map/reduce_scatter | solution.py:282
  1707.1 138.8 %reduce-scatter.29.cloned.1.call-done = f32[48,1536]{1,0:T(8,128)} async-done(((f32[1536,1536]{1,0:T(8,128)}), f32[48,1536]{1,0:T(8,128)}) %reduce-scatter.29.cloned.1.call-update) | async-done | bytes 294928 | tf_op jit(solution)/shard_map/reduce_scatter | solution.py:284
  1845.9 141.4 %reduce-scatter.27.cloned.1.call-done = f32[48,1536]{1,0:T(8,128)} async-done(((f32[1536,1536]{1,0:T(8,128)}), f32[48,1536]{1,0:T(8,128)}) %reduce-scatter.27.cloned.1.call-update) | async-done | bytes 294928 | tf_op jit(solution)/shard_map/reduce_scatter | solution.py:284
  1989.2 138.6 %reduce-scatter.17.cloned.1.call-done = f32[48,1536]{1,0:T(8,128)} async-done(((f32[1536,1536]{1,0:T(8,128)}), f32[48,1536]{1,0:T(8,128)}) %reduce-scatter.17.cloned.1.call-update) | async-done | bytes 294928 | tf_op jit(solution)/shard_map/reduce_scatter | solution.py:281
  2127.8 141.5 %reduce-scatter.15.cloned.1.call-done = f32[48,1536]{1,0:T(8,128)} async-done(((f32[1536,1536]{1,0:T(8,128)}), f32[48,1536]{1,0:T(8,128)}) %reduce-scatter.15.cloned.1.call-update) | async-done | bytes 294928 | tf_op jit(solution)/shard_map/reduce_scatter | solution.py:281
  2271.2 232.0 %reduce-scatter.33.cloned.1.call-done = bf16[192,7680]{1,0:T(8,128)(2,1)} async-done(((bf16[1536,7680]{1,0:T(8,128)(2,1)}), bf16[192,7680]{1,0:T(8,128)(2,1)}) %reduce-scatter.33.cloned.1.call-update) | async-done | bytes 2949136
  2516.0 220.2 %reduce-scatter.31.cloned.1.call-done = bf16[192,7680]{1,0:T(8,128)(2,1)} async-done(((bf16[1536,7680]{1,0:T(8,128)(2,1)}), bf16[192,7680]{1,0:T(8,128)(2,1)}) %reduce-scatter.31.cloned.1.call-update) | async-done | bytes 2949136
  (534 shorter events, 365.7 us)
Async XLA Ops:
  7.2 72.4 %all-gather.35.cloned.1.call-start = ((), (), s32[]{:S(2)}) async-start(), calls=%async_computation.27 | async-start | bytes 1622016 | tf_op jit(solution)/shard_map/all_gather | solution.py:322
  8.8 117.4 %all-gather.33.cloned.1.call-start = ((), (), s32[]{:S(2)}) async-start(), calls=%async_computation.26 | async-start | bytes 1622016 | tf_op jit(solution)/shard_map/all_gather | solution.py:323
  10.4 181.8 %all-gather.37.cloned.1.call-start = ((), (), s32[]{:S(2)}) async-start(), calls=%async_computation.28 | async-start | bytes 4866048 | tf_op jit(solution)/shard_map/all_gather | solution.py:321
  12.2 245.8 %all-gather.39.cloned.1.call-start = ((), (), s32[]{:S(2)}) async-start(), calls=%async_computation.29 | async-start | bytes 4866048 | tf_op jit(solution)/shard_map/all_gather | solution.py:324
  14.0 322.6 %all-gather.41.cloned.1.call-start = ((), (), s32[]{:S(2)}) async-start(), calls=%async_computation.30 | async-start | bytes 8847360 | tf_op jit(solution)/shard_map/all_gather | solution.py:327
  15.5 399.4 %all-gather.43.cloned.1.call-start = ((), (), s32[]{:S(2)}) async-start(), calls=%async_computation.31 | async-start | bytes 8847360 | tf_op jit(solution)/shard_map/all_gather | solution.py:328
  18.6 474.8 %all-gather.45.cloned.1.call-start = ((), (), s32[]{:S(2)}) async-start(), calls=%async_computation.32 | async-start | bytes 8847360 | tf_op jit(solution)/shard_map/all_gather | solution.py:329
  20.2 563.3 %all-gather.47.cloned.1.call-start = ((), (), s32[]{:S(2)}) async-start(), calls=%async_computation.33 | async-start | bytes 1622016 | tf_op jit(solution)/shard_map/all_gather | solution.py:323
  21.0 603.2 %all-gather.49.cloned.1.call-start = ((), (), s32[]{:S(2)}) async-start(), calls=%async_computation.34 | async-start | bytes 1622016 | tf_op jit(solution)/shard_map/all_gather | solution.py:322
  21.7 668.3 %all-gather.51.cloned.1.call-start = ((), (), s32[]{:S(2)}) async-start(), calls=%async_computation.35 | async-start | bytes 4866048 | tf_op jit(solution)/shard_map/all_gather | solution.py:321
  22.3 733.5 %all-gather.53.cloned.1.call-start = ((), (), s32[]{:S(2)}) async-start(), calls=%async_computation.36 | async-start | bytes 4866048 | tf_op jit(solution)/shard_map/all_gather | solution.py:324
  23.0 815.2 %all-gather.55.cloned.1.call-start = ((), (), s32[]{:S(2)}) async-start(), calls=%async_computation.37 | async-start | bytes 8847360 | tf_op jit(solution)/shard_map/all_gather | solution.py:327
  23.6 888.2 %all-gather.57.cloned.1.call-start = ((), (), s32[]{:S(2)}) async-start(), calls=%async_computation.38 | async-start | bytes 8847360 | tf_op jit(solution)/shard_map/all_gather | solution.py:328
  30.9 539.0 %copy-start.96 = (s32[1024]{0:T(1024)}, s32[1024]{0:T(1024)S(1)}, u32[]{:S(2)}) copy-start(s32[1024]{0:T(1024)S(1)} %get-tuple-element.131) | copy-start | bytes 12292
  35.5 232.8 %copy-start.108 = (pred[1600]{0:T(1024)(128)(4,1)}, pred[1600]{0:T(1024)(128)(4,1)S(1)}, u32[]{:S(2)}) copy-start(pred[1600]{0:T(1024)(128)(4,1)S(1)} %compare_and_fusion.1) | copy-start | bytes 4804
  78.8 117.7 %copy-start.58 = (f32[1536]{0:T(1024)}, f32[1536]{0:T(1024)S(1)}, u32[]{:S(2)}) copy-start(f32[1536]{0:T(1024)S(1)} %convert_element_type.280) | copy-start | bytes 18436
  79.0 117.6 %copy-start.103 = (f32[128]{0:T(128)}, f32[128]{0:T(128)S(1)}, u32[]{:S(2)}) copy-start(f32[128]{0:T(128)S(1)} %add_rsqrt_fusion.3) | copy-start | bytes 1540
  79.4 117.3 %copy-start.111 = (pred[128,128]{0,1:T(8,128)(4,1)}, pred[128,128]{0,1:T(8,128)(4,1)S(1)}, u32[]{:S(2)}) copy-start(pred[128,128]{0,1:T(8,128)(4,1)S(1)} %fusion.170) | copy-start | bytes 49156
  79.4 181.8 %copy-start.75 = (f32[1536]{0:T(1024)}, f32[1536]{0:T(1024)S(1)}, u32[]{:S(2)}) copy-start(f32[1536]{0:T(1024)S(1)} %convert_element_type.281) | copy-start | bytes 18436
  79.4 181.9 %copy-start.82 = (s32[2048]{0:T(1024)}, s32[2048]{0:T(1024)S(1)}, u32[]{:S(2)}) copy-start(s32[2048]{0:T(1024)S(1)} %pad_clamp_fusion.1) | copy-start | bytes 24580
  79.6 614.8 %copy-start.39 = (f32[128,32]{0,1:T(8,128)}, f32[128,32]{0,1:T(8,128)S(1)}, u32[]{:S(2)}) copy-start(f32[128,32]{0,1:T(8,128)S(1)} %get-tuple-element.134) | copy-start | bytes 49156
  128.3 69.9 %copy-start.62 = (bf16[128,512]{0,1:T(8,128)(2,1)}, bf16[128,512]{0,1:T(8,128)(2,1)S(1)}, u32[]{:S(2)}) copy-start(bf16[128,512]{0,1:T(8,128)(2,1)S(1)} %copy.143) | copy-start | bytes 393220
  261.2 322.0 %copy-start.6 = (f32[128,1536]{1,0:T(8,128)}, f32[128,1536]{1,0:T(8,128)S(1)}, u32[]{:S(2)}) copy-start(f32[128,1536]{1,0:T(8,128)S(1)} %get-tuple-element.142) | copy-start | bytes 2359300
  425.0 77.1 %copy-start.23 = (bf16[4,5,80,512]{3,2,0,1:T(8,128)(2,1)}, bf16[4,5,80,512]{3,2,0,1:T(8,128)(2,1)S(1)}, u32[]{:S(2)}) copy-start(bf16[4,5,80,512]{3,2,0,1:T(8,128)(2,1)S(1)} %get-tuple-element.143) | copy-start | bytes 4915204
  504.7 65.1 %all-to-all-start.1 = ((bf16[4,5,80,1536]{3,2,1,0:T(8,128)(2,1)}), bf16[4,5,80,1536]{3,2,1,0:T(8,128)(2,1)}, u32[]{:S(2)}, u32[]{:S(2)}) async-start(bf16[4,5,80,1536]{3,2,1,0:T(8,128)(2,1)} %copy.154), calls=%async_computation.1 | async-start | bytes 9830400 | tf_op jit(solution)/shard_map/all_to_all | solution.py:215
  509.9 479.7 %all-gather.59.cloned.1.call-start = ((), (), s32[]{:S(2)}) async-start(), calls=%async_computation.39 | async-start | bytes 8847360 | tf_op jit(solution)/shard_map/all_gather | solution.py:329
  510.7 69.4 %copy-start.92 = (s32[1024]{0:T(1024)}, s32[1024]{0:T(1024)S(1)}, u32[]{:S(2)}) copy-start(s32[1024]{0:T(1024)S(1)} %eq.74) | copy-start | bytes 12292
  523.1 237.0 %copy-start.83 = (s32[2048]{0:T(1024)}, s32[2048]{0:T(1024)S(1)}, u32[]{:S(2)}) copy-start(s32[2048]{0:T(1024)S(1)} %pad_clamp_fusion) | copy-start | bytes 24580
  523.2 235.9 %copy-start.79 = (f32[1536]{0:T(1024)}, f32[1536]{0:T(1024)S(1)}, u32[]{:S(2)}) copy-start(f32[1536]{0:T(1024)S(1)} %convert_element_type.283) | copy-start | bytes 18436
  523.3 243.8 %copy-start.110 = (pred[1600]{0:T(1024)(128)(4,1)}, pred[1600]{0:T(1024)(128)(4,1)S(1)}, u32[]{:S(2)}) copy-start(pred[1600]{0:T(1024)(128)(4,1)S(1)} %compare_and_fusion) | copy-start | bytes 4804
  583.3 110.9 %copy-start.117 = (f32[128]{0:T(128)}, f32[128]{0:T(128)S(1)}, u32[]{:S(2)}) copy-start(f32[128]{0:T(128)S(1)} %add_rsqrt_fusion.1) | copy-start | bytes 1540
  583.5 110.8 %copy-start.4 = (bf16[128,1536]{1,0:T(8,128)(2,1)}, bf16[128,1536]{1,0:T(8,128)(2,1)S(1)}, u32[]{:S(2)}) copy-start(bf16[128,1536]{1,0:T(8,128)(2,1)S(1)} %multiply_convert_fusion.1) | copy-start | bytes 1179652
  772.1 61.0 %all-to-all-start.2 = ((bf16[4,5,80,1536]{3,2,1,0:T(8,128)(2,1)}), bf16[4,5,80,1536]{3,2,1,0:T(8,128)(2,1)}, u32[]{:S(2)}, u32[]{:S(2)}) async-start(bf16[4,5,80,1536]{3,2,1,0:T(8,128)(2,1)} %bitcast.518), calls=%async_computation.2 | async-start | bytes 9830400 | tf_op jit(solution)/shard_map/all_to_all | solution.py:208
  833.1 87.9 %all-to-all-start.4 = ((bf16[4,5,80,1536]{3,2,1,0:T(8,128)(2,1)}), bf16[4,5,80,1536]{3,2,1,0:T(8,128)(2,1)}, u32[]{:S(2)}, u32[]{:S(2)}) async-start(bf16[4,5,80,1536]{3,2,1,0:T(8,128)(2,1)} %bitcast.516), calls=%async_computation.4 | async-start | bytes 9830400 | tf_op jit(solution)/shard_map/all_to_all | solution.py:234
  1023.2 60.8 %all-to-all-start.5 = ((bf16[4,5,80,1536]{3,2,1,0:T(8,128)(2,1)}), bf16[4,5,80,1536]{3,2,1,0:T(8,128)(2,1)}, u32[]{:S(2)}, u32[]{:S(2)}) async-start(bf16[4,5,80,1536]{3,2,1,0:T(8,128)(2,1)} %copy.169), calls=%async_computation.5 | async-start | bytes 9830400 | tf_op jit(solution)/shard_map/all_to_all | solution.py:268
  1084.0 60.0 %all-to-all-start.3 = ((bf16[4,5,80,1536]{3,2,1,0:T(8,128)(2,1)}), bf16[4,5,80,1536]{3,2,1,0:T(8,128)(2,1)}, u32[]{:S(2)}, u32[]{:S(2)}) async-start(bf16[4,5,80,1536]{3,2,1,0:T(8,128)(2,1)} %copy.166), calls=%async_computation.3 | async-start | bytes 9830400 | tf_op jit(solution)/shard_map/all_to_all | solution.py:215
  1183.9 68.5 %slice-start.2 = ((s8[7864320]{0:T(1024)(128)(4,1)}), s8[4194304]{0:T(1024)(128)(4,1)S(1)}, s32[]{:S(2)}) async-start(s8[7864320]{0:T(1024)(128)(4,1)} %bitcast.524), calls=%async_computation.44 | async-start | bytes 8388608
  1274.2 58.6 %all-to-all-start.7 = ((bf16[4,5,80,1536]{3,2,1,0:T(8,128)(2,1)}), bf16[4,5,80,1536]{3,2,1,0:T(8,128)(2,1)}, u32[]{:S(2)}, u32[]{:S(2)}) async-start(bf16[4,5,80,1536]{3,2,1,0:T(8,128)(2,1)} %copy.176), calls=%async_computation.7 | async-start | bytes 9830400 | tf_op jit(solution)/shard_map/all_to_all | solution.py:268
  1279.4 306.0 %reduce-scatter.25.cloned.1.call-start = ((), (), s32[]{:S(2)}) async-start(), calls=%async_computation.23 | async-start | bytes 3244032 | tf_op jit(solution)/shard_map/reduce_scatter | solution.py:283
  1281.7 303.7 %reduce-scatter.23.cloned.1.call-start = ((), (), s32[]{:S(2)}) async-start(), calls=%async_computation.22 | async-start | bytes 3244032 | tf_op jit(solution)/shard_map/reduce_scatter | solution.py:283
  1361.6 237.5 %reduce-scatter.21.cloned.1.call-start = ((), (), s32[]{:S(2)}) async-start(), calls=%async_computation.21 | async-start | bytes 3244032 | tf_op jit(solution)/shard_map/reduce_scatter | solution.py:282
  1364.9 340.6 %reduce-scatter.19.cloned.1.call-start = ((), (), s32[]{:S(2)}) async-start(), calls=%async_computation.20 | async-start | bytes 3244032 | tf_op jit(solution)/shard_map/reduce_scatter | solution.py:282
  1370.2 475.6 %reduce-scatter.29.cloned.1.call-start = ((), (), s32[]{:S(2)}) async-start(), calls=%async_computation.25 | async-start | bytes 9732096 | tf_op jit(solution)/shard_map/reduce_scatter | solution.py:284
  1375.4 611.8 %reduce-scatter.27.cloned.1.call-start = ((), (), s32[]{:S(2)}) async-start(), calls=%async_computation.24 | async-start | bytes 9732096 | tf_op jit(solution)/shard_map/reduce_scatter | solution.py:284
  1381.4 746.4 %reduce-scatter.17.cloned.1.call-start = ((), (), s32[]{:S(2)}) async-start(), calls=%async_computation.19 | async-start | bytes 9732096 | tf_op jit(solution)/shard_map/reduce_scatter | solution.py:281
  1386.7 882.6 %reduce-scatter.15.cloned.1.call-start = ((), (), s32[]{:S(2)}) async-start(), calls=%async_computation.18 | async-start | bytes 9732096 | tf_op jit(solution)/shard_map/reduce_scatter | solution.py:281
  1393.6 1109.6 %reduce-scatter.33.cloned.1.call-start = ((), (), s32[]{:S(2)}) async-start(), calls=%async_computation.41 | async-start | bytes 26542080
  1463.8 1272.4 %reduce-scatter.31.cloned.1.call-start = ((), (), s32[]{:S(2)}) async-start(), calls=%async_computation.40 | async-start | bytes 26542080
  (116 other events, 1607.8 us)
Sparse Core Ops, SparseCore 0:
  10.9 57.9 all-gather.34
  72.3 53.9 all-gather.32
  129.8 62.4 all-gather.36
  195.5 62.3 all-gather.38
  260.0 76.5 all-gather.40
  338.6 76.2 all-gather.42
  417.1 76.2 all-gather.44
  496.9 70.3 all-gather.46
  570.2 53.9 all-gather.48
  627.5 62.4 all-gather.50
  693.4 62.3 all-gather.52
  757.3 76.5 all-gather.54
  835.5 76.2 all-gather.56
  913.3 76.2 all-gather.58
  1285.9 100.5 reduce-scatter.24
  1391.8 100.4 reduce-scatter.22
  1498.2 100.8 reduce-scatter.20
  1605.0 100.4 reduce-scatter.18
  1711.4 134.4 reduce-scatter.28
  1852.6 134.5 reduce-scatter.26
  1993.2 134.5 reduce-scatter.16
  2134.7 134.5 reduce-scatter.14
  2271.7 231.4 reduce-scatter.32
  2505.4 230.7 reduce-scatter.30
where the time goes:
time: 2800 us; the launch traced here: 2780 us
  waiting for transfers between devices  1950 us (70%)
  matrix products  245 us (9%)
  local copies, waits for them, and re-layouts  226 us (8%)
  blocking collectives  202 us (7%)
  other arithmetic  113 us (4%)
  starting transfers between devices  32 us (1%)
    unnamed x26, waiting for transfers between devices  457 us
    reduce_scatter x2, waiting for transfers between devices, attn_sums(): lax.psum_scatter(grad_wo, ('fsdp', 'expert'), scatter_dimension=0, tiled=...  280 us
    reduce_scatter x2, waiting for transfers between devices, attn_sums(): lax.psum_scatter(grad_wq, ('fsdp', 'expert'), scatter_dimension=0, tiled=...  280 us
    all_gather x2, waiting for transfers between devices, shards(): lax.all_gather(w_down[layer_idx], 'fsdp', axis=0, tiled=True)  137 us
    all_gather x2, waiting for transfers between devices, shards(): lax.all_gather(w_up[layer_idx], 'fsdp', axis=0, tiled=True)  133 us
    all_gather x2, waiting for transfers between devices, shards(): lax.all_gather(query[layer_idx], ('fsdp', 'expert'), axis=0, tiled=True)  127 us
    reduce_scatter x2, waiting for transfers between devices, attn_sums(): lax.psum_scatter(grad_wk, ('fsdp', 'expert'), scatter_dimension=0, tiled=...  118 us
    all_gather x2, waiting for transfers between devices, shards(): lax.all_gather(output[layer_idx], ('fsdp', 'expert'), axis=0, tiled=True)  118 us
  transfers between devices with their start and end apart: 30, of which 24 were waited for; matrix products, arithmetic and copies ran while one was open for 15% of the time, Pallas kernels for 0%

commit v1 on v0

v1 whole, which is shorter than its diff:
```python
import math

import jax
import jax.numpy as jnp
from jax import lax
from jax.sharding import PartitionSpec as P

QUERY_HEADS = 24
KEY_VALUE_HEADS = 8
HEAD_DIMENSION = 64
CORES = 2

NORM_EPS = 1e-06
MASKED = -1000000000.0
AXES = ("fsdp", "expert")


class Place:
    def __init__(self):
        self.planes = lax.axis_size("fsdp") // CORES
        self.columns = lax.axis_size("expert")
        fsdp = lax.axis_index("fsdp")
        self.plane = fsdp // CORES
        self.core = fsdp % CORES
        self.column = lax.axis_index("expert")

    def hop(self, value, up=0, flip=0, swap=0):
        pairs = []
        for plane in range(self.planes):
            for core in range(CORES):
                for column in range(self.columns):
                    source = (plane * CORES + core) * self.columns + column
                    target = ((plane + up) % self.planes * CORES + (core ^ swap)) * self.columns
                    pairs.append((source, target + (column ^ flip)))
        return lax.ppermute(value, AXES, pairs)


def spread(place, block):
    if place.columns != 4:
        return [block] + [place.hop(block, flip=m) for m in range(1, place.columns)]
    half = block.shape[1] // 2
    one = place.hop(block, flip=1)
    two = place.hop(block, flip=2)
    head = place.hop(one[:, :half], flip=2)
    tail = place.hop(two[:, half:], flip=1)
    return [block, one, two, jnp.concatenate([head, tail], axis=1)]


def gather_tokens(place, block):
    own = block[None]
    others = jnp.stack([place.hop(block, up=k) for k in range(1, place.planes)])
    near = spread(place, own)
    far = spread(place, others)
    return [jnp.concatenate([a, b], axis=0) for a, b in zip(near, far)]


def fold(place, parts):
    wide = lambda value: value.astype(jnp.float32)
    if place.columns != 4:
        total = wide(parts[0])
        for m in range(1, place.columns):
            total = total + wide(place.hop(parts[m], flip=m))
        return total
    half = parts[0].shape[1] // 2
    head = place.hop(parts[3][:, :half], flip=2)
    tail = place.hop(parts[3][:, half:], flip=1)
    one_tail = place.hop(parts[1][:, half:], flip=1)
    two_head = place.hop(parts[2][:, :half], flip=2)
    one_head = place.hop((wide(parts[1][:, :half]) + wide(head)).astype(parts[1].dtype), flip=1)
    two_tail = place.hop((wide(parts[2][:, half:]) + wide(tail)).astype(parts[2].dtype), flip=2)
    upper = wide(parts[0][:, :half]) + wide(one_head) + wide(two_head)
    lower = wide(parts[0][:, half:]) + wide(one_tail) + wide(two_tail)
    return jnp.concatenate([upper, lower], axis=1)


def scatter_sums(place, parts):
    far = fold(place, [part[1:] for part in parts]).astype(parts[0].dtype)
    arrived = [place.hop(far[k - 1], up=-k) for k in range(1, place.planes)]
    total = fold(place, [part[:1] for part in parts])[0]
    for piece in arrived:
        total = total + piece.astype(jnp.float32)
    return total


def gather_gates(place, routes, gates, expert_count):
    names = jnp.arange(expert_count, dtype=jnp.int32)
    chosen = routes[:, None, :, :] == names[None, :, None, None]
    table = jnp.sum(jnp.where(chosen, gates[:, None, :, :], 0.0), axis=3)
    line = jnp.stack([table] + [place.hop(table, up=k) for k in range(1, place.planes)])
    owned = expert_count // place.columns
    found = []
    for m in range(place.columns):
        start = (place.column ^ m) * owned
        piece = lax.dynamic_slice_in_dim(line, start, owned, axis=2)
        found.append(place.hop(piece, flip=m) if m else piece)
    return found


def gather_experts(place, weights):
    rows, experts, hidden = weights[0].shape
    share = hidden // place.planes

    def cut(plane):
        pieces = [lax.dynamic_slice_in_dim(w, plane * share, share, axis=2) for w in weights]
        return jnp.stack([p.reshape(rows, experts * share) for p in pieces])

    own = [cut(place.plane)]
    for k in range(1, place.planes):
        own.append(place.hop(cut((place.plane + k) % place.planes), up=k))
    own = jnp.stack(own)
    sibling = place.hop(own, swap=1)
    both = jnp.concatenate([own, sibling])
    shard = jnp.arange(place.planes * CORES)
    index = ((shard % CORES) ^ place.core) * place.planes
    index = index + (place.plane - shard // CORES) % place.planes
    return [
        jnp.take(both[:, i], index, axis=0).reshape(-1, experts * share)
        for i in range(len(weights))
    ]


def scatter_experts(place, grads, experts):
    features, width = grads[0].shape
    rows = features // (place.planes * CORES)
    share = width // experts
    shape = (place.planes, CORES, rows, width)
    stacked = jnp.stack([g.reshape(shape) for g in grads], axis=1)
    mine = lax.dynamic_index_in_dim(stacked, place.core, axis=2, keepdims=False)
    others = lax.dynamic_index_in_dim(stacked, 1 - place.core, axis=2, keepdims=False)
    arrived = place.hop(others.astype(jnp.bfloat16), swap=1)
    total = (mine + arrived.astype(jnp.float32)).astype(jnp.bfloat16)
    pieces = [lax.dynamic_index_in_dim(total, place.plane, axis=0, keepdims=False)]
    for k in range(1, place.planes):
        target = (place.plane + k) % place.planes
        piece = lax.dynamic_index_in_dim(total, target, axis=0, keepdims=False)
        pieces.append(place.hop(piece, up=k))
    index = (place.plane - jnp.arange(place.planes)) % place.planes
    ordered = jnp.take(jnp.stack(pieces), index, axis=0)
    ordered = ordered.reshape(place.planes, len(grads), rows, experts, share)
    ordered = jnp.transpose(ordered, (1, 2, 3, 0, 4)).reshape(len(grads), rows, experts, -1)
    return [ordered[i].astype(jnp.float32) for i in range(len(grads))]


def positions(length_row, count_of_rows):
    ends = jnp.cumsum(length_row)
    token_order = jnp.arange(count_of_rows, dtype=jnp.int32)
    passed = token_order[:, None] >= ends[None, :]
    segment = jnp.sum(passed.astype(jnp.int32), axis=1)
    before = jnp.sum(jnp.where(passed, length_row[None, :], 0), axis=1)
    return (segment, token_order - before)


def rope_tables(seq_place, head_width):
    half_width = head_width // 2
    freq_table = jnp.exp(
        jnp.arange(half_width, dtype=jnp.float32) * (-2.0 * math.log(10000.0) / head_width)
    )
    angles = seq_place.astype(jnp.float32)[:, None] * freq_table[None, :]
    return (jnp.cos(angles), jnp.sin(angles))


def apply_rotation(vector, cosine_table, sine_table):
    half_width = vector.shape[-1] // 2
    former = vector[..., :half_width]
    latter = vector[..., half_width:]
    cos_wide = cosine_table[:, None, :]
    sin_wide = sine_table[:, None, :]
    return jnp.concatenate(
        [former * cos_wide - latter * sin_wide, latter * cos_wide + former * sin_wide], axis=-1
    )


def reverse_rotation(vector, cosine_table, sine_table):
    return apply_rotation(vector, cosine_table, -sine_table)


def rms_forward(residual, norm_gain):
    inverse = lax.rsqrt(jnp.mean(residual * residual, axis=-1, keepdims=True) + NORM_EPS)
    return (inverse, (residual * inverse * norm_gain).astype(jnp.bfloat16))


def rms_backward(residual, inverse, norm_gain, upstream):
    gain_grad = jnp.sum(upstream * residual * inverse, axis=0)
    scaled = upstream * norm_gain
    inner = jnp.mean(scaled * residual, axis=-1, keepdims=True)
    return (gain_grad, inverse * scaled - residual * inverse * inverse * inverse * inner)


def score_block(rotated_query, turned_k, allowed):
    scores = jnp.einsum(
        "qhgd,khd->hgqk", rotated_query, turned_k, preferred_element_type=jnp.float32
    ) * HEAD_DIMENSION ** (-0.5)
    return jnp.where(allowed, scores, MASKED)


def attend_forward(residual, allowed, tables, gain, matrices):
    w_in, w_output = matrices
    count_of_rows = residual.shape[0]
    query_width = QUERY_HEADS * HEAD_DIMENSION
    key_width = KEY_VALUE_HEADS * HEAD_DIMENSION
    inverse, normalized_input = rms_forward(residual, gain)
    projected = jnp.dot(normalized_input, w_in, preferred_element_type=jnp.float32)
    query_unrotated = projected[:, :query_width].reshape(count_of_rows, QUERY_HEADS, -1)
    key_unrotated = projected[:, query_width : query_width + key_width]
    key_unrotated = key_unrotated.reshape(count_of_rows, KEY_VALUE_HEADS, -1)
    value_rows = projected[:, query_width + key_width :].astype(jnp.bfloat16)
    value_rows = value_rows.reshape(count_of_rows, KEY_VALUE_HEADS, -1)
    rotated_query = (
        apply_rotation(query_unrotated, *tables)
        .astype(jnp.bfloat16)
        .reshape(count_of_rows, KEY_VALUE_HEADS, QUERY_HEADS // KEY_VALUE_HEADS, HEAD_DIMENSION)
    )
    turned_k = apply_rotation(key_unrotated, *tables).astype(jnp.bfloat16)
    scores = score_block(rotated_query, turned_k, allowed)
    row_top = jnp.max(scores, axis=-1, keepdims=True)
    exp_scores = jnp.exp(scores - row_top)
    row_total = jnp.sum(exp_scores, axis=-1, keepdims=True)
    attn_probs = (exp_scores / row_total).astype(jnp.bfloat16)
    log_total = row_top + jnp.log(row_total)
    mixed_heads = jnp.einsum(
        "hgqk,khd->qhgd", attn_probs, value_rows, preferred_element_type=jnp.float32
    )
    mixed_heads = mixed_heads.astype(jnp.bfloat16).reshape(count_of_rows, query_width)
    attn_out = jnp.dot(mixed_heads, w_output, preferred_element_type=jnp.float32)
    return (
        residual + attn_out,
        (inverse, normalized_input, rotated_query, turned_k, value_rows, log_total, mixed_heads),
    )


def attend_backward(residual, allowed, tables, gain, matrices, stash, upstream):
    w_in, w_output = matrices
    inverse, normalized_input, rotated_query, turned_k, value_rows, log_total, mixed_heads = stash
    count_of_rows = residual.shape[0]
    branch_grad = upstream.astype(jnp.bfloat16)
    grad_wo = jnp.einsum("td,te->de", mixed_heads, branch_grad, preferred_element_type=jnp.float32)
    mixed_gradient = jnp.einsum(
        "te,de->td", branch_grad, w_output, preferred_element_type=jnp.float32
    )
    mixed_gradient = mixed_gradient.astype(jnp.bfloat16).reshape(
        count_of_rows, KEY_VALUE_HEADS, QUERY_HEADS // KEY_VALUE_HEADS, HEAD_DIMENSION
    )
    attn_probs = jnp.exp(score_block(rotated_query, turned_k, allowed) - log_total)
    value_rows_gradient = jnp.einsum(
        "hgqk,qhgd->khd",
        attn_probs.astype(jnp.bfloat16),
        mixed_gradient,
        preferred_element_type=jnp.float32,
    )
    value_rows_gradient = value_rows_gradient.astype(jnp.bfloat16).reshape(count_of_rows, -1)
    grad_probs = jnp.einsum(
        "qhgd,khd->hgqk", mixed_gradient, value_rows, preferred_element_type=jnp.float32
    )
    grad_scores = attn_probs * (
        grad_probs - jnp.sum(attn_probs * grad_probs, axis=-1, keepdims=True)
    )
    grad_scores = grad_scores.astype(jnp.bfloat16)
    grad_tq = jnp.einsum(
        "hgqk,khd->qhgd", grad_scores, turned_k, preferred_element_type=jnp.float32
    ) * HEAD_DIMENSION ** (-0.5)
    turned_key_gradient = jnp.einsum(
        "hgqk,qhgd->khd", grad_scores, rotated_query, preferred_element_type=jnp.float32
    ) * HEAD_DIMENSION ** (-0.5)
    grad_query = reverse_rotation(
        grad_tq.reshape(count_of_rows, QUERY_HEADS, HEAD_DIMENSION), *tables
    )
    grad_query = grad_query.astype(jnp.bfloat16).reshape(count_of_rows, -1)
    grad_key = reverse_rotation(turned_key_gradient, *tables).astype(jnp.bfloat16)
    grad_key = grad_key.reshape(count_of_rows, -1)
    grad_in = jnp.concatenate([grad_query, grad_key, value_rows_gradient], axis=1)
    grad_w_in = jnp.einsum("td,te->de", normalized_input, grad_in, preferred_element_type=jnp.float32)
    grad_normed = jnp.einsum("te,de->td", grad_in, w_in, preferred_element_type=jnp.float32)
    gain_grad, residual_grad = rms_backward(residual, inverse, gain, grad_normed)
    return (upstream + residual_grad, gain_grad, grad_w_in, grad_wo)


def widen(gate_columns, share):
    return jnp.repeat(gate_columns, share, axis=1)


def experts_forward(place, middle, gain, gate_parts, weights):
    w_gate, w_up, w_down = weights
    share = w_gate.shape[1] // gate_parts[0].shape[1]
    model_width = middle.shape[1]
    inverse, normalized_input = rms_forward(middle, gain)
    chunks = gather_tokens(place, normalized_input)
    parts, kept = [], []
    for chunk, gate_columns in zip(chunks, gate_parts):
        rows = chunk.reshape(-1, model_width)
        gate_pre = jnp.dot(rows, w_gate, preferred_element_type=jnp.float32)
        up_pre = jnp.dot(rows, w_up, preferred_element_type=jnp.float32)
        weighed = gate_pre * jax.nn.sigmoid(gate_pre) * up_pre * widen(gate_columns, share)
        weighed = weighed.astype(jnp.bfloat16)
        produced = lax.dot_general(
            weighed, w_down, (((1,), (1,)), ((), ())), preferred_element_type=jnp.float32
        )
        parts.append(produced.astype(jnp.bfloat16).reshape(chunk.shape))
        kept.append((rows, gate_pre, up_pre, weighed))
    return (middle + scatter_sums(place, parts), (inverse, kept))


def experts_backward(place, middle, gain, gate_parts, weights, stash, upstream, chunks):
    w_gate, w_up, w_down = weights
    share = w_gate.shape[1] // gate_parts[0].shape[1]
    model_width = middle.shape[1]
    inverse, kept = stash
    parts, gate_grads, up_grads, row_grads = [], [], [], []
    for chunk, gate_columns, (rows, gate_pre, up_pre, weighed) in zip(chunks, gate_parts, kept):
        grads = chunk.reshape(-1, model_width)
        hidden_grad = jnp.dot(grads, w_down, preferred_element_type=jnp.float32)
        hidden_grad = hidden_grad * widen(gate_columns, share)
        gate_sig = jax.nn.sigmoid(gate_pre)
        gate_grad = hidden_grad * up_pre * gate_sig * (1.0 + gate_pre * (1.0 - gate_sig))
        gate_grad = gate_grad.astype(jnp.bfloat16)
        up_grad = (hidden_grad * gate_pre * gate_sig).astype(jnp.bfloat16)
        back = (((1,), (1,)), ((), ()))
        produced = lax.dot_general(gate_grad, w_gate, back, preferred_element_type=jnp.float32)
        produced = produced + lax.dot_general(
            up_grad, w_up, back, preferred_element_type=jnp.float32
        )
        parts.append(produced.astype(jnp.bfloat16).reshape(chunk.shape))
        gate_grads.append(gate_grad)
        up_grads.append(up_grad)
        row_grads.append(grads)
    normed_grad = scatter_sums(place, parts)
    rows = jnp.concatenate([entry[0] for entry in kept])
    weighed = jnp.concatenate([entry[3] for entry in kept])
    outer = (((0,), (0,)), ((), ()))
    weight_grads = [
        lax.dot_general(a, b, outer, preferred_element_type=jnp.float32)
        for a, b in (
            (rows, jnp.concatenate(gate_grads)),
            (rows, jnp.concatenate(up_grads)),
            (jnp.concatenate(row_grads), weighed),
        )
    ]
    gain_grad, middle_grad = rms_backward(middle, inverse, gain, normed_grad)
    return (upstream + middle_grad, gain_grad, weight_grads)


def shards(
    tokens,
    lengths,
    routes,
    gates,
    cotangent,
    norm_attn,
    norm_ffn,
    query,
    key,
    value,
    output,
    w_gate,
    w_up,
    w_down,
):
    place = Place()
    token_rows = tokens.shape[0]
    layer_count, _, experts, _ = w_gate.shape
    expert_count = experts * place.columns
    in_width = query.shape[2] + key.shape[2] + value.shape[2]
    segment, seq_place = positions(lengths[0], token_rows)
    tables = rope_tables(seq_place, HEAD_DIMENSION)
    token_order = jnp.arange(token_rows, dtype=jnp.int32)
    allowed = (segment[:, None] == segment[None, :]) & (
        token_order[:, None] >= token_order[None, :]
    )
    gains = jnp.concatenate([norm_attn, norm_ffn]).T
    packs = []
    for l in range(layer_count):
        pack = [query[l], key[l], value[l], output[l]]
        if l == 0:
            pack.append(jnp.pad(gains, ((0, 0), (0, 128 - gains.shape[1]))))
        packs.append(jnp.concatenate(pack, axis=1))
    full = lax.all_gather(packs[0], AXES, axis=0, tiled=True)
    gains = full[:, in_width + output.shape[2] :].T[: 2 * layer_count].astype(jnp.float32)
    gate_rows = gather_gates(place, routes, gates, expert_count)
    gate_parts = [
        [
            jnp.transpose(piece[:, l], (0, 2, 1)).reshape(-1, experts)
            for piece in gate_rows
        ]
        for l in range(layer_count)
    ]
    expert_weights = gather_experts(place, [w_gate[0], w_up[0], w_down[0]])
    last_grads = None

    residual = tokens.astype(jnp.float32)
    matrices, weights, stored = [], [], []
    for l in range(layer_count):
        matrices.append((full[:, :in_width], full[:, in_width : in_width + output.shape[2]]))
        weights.append(expert_weights)
        layer_input = residual
        middle, attn_stash = attend_forward(layer_input, allowed, tables, gains[l], matrices[l])
        if l + 1 < layer_count:
            held, pack, *shares = lax.optimization_barrier(
                (middle, packs[l + 1], w_gate[l + 1], w_up[l + 1], w_down[l + 1])
            )
            middle = held
            full = lax.all_gather(pack, AXES, axis=0, tiled=True)
            expert_weights = gather_experts(place, shares)
        residual, moe_stash = experts_forward(
            place, middle, gains[layer_count + l], gate_parts[l], weights[l]
        )
        if l + 2 == layer_count or layer_count == 1:
            held, last = lax.optimization_barrier((residual, cotangent))
            residual = held
            last_grads = gather_tokens(place, last)
        stored.append((layer_input, middle, attn_stash, moe_stash))
    result = residual.astype(jnp.bfloat16)

    upstream = cotangent.astype(jnp.float32)
    in_grads, out_grads = [None] * layer_count, [None] * layer_count
    gain_grads = [None] * (2 * layer_count)
    expert_grads = [None] * layer_count
    for l in reversed(range(layer_count)):
        layer_input, middle, attn_stash, moe_stash = stored[l]
        chunks = last_grads
        if l + 1 < layer_count:
            chunks = gather_tokens(place, upstream.astype(jnp.bfloat16))
        upstream, gain_grads[layer_count + l], weight_grads = experts_backward(
            place,
            middle,
            gains[layer_count + l],
            gate_parts[l],
            weights[l],
            moe_stash,
            upstream,
            chunks,
        )
        expert_grads[l] = scatter_experts(place, weight_grads, experts)
        upstream, gain_grads[l], grad_w_in, grad_wo = attend_backward(
            layer_input, allowed, tables, gains[l], matrices[l], attn_stash, upstream
        )
        summed = lax.psum_scatter(
            jnp.concatenate([grad_w_in, grad_wo], axis=1).astype(jnp.bfloat16),
            AXES,
            scatter_dimension=0,
            tiled=True,
        ).astype(jnp.float32)
        in_grads[l], out_grads[l] = summed[:, :in_width], summed[:, in_width:]
    gain_sums = lax.psum_scatter(jnp.stack(gain_grads), AXES, scatter_dimension=1, tiled=True)
    in_grads = jnp.stack(in_grads)
    key_start, value_start = query.shape[2], query.shape[2] + key.shape[2]
    return (
        result,
        upstream,
        gain_sums[:layer_count],
        gain_sums[layer_count:],
        in_grads[:, :, :key_start],
        in_grads[:, :, key_start:value_start],
        in_grads[:, :, value_start:],
        jnp.stack(out_grads),
        jnp.stack([entry[0] for entry in expert_grads]),
        jnp.stack([entry[1] for entry in expert_grads]),
        jnp.stack([entry[2] for entry in expert_grads]),
    )


def solution(mesh):
    rows = P(AXES, None)
    layered = P(None, AXES, None)
    expert = P(None, "fsdp", "expert", None)
    gain = P(None, AXES)
    return jax.shard_map(
        shards,
        mesh=mesh,
        in_specs=(rows, rows, layered, layered, rows, gain, gain)
        + (layered,) * 4
        + (expert,) * 3,
        out_specs=(rows, rows, gain, gain) + (layered,) * 4 + (expert,) * 3,
        check_vma=False,
    )
```

time: 2800 us -> 1600 us (0.57)
  waiting for transfers between devices: 1950 us -> 846 us
  blocking collectives: 202 us -> 0 us
  starting transfers between devices: 32 us -> 200 us
  matrix products: 245 us -> 172 us
    ppermute x0 -> x126, waiting for transfers between devices: none -> 578 us  [hop(): return lax.ppermute(value, AXES, pairs)]
    reduce_scatter x8 -> x2, waiting for transfers between devices: 679 us -> 161 us  [shards(): lax.psum_scatter(jnp.concatenate([grad_w_in, grad_wo], axis=1).astype(jnp...]
    all_gather x14 -> x2, waiting for transfers between devices: 603 us -> 108 us  [the longest x1 108 us: shards(): full = lax.all_gather(packs[0], AXES, axis=0, tiled=True)]
    unnamed x26 -> x6, waiting for transfers between devices: 457 us -> 0.08 us
    all_to_all x6 -> x0, waiting for transfers between devices: 209 us -> none  [the longest x2 97.1 us: experts_backward(): lax.all_to_all(rows_grad, 'expert', split_axis=0, concat_axis=0, tiled=True)]
    ppermute x0 -> x126, starting transfers between devices: none -> 199 us  [hop(): return lax.ppermute(value, AXES, pairs)]
    all_to_all x2 -> x0, blocking collectives: 118 us -> none  [the longest x1 60.2 us: experts_forward(): lax.all_to_all(outgoing, 'expert', split_axis=0, concat_axis=0, tiled=True)]
    unnamed x2 -> x0, blocking collectives: 83.6 us -> none
  transfers between devices with their start and end apart: 30 -> 131, of which waited for: 24 -> 57; matrix products, arithmetic and copies ran while one was open for 15% -> 28% of each run, Pallas kernels for 0% -> 0%
where the time goes in v1:
time: 1600 us; the launch traced here: 1590 us
  waiting for transfers between devices  846 us (53%)
  local copies, waits for them, and re-layouts  243 us (15%)
  starting transfers between devices  200 us (12%)
  matrix products  172 us (11%)
  other arithmetic  110 us (7%)
  between operations  18.4 us (1%)
    ppermute x126, waiting for transfers between devices, hop(): return lax.ppermute(value, AXES, pairs)  578 us
    ppermute x126, starting transfers between devices, hop(): return lax.ppermute(value, AXES, pairs)  199 us
    reduce_scatter x2, waiting for transfers between devices, shards(): lax.psum_scatter(jnp.concatenate([grad_w_in, grad_wo], axis=1).astype(jnp...  161 us
    all_gather x1, waiting for transfers between devices, shards(): full = lax.all_gather(packs[0], AXES, axis=0, tiled=True)  108 us
    unnamed x486, local copies, waits for them, and re-layouts  50.8 us
    dot_general x6, matrix products, experts_backward(): lax.dot_general(a, b, outer, preferred_element_type=jnp.float32)  39.6 us
  transfers between devices with their start and end apart: 131, of which 57 were waited for; matrix products, arithmetic and copies ran while one was open for 28% of the time, Pallas kernels for 0%

profile of v1, /device:TPU:0, one launch (start us, length us, event | category | flops | bytes accessed | tf_op | source)
XLA Modules:
  0.0 1589.7 jit_solution(6755246494648602457)
XLA Ops:
  42.0 107.8 %all-gather.3.cloned.1.call-done = bf16[1536,4224]{1,0:T(8,128)(2,1)} async-done(((bf16[48,4224]{1,0:T(8,128)(2,1)}), bf16[1536,4224]{1,0:T(8,128)(2,1)}) %all-gather.3.cloned.1.call-update) | async-done | bytes 12976144 | tf_op jit(solution)/shard_map/all_gather | solution.py:375
  182.8 13.8 collective-permute-done.5
  202.5 5.8 copy.435
  252.3 28.6 %collective-permute-done.39 = bf16[3,192,640]{2,1,0:T(8,128)(2,1)} collective-permute-done((bf16[3,192,640]{2,1,0:T(8,128)(2,1)}, bf16[3,192,640]{2,1,0:T(8,128)(2,1)}, u32[]{:S(2)}, u32[]{:S(2)}) %collective-permute-start.39) | collective-permute-done | bytes 737312 | tf_op jit(solution)/shard_map/ppermute | solution.py:35
  282.6 30.2 %collective-permute-done.40 = bf16[3,192,640]{2,1,0:T(8,128)(2,1)} collective-permute-done((bf16[3,192,640]{2,1,0:T(8,128)(2,1)S(1)}, bf16[3,192,640]{2,1,0:T(8,128)(2,1)}, u32[]{:S(2)}, u32[]{:S(2)}) %collective-permute-start.40) | collective-permute-done | bytes 737312 | tf_op jit(solution)/shard_map/ppermute | solution.py:35
  312.7 26.0 %collective-permute-start.2 = (bf16[128,1536]{1,0:T(8,128)(2,1)}, bf16[128,1536]{1,0:T(8,128)(2,1)}, u32[]{:S(2)}, u32[]{:S(2)}) collective-permute-start(bf16[128,1536]{1,0:T(8,128)(2,1)} %multiply_convert_fusion.26), channel_id=1, source_target_pairs={{0,24},{1,25},{2,26},{3,27},{4,28},{5,29},{6,30},{7,31},{8,0},{9,1... | collective-permute-start | bytes 1179656 | tf_op jit(solution)/shard_map/ppermute | solution.py:35
  346.3 5.7 copy.472
  382.1 13.2 collective-permute-done.14
  419.3 5.8 collective-permute-done.18
  443.0 6.7 broadcast_select_fusion.2
  481.1 23.0 %collective-permute-done.31 = bf16[3,64,1536]{2,1,0:T(8,128)(2,1)S(1)} collective-permute-done((bf16[3,64,1536]{2,1,0:T(8,128)(2,1)S(1)}, bf16[3,64,1536]{2,1,0:T(8,128)(2,1)S(1)}, u32[]{:S(2)}, u32[]{:S(2)}) %collective-permute-start.31) | collective-permute-done | bytes 589856 | tf_op jit(solution)/shard_map/ppermute | solution.py:35
  511.2 9.7 collective-permute-done.28
  530.0 5.9 collective-permute-done.33
  535.9 7.2 collective-permute-done.35
  543.2 15.2 collective-permute-done.34
  561.4 10.9 collective-permute-done.68
  572.3 17.1 %collective-permute-done.67 = bf16[128,1536]{1,0:T(8,128)(2,1)S(1)} collective-permute-done((bf16[128,1536]{1,0:T(8,128)(2,1)S(1)}, bf16[128,1536]{1,0:T(8,128)(2,1)S(1)}, u32[]{:S(2)}, u32[]{:S(2)}) %collective-permute-start.67) | collective-permute-done | bytes 393248 | tf_op jit(solution)/shard_map/ppermute | solution.py:35
  602.2 17.6 %collective-permute-done.75 = bf16[3,128,1536]{2,1,0:T(8,128)(2,1)S(1)} collective-permute-done((bf16[3,128,1536]{2,1,0:T(8,128)(2,1)}, bf16[3,128,1536]{2,1,0:T(8,128)(2,1)S(1)}, u32[]{:S(2)}, u32[]{:S(2)}) %collective-permute-start.75) | collective-permute-done | bytes 1179680 | tf_op jit(solution)/shard_map/ppermute | solution.py:35
  635.3 7.5 collective-permute-done.73
  664.6 17.5 %collective-permute-done.37 = bf16[128,1536]{1,0:T(8,128)(2,1)S(1)} collective-permute-done((bf16[128,1536]{1,0:T(8,128)(2,1)S(1)}, bf16[128,1536]{1,0:T(8,128)(2,1)S(1)}, u32[]{:S(2)}, u32[]{:S(2)}) %collective-permute-start.37) | collective-permute-done | bytes 393248 | tf_op jit(solution)/shard_map/ppermute | solution.py:35
  699.8 13.0 collective-permute-done.44
  783.7 9.4 collective-permute-done.82
  795.5 13.9 collective-permute-done.87
  825.9 8.8 collective-permute-done.84
  844.2 11.8 collective-permute-start.91
  868.4 24.0 %collective-permute-done.90 = bf16[128,1536]{1,0:T(8,128)(2,1)S(1)} collective-permute-done((bf16[128,1536]{1,0:T(8,128)(2,1)S(1)}, bf16[128,1536]{1,0:T(8,128)(2,1)S(1)}, u32[]{:S(2)}, u32[]{:S(2)}) %collective-permute-start.90) | collective-permute-done | bytes 393248 | tf_op jit(solution)/shard_map/ppermute | solution.py:35
  893.4 11.0 collective-permute-done.64
  915.9 6.1 multiply_reduce_fusion.2
  928.3 5.6 convolution_convert_fusion
  938.7 17.3 %collective-permute-done.93 = bf16[128,1536]{1,0:T(8,128)(2,1)S(1)} collective-permute-done((bf16[128,1536]{1,0:T(8,128)(2,1)S(1)}, bf16[128,1536]{1,0:T(8,128)(2,1)S(1)}, u32[]{:S(2)}, u32[]{:S(2)}) %collective-permute-start.93) | collective-permute-done | bytes 393248 | tf_op jit(solution)/shard_map/ppermute | solution.py:35
  966.9 18.1 %collective-permute-done.101 = bf16[3,128,1536]{2,1,0:T(8,128)(2,1)S(1)} collective-permute-done((bf16[3,128,1536]{2,1,0:T(8,128)(2,1)S(1)}, bf16[3,128,1536]{2,1,0:T(8,128)(2,1)S(1)}, u32[]{:S(2)}, u32[]{:S(2)}) %collective-permute-start.101) | collective-permute-done | bytes 1179680 | tf_op jit(solution)/shard_map/ppermute | solution.py:35
  1013.4 14.6 collective-permute-done.109
  1044.8 6.6 collective-permute-start.117
  1058.0 7.7 collective-permute-done.117
  1065.7 11.5 collective-permute-done.116
  1086.5 6.9 fusion.132
  1094.7 10.7 pad_maximum_fusion.1
  1110.2 5.7 pad_maximum_fusion
  1117.3 8.5 fusion.16
  1131.3 5.5 fusion.69
  1146.0 8.0 fusion.8
  1159.4 7.0 fusion.46
  1180.4 18.2 %collective-permute-done.125 = bf16[3,192,640]{2,1,0:T(8,128)(2,1)S(1)} collective-permute-done((bf16[3,192,640]{2,1,0:T(8,128)(2,1)S(1)}, bf16[3,192,640]{2,1,0:T(8,128)(2,1)S(1)}, u32[]{:S(2)}, u32[]{:S(2)}) %collective-permute-start.125) | collective-permute-done | bytes 737312 | tf_op jit(solution)/shard_map/ppermute | solution.py:35
  1198.5 44.5 %collective-permute-done.124 = bf16[3,192,640]{2,1,0:T(8,128)(2,1)S(1)} collective-permute-done((bf16[3,192,640]{2,1,0:T(8,128)(2,1)S(1)}, bf16[3,192,640]{2,1,0:T(8,128)(2,1)S(1)}, u32[]{:S(2)}, u32[]{:S(2)}) %collective-permute-start.124) | collective-permute-done | bytes 737312 | tf_op jit(solution)/shard_map/ppermute | solution.py:35
  1263.2 9.7 collective-permute-done.121
  1272.9 81.2 %collective-permute-done.120 = bf16[3,192,640]{2,1,0:T(8,128)(2,1)} collective-permute-done((bf16[3,192,640]{2,1,0:T(8,128)(2,1)}, bf16[3,192,640]{2,1,0:T(8,128)(2,1)}, u32[]{:S(2)}, u32[]{:S(2)}) %collective-permute-start.120) | collective-permute-done | bytes 737312 | tf_op jit(solution)/shard_map/ppermute | solution.py:35
  1366.9 5.7 copy.506
  1419.1 160.3 %reduce-scatter.6.cloned.1.call-done = bf16[48,4096]{1,0:T(8,128)(2,1)} async-done(((bf16[1536,4096]{1,0:T(8,128)(2,1)}), bf16[48,4096]{1,0:T(8,128)(2,1)}) %reduce-scatter.6.cloned.1.call-update) | async-done | bytes 393232 | tf_op jit(solution)/shard_map/reduce_scatter | solution.py:435
  (1129 shorter events, 645.0 us)
Async XLA Ops:
  7.2 142.6 %all-gather.3.cloned.1.call-start = ((), (), s32[]{:S(2)}) async-start(), calls=%async_computation.3 | async-start | bytes 13381632 | tf_op jit(solution)/shard_map/all_gather | solution.py:375
  12.3 631.8 %all-gather.5.cloned.1.call-start = ((), (), s32[]{:S(2)}) async-start(), calls=%async_computation.4 | async-start | bytes 12976128 | tf_op jit(solution)/shard_map/all_gather | solution.py:400
  13.7 155.3 %collective-permute-start.9 = (f32[2,20,128]{2,1,0:T(8,128)}, f32[2,20,128]{2,1,0:T(8,128)}, u32[]{:S(2)}, u32[]{:S(2)}) collective-permute-start(f32[2,20,128]{2,1,0:T(8,128)} %select_reduce_fusion), channel_id=1, source_target_pairs={{0,24},{1,25},{2,26},{3,27},{4,28},{5,29},{6,30},{7,31},{8,0},{9,1... | collective-permute-start | bytes 61448 | tf_op jit(solution)/shard_map/ppermute | solution.py:35
  18.7 152.0 %collective-permute-start.8 = (f32[2,20,128]{2,1,0:T(8,128)}, f32[2,20,128]{2,1,0:T(8,128)}, u32[]{:S(2)}, u32[]{:S(2)}) collective-permute-start(f32[2,20,128]{2,1,0:T(8,128)} %select_reduce_fusion), channel_id=1, source_target_pairs={{0,16},{1,17},{2,18},{3,19},{4,20},{5,21},{6,22},{7,23},{8,24},{9,... | collective-permute-start | bytes 61448 | tf_op jit(solution)/shard_map/ppermute | solution.py:35
  18.7 152.0 %collective-permute-start.7 = (f32[2,20,128]{2,1,0:T(8,128)}, f32[2,20,128]{2,1,0:T(8,128)}, u32[]{:S(2)}, u32[]{:S(2)}) collective-permute-start(f32[2,20,128]{2,1,0:T(8,128)} %select_reduce_fusion), channel_id=1, source_target_pairs={{0,8},{1,9},{2,10},{3,11},{4,12},{5,13},{6,14},{7,15},{8,16},{9,17... | collective-permute-start | bytes 61448 | tf_op jit(solution)/shard_map/ppermute | solution.py:35
  31.1 147.7 %collective-permute-start.3 = (bf16[3,192,640]{2,1,0:T(8,128)(2,1)}, bf16[3,192,640]{2,1,0:T(8,128)(2,1)}, u32[]{:S(2)}, u32[]{:S(2)}) collective-permute-start(bf16[3,192,640]{2,1,0:T(8,128)(2,1)} %copy.423), channel_id=1, source_target_pairs={{0,8},{1,9},{2,10},{3,11},{4,12},{5,13},{6,14},{7,15},{8,16},{9,17... | collective-permute-start | bytes 2211848 | tf_op jit(solution)/shard_map/ppermute | solution.py:35
  35.6 144.9 %collective-permute-start.4 = (bf16[3,192,640]{2,1,0:T(8,128)(2,1)}, bf16[3,192,640]{2,1,0:T(8,128)(2,1)}, u32[]{:S(2)}, u32[]{:S(2)}) collective-permute-start(bf16[3,192,640]{2,1,0:T(8,128)(2,1)} %copy.428), channel_id=1, source_target_pairs={{0,16},{1,17},{2,18},{3,19},{4,20},{5,21},{6,22},{7,23},{8,24},{9,... | collective-permute-start | bytes 2211848 | tf_op jit(solution)/shard_map/ppermute | solution.py:35
  163.7 1097.3 %reduce-scatter.10.cloned.1.call-start = ((), (), s32[]{:S(2)}) async-start(), calls=%async_computation.7 | async-start | bytes 811008
  208.2 143.8 %collective-permute-start.6 = (bf16[4,3,192,640]{3,2,1,0:T(8,128)(2,1)}, bf16[4,3,192,640]{3,2,1,0:T(8,128)(2,1)}, u32[]{:S(2)}, u32[]{:S(2)}) collective-permute-start(bf16[4,3,192,640]{3,2,1,0:T(8,128)(2,1)} %copy.435), channel_id=1, source_target_pairs={{0,4},{1,5},{2,6},{3,7},{4,0},{5,1},{6,2},{7,3},{8,12},{9,13},{10,... | collective-permute-start | bytes 8847368 | tf_op jit(solution)/shard_map/ppermute | solution.py:35
  243.6 37.2 %collective-permute-start.39 = (bf16[3,192,640]{2,1,0:T(8,128)(2,1)}, bf16[3,192,640]{2,1,0:T(8,128)(2,1)}, u32[]{:S(2)}, u32[]{:S(2)}) collective-permute-start(bf16[3,192,640]{2,1,0:T(8,128)(2,1)} %copy.460), channel_id=1, source_target_pairs={{0,8},{1,9},{2,10},{3,11},{4,12},{5,13},{6,14},{7,15},{8,16},{9,17... | collective-permute-start | bytes 2211848 | tf_op jit(solution)/shard_map/ppermute | solution.py:35
  244.6 68.1 %collective-permute-start.40 = (bf16[3,192,640]{2,1,0:T(8,128)(2,1)S(1)}, bf16[3,192,640]{2,1,0:T(8,128)(2,1)}, u32[]{:S(2)}, u32[]{:S(2)}) collective-permute-start(bf16[3,192,640]{2,1,0:T(8,128)(2,1)S(1)} %copy-done.119), channel_id=1, source_target_pairs={{0,16},{1,17},{2,18},{3,19},{4,20},{5,21},{6,22},{7,23},{8,24},{9,... | collective-permute-start | bytes 2211848 | tf_op jit(solution)/shard_map/ppermute | solution.py:35
  247.6 92.8 %collective-permute-start.41 = (bf16[3,192,640]{2,1,0:T(8,128)(2,1)}, bf16[3,192,640]{2,1,0:T(8,128)(2,1)}, u32[]{:S(2)}, u32[]{:S(2)}) collective-permute-start(bf16[3,192,640]{2,1,0:T(8,128)(2,1)} %copy.470), channel_id=1, source_target_pairs={{0,24},{1,25},{2,26},{3,27},{4,28},{5,29},{6,30},{7,31},{8,0},{9,1... | collective-permute-start | bytes 2211848 | tf_op jit(solution)/shard_map/ppermute | solution.py:35
  249.3 106.5 %collective-permute-start.1 = (bf16[128,1536]{1,0:T(8,128)(2,1)}, bf16[128,1536]{1,0:T(8,128)(2,1)S(1)}, u32[]{:S(2)}, u32[]{:S(2)}) collective-permute-start(bf16[128,1536]{1,0:T(8,128)(2,1)} %multiply_convert_fusion.26), channel_id=1, source_target_pairs={{0,16},{1,17},{2,18},{3,19},{4,20},{5,21},{6,22},{7,23},{8,24},{9,... | collective-permute-start | bytes 1179656 | tf_op jit(solution)/shard_map/ppermute | solution.py:35
  280.9 74.9 %collective-permute-start = (bf16[128,1536]{1,0:T(8,128)(2,1)}, bf16[128,1536]{1,0:T(8,128)(2,1)S(1)}, u32[]{:S(2)}, u32[]{:S(2)}) collective-permute-start(bf16[128,1536]{1,0:T(8,128)(2,1)} %multiply_convert_fusion.26), channel_id=1, source_target_pairs={{0,8},{1,9},{2,10},{3,11},{4,12},{5,13},{6,14},{7,15},{8,16},{9,17... | collective-permute-start | bytes 1179656 | tf_op jit(solution)/shard_map/ppermute | solution.py:35
  312.7 43.1 %collective-permute-start.2 = (bf16[128,1536]{1,0:T(8,128)(2,1)}, bf16[128,1536]{1,0:T(8,128)(2,1)}, u32[]{:S(2)}, u32[]{:S(2)}) collective-permute-start(bf16[128,1536]{1,0:T(8,128)(2,1)} %multiply_convert_fusion.26), channel_id=1, source_target_pairs={{0,24},{1,25},{2,26},{3,27},{4,28},{5,29},{6,30},{7,31},{8,0},{9,1... | collective-permute-start | bytes 1179656 | tf_op jit(solution)/shard_map/ppermute | solution.py:35
  352.0 76.8 %collective-permute-start.42 = (bf16[4,3,192,640]{3,2,1,0:T(8,128)(2,1)}, bf16[4,3,192,640]{3,2,1,0:T(8,128)(2,1)}, u32[]{:S(2)}, u32[]{:S(2)}) collective-permute-start(bf16[4,3,192,640]{3,2,1,0:T(8,128)(2,1)} %copy.472), channel_id=1, source_target_pairs={{0,4},{1,5},{2,6},{3,7},{4,0},{5,1},{6,2},{7,3},{8,12},{9,13},{10,... | collective-permute-start | bytes 8847368 | tf_op jit(solution)/shard_map/ppermute | solution.py:35
  358.2 51.3 %collective-permute-start.17 = (bf16[3,128,1536]{2,1,0:T(8,128)(2,1)}, bf16[3,128,1536]{2,1,0:T(8,128)(2,1)}, u32[]{:S(2)}, u32[]{:S(2)}) collective-permute-start(bf16[3,128,1536]{2,1,0:T(8,128)(2,1)} %pad_maximum_fusion.22), channel_id=1, source_target_pairs={{0,2},{1,3},{2,0},{3,1},{4,6},{5,7},{6,4},{7,5},{8,10},{9,11},{10,... | collective-permute-start | bytes 3538952 | tf_op jit(solution)/shard_map/ppermute | solution.py:35
  359.8 51.4 %collective-permute-start.11 = (bf16[3,128,1536]{2,1,0:T(8,128)(2,1)}, bf16[3,128,1536]{2,1,0:T(8,128)(2,1)}, u32[]{:S(2)}, u32[]{:S(2)}) collective-permute-start(bf16[3,128,1536]{2,1,0:T(8,128)(2,1)} %pad_maximum_fusion.22), channel_id=1, source_target_pairs={{0,1},{1,0},{2,3},{3,2},{4,5},{5,4},{6,7},{7,6},{8,9},{9,8},{10,11... | collective-permute-start | bytes 3538952 | tf_op jit(solution)/shard_map/ppermute | solution.py:35
  362.2 33.1 %collective-permute-start.14 = (bf16[1,128,1536]{2,1,0:T(8,128)(2,1)}, bf16[1,128,1536]{2,1,0:T(8,128)(2,1)}, u32[]{:S(2)}, u32[]{:S(2)}) collective-permute-start(bf16[1,128,1536]{2,1,0:T(8,128)(2,1)} %fusion.357), channel_id=1, source_target_pairs={{0,2},{1,3},{2,0},{3,1},{4,6},{5,7},{6,4},{7,5},{8,10},{9,11},{10,... | collective-permute-start | bytes 1179656 | tf_op jit(solution)/shard_map/ppermute | solution.py:35
  362.7 35.8 %collective-permute-start.10 = (bf16[1,128,1536]{2,1,0:T(8,128)(2,1)}, bf16[1,128,1536]{2,1,0:T(8,128)(2,1)}, u32[]{:S(2)}, u32[]{:S(2)}) collective-permute-start(bf16[1,128,1536]{2,1,0:T(8,128)(2,1)} %fusion.357), channel_id=1, source_target_pairs={{0,1},{1,0},{2,3},{3,2},{4,5},{5,4},{6,7},{7,6},{8,9},{9,8},{10,11... | collective-permute-start | bytes 1179656 | tf_op jit(solution)/shard_map/ppermute | solution.py:35
  475.1 34.7 %collective-permute-start.30 = (bf16[3,64,1536]{2,1,0:T(8,128)(2,1)S(1)}, bf16[3,64,1536]{2,1,0:T(8,128)(2,1)S(1)}, u32[]{:S(2)}, u32[]{:S(2)}) collective-permute-start(bf16[3,64,1536]{2,1,0:T(8,128)(2,1)S(1)} %slice.996), channel_id=1, source_target_pairs={{0,1},{1,0},{2,3},{3,2},{4,5},{5,4},{6,7},{7,6},{8,9},{9,8},{10,11... | collective-permute-start | bytes 1769480 | tf_op jit(solution)/shard_map/ppermute | solution.py:35
  661.5 36.3 %collective-permute-start.46 = (bf16[1,128,1536]{2,1,0:T(8,128)(2,1)S(1)}, bf16[1,128,1536]{2,1,0:T(8,128)(2,1)S(1)}, u32[]{:S(2)}, u32[]{:S(2)}) collective-permute-start(bf16[1,128,1536]{2,1,0:T(8,128)(2,1)S(1)} %fusion.356), channel_id=1, source_target_pairs={{0,2},{1,3},{2,0},{3,1},{4,6},{5,7},{6,4},{7,5},{8,10},{9,11},{10,... | collective-permute-start | bytes 1179656 | tf_op jit(solution)/shard_map/ppermute | solution.py:35
  662.3 36.8 %collective-permute-start.43 = (bf16[1,128,1536]{2,1,0:T(8,128)(2,1)S(1)}, bf16[1,128,1536]{2,1,0:T(8,128)(2,1)S(1)}, u32[]{:S(2)}, u32[]{:S(2)}) collective-permute-start(bf16[1,128,1536]{2,1,0:T(8,128)(2,1)S(1)} %fusion.356), channel_id=1, source_target_pairs={{0,1},{1,0},{2,3},{3,2},{4,5},{5,4},{6,7},{7,6},{8,9},{9,8},{10,11... | collective-permute-start | bytes 1179656 | tf_op jit(solution)/shard_map/ppermute | solution.py:35
  697.8 39.9 %collective-permute-start.47 = (bf16[1,64,1536]{2,1,0:T(8,128)(2,1)S(1)}, bf16[1,64,1536]{2,1,0:T(8,128)(2,1)S(1)}, u32[]{:S(2)}, u32[]{:S(2)}) collective-permute-start(bf16[1,64,1536]{2,1,0:T(8,128)(2,1)S(1)} %slice.1023), channel_id=1, source_target_pairs={{0,1},{1,0},{2,3},{3,2},{4,5},{5,4},{6,7},{7,6},{8,9},{9,8},{10,11... | collective-permute-start | bytes 589832 | tf_op jit(solution)/shard_map/ppermute | solution.py:35
  699.1 39.6 %collective-permute-start.45 = (bf16[1,64,1536]{2,1,0:T(8,128)(2,1)S(1)}, bf16[1,64,1536]{2,1,0:T(8,128)(2,1)S(1)}, u32[]{:S(2)}, u32[]{:S(2)}) collective-permute-start(bf16[1,64,1536]{2,1,0:T(8,128)(2,1)S(1)} %slice.1022), channel_id=1, source_target_pairs={{0,2},{1,3},{2,0},{3,1},{4,6},{5,7},{6,4},{7,5},{8,10},{9,11},{10,... | collective-permute-start | bytes 589832 | tf_op jit(solution)/shard_map/ppermute | solution.py:35
  737.1 32.9 %collective-permute-start.54 = (bf16[1,64,1536]{2,1,0:T(8,128)(2,1)S(1)}, bf16[1,64,1536]{2,1,0:T(8,128)(2,1)S(1)}, u32[]{:S(2)}, u32[]{:S(2)}) collective-permute-start(bf16[1,64,1536]{2,1,0:T(8,128)(2,1)S(1)} %slice.1033), channel_id=1, source_target_pairs={{0,1},{1,0},{2,3},{3,2},{4,5},{5,4},{6,7},{7,6},{8,9},{9,8},{10,11... | collective-permute-start | bytes 589832 | tf_op jit(solution)/shard_map/ppermute | solution.py:35
  737.7 34.5 %collective-permute-start.53 = (bf16[1,64,1536]{2,1,0:T(8,128)(2,1)S(1)}, bf16[1,64,1536]{2,1,0:T(8,128)(2,1)S(1)}, u32[]{:S(2)}, u32[]{:S(2)}) collective-permute-start(bf16[1,64,1536]{2,1,0:T(8,128)(2,1)S(1)} %slice.1031), channel_id=1, source_target_pairs={{0,2},{1,3},{2,0},{3,1},{4,6},{5,7},{6,4},{7,5},{8,10},{9,11},{10,... | collective-permute-start | bytes 589832 | tf_op jit(solution)/shard_map/ppermute | solution.py:35
  738.7 39.3 %collective-permute-start.79 = (bf16[1,64,1536]{2,1,0:T(8,128)(2,1)S(1)}, bf16[1,64,1536]{2,1,0:T(8,128)(2,1)S(1)}, u32[]{:S(2)}, u32[]{:S(2)}) collective-permute-start(bf16[1,64,1536]{2,1,0:T(8,128)(2,1)S(1)} %slice.1063), channel_id=1, source_target_pairs={{0,2},{1,3},{2,0},{3,1},{4,6},{5,7},{6,4},{7,5},{8,10},{9,11},{10,... | collective-permute-start | bytes 589832 | tf_op jit(solution)/shard_map/ppermute | solution.py:35
  778.0 45.8 %collective-permute-start.85 = (bf16[3,64,1536]{2,1,0:T(8,128)(2,1)S(1)}, bf16[3,64,1536]{2,1,0:T(8,128)(2,1)S(1)}, u32[]{:S(2)}, u32[]{:S(2)}) collective-permute-start(bf16[3,64,1536]{2,1,0:T(8,128)(2,1)S(1)} %slice.1075), channel_id=1, source_target_pairs={{0,2},{1,3},{2,0},{3,1},{4,6},{5,7},{6,4},{7,5},{8,10},{9,11},{10,... | collective-permute-start | bytes 1769480 | tf_op jit(solution)/shard_map/ppermute | solution.py:35
  778.6 47.3 %collective-permute-start.86 = (bf16[3,64,1536]{2,1,0:T(8,128)(2,1)S(1)}, bf16[3,64,1536]{2,1,0:T(8,128)(2,1)S(1)}, u32[]{:S(2)}, u32[]{:S(2)}) collective-permute-start(bf16[3,64,1536]{2,1,0:T(8,128)(2,1)S(1)} %slice.1077), channel_id=1, source_target_pairs={{0,1},{1,0},{2,3},{3,2},{4,5},{5,4},{6,7},{7,6},{8,9},{9,8},{10,11... | collective-permute-start | bytes 1769480 | tf_op jit(solution)/shard_map/ppermute | solution.py:35
  782.8 32.8 %collective-permute-start.57 = (bf16[3,64,1536]{2,1,0:T(8,128)(2,1)S(1)}, bf16[3,64,1536]{2,1,0:T(8,128)(2,1)S(1)}, u32[]{:S(2)}, u32[]{:S(2)}) collective-permute-start(bf16[3,64,1536]{2,1,0:T(8,128)(2,1)S(1)} %get-tuple-element.112), channel_id=1, source_target_pairs={{0,2},{1,3},{2,0},{3,1},{4,6},{5,7},{6,4},{7,5},{8,10},{9,11},{10,... | collective-permute-start | bytes 1769480 | tf_op jit(solution)/shard_map/ppermute | solution.py:35
  856.0 36.4 %collective-permute-start.90 = (bf16[128,1536]{1,0:T(8,128)(2,1)S(1)}, bf16[128,1536]{1,0:T(8,128)(2,1)S(1)}, u32[]{:S(2)}, u32[]{:S(2)}) collective-permute-start(bf16[128,1536]{1,0:T(8,128)(2,1)S(1)} %get-tuple-element.102), channel_id=1, source_target_pairs={{0,16},{1,17},{2,18},{3,19},{4,20},{5,21},{6,22},{7,23},{8,24},{9,... | collective-permute-start | bytes 1179656 | tf_op jit(solution)/shard_map/ppermute | solution.py:35
  856.5 36.8 %collective-permute-start.63 = (bf16[128,1536]{1,0:T(8,128)(2,1)S(1)}, bf16[128,1536]{1,0:T(8,128)(2,1)S(1)}, u32[]{:S(2)}, u32[]{:S(2)}) collective-permute-start(bf16[128,1536]{1,0:T(8,128)(2,1)S(1)} %get-tuple-element.107), channel_id=1, source_target_pairs={{0,24},{1,25},{2,26},{3,27},{4,28},{5,29},{6,30},{7,31},{8,0},{9,1... | collective-permute-start | bytes 1179656 | tf_op jit(solution)/shard_map/ppermute | solution.py:35
  858.9 34.4 %collective-permute-start.65 = (bf16[128,1536]{1,0:T(8,128)(2,1)S(1)}, bf16[128,1536]{1,0:T(8,128)(2,1)S(1)}, u32[]{:S(2)}, u32[]{:S(2)}) collective-permute-start(bf16[128,1536]{1,0:T(8,128)(2,1)S(1)} %get-tuple-element.108), channel_id=1, source_target_pairs={{0,8},{1,9},{2,10},{3,11},{4,12},{5,13},{6,14},{7,15},{8,16},{9,17... | collective-permute-start | bytes 1179656 | tf_op jit(solution)/shard_map/ppermute | solution.py:35
  863.0 41.4 %collective-permute-start.64 = (bf16[128,1536]{1,0:T(8,128)(2,1)S(1)}, bf16[128,1536]{1,0:T(8,128)(2,1)S(1)}, u32[]{:S(2)}, u32[]{:S(2)}) collective-permute-start(bf16[128,1536]{1,0:T(8,128)(2,1)S(1)} %get-tuple-element.109), channel_id=1, source_target_pairs={{0,16},{1,17},{2,18},{3,19},{4,20},{5,21},{6,22},{7,23},{8,24},{9,... | collective-permute-start | bytes 1179656 | tf_op jit(solution)/shard_map/ppermute | solution.py:35
  922.3 35.8 %collective-permute-start.98 = (bf16[1,128,1536]{2,1,0:T(8,128)(2,1)S(1)}, bf16[1,128,1536]{2,1,0:T(8,128)(2,1)S(1)}, u32[]{:S(2)}, u32[]{:S(2)}) collective-permute-start(bf16[1,128,1536]{2,1,0:T(8,128)(2,1)S(1)} %bitcast.795), channel_id=1, source_target_pairs={{0,2},{1,3},{2,0},{3,1},{4,6},{5,7},{6,4},{7,5},{8,10},{9,11},{10,... | collective-permute-start | bytes 1179656 | tf_op jit(solution)/shard_map/ppermute | solution.py:35
  923.8 36.4 %collective-permute-start.95 = (bf16[1,128,1536]{2,1,0:T(8,128)(2,1)S(1)}, bf16[1,128,1536]{2,1,0:T(8,128)(2,1)S(1)}, u32[]{:S(2)}, u32[]{:S(2)}) collective-permute-start(bf16[1,128,1536]{2,1,0:T(8,128)(2,1)S(1)} %bitcast.796), channel_id=1, source_target_pairs={{0,1},{1,0},{2,3},{3,2},{4,5},{5,4},{6,7},{7,6},{8,9},{9,8},{10,11... | collective-permute-start | bytes 1179656 | tf_op jit(solution)/shard_map/ppermute | solution.py:35
  958.2 43.5 %collective-permute-start.99 = (bf16[1,64,1536]{2,1,0:T(8,128)(2,1)S(1)}, bf16[1,64,1536]{2,1,0:T(8,128)(2,1)S(1)}, u32[]{:S(2)}, u32[]{:S(2)}) collective-permute-start(bf16[1,64,1536]{2,1,0:T(8,128)(2,1)S(1)} %slice.1093), channel_id=1, source_target_pairs={{0,1},{1,0},{2,3},{3,2},{4,5},{5,4},{6,7},{7,6},{8,9},{9,8},{10,11... | collective-permute-start | bytes 589832 | tf_op jit(solution)/shard_map/ppermute | solution.py:35
  960.2 43.6 %collective-permute-start.97 = (bf16[1,64,1536]{2,1,0:T(8,128)(2,1)S(1)}, bf16[1,64,1536]{2,1,0:T(8,128)(2,1)S(1)}, u32[]{:S(2)}, u32[]{:S(2)}) collective-permute-start(bf16[1,64,1536]{2,1,0:T(8,128)(2,1)S(1)} %slice.1092), channel_id=1, source_target_pairs={{0,2},{1,3},{2,0},{3,1},{4,6},{5,7},{6,4},{7,5},{8,10},{9,11},{10,... | collective-permute-start | bytes 589832 | tf_op jit(solution)/shard_map/ppermute | solution.py:35
  1001.5 35.0 %collective-permute-start.112 = (bf16[3,64,1536]{2,1,0:T(8,128)(2,1)S(1)}, bf16[3,64,1536]{2,1,0:T(8,128)(2,1)S(1)}, u32[]{:S(2)}, u32[]{:S(2)}) collective-permute-start(bf16[3,64,1536]{2,1,0:T(8,128)(2,1)S(1)} %slice.1113), channel_id=1, source_target_pairs={{0,1},{1,0},{2,3},{3,2},{4,5},{5,4},{6,7},{7,6},{8,9},{9,8},{10,11... | collective-permute-start | bytes 1769480 | tf_op jit(solution)/shard_map/ppermute | solution.py:35
  1001.6 36.3 %collective-permute-start.111 = (bf16[3,64,1536]{2,1,0:T(8,128)(2,1)S(1)}, bf16[3,64,1536]{2,1,0:T(8,128)(2,1)S(1)}, u32[]{:S(2)}, u32[]{:S(2)}) collective-permute-start(bf16[3,64,1536]{2,1,0:T(8,128)(2,1)S(1)} %slice.1111), channel_id=1, source_target_pairs={{0,2},{1,3},{2,0},{3,1},{4,6},{5,7},{6,4},{7,5},{8,10},{9,11},{10,... | collective-permute-start | bytes 1769480 | tf_op jit(solution)/shard_map/ppermute | solution.py:35
  1094.7 323.3 %reduce-scatter.8.cloned.1.call-start = ((), (), s32[]{:S(2)}) async-start(), calls=%async_computation.6 | async-start | bytes 12976128 | tf_op jit(solution)/shard_map/reduce_scatter | solution.py:435
  1105.4 473.9 %reduce-scatter.6.cloned.1.call-start = ((), (), s32[]{:S(2)}) async-start(), calls=%async_computation.5 | async-start | bytes 12976128 | tf_op jit(solution)/shard_map/reduce_scatter | solution.py:435
  1173.9 74.1 %collective-permute-start.118 = (bf16[4,3,192,640]{3,2,1,0:T(8,128)(2,1)}, bf16[4,3,192,640]{3,2,1,0:T(8,128)(2,1)}, u32[]{:S(2)}, u32[]{:S(2)}) collective-permute-start(bf16[4,3,192,640]{3,2,1,0:T(8,128)(2,1)} %fusion.44), channel_id=1, source_target_pairs={{0,4},{1,5},{2,6},{3,7},{4,0},{5,1},{6,2},{7,3},{8,12},{9,13},{10,... | collective-permute-start | bytes 8847368 | tf_op jit(solution)/shard_map/ppermute | solution.py:35
  1179.7 63.4 %collective-permute-start.124 = (bf16[3,192,640]{2,1,0:T(8,128)(2,1)S(1)}, bf16[3,192,640]{2,1,0:T(8,128)(2,1)S(1)}, u32[]{:S(2)}, u32[]{:S(2)}) collective-permute-start(bf16[3,192,640]{2,1,0:T(8,128)(2,1)S(1)} %get-tuple-element.65), channel_id=1, source_target_pairs={{0,16},{1,17},{2,18},{3,19},{4,20},{5,21},{6,22},{7,23},{8,24},{9,... | collective-permute-start | bytes 2211848 | tf_op jit(solution)/shard_map/ppermute | solution.py:35
  1179.7 63.4 %collective-permute-start.123 = (bf16[3,192,640]{2,1,0:T(8,128)(2,1)S(1)}, bf16[3,192,640]{2,1,0:T(8,128)(2,1)S(1)}, u32[]{:S(2)}, u32[]{:S(2)}) collective-permute-start(bf16[3,192,640]{2,1,0:T(8,128)(2,1)S(1)} %get-tuple-element.66), channel_id=1, source_target_pairs={{0,8},{1,9},{2,10},{3,11},{4,12},{5,13},{6,14},{7,15},{8,16},{9,17... | collective-permute-start | bytes 2211848 | tf_op jit(solution)/shard_map/ppermute | solution.py:35
  1254.5 99.6 %collective-permute-start.120 = (bf16[3,192,640]{2,1,0:T(8,128)(2,1)}, bf16[3,192,640]{2,1,0:T(8,128)(2,1)}, u32[]{:S(2)}, u32[]{:S(2)}) collective-permute-start(bf16[3,192,640]{2,1,0:T(8,128)(2,1)} %get-tuple-element.61), channel_id=1, source_target_pairs={{0,16},{1,17},{2,18},{3,19},{4,20},{5,21},{6,22},{7,23},{8,24},{9,... | collective-permute-start | bytes 2211848 | tf_op jit(solution)/shard_map/ppermute | solution.py:35
  1257.8 96.3 %collective-permute-start.119 = (bf16[3,192,640]{2,1,0:T(8,128)(2,1)}, bf16[3,192,640]{2,1,0:T(8,128)(2,1)}, u32[]{:S(2)}, u32[]{:S(2)}) collective-permute-start(bf16[3,192,640]{2,1,0:T(8,128)(2,1)} %get-tuple-element.62), channel_id=1, source_target_pairs={{0,8},{1,9},{2,10},{3,11},{4,12},{5,13},{6,14},{7,15},{8,16},{9,17... | collective-permute-start | bytes 2211848 | tf_op jit(solution)/shard_map/ppermute | solution.py:35
  (318 other events, 3611.0 us)
Sparse Core Ops, SparseCore 0:
  12.4 137.3 all-gather.2
  163.8 143.3 all-gather.4
  1094.8 93.6 reduce-scatter.9
  1194.4 223.4 reduce-scatter.7
  1424.9 154.4 reduce-scatter.5

commit v2 on v1

--- a/solution.py
+++ b/solution.py
@@ -1,8 +1,11 @@
+import functools
 import math
 
 import jax
 import jax.numpy as jnp
 from jax import lax
+from jax.experimental import pallas as pl
+from jax.experimental.pallas import tpu as pltpu
 from jax.sharding import PartitionSpec as P
 
 QUERY_HEADS = 24
@@ -457,13 +460,955 @@
     )
 
 
+HEADS_PER_TURN = 6
+LANES = 128
+EXTRA = 128
+HALF = 64
+TILE = 256
+MIB = 1 << 20
+
+
+def any_spec():
+    return pl.BlockSpec(memory_space=pl.ANY)
+
+
+def whole_spec():
+    return pl.BlockSpec(memory_space=pltpu.VMEM)
+
+
+def scalar_spec():
+    return pl.BlockSpec(memory_space=pltpu.SMEM)
+
+
+def shape_of(*dims, dtype=jnp.bfloat16):
+    return jax.ShapeDtypeStruct(dims, dtype)
+
+
+class Copies:
+    def __init__(self, semaphores, first=0):
+        self.semaphores = semaphores
+        self.used = first
+        self.open = []
+
+    def start(self, source, target):
+        copy = pltpu.make_async_copy(source, target, self.semaphores.at[self.used])
+        self.used += 1
+        copy.start()
+        self.open.append(copy)
+
+    def wait(self):
+        for copy in self.open:
+            copy.wait()
+        self.open = []
+
+
+def shard_row(where, swapped, m, k, rows):
+    plane = lax.rem(where[0] - k + 4, 4)
+    fsdp = plane * CORES + (where[1] ^ swapped)
+    return pl.multiple_of((fsdp * 4 + (where[2] ^ m)) * rows, 16)
+
+
+def load_matrices(copies, where, pieces, full, rows, cut):
+    at = 0
+    for swapped in range(CORES):
+        for first, count in ((0, 1), (1, 3)):
+            for m, low, high in ((0, 0, None), (1, 0, None), (2, 0, None), (3, 0, cut), (3, cut, None)):
+                piece = pieces[at]
+                at += 1
+                high = full.shape[1] if high is None else high
+                for n in range(count):
+                    row = shard_row(where, swapped, m, first + n, rows)
+                    copies.start(
+                        piece.at[pl.ds(n * rows, rows), :],
+                        full.at[pl.ds(row, rows), pl.ds(low, high - low)],
+                    )
+
+
+MATRIX_PIECES = 20
+MATRIX_COPIES = 40
+
+
+def half_swap(x):
+    lane = lax.broadcasted_iota(jnp.int32, x.shape, 1)
+    return jnp.where(lane % 64 < 32, pltpu.roll(x, 96, 1), pltpu.roll(x, 32, 1))
+
+
+def both_sides(pair, side):
+    lane = lax.broadcasted_iota(jnp.int32, pair.shape, 1)
+    wide = pair.astype(jnp.float32)
+    here = jnp.where(lane // 64 == side, wide, 0.0)
+    there = pltpu.roll(here, 64, 1)
+    here, there = here.astype(jnp.bfloat16), there.astype(jnp.bfloat16)
+    return (here, there) if side == 0 else (there, here)
+
+
+def merge_sides(even, odd, side):
+    lane = lax.broadcasted_iota(jnp.int32, even.shape, 1)
+    if side == 0:
+        return jnp.where(lane < 64, even + pltpu.roll(odd, 64, 1), 0.0)
+    return jnp.where(lane < 64, 0.0, odd + pltpu.roll(even, 64, 1))
+
+
+def contract(a, b, dims):
+    return lax.dot_general(a, b, (dims, ((), ())), preferred_element_type=jnp.float32)
+
+
+PLAIN = ((1,), (0,))
+ACROSS = ((1,), (1,))
+OUTER = ((0,), (0,))
+
+
+def read_sum(base, terms):
+    if not terms:
+        return base[...].astype(jnp.float32)
+    halves = []
+    for side in range(2):
+        rows = pl.ds(side * HALF, HALF)
+        total = base[rows, :].astype(jnp.float32)
+        for term in terms:
+            part = term[side][...] if isinstance(term, tuple) else term[rows, :]
+            total = total + part.astype(jnp.float32)
+        halves.append(total)
+    return jnp.concatenate(halves, axis=0)
+
+
+def attend_forward_kernel(terms, width, where, base, *refs):
+    refs = list(refs)
+    extra = [refs.pop(0) for _ in range(terms)]
+    cosine, sine, allowed = refs[:3]
+    pieces = refs[3 : 3 + MATRIX_PIECES]
+    refs = refs[3 + MATRIX_PIECES :]
+    h_out, m_out, nf_out, na_out, q_out, k_out, v_out, o_out, lse_out, gain_out = refs[:10]
+    full, proj, mixed, semaphores = refs[10:]
+    copies = Copies(semaphores)
+    load_matrices(copies, where, pieces, full, full.shape[0] // 32, pieces[3].shape[1])
+    h = read_sum(base, group_terms(extra))
+    h_out[...] = h
+    inverse = lax.rsqrt(jnp.mean(h * h, axis=1, keepdims=True) + NORM_EPS)
+    model = h.shape[1]
+    in_width = width
+    key_start = model
+    value_start = model + (in_width - model) // 2
+    copies.wait()
+    gains = full[:, pl.ds(in_width + model, EXTRA)].astype(jnp.float32).T
+    gain_out[...] = gains[:8]
+    na_out[...] = (h * inverse * gains[0:1]).astype(jnp.bfloat16)
+    step = 512
+
+    @pl.loop(0, in_width // step)
+    def _(i):
+        columns = pl.ds(pl.multiple_of(i * step, step), step)
+        proj[:, columns] = contract(na_out[...], full[:, columns], PLAIN)
+
+    cos, sin = cosine[...], sine[...]
+
+    @pl.loop(0, key_start // LANES)
+    def _(i):
+        columns = pl.ds(pl.multiple_of(i * LANES, LANES), LANES)
+        x = proj[:, columns]
+        q_out[:, columns] = (x * cos + half_swap(x) * sin).astype(jnp.bfloat16)
+
+    @pl.loop(0, (value_start - key_start) // LANES)
+    def _(i):
+        start = pl.multiple_of(i * LANES, LANES)
+        x = proj[:, pl.ds(key_start + start, LANES)]
+        k_out[:, pl.ds(start, LANES)] = (x * cos + half_swap(x) * sin).astype(jnp.bfloat16)
+
+    v_out[...] = proj[:, value_start:in_width].astype(jnp.bfloat16)
+    lse_out[...] = jnp.zeros_like(lse_out)
+    open_keys = allowed[...] > 0.5
+    lane = lax.broadcasted_iota(jnp.int32, open_keys.shape, 1)
+
+    @pl.loop(0, KEY_VALUE_HEADS // 2)
+    def _(turn):
+        pair = pl.ds(pl.multiple_of(turn * LANES, LANES), LANES)
+        keys = [both_sides(k_out[:, pair], side) for side in range(2)]
+        values = [both_sides(v_out[:, pair], side) for side in range(2)]
+        lse = lse_out[...]
+        for group in range(HEADS_PER_TURN // 2):
+            columns = pl.ds(
+                pl.multiple_of(turn * (HEADS_PER_TURN * 64) + group * LANES, LANES), LANES
+            )
+            total = jnp.zeros((h.shape[0], LANES), jnp.float32)
+            for side in range(2):
+                head = group * 2 + side
+                scores = contract(q_out[:, columns], keys[head // 3][side], ACROSS)
+                scores = jnp.where(open_keys, scores * HEAD_DIMENSION ** (-0.5), MASKED)
+                top = jnp.max(scores, axis=1, keepdims=True)
+                weights = jnp.exp(scores - top)
+                row_total = jnp.sum(weights, axis=1, keepdims=True)
+                probs = (weights / row_total).astype(jnp.bfloat16)
+                lse = jnp.where(lane == turn * HEADS_PER_TURN + head, top + jnp.log(row_total), lse)
+                total = total + contract(probs, values[head // 3][side], PLAIN)
+            o_out[:, columns] = total.astype(jnp.bfloat16)
+        lse_out[...] = lse
+
+    @pl.loop(0, model // step)
+    def _(i):
+        columns = pl.ds(pl.multiple_of(i * step, step), step)
+        weights = full[:, pl.ds(pl.multiple_of(in_width + i * step, step), step)]
+        mixed[:, columns] = contract(o_out[...], weights, PLAIN)
+
+    m = h_out[...] + mixed[...]
+    m_out[...] = m
+    inverse = lax.rsqrt(jnp.mean(m * m, axis=1, keepdims=True) + NORM_EPS)
+    nf_out[...] = (m * inverse * gain_out[1:2]).astype(jnp.bfloat16)
+
+
+def group_terms(extra):
+    if not extra:
+        return []
+    whole, halves = extra[:4], extra[4:]
+    return list(whole) + [(halves[i], halves[i + 1]) for i in range(0, len(halves), 2)]
+
+
+def attend_forward_fast(where, base, extra, tables, pieces, in_width, after=()):
+    rows, model = base.shape
+    bf, f32 = jnp.bfloat16, jnp.float32
+    key_width = (in_width - model) // 2
+    total = in_width + model + EXTRA
+    shapes = [
+        shape_of(rows, model, dtype=f32),
+        shape_of(rows, model, dtype=f32),
+        shape_of(rows, model),
+        shape_of(rows, model),
+        shape_of(rows, model),
+        shape_of(rows, key_width),
+        shape_of(rows, key_width),
+        shape_of(rows, model),
+        shape_of(rows, LANES, dtype=f32),
+        shape_of(8, model, dtype=f32),
+    ]
+
+    def body(*refs):
+        used = 2 + len(extra) + 3 + MATRIX_PIECES
+        attend_forward_kernel(
+            len(extra), in_width, *refs[:used], *refs[used + len(after) :]
+        )
+
+    return pl.pallas_call(
+        body,
+        name="attend_forward",
+        out_shape=shapes,
+        in_specs=[scalar_spec()]
+        + [whole_spec()] * (4 + len(extra))
+        + [any_spec()] * (MATRIX_PIECES + len(after)),
+        out_specs=[whole_spec()] * len(shapes),
+        scratch_shapes=[
+            pltpu.VMEM((model, total), bf),
+            pltpu.VMEM((rows, in_width), f32),
+            pltpu.VMEM((rows, model), f32),
+            pltpu.SemaphoreType.DMA((MATRIX_COPIES,)),
+        ],
+        compiler_params=pltpu.CompilerParams(vmem_limit_bytes=44 * MIB),
+        cost_estimate=pl.CostEstimate(
+            flops=2 * rows * model * total, bytes_accessed=2 * model * total, transcendentals=0
+        ),
+    )(where, base, *extra, *tables, *pieces, *after)
+
+
+def attend_backward_kernel(terms, width, where, base, upstream, *refs):
+    refs = list(refs)
+    extra = [refs.pop(0) for _ in range(terms)]
+    h_in, m_in, na, q, k, v, o, lse_in, gains, cosine, sine, allowed = refs[:12]
+    pieces = refs[12 : 12 + MATRIX_PIECES]
+    refs = refs[12 + MATRIX_PIECES :]
+    gh_out, gh_low, mine, other = refs[:4]
+    full, sums, mixed, grad_in, turned, semaphores = refs[4:]
+    rows, model = h_in.shape
+    in_width = width
+    key_start = model
+    value_start = model + (in_width - model) // 2
+    shard = full.shape[0] // 32
+    copies = Copies(semaphores)
+    load_matrices(copies, where, pieces, full, shard, pieces[3].shape[1])
+    gnf = read_sum(base, group_terms(extra))
+    m = m_in[...]
+    inverse = lax.rsqrt(jnp.mean(m * m, axis=1, keepdims=True) + NORM_EPS)
+    gain_ffn = jnp.sum(gnf * m * inverse, axis=0, keepdims=True)
+    scaled = gnf * gains[1:2]
+    inner = jnp.mean(scaled * m, axis=1, keepdims=True)
+    gm = upstream[...].astype(jnp.float32)
+    gm = gm + inverse * scaled - m * (inverse * inverse * inverse) * inner
+    gh_out[...] = gm
+    gh_low[...] = gm.astype(jnp.bfloat16)
+    copies.wait()
+    step = 512
+
+    @pl.loop(0, model // step)
+    def _(i):
+        row = pl.ds(pl.multiple_of(i * step, step), step)
+        mixed[:, row] = contract(gh_low[...], full[row, in_width : in_width + model], ACROSS).astype(
+            jnp.bfloat16
+        )
+
+    open_keys = allowed[...] > 0.5
+    lane = lax.broadcasted_iota(jnp.int32, open_keys.shape, 1)
+    cos, sin = cosine[...], sine[...]
+    scale = HEAD_DIMENSION ** (-0.5)
+
+    @pl.loop(0, KEY_VALUE_HEADS // 2)
+    def _(turn):
+        start = pl.multiple_of(turn * LANES, LANES)
+        pair = pl.ds(start, LANES)
+        keys = [both_sides(k[:, pair], side) for side in range(2)]
+        values = [both_sides(v[:, pair], side) for side in range(2)]
+        zero = jnp.zeros((rows, LANES), jnp.float32)
+        grad_k = [[zero, zero], [zero, zero]]
+        grad_v = [[zero, zero], [zero, zero]]
+        lse = lse_in[...]
+        for group in range(HEADS_PER_TURN // 2):
+            columns = pl.ds(
+                pl.multiple_of(turn * (HEADS_PER_TURN * 64) + group * LANES, LANES), LANES
+            )
+            grad_q = zero
+            for side in range(2):
+                head = group * 2 + side
+                kv = head // 3
+                top = jnp.sum(
+                    jnp.where(lane == turn * HEADS_PER_TURN + head, lse, 0.0), axis=1, keepdims=True
+                )
+                scores = contract(q[:, columns], keys[kv][side], ACROSS) * scale
+                probs = jnp.exp(jnp.where(open_keys, scores, MASKED) - top)
+                go = mixed[:, columns]
+                grad_v[kv][side] = grad_v[kv][side] + contract(
+                    probs.astype(jnp.bfloat16), go, OUTER
+                )
+                grad_p = contract(go, values[kv][side], ACROSS)
+                grad_s = probs * (grad_p - jnp.sum(probs * grad_p, axis=1, keepdims=True))
+                grad_s = grad_s.astype(jnp.bfloat16)
+                grad_q = grad_q + contract(grad_s, keys[kv][side], PLAIN)
+                grad_k[kv][side] = grad_k[kv][side] + contract(grad_s, q[:, columns], OUTER)
+            grad_q = grad_q * scale
+            grad_in[:, columns] = (grad_q * cos - half_swap(grad_q) * sin).astype(jnp.bfloat16)
+        key_grad = merge_sides(*grad_k[0], 0) + merge_sides(*grad_k[1], 1)
+        key_grad = key_grad * scale
+        key_grad = key_grad * cos - half_swap(key_grad) * sin
+        value_grad = merge_sides(*grad_v[0], 0) + merge_sides(*grad_v[1], 1)
+        grad_in[:, pl.ds(key_start + start, LANES)] = key_grad.astype(jnp.bfloat16)
+        grad_in[:, pl.ds(value_start + start, LANES)] = value_grad.astype(jnp.bfloat16)
+
+    turned[...] = jnp.zeros_like(turned)
+
+    @pl.loop(0, in_width // step)
+    def _(i):
+        columns = pl.ds(pl.multiple_of(i * step, step), step)
+        turned[...] += contract(grad_in[:, columns], full[:, columns], ACROSS)
+
+    grad_na = turned[...]
+    h = h_in[...]
+    inverse = lax.rsqrt(jnp.mean(h * h, axis=1, keepdims=True) + NORM_EPS)
+    gain_attn = jnp.sum(grad_na * h * inverse, axis=0, keepdims=True)
+    scaled = grad_na * gains[0:1]
+    inner = jnp.mean(scaled * h, axis=1, keepdims=True)
+    band = 384
+
+    @pl.loop(0, model // band)
+    def _(i):
+        start = pl.multiple_of(i * band, band)
+        row = pl.ds(start, band)
+        sums[row, in_width : in_width + model] = contract(o[:, row], gh_low[...], OUTER).astype(
+            jnp.bfloat16
+        )
+        sums[row, :in_width] = contract(na[:, row], grad_in[...], OUTER).astype(jnp.bfloat16)
+
+    both = jnp.concatenate([gain_attn, gain_ffn, jnp.zeros((EXTRA - 2, model), jnp.float32)], axis=0)
+    sums[:, pl.ds(in_width + model, EXTRA)] = both.T.astype(jnp.bfloat16)
+    for m_index in range(4):
+        for n in range(4):
+            for swapped, target in ((1, other), (0, mine)):
+                row = shard_row(where, swapped, m_index, n, shard)
+                copies.start(
+                    sums.at[pl.ds(row, shard), :],
+                    target.at[pl.ds((m_index * 4 + n) * shard, shard), :],
+                )
+    gh = gh_out[...] + inverse * scaled - h * (inverse * inverse * inverse) * inner
+    gh_out[...] = gh
+    gh_low[...] = gh.astype(jnp.bfloat16)
+    copies.wait()
+
+
+def attend_backward_fast(where, base, upstream, extra, stash, tables, pieces, in_width, after=()):
+    rows, model = upstream.shape
+    bf, f32 = jnp.bfloat16, jnp.float32
+    total = in_width + model + EXTRA
+    shapes = [
+        shape_of(rows, model, dtype=f32),
+        shape_of(rows, model),
+        shape_of(model // 2, total),
+        shape_of(model // 2, total),
+    ]
+
+    def body(*refs):
+        used = 3 + len(extra) + 12 + MATRIX_PIECES
+        attend_backward_kernel(len(extra), in_width, *refs[:used], *refs[used + len(after) :])
+
+    return pl.pallas_call(
+        body,
+        name="attend_backward",
+        out_shape=shapes,
+        in_specs=[scalar_spec()]
+        + [whole_spec()] * (2 + len(extra) + 12)
+        + [any_spec()] * (MATRIX_PIECES + len(after)),
+        out_specs=[whole_spec()] * 2 + [any_spec()] * 2,
+        scratch_shapes=[
+            pltpu.VMEM((model, total), bf),
+            pltpu.VMEM((model, total), bf),
+            pltpu.VMEM((rows, model), bf),
+            pltpu.VMEM((rows, in_width), bf),
+            pltpu.VMEM((rows, model), f32),
+            pltpu.SemaphoreType.DMA((MATRIX_COPIES + 32,)),
+        ],
+        compiler_params=pltpu.CompilerParams(vmem_limit_bytes=56 * MIB),
+        cost_estimate=pl.CostEstimate(
+            flops=4 * rows * model * total, bytes_accessed=4 * model * total, transcendentals=0
+        ),
+    )(where, base, upstream, *extra, *stash, *tables, *pieces, *after)
+
+
+def load_experts(copies, where, pieces, targets):
+    at = 0
+    for swapped in range(CORES):
+        for k in range(4):
+            piece = pieces[at]
+            at += 1
+            _, experts, rows, share = piece.shape
+            fsdp = lax.rem(where[0] - k + 4, 4) * CORES + (where[1] ^ swapped)
+            row = pl.ds(pl.multiple_of(fsdp * rows, 16), rows)
+            for i, target in enumerate(targets):
+                for e in range(experts):
+                    copies.start(piece.at[i, e], target.at[row, pl.ds(e * share, share)])
+
+
+def widen_tile(columns, share, width):
+    lane = lax.broadcasted_iota(jnp.int32, (columns.shape[0], width), 1)
+    wide = jnp.broadcast_to(columns[:, 0:1], lane.shape)
+    for e in range(1, width // share):
+        wide = jnp.where(lane >= e * share, columns[:, e : e + 1], wide)
+    return wide
+
+
+def start_rows(copies, pieces, rows_ref):
+    at = 0
+    for piece in pieces:
+        rows = piece.shape[0]
+        copies.start(piece, rows_ref.at[pl.ds(at, rows), :])
+        at += rows
+
+
+def part_rows(n):
+    return [n] + [n // 2] * 6
+
+
+def experts_forward_kernel(where, gates, *refs):
+    pieces, weights = refs[:5], refs[5:13]
+    parts, x_out, g_out, u_out = refs[13:20], *refs[20:23]
+    x, y, g, u, w_gate, w_up, w_down, semaphores = refs[23:]
+    copies = Copies(semaphores)
+    start_rows(copies, pieces, x)
+    load_experts(copies, where, weights, (w_gate, w_up, w_down))
+    share = weights[0].shape[3]
+    width = w_gate.shape[1]
+    copies.wait()
+    copies.start(x, x_out)
+
+    @pl.loop(0, x.shape[0] // TILE)
+    def _(i):
+        row = pl.ds(pl.multiple_of(i * TILE, TILE), TILE)
+        gate_pre = contract(x[row, :], w_gate[...], PLAIN)
+        up_pre = contract(x[row, :], w_up[...], PLAIN)
+        g[row, :] = gate_pre
+        u[row, :] = up_pre
+        wide = widen_tile(gates[row, :], share, width)
+        weighed = (gate_pre * jax.nn.sigmoid(gate_pre) * up_pre * wide).astype(jnp.bfloat16)
+        y[row, :] = contract(weighed, w_down[...], ACROSS).astype(jnp.bfloat16)
+
+    copies.start(g, g_out)
+    copies.start(u, u_out)
+    at = 0
+    for part in parts:
+        copies.start(y.at[pl.ds(at, part.shape[0]), :], part)
+        at += part.shape[0]
+    copies.wait()
+
+
+def experts_forward_fast(where, gates, pieces, weights, after=()):
+    n, model = pieces[0].shape
+    _, experts, _, share = weights[0].shape
+    rows, width = 4 * n, experts * share
+    bf, f32 = jnp.bfloat16, jnp.float32
+    shapes = [shape_of(r, model) for r in part_rows(n)]
+    shapes += [shape_of(rows, model)] + [shape_of(rows, width, dtype=f32)] * 2
+
+    def body(*refs):
+        experts_forward_kernel(*refs[:15], *refs[15 + len(after) :])
+
+    return pl.pallas_call(
+        body,
+        name="experts_forward",
+        out_shape=shapes,
+        in_specs=[scalar_spec(), whole_spec()] + [any_spec()] * (13 + len(after)),
+        out_specs=[any_spec()] * len(shapes),
+        scratch_shapes=[
+            pltpu.VMEM((rows, model), bf),
+            pltpu.VMEM((rows, model), bf),
+            pltpu.VMEM((rows, width), f32),
+            pltpu.VMEM((rows, width), f32),
+        ]
+        + [pltpu.VMEM((model, width), bf)] * 3
+        + [pltpu.SemaphoreType.DMA((5 + 24 * experts + 10,))],
+        compiler_params=pltpu.CompilerParams(vmem_limit_bytes=48 * MIB),
+        cost_estimate=pl.CostEstimate(
+            flops=6 * rows * model * width, bytes_accessed=8 * rows * model, transcendentals=0
+        ),
+    )(where, gates, *pieces, *weights, *after)
+
+
+def experts_backward_kernel(where, gates, *refs):
+    pieces, g_in, u_in, weights = refs[:5], refs[5], refs[6], refs[7:15]
+    parts, r_out, gg_out, gu_out, p_out = refs[15:22], *refs[22:26]
+    x, y, g, u, gg, gu, p, w_gate, w_up, w_down, semaphores = refs[26:]
+    copies = Copies(semaphores)
+    start_rows(copies, pieces, x)
+    load_experts(copies, where, weights, (w_gate, w_up, w_down))
+    copies.start(g_in, g)
+    copies.start(u_in, u)
+    share = weights[0].shape[3]
+    width = w_gate.shape[1]
+    copies.wait()
+    copies.start(x, r_out)
+
+    @pl.loop(0, x.shape[0] // TILE)
+    def _(i):
+        row = pl.ds(pl.multiple_of(i * TILE, TILE), TILE)
+        wide = widen_tile(gates[row, :], share, width)
+        hidden_grad = contract(x[row, :], w_down[...], PLAIN) * wide
+        gate_pre, up_pre = g[row, :], u[row, :]
+        sig = jax.nn.sigmoid(gate_pre)
+        active = gate_pre * sig
+        p[row, :] = (active * up_pre * wide).astype(jnp.bfloat16)
+        gate_grad = hidden_grad * up_pre * sig * (1.0 + gate_pre * (1.0 - sig))
+        gg[row, :] = gate_grad.astype(jnp.bfloat16)
+        gu[row, :] = (hidden_grad * active).astype(jnp.bfloat16)
+        back = contract(gg[row, :], w_gate[...], ACROSS)
+        back = back + contract(gu[row, :], w_up[...], ACROSS)
+        y[row, :] = back.astype(jnp.bfloat16)
+
+    at = 0
+    for part in parts:
+        copies.start(y.at[pl.ds(at, part.shape[0]), :], part)
+        at += part.shape[0]
+    copies.start(gg, gg_out)
+    copies.start(gu, gu_out)
+    copies.start(p, p_out)
+    copies.wait()
+
+
+def experts_backward_fast(where, gates, pieces, stash, weights, after=()):
+    n, model = pieces[0].shape
+    _, experts, _, share = weights[0].shape
+    rows, width = 4 * n, experts * share
+    bf, f32 = jnp.bfloat16, jnp.float32
+    shapes = [shape_of(r, model) for r in part_rows(n)]
+    shapes += [shape_of(rows, model)] + [shape_of(rows, width)] * 3
+
+    def body(*refs):
+        experts_backward_kernel(*refs[:17], *refs[17 + len(after) :])
+
+    return pl.pallas_call(
+        body,
+        name="experts_backward",
+        out_shape=shapes,
+        in_specs=[scalar_spec(), whole_spec()] + [any_spec()] * (15 + len(after)),
+        out_specs=[any_spec()] * len(shapes),
+        scratch_shapes=[
+            pltpu.VMEM((rows, model), bf),
+            pltpu.VMEM((rows, model), bf),
+            pltpu.VMEM((rows, width), f32),
+            pltpu.VMEM((rows, width), f32),
+            pltpu.VMEM((rows, width), bf),
+            pltpu.VMEM((rows, width), bf),
+            pltpu.VMEM((rows, width), bf),
+        ]
+        + [pltpu.VMEM((model, width), bf)] * 3
+        + [pltpu.SemaphoreType.DMA((5 + 24 * experts + 13,))],
+        compiler_params=pltpu.CompilerParams(vmem_limit_bytes=52 * MIB),
+        cost_estimate=pl.CostEstimate(
+            flops=6 * rows * model * width, bytes_accessed=12 * rows * model, transcendentals=0
+        ),
+    )(where, gates, *pieces, *stash, *weights, *after)
+
+
+def weight_grads_kernel(experts, where, *refs):
+    sources, mine, other = refs[:10], refs[10], refs[11]
+    x, r, gg, gu, p, out, semaphores = refs[12:]
+    copies = Copies(semaphores)
+    for target, near, far in zip((x, r, gg, gu, p), sources[:5], sources[5:]):
+        start_rows(copies, (near, far), target)
+    copies.wait()
+    band = x.shape[1] // 4
+    rows = band // CORES
+    share = gg.shape[1] // experts
+
+    @pl.loop(0, 4)
+    def _(z):
+        columns = pl.ds(pl.multiple_of(z * band, band), band)
+        k = lax.rem(z - where[0] + 4, 4)
+        for i, (a, b) in enumerate(((x, gg), (x, gu), (r, p))):
+            grads = contract(a[:, columns], b[...], OUTER).astype(jnp.bfloat16)
+            for core in range(CORES):
+                for e in range(experts):
+                    out[core, k, i, e] = grads[
+                        core * rows : (core + 1) * rows, e * share : (e + 1) * share
+                    ]
+
+    copies.start(out.at[1 - where[1]], other)
+    copies.start(out.at[where[1]], mine)
+    copies.wait()
+
+
+def weight_grads_fast(where, near, far, experts, after=()):
+    model, width = near[0].shape[1], near[2].shape[1]
+    count = near[0].shape[0] + far[0].shape[0]
+    rows, share = model // 8, width // experts
+    bf = jnp.bfloat16
+
+    def body(*refs):
+        weight_grads_kernel(experts, *refs[:11], *refs[11 + len(after) :])
+
+    return pl.pallas_call(
+        body,
+        name="weight_grads",
+        out_shape=[shape_of(4, 3, experts, rows, share)] * 2,
+        in_specs=[scalar_spec()] + [any_spec()] * (10 + len(after)),
+        out_specs=[any_spec()] * 2,
+        scratch_shapes=[
+            pltpu.VMEM((count, model), bf),
+            pltpu.VMEM((count, model), bf),
+            pltpu.VMEM((count, width), bf),
+            pltpu.VMEM((count, width), bf),
+            pltpu.VMEM((count, width), bf),
+            pltpu.VMEM((CORES, 4, 3, experts, rows, share), bf),
+            pltpu.SemaphoreType.DMA((12,)),
+        ],
+        compiler_params=pltpu.CompilerParams(vmem_limit_bytes=56 * MIB),
+        cost_estimate=pl.CostEstimate(
+            flops=6 * count * model * width, bytes_accessed=8 * count * model, transcendentals=0
+        ),
+    )(where, *near, *far, *after)
+
+
+def cut_kernel(layer, where, w_gate, w_up, w_down, *refs):
+    outs, semaphores = refs[:4], refs[4]
+    copies = Copies(semaphores)
+    share = outs[0].shape[3]
+    for k, out in enumerate(outs):
+        columns = pl.ds(pl.multiple_of(lax.rem(where[0] + k, 4) * share, share), share)
+        for i, w in enumerate((w_gate, w_up, w_down)):
+            copies.start(w.at[layer, :, :, columns], out.at[i])
+    copies.wait()
+
+
+def cut_experts(where, weights, layer, after=()):
+    _, experts, rows, hidden = weights[0].shape
+
+    def body(*refs):
+        cut_kernel(layer, *refs[:4], *refs[4 + len(after) :])
+
+    return pl.pallas_call(
+        body,
+        name="cut_experts",
+        out_shape=[shape_of(3, experts, rows, hidden // 4)] * 4,
+        in_specs=[scalar_spec()] + [any_spec()] * (3 + len(after)),
+        out_specs=[any_spec()] * 4,
+        scratch_shapes=[pltpu.SemaphoreType.DMA((12,))],
+    )(where, *weights, *after)
+
+
+def join_kernel(layer, where, *refs):
+    pieces, outs = refs[:4], refs[-3:]
+    i = pl.program_id(0)
+    share = pieces[0].shape[3]
+    for index, out in enumerate(outs):
+
+        @pl.when(i == index)
+        def _():
+            for k, piece in enumerate(pieces):
+                columns = pl.ds(pl.multiple_of(lax.rem(where[0] - k + 4, 4) * share, share), share)
+                out[0, :, :, columns] = piece[0].astype(jnp.float32)
+
+
+def join_experts(where, pieces, layer, layers, earlier=None):
+    mats, experts, rows, share = pieces[0].shape
+    shape = shape_of(layers, experts, rows, 4 * share, dtype=jnp.float32)
+    given = [] if earlier is None else list(earlier)
+
+    return pl.pallas_call(
+        functools.partial(join_kernel, layer),
+        name="join_experts",
+        grid=(mats,),
+        out_shape=[shape] * mats,
+        in_specs=[scalar_spec()]
+        + [pl.BlockSpec((1, experts, rows, share), lambda i: (i, 0, 0, 0))] * 4
+        + [any_spec()] * len(given),
+        out_specs=[pl.BlockSpec((1, experts, rows, 4 * share), lambda i: (layer, 0, 0, 0))] * mats,
+        input_output_aliases={5 + j: j for j in range(len(given))},
+        compiler_params=pltpu.CompilerParams(vmem_limit_bytes=40 * MIB),
+    )(where, *pieces, *given)
+
+
+def spread_pieces(place, block, axis=0):
+    half = block.shape[axis] // 2 // 128 * 128 if axis else block.shape[axis] // 2
+    one = place.hop(block, flip=1)
+    two = place.hop(block, flip=2)
+    head = place.hop(lax.slice_in_dim(one, 0, half, axis=axis), flip=2)
+    tail = place.hop(lax.slice_in_dim(two, half, None, axis=axis), flip=1)
+    return [block, one, two, head, tail]
+
+
+def up_hops(place, block):
+    return jnp.concatenate([place.hop(block, up=k) for k in range(1, 4)])
+
+
+def gather_pieces(place, block, axis=0):
+    far = up_hops(place, block)
+    return spread_pieces(place, block, axis), spread_pieces(place, far, axis)
+
+
+def add_low(a, b):
+    return (a.astype(jnp.float32) + b.astype(jnp.float32)).astype(a.dtype)
+
+
+def fold_pieces(place, parts):
+    own, one_head, one_tail, two_head, two_tail, last_head, last_tail = parts
+    head = place.hop(last_head, flip=2)
+    tail = place.hop(last_tail, flip=1)
+    one_tail = place.hop(one_tail, flip=1)
+    two_head = place.hop(two_head, flip=2)
+    one_head = place.hop(add_low(one_head, head), flip=1)
+    two_tail = place.hop(add_low(two_tail, tail), flip=2)
+    return own, one_head, one_tail, two_head, two_tail
+
+
+def add_pieces(own, one_head, one_tail, two_head, two_tail, axis=0):
+    wide = lambda value: value.astype(jnp.float32)
+    one = jnp.concatenate([one_head, one_tail], axis=axis)
+    two = jnp.concatenate([two_head, two_tail], axis=axis)
+    return wide(own) + wide(one) + wide(two)
+
+
+def blocks_kernel(own, one_head, one_tail, two_head, two_tail, *outs):
+    half = one_head.shape[0]
+    rows = outs[0].shape[0]
+    step = HALF
+    for start in range(0, own.shape[0], step):
+        first, second = (one_head, two_head) if start < half else (one_tail, two_tail)
+        at = pl.ds(start % half, step)
+        total = own[pl.ds(start, step), :].astype(jnp.float32)
+        total = total + first[at, :].astype(jnp.float32) + second[at, :].astype(jnp.float32)
+        outs[start // rows][pl.ds(start % rows, step), :] = total.astype(jnp.bfloat16)
+
+
+def sum_blocks(own, *halves):
+    rows, model = own.shape
+    return pl.pallas_call(
+        blocks_kernel,
+        name="sum_blocks",
+        out_shape=[shape_of(rows // 3, model)] * 3,
+        in_specs=[whole_spec()] * 5,
+        out_specs=[whole_spec()] * 3,
+    )(own, *halves)
+
+
+def scatter_pieces(place, near, far):
+    blocks = sum_blocks(*fold_pieces(place, far))
+    arrived = [place.hop(blocks[k - 1], up=-k) for k in range(1, 4)]
+    own, one_head, one_tail, two_head, two_tail = fold_pieces(place, near)
+    return [own, *arrived, one_head, one_tail, two_head, two_tail]
+
+
+def total_of(base, extra):
+    total = base.astype(jnp.float32)
+    for block in extra[:4]:
+        total = total + block.astype(jnp.float32)
+    for head, tail in (extra[4:6], extra[6:8]):
+        total = total + jnp.concatenate([head, tail]).astype(jnp.float32)
+    return total
+
+
+def gather_matrices(place, pack):
+    near, far = gather_pieces(place, pack, axis=1)
+    own = near + far
+    return own + [place.hop(piece, swap=1) for piece in own]
+
+
+def scatter_matrices(place, mine, other, cut):
+    arrived = place.hop(other, swap=1)
+    total = add_low(mine, arrived)
+    rows = mine.shape[0] // 16
+    chunks = [total[m * 4 * rows : (m + 1) * 4 * rows] for m in range(4)]
+
+    def parts(first, last):
+        piece = [chunk[first * rows : last * rows] for chunk in chunks]
+        found = [piece[0]]
+        for m in range(1, 4):
+            found += [piece[m][:, :cut], piece[m][:, cut:]]
+        return found
+
+    far = add_pieces(*fold_pieces(place, parts(1, 4)), axis=1).astype(jnp.bfloat16)
+    arrived = [
+        place.hop(far[(k - 1) * rows : k * rows], up=-k) for k in range(1, 4)
+    ]
+    final = add_pieces(*fold_pieces(place, parts(0, 1)), axis=1)
+    for block in arrived:
+        final = final + block.astype(jnp.float32)
+    return final
+
+
+def tables_of(length_row, rows):
+    order = jnp.arange(rows, dtype=jnp.int32)
+    index = jnp.arange(length_row.shape[0], dtype=jnp.int32)
+    ends = jnp.sum(jnp.where(index[:, None] <= index[None, :], length_row[:, None], 0), axis=0)
+    passed = order[:, None] >= ends[None, :]
+    segment = jnp.sum(passed.astype(jnp.int32), axis=1)
+    begin = jnp.sum(jnp.where(passed, length_row[None, :], 0), axis=1)
+    cosine, sine = rope_tables(order - begin, HEAD_DIMENSION)
+    allowed = (segment[:, None] == segment[None, :]) & (order[:, None] >= order[None, :])
+    return (
+        jnp.concatenate([cosine] * 4, axis=1),
+        jnp.concatenate([-sine, sine] * 2, axis=1),
+        allowed.astype(jnp.float32),
+    )
+
+
+def tie(value, *events):
+    flat, tree = jax.tree.flatten(value)
+    held = lax.optimization_barrier((*flat, *events))
+    return jax.tree.unflatten(tree, held[: len(flat)])
+
+
+def gate_rows_of(place, routes, gates, expert_count):
+    found = gather_gates(place, routes, gates, expert_count)
+    owned = expert_count // place.columns
+    order = jnp.stack(found)
+    order = jnp.transpose(order, (2, 0, 1, 4, 3))
+    order = jnp.pad(order, ((0, 0),) * 4 + ((0, 8 - owned),))
+    return [
+        (layer[:, :1].reshape(-1, 8), layer[:, 1:].reshape(-1, 8)) for layer in order
+    ]
+
+
+def shards_fast(
+    tokens,
+    lengths,
+    routes,
+    gates,
+    cotangent,
+    norm_attn,
+    norm_ffn,
+    query,
+    key,
+    value,
+    output,
+    w_gate,
+    w_up,
+    w_down,
+):
+    place = Place()
+    where = jnp.stack([place.plane, place.core, place.column]).astype(jnp.int32)
+    rows, model = tokens.shape
+    layer_count, _, experts, _ = w_gate.shape
+    expert_count = experts * place.columns
+    in_width = query.shape[2] + key.shape[2] + value.shape[2]
+    packs = []
+    for l in range(layer_count):
+        gains = jnp.stack([norm_attn[l], norm_ffn[l]], axis=1)
+        gains = jnp.pad(gains, ((0, 0), (0, EXTRA - 2)))
+        packs.append(jnp.concatenate([query[l], key[l], value[l], output[l], gains], axis=1))
+    cut = packs[0].shape[1] // 2 // 128 * 128
+    weights = [jnp.transpose(w, (0, 2, 1, 3)) for w in (w_gate, w_up, w_down)]
+    tables = tables_of(lengths[0], rows)
+
+    def bring_experts(layer, after):
+        cuts = cut_experts(where, weights, layer, after=after)
+        own = [cuts[0]] + [place.hop(cuts[k], up=k) for k in range(1, 4)]
+        return own + [place.hop(piece, swap=1) for piece in own]
+
+    matrices = [gather_matrices(place, packs[0])]
+    bank = [bring_experts(0, (matrices[0][5],))]
+    gate_rows = gate_rows_of(place, routes, gates, expert_count)
+
+    base, extra = tokens.astype(jnp.float32), []
+    stored = []
+    last = None
+    for l in range(layer_count):
+        outs = attend_forward_fast(where, base, extra, tables, matrices[l], in_width)
+        h, m, nf = outs[:3]
+        near, far = gather_pieces(place, nf)
+        if l + 1 < layer_count:
+            matrices.append(gather_matrices(place, tie(packs[l + 1], nf)))
+        y_near = experts_forward_fast(where, gate_rows[l][0], near, bank[l])
+        y_far = experts_forward_fast(where, gate_rows[l][1], far, bank[l])
+        if l + 1 < layer_count:
+            bank.append(bring_experts(l + 1, (y_far[0],)))
+        else:
+            last = gather_pieces(place, tie(cotangent, y_far[0]))
+        base, extra = m, scatter_pieces(place, y_near[:7], y_far[:7])
+        stored.append((h, outs, y_near[7:], y_far[7:]))
+    result = total_of(base, extra).astype(jnp.bfloat16)
+
+    upstream = cotangent.astype(jnp.float32)
+    zero = jnp.zeros((rows, model), jnp.bfloat16)
+    sums = [None] * layer_count
+    joined = None
+    for l in reversed(range(layer_count)):
+        h, outs, kept_near, kept_far = stored[l]
+        near, far = last
+        b_near = experts_backward_fast(where, gate_rows[l][0], near, kept_near[1:], bank[l])
+        b_far = experts_backward_fast(where, gate_rows[l][1], far, kept_far[1:], bank[l])
+        extra = scatter_pieces(place, b_near[:7], b_far[:7])
+        mine, other = weight_grads_fast(
+            where, (kept_near[0], *b_near[7:]), (kept_far[0], *b_far[7:]), experts
+        )
+        arrived = place.hop(other, swap=1)
+        total = [add_low(mine[k], arrived[k]) for k in range(4)]
+        pieces = [total[0]] + [place.hop(total[k], up=k) for k in range(1, 4)]
+        m, na, q, k, v, o, lse, gains = outs[1], *outs[3:]
+        upstream, low, mine, other = attend_backward_fast(
+            where,
+            zero,
+            upstream,
+            extra,
+            (h, m, na, q, k, v, o, lse, gains),
+            tables,
+            matrices[l],
+            in_width,
+        )
+        if l:
+            last = gather_pieces(place, low)
+        sums[l] = scatter_matrices(place, mine, other, cut)
+        joined = join_experts(where, pieces, l, layer_count, joined)
+    sums = jnp.stack(sums)
+    gain_sums = sums[:, :, in_width + model :]
+    starts = (0, query.shape[2], query.shape[2] + key.shape[2], in_width, in_width + model)
+    return (
+        result,
+        upstream,
+        gain_sums[:, :, 0],
+        gain_sums[:, :, 1],
+        *[sums[:, :, a:b] for a, b in zip(starts, starts[1:])],
+        *[jnp.transpose(grads, (0, 2, 1, 3)) for grads in joined],
+    )
+
+
 def solution(mesh):
     rows = P(AXES, None)
     layered = P(None, AXES, None)
     expert = P(None, "fsdp", "expert", None)
     gain = P(None, AXES)
+    regular = mesh.shape["fsdp"] == 8 and mesh.shape["expert"] == 4
     return jax.shard_map(
-        shards,
+        shards_fast if regular else shards,
         mesh=mesh,
         in_specs=(rows, rows, layered, layered, rows, gain, gain)
         + (layered,) * 4

time: 1600 us -> 1670 us (1.044)
  Pallas kernels: 0 us -> 488 us
  matrix products: 172 us -> 0 us
  waiting for transfers between devices: 846 us -> 679 us
  local copies, waits for them, and re-layouts: 243 us -> 93 us
  starting transfers between devices: 200 us -> 350 us
  other arithmetic: 110 us -> 51.3 us
    pallas_call x0 -> x22, Pallas kernels: none -> 488 us  [the longest x2 182 us: cut_experts(): pl.pallas_call(body, name='cut_experts', out_shape=[shape_of(3, experts,...]
    dot_general x78 -> x0, matrix products: 172 us -> none  [the longest x6 39.6 us: experts_backward(): lax.dot_general(a, b, outer, preferred_element_type=jnp.float32)]
    reduce_scatter x2 -> x0, waiting for transfers between devices: 161 us -> none  [shards(): lax.psum_scatter(jnp.concatenate([grad_w_in, grad_wo], axis=1).astype(jnp...]
    ppermute x126 -> x206, starting transfers between devices: 199 us -> 350 us  [hop(): return lax.ppermute(value, AXES, pairs)]
    all_gather x2 -> x0, waiting for transfers between devices: 108 us -> none  [the longest x1 108 us: shards(): full = lax.all_gather(packs[0], AXES, axis=0, tiled=True)]
    ppermute x126 -> x206, waiting for transfers between devices: 578 us -> 679 us  [hop(): return lax.ppermute(value, AXES, pairs)]
    concatenate x23 -> x1, other arithmetic: 35.1 us -> 0.17 us  [tables_of(): jnp.concatenate([cosine] * 4, axis=1)]
    another operation x38 -> x6, other arithmetic: 35.3 us -> 4.3 us  [the longest x4 3.57 us: shards_fast(): sums = jnp.stack(sums)]
  transfers between devices with their start and end apart: 131 -> 206, of which waited for: 57 -> 79; matrix products, arithmetic and copies ran while one was open for 28% -> 5% of each run, Pallas kernels for 0% -> 27%
where the time goes in v2:
time: 1670 us; the launch traced here: 1660 us
  waiting for transfers between devices  679 us (41%)
  Pallas kernels  488 us (29%)
  starting transfers between devices  350 us (21%)
  local copies, waits for them, and re-layouts  93 us (6%)
  other arithmetic  51.3 us (3%)
    ppermute x206, waiting for transfers between devices, hop(): return lax.ppermute(value, AXES, pairs)  679 us
    ppermute x206, starting transfers between devices, hop(): return lax.ppermute(value, AXES, pairs)  350 us
    pallas_call x2, Pallas kernels, cut_experts(): pl.pallas_call(body, name='cut_experts', out_shape=[shape_of(3, experts,...  182 us
    pallas_call x4, Pallas kernels, experts_backward_fast(): pl.pallas_call(body, name='experts_backward', out_shape=shapes, in_specs=...  75.3 us
    pallas_call x4, Pallas kernels, experts_forward_fast(): pl.pallas_call(body, name='experts_forward', out_shape=shapes, in_specs=[...  63.6 us
    unnamed x400, local copies, waits for them, and re-layouts  61.3 us
    pallas_call x2, Pallas kernels, attend_backward_fast(): pl.pallas_call(body, name='attend_backward', out_shape=shapes, in_specs=[...  60.4 us
    pallas_call x2, Pallas kernels, weight_grads_fast(): pl.pallas_call(body, name='weight_grads', out_shape=[shape_of(4, 3, exper...  51.9 us
  transfers between devices with their start and end apart: 206, of which 79 were waited for; matrix products, arithmetic and copies ran while one was open for 5% of the time, Pallas kernels for 27%

profile of v2, /device:TPU:0, one launch (start us, length us, event | category | flops | bytes accessed | tf_op | source)
XLA Modules:
  0.0 1664.5 jit_solution(4369254593488743687)
XLA Ops:
  22.2 15.8 collective-permute-done.5
  64.1 12.9 collective-permute-done.refs_6_.refs_24_
  111.0 91.2 %cut_experts.2 = (bf16[3,5,192,128]{3,2,1,0:T(8,128)(2,1)}, bf16[3,5,192,128]{3,2,1,0:T(8,128)(2,1)}, bf16[3,5,192,128]{3,2,1,0:T(8,128)(2,1)}, bf16[3,5,192,128]{3,2,1,0:T(8,128)(2,1)}) custom-call(s32[3]{0:T(128)} %pad_add_fusion.refs_0_.where, bf16[2,5,192,512]{3,2,1,0:T(8,128)(2,1)} %bitcast.77, bf16[2,5,192,512]{3,2,1,0:T(8,128)(2,1)} %bitcast.79, ...), custom_call_target="tpu_custom_call" | custom-call | tf_op jit(solution)/shard_map/cut_experts/pallas_call | solution.py:1118
  223.6 16.4 attend_forward.2
  247.0 13.7 collective-permute-done.32.refs_9_.refs_11_
  260.7 14.5 collective-permute-start.38
  290.4 13.9 collective-permute-done.39
  309.6 11.4 collective-permute-start.65
  325.3 13.5 collective-permute-done.65
  341.7 14.3 collective-permute-done.29.refs_5_
  363.1 11.5 experts_forward.4
  385.3 14.2 collective-permute-done.54
  405.0 20.3 %experts_forward.5 = (bf16[384,1536]{1,0:T(8,128)(2,1)}, bf16[192,1536]{1,0:T(8,128)(2,1)S(1)}, bf16[192,1536]{1,0:T(8,128)(2,1)S(1)}, bf16[192,1536]{1,0:T(8,12...) custom-call(s32[3]{0:T(128)S(1)} %copy-done.80, ...), custom_call_target="tpu_custom_call" | custom-call | flops 9059696640 | bytes 18874368 | tf_op jit(solution)/shard_map/experts_forward/pallas_call | solution.py:946
  435.7 12.7 collective-permute-done.55.refs_6_
  450.0 11.9 collective-permute-done.70.refs_22_.refs_32_
  511.9 23.9 %collective-permute-done.52.refs_4_ = bf16[128,1536]{1,0:T(8,128)(2,1)S(1)} collective-permute-done((bf16[128,1536]{1,0:T(8,128)(2,1)}, bf16[128,1536]{1,0:T(8,128)(2,1)S(1)}, u32[]{:S(2)}, u32[]{:S(2)}) %collective-permute-start.52) | collective-permute-done | bytes 393248 | tf_op jit(solution)/shard_map/ppermute | solution.py:38
  548.2 17.2 %attend_forward.3 = (f32[128,1536]{1,0:T(8,128)}, f32[128,1536]{1,0:T(8,128)}, bf16[128,1536]{1,0:T(8,128)(2,1)}, bf16[128,1536]{1,0:T(8,128)(2,1)S(1)}, bf16[12...) custom-call(s32[3]{0:T(128)S(1)} %copy-done.80, ...), custom_call_target="tpu_custom_call" | custom-call | flops 1660944384 | bytes 12976128 | tf_op jit(solution)/shard_map/attend_forward/pallas_call | solution.py:689
  572.1 91.2 %cut_experts.3 = (bf16[3,5,192,128]{3,2,1,0:T(8,128)(2,1)}, bf16[3,5,192,128]{3,2,1,0:T(8,128)(2,1)}, bf16[3,5,192,128]{3,2,1,0:T(8,128)(2,1)}, bf16[3,5,192,128]{3,2,1,0:T(8,128)(2,1)}) custom-call(s32[3]{0:T(128)} %pad_add_fusion.refs_0_.where, bf16[2,5,192,512]{3,2,1,0:T(8,128)(2,1)} %bitcast.78, bf16[2,5,192,512]{3,2,1,0:T(8,128)(2,1)} %bitcast.80, ...), custom_call_target="tpu_custom_call" | custom-call | tf_op jit(solution)/shard_map/cut_experts/pallas_call | solution.py:1118
  667.4 22.9 %collective-permute-done.94 = bf16[128,1536]{1,0:T(8,128)(2,1)S(1)} collective-permute-done((bf16[128,1536]{1,0:T(8,128)(2,1)}, bf16[128,1536]{1,0:T(8,128)(2,1)S(1)}, u32[]{:S(2)}, u32[]{:S(2)}) %collective-permute-start.94) | collective-permute-done | bytes 393248 | tf_op jit(solution)/shard_map/ppermute | solution.py:38
  694.7 31.0 %collective-permute-done.86.refs_9_.refs_11_ = bf16[3,5,192,128]{3,2,1,0:T(8,128)(2,1)S(1)} collective-permute-done((bf16[3,5,192,128]{3,2,1,0:T(8,128)(2,1)S(1)}, bf16[3,5,192,128]{3,2,1,0:T(8,128)(2,1)S(1)}, u32[]{:S(2)}, u32[]{:S(2)}) %collective-permute-start.86) | collective-permute-done | bytes 737312 | tf_op jit(solution)/shard_map/ppermute | solution.py:38
  746.4 20.4 %experts_forward.7 = (bf16[384,1536]{1,0:T(8,128)(2,1)}, bf16[192,1536]{1,0:T(8,128)(2,1)S(1)}, bf16[192,1536]{1,0:T(8,128)(2,1)S(1)}, bf16[192,1536]{1,0:T(8,12...) custom-call(s32[3]{0:T(128)S(1)} %copy-done.81, ...), custom_call_target="tpu_custom_call" | custom-call | flops 9059696640 | bytes 18874368 | tf_op jit(solution)/shard_map/experts_forward/pallas_call | solution.py:946
  766.9 15.4 collective-permute-start.118
  793.2 15.3 collective-permute-done.119
  810.9 25.5 %collective-permute-done.121.refs_3_ = bf16[384,1536]{1,0:T(8,128)(2,1)S(1)} collective-permute-done((bf16[384,1536]{1,0:T(8,128)(2,1)S(1)}, bf16[384,1536]{1,0:T(8,128)(2,1)S(1)}, u32[]{:S(2)}, u32[]{:S(2)}) %collective-permute-start.121) | collective-permute-done | bytes 1179680 | tf_op jit(solution)/shard_map/ppermute | solution.py:38
  840.8 19.4 %collective-permute-done.81.refs_3_ = bf16[128,1536]{1,0:T(8,128)(2,1)S(1)} collective-permute-done((bf16[128,1536]{1,0:T(8,128)(2,1)}, bf16[128,1536]{1,0:T(8,128)(2,1)S(1)}, u32[]{:S(2)}, u32[]{:S(2)}) %collective-permute-start.81) | collective-permute-done | bytes 393248 | tf_op jit(solution)/shard_map/ppermute | solution.py:38
  865.9 24.8 %experts_backward.5 = (bf16[384,1536]{1,0:T(8,128)(2,1)}, bf16[192,1536]{1,0:T(8,128)(2,1)S(1)}, bf16[192,1536]{1,0:T(8,128)(2,1)S(1)}, bf16[192,1536]{1,0:T(8,1...) custom-call(s32[3]{0:T(128)S(1)} %copy-done.81, ...), custom_call_target="tpu_custom_call" | custom-call | flops 9059696640 | bytes 28311552 | tf_op jit(solution)/shard_map/experts_backward/pallas_call | solution.py:1018
  905.2 11.4 experts_forward.6
  919.6 12.4 experts_backward.4
  940.9 11.6 collective-permute-done.127.one_tail
  990.0 14.5 collective-permute-done.132.refs_5_
  1006.3 30.2 %attend_backward.2 = (f32[128,1536]{1,0:T(8,128)}, bf16[128,1536]{1,0:T(8,128)(2,1)}, bf16[768,4224]{1,0:T(8,128)(2,1)}, bf16[768,4224]{1,0:T(8,128)(2,1)}) custom-call(s32[3]{0:T(128)} %pad_add_fusion.refs_0_.where, bf16[128,1536]{1,0:T(8,128)(2,1)} %broadcast_in_dim.61.refs_1_, f32[128,1536]{1,0:T(8,128)} %convert_element_type.484.refs_2_, ...), custom_call_target="tpu_custom_call" | custom-call | flops 3321888768 | bytes 25952256 | tf_op jit(solution)/shard_map/attend_backward/pallas_call | solution.py:846
  1038.7 12.0 collective-permute-done.144
  1086.3 11.3 collective-permute-done.104.two_tail
  1099.4 17.4 %collective-permute-done.100.one_head = bf16[192,1536]{1,0:T(8,128)(2,1)S(1)} collective-permute-done((bf16[192,1536]{1,0:T(8,128)(2,1)S(1)}, bf16[192,1536]{1,0:T(8,128)(2,1)S(1)}, u32[]{:S(2)}, u32[]{:S(2)}) %collective-permute-start.100) | collective-permute-done | bytes 589856 | tf_op jit(solution)/shard_map/ppermute | solution.py:38
  1132.9 25.9 %weight_grads.3 = (bf16[4,3,5,192,128]{4,3,2,1,0:T(8,128)(2,1)}, bf16[4,3,5,192,128]{4,3,2,1,0:T(8,128)(2,1)}) custom-call(s32[3]{0:T(128)} %pad_add_fusion.refs_0_.where, bf16[512,1536]{1,0:T(8,128)(2,1)} %get-tuple-element.279.refs_1_, bf16[512,1536]{1,0:T(8,128)(2,1)} %get-tuple-element.280.refs_2_, bf16[512,640]{1,0:T(8,128)(2,1)} %get-tuple-element.281.refs_3_, ...), custom_call_target="tpu_custom_call" | custom-call | flops 12079595520 | bytes 25165824 | tf_op jit(solution)/shard_map/weight_grads/pallas_call | solution.py:1079
  1161.0 13.3 experts_backward.6
  1184.6 24.8 %experts_backward.7 = (bf16[384,1536]{1,0:T(8,128)(2,1)}, bf16[192,1536]{1,0:T(8,128)(2,1)S(1)}, bf16[192,1536]{1,0:T(8,128)(2,1)S(1)}, bf16[192,1536]{1,0:T(8,1...) custom-call(s32[3]{0:T(128)S(1)} %copy-done.82, ...), custom_call_target="tpu_custom_call" | custom-call | flops 9059696640 | bytes 28311552 | tf_op jit(solution)/shard_map/experts_backward/pallas_call | solution.py:1018
  1212.5 25.9 %weight_grads.2 = (bf16[4,3,5,192,128]{4,3,2,1,0:T(8,128)(2,1)}, bf16[4,3,5,192,128]{4,3,2,1,0:T(8,128)(2,1)}) custom-call(s32[3]{0:T(128)} %pad_add_fusion.refs_0_.where, bf16[512,1536]{1,0:T(8,128)(2,1)} %get-tuple-element.267.refs_1_, bf16[512,1536]{1,0:T(8,128)(2,1)} %get-tuple-element.268.refs_2_, bf16[512,640]{1,0:T(8,128)(2,1)} %get-tuple-element.269.refs_3_, ...), custom_call_target="tpu_custom_call" | custom-call | flops 12079595520 | bytes 25165824 | tf_op jit(solution)/shard_map/weight_grads/pallas_call | solution.py:1079
  1253.0 12.5 collective-permute-done.161.refs_7_
  1267.6 11.6 collective-permute-done.151
  1314.1 39.6 %collective-permute-start.158 = (bf16[128,1536]{1,0:T(8,128)(2,1)}, bf16[128,1536]{1,0:T(8,128)(2,1)S(1)}, u32[]{:S(2)}, u32[]{:S(2)}) collective-permute-start(bf16[128,1536]{1,0:T(8,128)(2,1)} %get-tuple-element.246), channel_id=1, source_target_pairs={{0,16},{1,17},{2,18},{3,19},{4,20},{5,21},{6,22},{7,23},{8,24},{9,... | collective-permute-start | bytes 1179656 | tf_op jit(solution)/shard_map/ppermute | solution.py:38
  1358.7 13.2 collective-permute-start.159
  1372.7 25.2 %collective-permute-start.200 = (bf16[3,5,192,128]{3,2,1,0:T(8,128)(2,1)}, bf16[3,5,192,128]{3,2,1,0:T(8,128)(2,1)S(1)}, u32[]{:S(2)}, u32[]{:S(2)}) collective-permute-start(bf16[3,5,192,128]{3,2,1,0:T(8,128)(2,1)} %get-tuple-element.322), channel_id=1, source_target_pairs={{0,16},{1,17},{2,18},{3,19},{4,20},{5,21},{6,22},{7,23},{8,24},{9,... | collective-permute-start | bytes 2211848 | tf_op jit(solution)/shard_map/ppermute | solution.py:38
  1398.0 23.8 %collective-permute-done.158.refs_5_ = bf16[128,1536]{1,0:T(8,128)(2,1)S(1)} collective-permute-done((bf16[128,1536]{1,0:T(8,128)(2,1)}, bf16[128,1536]{1,0:T(8,128)(2,1)S(1)}, u32[]{:S(2)}, u32[]{:S(2)}) %collective-permute-start.158) | collective-permute-done | bytes 393248 | tf_op jit(solution)/shard_map/ppermute | solution.py:38
  1428.9 30.2 %attend_backward.3 = (f32[128,1536]{1,0:T(8,128)}, bf16[128,1536]{1,0:T(8,128)(2,1)}, bf16[768,4224]{1,0:T(8,128)(2,1)}, bf16[768,4224]{1,0:T(8,128)(2,1)}) custom-call(s32[3]{0:T(128)} %pad_add_fusion.refs_0_.where, bf16[128,1536]{1,0:T(8,128)(2,1)} %broadcast_in_dim.61.refs_1_, f32[128,1536]{1,0:T(8,128)} %get-tuple-element.231.refs_2_, ...), custom_call_target="tpu_custom_call" | custom-call | flops 3321888768 | bytes 25952256 | tf_op jit(solution)/shard_map/attend_backward/pallas_call | solution.py:846
  1514.3 12.6 collective-permute-done.190
  1604.0 21.0 %collective-permute-done.196 = bf16[48,4224]{1,0:T(8,128)(2,1)S(1)} collective-permute-done((bf16[48,4224]{1,0:T(8,128)(2,1)S(1)}, bf16[48,4224]{1,0:T(8,128)(2,1)S(1)}, u32[]{:S(2)}, u32[]{:S(2)}) %collective-permute-start.196) | collective-permute-done | bytes 405536 | tf_op jit(solution)/shard_map/ppermute | solution.py:38
  1636.1 25.3 %collective-permute-done.180 = bf16[48,4224]{1,0:T(8,128)(2,1)S(1)} collective-permute-done((bf16[48,4224]{1,0:T(8,128)(2,1)S(1)}, bf16[48,4224]{1,0:T(8,128)(2,1)S(1)}, u32[]{:S(2)}, u32[]{:S(2)}) %collective-permute-start.180) | collective-permute-done | bytes 405536 | tf_op jit(solution)/shard_map/ppermute | solution.py:38
  (897 shorter events, 640.4 us)
Async XLA Ops:
  39.5 53.0 %collective-permute-start.7 = (bf16[144,4224]{1,0:T(8,128)(2,1)}, bf16[144,4224]{1,0:T(8,128)(2,1)}, u32[]{:S(2)}, u32[]{:S(2)}) collective-permute-start(bf16[144,4224]{1,0:T(8,128)(2,1)} %constant_dynamic-update-slice_fusion.3.refs_10_.refs_4_.refs_28_), channel_id=1, source_target_pairs={{0,1},{1,0},{2,3},{3,2},{4,5},{5,4},{6,7},{7,6},{8,9},{9,8},{10,11... | collective-permute-start | bytes 3649544 | tf_op jit(solution)/shard_map/ppermute | solution.py:38
  41.0 55.3 %collective-permute-start.8 = (bf16[144,4224]{1,0:T(8,128)(2,1)}, bf16[144,4224]{1,0:T(8,128)(2,1)}, u32[]{:S(2)}, u32[]{:S(2)}) collective-permute-start(bf16[144,4224]{1,0:T(8,128)(2,1)} %constant_dynamic-update-slice_fusion.3.refs_10_.refs_4_.refs_28_), channel_id=1, source_target_pairs={{0,2},{1,3},{2,0},{3,1},{4,6},{5,7},{6,4},{7,5},{8,10},{9,11},{10,... | collective-permute-start | bytes 3649544 | tf_op jit(solution)/shard_map/ppermute | solution.py:38
  92.5 109.8 %collective-permute-start.16 = (bf16[144,4224]{1,0:T(8,128)(2,1)}, bf16[144,4224]{1,0:T(8,128)(2,1)}, u32[]{:S(2)}, u32[]{:S(2)}) collective-permute-start(bf16[144,4224]{1,0:T(8,128)(2,1)} %constant_dynamic-update-slice_fusion.3.refs_10_.refs_4_.refs_28_), channel_id=1, source_target_pairs={{0,4},{1,5},{2,6},{3,7},{4,0},{5,1},{6,2},{7,3},{8,12},{9,13},{10,... | collective-permute-start | bytes 3649544 | tf_op jit(solution)/shard_map/ppermute | solution.py:38
  96.3 118.1 %collective-permute-start.17 = (bf16[144,4224]{1,0:T(8,128)(2,1)}, bf16[144,4224]{1,0:T(8,128)(2,1)}, u32[]{:S(2)}, u32[]{:S(2)}) collective-permute-start(bf16[144,4224]{1,0:T(8,128)(2,1)} %collective-permute-done.7.refs_11_.refs_29_), channel_id=1, source_target_pairs={{0,4},{1,5},{2,6},{3,7},{4,0},{5,1},{6,2},{7,3},{8,12},{9,13},{10,... | collective-permute-start | bytes 3649544 | tf_op jit(solution)/shard_map/ppermute | solution.py:38
  96.4 119.5 %collective-permute-start.18 = (bf16[144,4224]{1,0:T(8,128)(2,1)}, bf16[144,4224]{1,0:T(8,128)(2,1)}, u32[]{:S(2)}, u32[]{:S(2)}) collective-permute-start(bf16[144,4224]{1,0:T(8,128)(2,1)} %collective-permute-done.8.refs_12_.refs_30_), channel_id=1, source_target_pairs={{0,4},{1,5},{2,6},{3,7},{4,0},{5,1},{6,2},{7,3},{8,12},{9,13},{10,... | collective-permute-start | bytes 3649544 | tf_op jit(solution)/shard_map/ppermute | solution.py:38
  100.5 110.3 %collective-permute-start.10 = (bf16[144,2176]{1,0:T(8,128)(2,1)}, bf16[144,2176]{1,0:T(8,128)(2,1)S(1)}, u32[]{:S(2)}, u32[]{:S(2)}) collective-permute-start(bf16[144,2176]{1,0:T(8,128)(2,1)} %slice.450), channel_id=1, source_target_pairs={{0,1},{1,0},{2,3},{3,2},{4,5},{5,4},{6,7},{7,6},{8,9},{9,8},{10,11... | collective-permute-start | bytes 1880072 | tf_op jit(solution)/shard_map/ppermute | solution.py:38
  110.1 102.1 %collective-permute-start.19 = (bf16[144,2048]{1,0:T(8,128)(2,1)S(1)}, bf16[144,2048]{1,0:T(8,128)(2,1)S(1)}, u32[]{:S(2)}, u32[]{:S(2)}) collective-permute-start(bf16[144,2048]{1,0:T(8,128)(2,1)S(1)} %collective-permute-done.9.refs_13_.refs_31_), channel_id=1, source_target_pairs={{0,4},{1,5},{2,6},{3,7},{4,0},{5,1},{6,2},{7,3},{8,12},{9,13},{10,... | collective-permute-start | bytes 1769480 | tf_op jit(solution)/shard_map/ppermute | solution.py:38
  202.3 44.1 %collective-permute-start.31 = (bf16[3,5,192,128]{3,2,1,0:T(8,128)(2,1)}, bf16[3,5,192,128]{3,2,1,0:T(8,128)(2,1)}, u32[]{:S(2)}, u32[]{:S(2)}) collective-permute-start(bf16[3,5,192,128]{3,2,1,0:T(8,128)(2,1)} %get-tuple-element.157), channel_id=1, source_target_pairs={{0,8},{1,9},{2,10},{3,11},{4,12},{5,13},{6,14},{7,15},{8,16},{9,17... | collective-permute-start | bytes 2211848 | tf_op jit(solution)/shard_map/ppermute | solution.py:38
  210.9 49.8 %collective-permute-start.32 = (bf16[3,5,192,128]{3,2,1,0:T(8,128)(2,1)}, bf16[3,5,192,128]{3,2,1,0:T(8,128)(2,1)}, u32[]{:S(2)}, u32[]{:S(2)}) collective-permute-start(bf16[3,5,192,128]{3,2,1,0:T(8,128)(2,1)} %get-tuple-element.158), channel_id=1, source_target_pairs={{0,16},{1,17},{2,18},{3,19},{4,20},{5,21},{6,22},{7,23},{8,24},{9,... | collective-permute-start | bytes 2211848 | tf_op jit(solution)/shard_map/ppermute | solution.py:38
  214.5 60.8 %collective-permute-start.33 = (bf16[3,5,192,128]{3,2,1,0:T(8,128)(2,1)}, bf16[3,5,192,128]{3,2,1,0:T(8,128)(2,1)}, u32[]{:S(2)}, u32[]{:S(2)}) collective-permute-start(bf16[3,5,192,128]{3,2,1,0:T(8,128)(2,1)} %get-tuple-element.159), channel_id=1, source_target_pairs={{0,24},{1,25},{2,26},{3,27},{4,28},{5,29},{6,30},{7,31},{8,0},{9,1... | collective-permute-start | bytes 2211848 | tf_op jit(solution)/shard_map/ppermute | solution.py:38
  215.8 62.9 %collective-permute-start.34 = (bf16[3,5,192,128]{3,2,1,0:T(8,128)(2,1)}, bf16[3,5,192,128]{3,2,1,0:T(8,128)(2,1)}, u32[]{:S(2)}, u32[]{:S(2)}) collective-permute-start(bf16[3,5,192,128]{3,2,1,0:T(8,128)(2,1)} %get-tuple-element.156.refs_7_.refs_9_), channel_id=1, source_target_pairs={{0,4},{1,5},{2,6},{3,7},{4,0},{5,1},{6,2},{7,3},{8,12},{9,13},{10,... | collective-permute-start | bytes 2211848 | tf_op jit(solution)/shard_map/ppermute | solution.py:38
  280.1 41.0 %collective-permute-start.35 = (bf16[3,5,192,128]{3,2,1,0:T(8,128)(2,1)}, bf16[3,5,192,128]{3,2,1,0:T(8,128)(2,1)}, u32[]{:S(2)}, u32[]{:S(2)}) collective-permute-start(bf16[3,5,192,128]{3,2,1,0:T(8,128)(2,1)} %collective-permute-done.31.refs_8_.refs_10_), channel_id=1, source_target_pairs={{0,4},{1,5},{2,6},{3,7},{4,0},{5,1},{6,2},{7,3},{8,12},{9,13},{10,... | collective-permute-start | bytes 2211848 | tf_op jit(solution)/shard_map/ppermute | solution.py:38
  280.2 42.5 %collective-permute-start.36 = (bf16[3,5,192,128]{3,2,1,0:T(8,128)(2,1)}, bf16[3,5,192,128]{3,2,1,0:T(8,128)(2,1)}, u32[]{:S(2)}, u32[]{:S(2)}) collective-permute-start(bf16[3,5,192,128]{3,2,1,0:T(8,128)(2,1)} %collective-permute-done.32.refs_9_.refs_11_), channel_id=1, source_target_pairs={{0,4},{1,5},{2,6},{3,7},{4,0},{5,1},{6,2},{7,3},{8,12},{9,13},{10,... | collective-permute-start | bytes 2211848 | tf_op jit(solution)/shard_map/ppermute | solution.py:38
  324.2 50.5 %collective-permute-start.41 = (bf16[384,1536]{1,0:T(8,128)(2,1)S(1)}, bf16[384,1536]{1,0:T(8,128)(2,1)S(1)}, u32[]{:S(2)}, u32[]{:S(2)}) collective-permute-start(bf16[384,1536]{1,0:T(8,128)(2,1)S(1)} %constant_dynamic-update-slice_fusion.6.refs_2_), channel_id=1, source_target_pairs={{0,1},{1,0},{2,3},{3,2},{4,5},{5,4},{6,7},{7,6},{8,9},{9,8},{10,11... | collective-permute-start | bytes 3538952 | tf_op jit(solution)/shard_map/ppermute | solution.py:38
  324.7 51.6 %collective-permute-start.42 = (bf16[384,1536]{1,0:T(8,128)(2,1)S(1)}, bf16[384,1536]{1,0:T(8,128)(2,1)S(1)}, u32[]{:S(2)}, u32[]{:S(2)}) collective-permute-start(bf16[384,1536]{1,0:T(8,128)(2,1)S(1)} %constant_dynamic-update-slice_fusion.6.refs_2_), channel_id=1, source_target_pairs={{0,2},{1,3},{2,0},{3,1},{4,6},{5,7},{6,4},{7,5},{8,10},{9,11},{10,... | collective-permute-start | bytes 3538952 | tf_op jit(solution)/shard_map/ppermute | solution.py:38
  450.0 43.0 %collective-permute-start.76 = (bf16[144,4224]{1,0:T(8,128)(2,1)}, bf16[144,4224]{1,0:T(8,128)(2,1)}, u32[]{:S(2)}, u32[]{:S(2)}) collective-permute-start(bf16[144,4224]{1,0:T(8,128)(2,1)} %constant_dynamic-update-slice_fusion.12.refs_18_.refs_28_), channel_id=1, source_target_pairs={{0,4},{1,5},{2,6},{3,7},{4,0},{5,1},{6,2},{7,3},{8,12},{9,13},{10,... | collective-permute-start | bytes 3649544 | tf_op jit(solution)/shard_map/ppermute | solution.py:38
  461.9 40.1 %collective-permute-start.77 = (bf16[144,4224]{1,0:T(8,128)(2,1)}, bf16[144,4224]{1,0:T(8,128)(2,1)}, u32[]{:S(2)}, u32[]{:S(2)}) collective-permute-start(bf16[144,4224]{1,0:T(8,128)(2,1)} %collective-permute-done.67.refs_19_.refs_29_), channel_id=1, source_target_pairs={{0,4},{1,5},{2,6},{3,7},{4,0},{5,1},{6,2},{7,3},{8,12},{9,13},{10,... | collective-permute-start | bytes 3649544 | tf_op jit(solution)/shard_map/ppermute | solution.py:38
  569.6 97.7 %collective-permute-start.92 = (bf16[128,1536]{1,0:T(8,128)(2,1)}, bf16[128,1536]{1,0:T(8,128)(2,1)S(1)}, u32[]{:S(2)}, u32[]{:S(2)}) collective-permute-start(bf16[128,1536]{1,0:T(8,128)(2,1)} %get-tuple-element.179.refs_2_), channel_id=1, source_target_pairs={{0,8},{1,9},{2,10},{3,11},{4,12},{5,13},{6,14},{7,15},{8,16},{9,17... | collective-permute-start | bytes 1179656 | tf_op jit(solution)/shard_map/ppermute | solution.py:38
  570.3 97.0 %collective-permute-start.93 = (bf16[128,1536]{1,0:T(8,128)(2,1)}, bf16[128,1536]{1,0:T(8,128)(2,1)S(1)}, u32[]{:S(2)}, u32[]{:S(2)}) collective-permute-start(bf16[128,1536]{1,0:T(8,128)(2,1)} %get-tuple-element.179.refs_2_), channel_id=1, source_target_pairs={{0,16},{1,17},{2,18},{3,19},{4,20},{5,21},{6,22},{7,23},{8,24},{9,... | collective-permute-start | bytes 1179656 | tf_op jit(solution)/shard_map/ppermute | solution.py:38
  860.2 37.4 %collective-permute-start.83 = (bf16[64,1536]{1,0:T(8,128)(2,1)S(1)}, bf16[64,1536]{1,0:T(8,128)(2,1)S(1)}, u32[]{:S(2)}, u32[]{:S(2)}) collective-permute-start(bf16[64,1536]{1,0:T(8,128)(2,1)S(1)} %slice.462), channel_id=1, source_target_pairs={{0,2},{1,3},{2,0},{3,1},{4,6},{5,7},{6,4},{7,5},{8,10},{9,11},{10,... | collective-permute-start | bytes 589832 | tf_op jit(solution)/shard_map/ppermute | solution.py:38
  892.4 42.7 %collective-permute-start.129 = (bf16[192,1536]{1,0:T(8,128)(2,1)}, bf16[192,1536]{1,0:T(8,128)(2,1)}, u32[]{:S(2)}, u32[]{:S(2)}) collective-permute-start(bf16[192,1536]{1,0:T(8,128)(2,1)} %get-tuple-element.213), channel_id=1, source_target_pairs={{0,1},{1,0},{2,3},{3,2},{4,5},{5,4},{6,7},{7,6},{8,9},{9,8},{10,11... | collective-permute-start | bytes 1769480 | tf_op jit(solution)/shard_map/ppermute | solution.py:38
  963.0 73.6 %collective-permute-start.103 = (bf16[192,1536]{1,0:T(8,128)(2,1)}, bf16[192,1536]{1,0:T(8,128)(2,1)S(1)}, u32[]{:S(2)}, u32[]{:S(2)}) collective-permute-start(bf16[192,1536]{1,0:T(8,128)(2,1)} %get-tuple-element.191), channel_id=1, source_target_pairs={{0,1},{1,0},{2,3},{3,2},{4,5},{5,4},{6,7},{7,6},{8,9},{9,8},{10,11... | collective-permute-start | bytes 1769480 | tf_op jit(solution)/shard_map/ppermute | solution.py:38
  987.7 82.9 %collective-permute-start.112 = (bf16[64,1536]{1,0:T(8,128)(2,1)S(1)}, bf16[64,1536]{1,0:T(8,128)(2,1)S(1)}, u32[]{:S(2)}, u32[]{:S(2)}) collective-permute-start(bf16[64,1536]{1,0:T(8,128)(2,1)S(1)} %copy-done.109), channel_id=1, source_target_pairs={{0,1},{1,0},{2,3},{3,2},{4,5},{5,4},{6,7},{7,6},{8,9},{9,8},{10,11... | collective-permute-start | bytes 589832 | tf_op jit(solution)/shard_map/ppermute | solution.py:38
  989.2 82.3 %collective-permute-start.108 = (bf16[64,1536]{1,0:T(8,128)(2,1)S(1)}, bf16[64,1536]{1,0:T(8,128)(2,1)S(1)}, u32[]{:S(2)}, u32[]{:S(2)}) collective-permute-start(bf16[64,1536]{1,0:T(8,128)(2,1)S(1)} %copy-done.107), channel_id=1, source_target_pairs={{0,2},{1,3},{2,0},{3,1},{4,6},{5,7},{6,4},{7,5},{8,10},{9,11},{10,... | collective-permute-start | bytes 589832 | tf_op jit(solution)/shard_map/ppermute | solution.py:38
  1004.5 68.3 %collective-permute-start.99 = (bf16[192,1536]{1,0:T(8,128)(2,1)S(1)}, bf16[192,1536]{1,0:T(8,128)(2,1)S(1)}, u32[]{:S(2)}, u32[]{:S(2)}) collective-permute-start(bf16[192,1536]{1,0:T(8,128)(2,1)S(1)} %copy-done.97), channel_id=1, source_target_pairs={{0,2},{1,3},{2,0},{3,1},{4,6},{5,7},{6,4},{7,5},{8,10},{9,11},{10,... | collective-permute-start | bytes 1769480 | tf_op jit(solution)/shard_map/ppermute | solution.py:38
  1071.5 57.2 %collective-permute-start.147 = (bf16[384,1536]{1,0:T(8,128)(2,1)}, bf16[384,1536]{1,0:T(8,128)(2,1)}, u32[]{:S(2)}, u32[]{:S(2)}) collective-permute-start(bf16[384,1536]{1,0:T(8,128)(2,1)} %constant_dynamic-update-slice_fusion.21.refs_2_), channel_id=1, source_target_pairs={{0,1},{1,0},{2,3},{3,2},{4,5},{5,4},{6,7},{7,6},{8,9},{9,8},{10,11... | collective-permute-start | bytes 3538952 | tf_op jit(solution)/shard_map/ppermute | solution.py:38
  1072.8 57.4 %collective-permute-start.148 = (bf16[384,1536]{1,0:T(8,128)(2,1)}, bf16[384,1536]{1,0:T(8,128)(2,1)}, u32[]{:S(2)}, u32[]{:S(2)}) collective-permute-start(bf16[384,1536]{1,0:T(8,128)(2,1)} %constant_dynamic-update-slice_fusion.21.refs_2_), channel_id=1, source_target_pairs={{0,2},{1,3},{2,0},{3,1},{4,6},{5,7},{6,4},{7,5},{8,10},{9,11},{10,... | collective-permute-start | bytes 3538952 | tf_op jit(solution)/shard_map/ppermute | solution.py:38
  1078.9 37.9 %collective-permute-start.100 = (bf16[192,1536]{1,0:T(8,128)(2,1)S(1)}, bf16[192,1536]{1,0:T(8,128)(2,1)S(1)}, u32[]{:S(2)}, u32[]{:S(2)}) collective-permute-start(bf16[192,1536]{1,0:T(8,128)(2,1)S(1)} %add_convert_fusion.21), channel_id=1, source_target_pairs={{0,1},{1,0},{2,3},{3,2},{4,5},{5,4},{6,7},{7,6},{8,9},{9,8},{10,11... | collective-permute-start | bytes 1769480 | tf_op jit(solution)/shard_map/ppermute | solution.py:38
  1085.0 39.8 %collective-permute-start.140 = (bf16[128,1536]{1,0:T(8,128)(2,1)}, bf16[128,1536]{1,0:T(8,128)(2,1)S(1)}, u32[]{:S(2)}, u32[]{:S(2)}) collective-permute-start(bf16[128,1536]{1,0:T(8,128)(2,1)} %get-tuple-element.232.refs_2_), channel_id=1, source_target_pairs={{0,1},{1,0},{2,3},{3,2},{4,5},{5,4},{6,7},{7,6},{8,9},{9,8},{10,11... | collective-permute-start | bytes 1179656 | tf_op jit(solution)/shard_map/ppermute | solution.py:38
  1116.9 57.5 %collective-permute-start.110 = (bf16[64,1536]{1,0:T(8,128)(2,1)S(1)}, bf16[64,1536]{1,0:T(8,128)(2,1)S(1)}, u32[]{:S(2)}, u32[]{:S(2)}) collective-permute-start(bf16[64,1536]{1,0:T(8,128)(2,1)S(1)} %copy-done.105), channel_id=1, source_target_pairs={{0,1},{1,0},{2,3},{3,2},{4,5},{5,4},{6,7},{7,6},{8,9},{9,8},{10,11... | collective-permute-start | bytes 589832 | tf_op jit(solution)/shard_map/ppermute | solution.py:38
  1129.8 52.0 %collective-permute-start.149 = (bf16[192,1536]{1,0:T(8,128)(2,1)S(1)}, bf16[192,1536]{1,0:T(8,128)(2,1)S(1)}, u32[]{:S(2)}, u32[]{:S(2)}) collective-permute-start(bf16[192,1536]{1,0:T(8,128)(2,1)S(1)} %slice.473), channel_id=1, source_target_pairs={{0,2},{1,3},{2,0},{3,1},{4,6},{5,7},{6,4},{7,5},{8,10},{9,11},{10,... | collective-permute-start | bytes 1769480 | tf_op jit(solution)/shard_map/ppermute | solution.py:38
  1131.3 52.5 %collective-permute-start.150 = (bf16[192,1536]{1,0:T(8,128)(2,1)S(1)}, bf16[192,1536]{1,0:T(8,128)(2,1)S(1)}, u32[]{:S(2)}, u32[]{:S(2)}) collective-permute-start(bf16[192,1536]{1,0:T(8,128)(2,1)S(1)} %slice.474), channel_id=1, source_target_pairs={{0,1},{1,0},{2,3},{3,2},{4,5},{5,4},{6,7},{7,6},{8,9},{9,8},{10,11... | collective-permute-start | bytes 1769480 | tf_op jit(solution)/shard_map/ppermute | solution.py:38
  1159.6 49.9 %collective-permute-start.113 = (bf16[64,1536]{1,0:T(8,128)(2,1)}, bf16[64,1536]{1,0:T(8,128)(2,1)S(1)}, u32[]{:S(2)}, u32[]{:S(2)}) collective-permute-start(bf16[64,1536]{1,0:T(8,128)(2,1)} %add_convert_fusion.33), channel_id=1, source_target_pairs={{0,2},{1,3},{2,0},{3,1},{4,6},{5,7},{6,4},{7,5},{8,10},{9,11},{10,... | collective-permute-start | bytes 589832 | tf_op jit(solution)/shard_map/ppermute | solution.py:38
  1174.3 37.3 %collective-permute-start.109 = (bf16[64,1536]{1,0:T(8,128)(2,1)S(1)}, bf16[64,1536]{1,0:T(8,128)(2,1)S(1)}, u32[]{:S(2)}, u32[]{:S(2)}) collective-permute-start(bf16[64,1536]{1,0:T(8,128)(2,1)S(1)} %copy-done.168), channel_id=1, source_target_pairs={{0,1},{1,0},{2,3},{3,2},{4,5},{5,4},{6,7},{7,6},{8,9},{9,8},{10,11... | collective-permute-start | bytes 589832 | tf_op jit(solution)/shard_map/ppermute | solution.py:38
  1174.9 36.8 %collective-permute-start.105 = (bf16[128,1536]{1,0:T(8,128)(2,1)S(1)}, bf16[128,1536]{1,0:T(8,128)(2,1)S(1)}, u32[]{:S(2)}, u32[]{:S(2)}) collective-permute-start(bf16[128,1536]{1,0:T(8,128)(2,1)S(1)} %copy-done.190), channel_id=1, source_target_pairs={{0,24},{1,25},{2,26},{3,27},{4,28},{5,29},{6,30},{7,31},{8,0},{9,1... | collective-permute-start | bytes 1179656 | tf_op jit(solution)/shard_map/ppermute | solution.py:38
  1183.8 279.6 %collective-permute-start.182 = (bf16[768,4224]{1,0:T(8,128)(2,1)}, bf16[768,4224]{1,0:T(8,128)(2,1)}, u32[]{:S(2)}, u32[]{:S(2)}) collective-permute-start(bf16[768,4224]{1,0:T(8,128)(2,1)} %get-tuple-element.266), channel_id=1, source_target_pairs={{0,4},{1,5},{2,6},{3,7},{4,0},{5,1},{6,2},{7,3},{8,12},{9,13},{10,... | collective-permute-start | bytes 19464200 | tf_op jit(solution)/shard_map/ppermute | solution.py:38
  1211.7 68.7 %collective-permute-start.202 = (bf16[4,3,5,192,128]{4,3,2,1,0:T(8,128)(2,1)}, bf16[4,3,5,192,128]{4,3,2,1,0:T(8,128)(2,1)}, u32[]{:S(2)}, u32[]{:S(2)}) collective-permute-start(bf16[4,3,5,192,128]{4,3,2,1,0:T(8,128)(2,1)} %get-tuple-element.290), channel_id=1, source_target_pairs={{0,4},{1,5},{2,6},{3,7},{4,0},{5,1},{6,2},{7,3},{8,12},{9,13},{10,... | collective-permute-start | bytes 8847368 | tf_op jit(solution)/shard_map/ppermute | solution.py:38
  1241.9 72.2 %collective-permute-start.198 = (bf16[4,3,5,192,128]{4,3,2,1,0:T(8,128)(2,1)}, bf16[4,3,5,192,128]{4,3,2,1,0:T(8,128)(2,1)}, u32[]{:S(2)}, u32[]{:S(2)}) collective-permute-start(bf16[4,3,5,192,128]{4,3,2,1,0:T(8,128)(2,1)} %get-tuple-element.278), channel_id=1, source_target_pairs={{0,4},{1,5},{2,6},{3,7},{4,0},{5,1},{6,2},{7,3},{8,12},{9,13},{10,... | collective-permute-start | bytes 8847368 | tf_op jit(solution)/shard_map/ppermute | solution.py:38
  1304.4 54.3 %collective-permute-start.204 = (bf16[3,5,192,128]{3,2,1,0:T(8,128)(2,1)}, bf16[3,5,192,128]{3,2,1,0:T(8,128)(2,1)S(1)}, u32[]{:S(2)}, u32[]{:S(2)}) collective-permute-start(bf16[3,5,192,128]{3,2,1,0:T(8,128)(2,1)} %get-tuple-element.318), channel_id=1, source_target_pairs={{0,16},{1,17},{2,18},{3,19},{4,20},{5,21},{6,22},{7,23},{8,24},{9,... | collective-permute-start | bytes 2211848 | tf_op jit(solution)/shard_map/ppermute | solution.py:38
  1305.2 66.7 %collective-permute-start.205 = (bf16[3,5,192,128]{3,2,1,0:T(8,128)(2,1)}, bf16[3,5,192,128]{3,2,1,0:T(8,128)(2,1)S(1)}, u32[]{:S(2)}, u32[]{:S(2)}) collective-permute-start(bf16[3,5,192,128]{3,2,1,0:T(8,128)(2,1)} %get-tuple-element.317), channel_id=1, source_target_pairs={{0,24},{1,25},{2,26},{3,27},{4,28},{5,29},{6,30},{7,31},{8,0},{9,1... | collective-permute-start | bytes 2211848 | tf_op jit(solution)/shard_map/ppermute | solution.py:38
  1314.1 57.9 %collective-permute-start.157 = (bf16[128,1536]{1,0:T(8,128)(2,1)}, bf16[128,1536]{1,0:T(8,128)(2,1)S(1)}, u32[]{:S(2)}, u32[]{:S(2)}) collective-permute-start(bf16[128,1536]{1,0:T(8,128)(2,1)} %get-tuple-element.245), channel_id=1, source_target_pairs={{0,24},{1,25},{2,26},{3,27},{4,28},{5,29},{6,30},{7,31},{8,0},{9,1... | collective-permute-start | bytes 1179656 | tf_op jit(solution)/shard_map/ppermute | solution.py:38
  1314.1 107.7 %collective-permute-start.158 = (bf16[128,1536]{1,0:T(8,128)(2,1)}, bf16[128,1536]{1,0:T(8,128)(2,1)S(1)}, u32[]{:S(2)}, u32[]{:S(2)}) collective-permute-start(bf16[128,1536]{1,0:T(8,128)(2,1)} %get-tuple-element.246), channel_id=1, source_target_pairs={{0,16},{1,17},{2,18},{3,19},{4,20},{5,21},{6,22},{7,23},{8,24},{9,... | collective-permute-start | bytes 1179656 | tf_op jit(solution)/shard_map/ppermute | solution.py:38
  1358.7 69.4 %collective-permute-start.159 = (bf16[128,1536]{1,0:T(8,128)(2,1)S(1)}, bf16[128,1536]{1,0:T(8,128)(2,1)S(1)}, u32[]{:S(2)}, u32[]{:S(2)}) collective-permute-start(bf16[128,1536]{1,0:T(8,128)(2,1)S(1)} %copy-done.191), channel_id=1, source_target_pairs={{0,8},{1,9},{2,10},{3,11},{4,12},{5,13},{6,14},{7,15},{8,16},{9,17... | collective-permute-start | bytes 1179656 | tf_op jit(solution)/shard_map/ppermute | solution.py:38
  1371.9 87.2 %collective-permute-start.199 = (bf16[3,5,192,128]{3,2,1,0:T(8,128)(2,1)}, bf16[3,5,192,128]{3,2,1,0:T(8,128)(2,1)S(1)}, u32[]{:S(2)}, u32[]{:S(2)}) collective-permute-start(bf16[3,5,192,128]{3,2,1,0:T(8,128)(2,1)} %get-tuple-element.323), channel_id=1, source_target_pairs={{0,8},{1,9},{2,10},{3,11},{4,12},{5,13},{6,14},{7,15},{8,16},{9,17... | collective-permute-start | bytes 2211848 | tf_op jit(solution)/shard_map/ppermute | solution.py:38
  1372.7 86.4 %collective-permute-start.200 = (bf16[3,5,192,128]{3,2,1,0:T(8,128)(2,1)}, bf16[3,5,192,128]{3,2,1,0:T(8,128)(2,1)S(1)}, u32[]{:S(2)}, u32[]{:S(2)}) collective-permute-start(bf16[3,5,192,128]{3,2,1,0:T(8,128)(2,1)} %get-tuple-element.322), channel_id=1, source_target_pairs={{0,16},{1,17},{2,18},{3,19},{4,20},{5,21},{6,22},{7,23},{8,24},{9,... | collective-permute-start | bytes 2211848 | tf_op jit(solution)/shard_map/ppermute | solution.py:38
  1422.6 36.6 %collective-permute-start.201 = (bf16[3,5,192,128]{3,2,1,0:T(8,128)(2,1)S(1)}, bf16[3,5,192,128]{3,2,1,0:T(8,128)(2,1)S(1)}, u32[]{:S(2)}, u32[]{:S(2)}) collective-permute-start(bf16[3,5,192,128]{3,2,1,0:T(8,128)(2,1)S(1)} %get-tuple-element.321), channel_id=1, source_target_pairs={{0,24},{1,25},{2,26},{3,27},{4,28},{5,29},{6,30},{7,31},{8,0},{9,1... | collective-permute-start | bytes 2211848 | tf_op jit(solution)/shard_map/ppermute | solution.py:38
  1459.1 69.7 %collective-permute-start.166 = (bf16[768,4224]{1,0:T(8,128)(2,1)}, bf16[768,4224]{1,0:T(8,128)(2,1)}, u32[]{:S(2)}, u32[]{:S(2)}) collective-permute-start(bf16[768,4224]{1,0:T(8,128)(2,1)} %get-tuple-element.264), channel_id=1, source_target_pairs={{0,4},{1,5},{2,6},{3,7},{4,0},{5,1},{6,2},{7,3},{8,12},{9,13},{10,... | collective-permute-start | bytes 19464200 | tf_op jit(solution)/shard_map/ppermute | solution.py:38
  1509.6 86.6 %collective-permute-start.185 = (bf16[48,2176]{1,0:T(8,128)(2,1)S(1)}, bf16[48,2176]{1,0:T(8,128)(2,1)S(1)}, u32[]{:S(2)}, u32[]{:S(2)}) collective-permute-start(bf16[48,2176]{1,0:T(8,128)(2,1)S(1)} %get-tuple-element.312), channel_id=1, source_target_pairs={{0,1},{1,0},{2,3},{3,2},{4,5},{5,4},{6,7},{7,6},{8,9},{9,8},{10,11... | collective-permute-start | bytes 626696 | tf_op jit(solution)/shard_map/ppermute | solution.py:38
  (350 other events, 8530.5 us)

commit v3 on v2

--- a/solution.py
+++ b/solution.py
@@ -85,18 +85,25 @@
     return total
 
 
-def gather_gates(place, routes, gates, expert_count):
+def gates_line(place, routes, gates, expert_count):
     names = jnp.arange(expert_count, dtype=jnp.int32)
     chosen = routes[:, None, :, :] == names[None, :, None, None]
     table = jnp.sum(jnp.where(chosen, gates[:, None, :, :], 0.0), axis=3)
-    line = jnp.stack([table] + [place.hop(table, up=k) for k in range(1, place.planes)])
-    owned = expert_count // place.columns
+    return jnp.stack([table] + [place.hop(table, up=k) for k in range(1, place.planes)])
+
+
+def spread_gates(place, line):
+    owned = line.shape[2] // place.columns
     found = []
     for m in range(place.columns):
         start = (place.column ^ m) * owned
         piece = lax.dynamic_slice_in_dim(line, start, owned, axis=2)
         found.append(place.hop(piece, flip=m) if m else piece)
     return found
+
+
+def gather_gates(place, routes, gates, expert_count):
+    return spread_gates(place, gates_line(place, routes, gates, expert_count))
 
 
 def gather_experts(place, weights):
@@ -466,6 +473,11 @@
 HALF = 64
 TILE = 256
 MIB = 1 << 20
+COST_PART = 16
+
+
+def cost(flops):
+    return pl.CostEstimate(flops=flops // COST_PART, bytes_accessed=0, transcendentals=0)
 
 
 def any_spec():
@@ -508,24 +520,21 @@
     return pl.multiple_of((fsdp * 4 + (where[2] ^ m)) * rows, 16)
 
 
-def load_matrices(copies, where, pieces, full, rows, cut):
-    at = 0
+MATRIX_PIECES = 10
+MATRIX_COPIES = 40
+
+
+def load_matrices(copies, where, pieces, full):
+    rows, cut = pieces[0].shape[0] // 4, pieces[3].shape[1]
+    spans = ((0, 0, full.shape[1]),) * 3 + ((3, 0, cut), (3, cut, full.shape[1] - cut))
     for swapped in range(CORES):
-        for first, count in ((0, 1), (1, 3)):
-            for m, low, high in ((0, 0, None), (1, 0, None), (2, 0, None), (3, 0, cut), (3, cut, None)):
-                piece = pieces[at]
-                at += 1
-                high = full.shape[1] if high is None else high
-                for n in range(count):
-                    row = shard_row(where, swapped, m, first + n, rows)
-                    copies.start(
-                        piece.at[pl.ds(n * rows, rows), :],
-                        full.at[pl.ds(row, rows), pl.ds(low, high - low)],
-                    )
-
-
-MATRIX_PIECES = 20
-MATRIX_COPIES = 40
+        for index, (m, low, width) in enumerate(spans):
+            piece = pieces[swapped * 5 + index]
+            for k in range(4):
+                row = shard_row(where, swapped, m or index, k, rows)
+                copies.start(
+                    piece.at[pl.ds(k * rows, rows), :], full.at[pl.ds(row, rows), pl.ds(low, width)]
+                )
 
 
 def half_swap(x):
@@ -558,16 +567,19 @@
 OUTER = ((0,), (0,))
 
 
-def read_sum(base, terms):
-    if not terms:
+def read_sum(base, extra):
+    if not extra:
         return base[...].astype(jnp.float32)
+    *blocks, one_head, two_tail, by_one, by_two = extra
+    top = pl.ds(0, HALF)
     halves = []
-    for side in range(2):
+    for side, terms in enumerate(((one_head, by_two), (two_tail, by_one))):
         rows = pl.ds(side * HALF, HALF)
         total = base[rows, :].astype(jnp.float32)
+        for block in blocks:
+            total = total + block[rows, :].astype(jnp.float32)
         for term in terms:
-            part = term[side][...] if isinstance(term, tuple) else term[rows, :]
-            total = total + part.astype(jnp.float32)
+            total = total + term[top, :].astype(jnp.float32)
         halves.append(total)
     return jnp.concatenate(halves, axis=0)
 
@@ -581,8 +593,8 @@
     h_out, m_out, nf_out, na_out, q_out, k_out, v_out, o_out, lse_out, gain_out = refs[:10]
     full, proj, mixed, semaphores = refs[10:]
     copies = Copies(semaphores)
-    load_matrices(copies, where, pieces, full, full.shape[0] // 32, pieces[3].shape[1])
-    h = read_sum(base, group_terms(extra))
+    load_matrices(copies, where, pieces, full)
+    h = read_sum(base, extra)
     h_out[...] = h
     inverse = lax.rsqrt(jnp.mean(h * h, axis=1, keepdims=True) + NORM_EPS)
     model = h.shape[1]
@@ -655,13 +667,6 @@
     nf_out[...] = (m * inverse * gain_out[1:2]).astype(jnp.bfloat16)
 
 
-def group_terms(extra):
-    if not extra:
-        return []
-    whole, halves = extra[:4], extra[4:]
-    return list(whole) + [(halves[i], halves[i + 1]) for i in range(0, len(halves), 2)]
-
-
 def attend_forward_fast(where, base, extra, tables, pieces, in_width, after=()):
     rows, model = base.shape
     bf, f32 = jnp.bfloat16, jnp.float32
@@ -682,9 +687,7 @@
 
     def body(*refs):
         used = 2 + len(extra) + 3 + MATRIX_PIECES
-        attend_forward_kernel(
-            len(extra), in_width, *refs[:used], *refs[used + len(after) :]
-        )
+        attend_forward_kernel(len(extra), in_width, *refs[:used], *refs[used + len(after) :])
 
     return pl.pallas_call(
         body,
@@ -701,9 +704,7 @@
             pltpu.SemaphoreType.DMA((MATRIX_COPIES,)),
         ],
         compiler_params=pltpu.CompilerParams(vmem_limit_bytes=44 * MIB),
-        cost_estimate=pl.CostEstimate(
-            flops=2 * rows * model * total, bytes_accessed=2 * model * total, transcendentals=0
-        ),
+        cost_estimate=cost(2 * rows * model * total),
     )(where, base, *extra, *tables, *pieces, *after)
 
 
@@ -712,17 +713,17 @@
     extra = [refs.pop(0) for _ in range(terms)]
     h_in, m_in, na, q, k, v, o, lse_in, gains, cosine, sine, allowed = refs[:12]
     pieces = refs[12 : 12 + MATRIX_PIECES]
-    refs = refs[12 + MATRIX_PIECES :]
-    gh_out, gh_low, mine, other = refs[:4]
-    full, sums, mixed, grad_in, turned, semaphores = refs[4:]
+    outs, refs = refs[12 + MATRIX_PIECES : -6], refs[-6:]
+    gh_out, gh_low = outs[:2]
+    full, sums, mixed, grad_in, turned, semaphores = refs
     rows, model = h_in.shape
     in_width = width
     key_start = model
     value_start = model + (in_width - model) // 2
     shard = full.shape[0] // 32
     copies = Copies(semaphores)
-    load_matrices(copies, where, pieces, full, shard, pieces[3].shape[1])
-    gnf = read_sum(base, group_terms(extra))
+    load_matrices(copies, where, pieces, full)
+    gnf = read_sum(base, extra)
     m = m_in[...]
     inverse = lax.rsqrt(jnp.mean(m * m, axis=1, keepdims=True) + NORM_EPS)
     gain_ffn = jnp.sum(gnf * m * inverse, axis=0, keepdims=True)
@@ -814,30 +815,39 @@
 
     both = jnp.concatenate([gain_attn, gain_ffn, jnp.zeros((EXTRA - 2, model), jnp.float32)], axis=0)
     sums[:, pl.ds(in_width + model, EXTRA)] = both.T.astype(jnp.bfloat16)
-    for m_index in range(4):
-        for n in range(4):
-            for swapped, target in ((1, other), (0, mine)):
-                row = shard_row(where, swapped, m_index, n, shard)
-                copies.start(
-                    sums.at[pl.ds(row, shard), :],
-                    target.at[pl.ds((m_index * 4 + n) * shard, shard), :],
-                )
+    if len(outs) == 3:
+        copies.start(sums, outs[2])
+    else:
+        for swapped in (1, 0):
+            for first, count in ((1, 3), (0, 1)):
+                target = outs[2 + 2 * (1 - swapped) + (1 - first)]
+                for m_index in range(4):
+                    for n in range(count):
+                        row = shard_row(where, swapped, m_index, first + n, shard)
+                        copies.start(
+                            sums.at[pl.ds(row, shard), :],
+                            target.at[pl.ds((m_index * count + n) * shard, shard), :],
+                        )
     gh = gh_out[...] + inverse * scaled - h * (inverse * inverse * inverse) * inner
     gh_out[...] = gh
     gh_low[...] = gh.astype(jnp.bfloat16)
     copies.wait()
 
 
-def attend_backward_fast(where, base, upstream, extra, stash, tables, pieces, in_width, after=()):
+def attend_backward_fast(
+    split, where, base, upstream, extra, stash, tables, pieces, in_width, after=()
+):
     rows, model = upstream.shape
     bf, f32 = jnp.bfloat16, jnp.float32
     total = in_width + model + EXTRA
     shapes = [
         shape_of(rows, model, dtype=f32),
         shape_of(rows, model),
-        shape_of(model // 2, total),
-        shape_of(model // 2, total),
     ]
+    if split:
+        shapes += [shape_of(model // 8 * part, total) for part in (3, 1, 3, 1)]
+    else:
+        shapes += [shape_of(model, total)]
 
     def body(*refs):
         used = 3 + len(extra) + 12 + MATRIX_PIECES
@@ -850,7 +860,7 @@
         in_specs=[scalar_spec()]
         + [whole_spec()] * (2 + len(extra) + 12)
         + [any_spec()] * (MATRIX_PIECES + len(after)),
-        out_specs=[whole_spec()] * 2 + [any_spec()] * 2,
+        out_specs=[whole_spec()] * 2 + [any_spec()] * (len(shapes) - 2),
         scratch_shapes=[
             pltpu.VMEM((model, total), bf),
             pltpu.VMEM((model, total), bf),
@@ -860,22 +870,24 @@
             pltpu.SemaphoreType.DMA((MATRIX_COPIES + 32,)),
         ],
         compiler_params=pltpu.CompilerParams(vmem_limit_bytes=56 * MIB),
-        cost_estimate=pl.CostEstimate(
-            flops=4 * rows * model * total, bytes_accessed=4 * model * total, transcendentals=0
-        ),
+        cost_estimate=cost(4 * rows * model * total),
     )(where, base, upstream, *extra, *stash, *tables, *pieces, *after)
+
+
+SHARES = ((0, 0, 3), (1, 0, 3), (3, 0, 3), (2, 0, 1), (2, 1, 2))
+WEIGHT_PIECES = CORES * len(SHARES)
 
 
 def load_experts(copies, where, pieces, targets):
     at = 0
     for swapped in range(CORES):
-        for k in range(4):
+        for k, first, count in SHARES:
             piece = pieces[at]
             at += 1
             _, experts, rows, share = piece.shape
             fsdp = lax.rem(where[0] - k + 4, 4) * CORES + (where[1] ^ swapped)
             row = pl.ds(pl.multiple_of(fsdp * rows, 16), rows)
-            for i, target in enumerate(targets):
+            for i, target in enumerate(targets[first : first + count]):
                 for e in range(experts):
                     copies.start(piece.at[i, e], target.at[row, pl.ds(e * share, share)])
 
@@ -888,22 +900,46 @@
     return wide
 
 
-def start_rows(copies, pieces, rows_ref):
+def start_rows(copies, pieces, rows_ref, spans=None):
     at = 0
-    for piece in pieces:
-        rows = piece.shape[0]
-        copies.start(piece, rows_ref.at[pl.ds(at, rows), :])
+    for index, piece in enumerate(pieces):
+        first, rows = spans[index] if spans else (0, piece.shape[0])
+        if rows:
+            copies.start(piece.at[pl.ds(first, rows), :], rows_ref.at[pl.ds(at, rows), :])
         at += rows
 
 
+def spans_of(far):
+    if far:
+        return ((HALF * 2, HALF * 6),) * 3 + ((HALF * 2, HALF * 2), (0, HALF * 4))
+    return ((0, HALF * 2),) * 4 + ((0, 0),)
+
+
 def part_rows(n):
-    return [n] + [n // 2] * 6
+    return [n, n // 2, n // 2, n, n]
+
+
+def start_parts(copies, y, parts):
+    n = parts[0].shape[0]
+    half = n // 2
+
+    def start(first, count, part, at=0):
+        copies.start(y.at[pl.ds(first, count), :], part.at[pl.ds(at, count), :])
+
+    own, one_head, two_tail, to_one, to_two = parts
+    start(0, n, own)
+    start(n, half, one_head)
+    start(2 * n + half, half, two_tail)
+    start(n + half, half, to_one)
+    start(3 * n + half, half, to_one, half)
+    start(2 * n, half, to_two)
+    start(3 * n, half, to_two, half)
 
 
 def experts_forward_kernel(where, gates, *refs):
-    pieces, weights = refs[:5], refs[5:13]
-    parts, x_out, g_out, u_out = refs[13:20], *refs[20:23]
-    x, y, g, u, w_gate, w_up, w_down, semaphores = refs[23:]
+    pieces, weights, refs = refs[:5], refs[5 : 5 + WEIGHT_PIECES], refs[5 + WEIGHT_PIECES :]
+    parts, x_out, g_out, u_out = refs[:5], *refs[5:8]
+    x, y, g, u, w_gate, w_up, w_down, semaphores = refs[8:]
     copies = Copies(semaphores)
     start_rows(copies, pieces, x)
     load_experts(copies, where, weights, (w_gate, w_up, w_down))
@@ -923,12 +959,9 @@
         weighed = (gate_pre * jax.nn.sigmoid(gate_pre) * up_pre * wide).astype(jnp.bfloat16)
         y[row, :] = contract(weighed, w_down[...], ACROSS).astype(jnp.bfloat16)
 
+    start_parts(copies, y, parts)
     copies.start(g, g_out)
     copies.start(u, u_out)
-    at = 0
-    for part in parts:
-        copies.start(y.at[pl.ds(at, part.shape[0]), :], part)
-        at += part.shape[0]
     copies.wait()
 
 
@@ -941,13 +974,14 @@
     shapes += [shape_of(rows, model)] + [shape_of(rows, width, dtype=f32)] * 2
 
     def body(*refs):
-        experts_forward_kernel(*refs[:15], *refs[15 + len(after) :])
+        used = 7 + WEIGHT_PIECES
+        experts_forward_kernel(*refs[:used], *refs[used + len(after) :])
 
     return pl.pallas_call(
         body,
         name="experts_forward",
         out_shape=shapes,
-        in_specs=[scalar_spec(), whole_spec()] + [any_spec()] * (13 + len(after)),
+        in_specs=[scalar_spec(), whole_spec()] + [any_spec()] * (5 + WEIGHT_PIECES + len(after)),
         out_specs=[any_spec()] * len(shapes),
         scratch_shapes=[
             pltpu.VMEM((rows, model), bf),
@@ -956,20 +990,19 @@
             pltpu.VMEM((rows, width), f32),
         ]
         + [pltpu.VMEM((model, width), bf)] * 3
-        + [pltpu.SemaphoreType.DMA((5 + 24 * experts + 10,))],
+        + [pltpu.SemaphoreType.DMA((5 + 24 * experts + 20,))],
         compiler_params=pltpu.CompilerParams(vmem_limit_bytes=48 * MIB),
-        cost_estimate=pl.CostEstimate(
-            flops=6 * rows * model * width, bytes_accessed=8 * rows * model, transcendentals=0
-        ),
+        cost_estimate=cost(6 * rows * model * width),
     )(where, gates, *pieces, *weights, *after)
 
 
-def experts_backward_kernel(where, gates, *refs):
-    pieces, g_in, u_in, weights = refs[:5], refs[5], refs[6], refs[7:15]
-    parts, r_out, gg_out, gu_out, p_out = refs[15:22], *refs[22:26]
-    x, y, g, u, gg, gu, p, w_gate, w_up, w_down, semaphores = refs[26:]
+def experts_backward_kernel(spans, where, gates, *refs):
+    pieces, g_in, u_in = refs[:5], refs[5], refs[6]
+    weights, refs = refs[7 : 7 + WEIGHT_PIECES], refs[7 + WEIGHT_PIECES :]
+    parts, r_out, gg_out, gu_out, p_out = refs[:5], *refs[5:9]
+    x, y, g, u, gg, gu, p, w_gate, w_up, w_down, semaphores = refs[9:]
     copies = Copies(semaphores)
-    start_rows(copies, pieces, x)
+    start_rows(copies, pieces, x, spans)
     load_experts(copies, where, weights, (w_gate, w_up, w_down))
     copies.start(g_in, g)
     copies.start(u_in, u)
@@ -994,18 +1027,15 @@
         back = back + contract(gu[row, :], w_up[...], ACROSS)
         y[row, :] = back.astype(jnp.bfloat16)
 
-    at = 0
-    for part in parts:
-        copies.start(y.at[pl.ds(at, part.shape[0]), :], part)
-        at += part.shape[0]
+    start_parts(copies, y, parts)
     copies.start(gg, gg_out)
     copies.start(gu, gu_out)
     copies.start(p, p_out)
     copies.wait()
 
 
-def experts_backward_fast(where, gates, pieces, stash, weights, after=()):
-    n, model = pieces[0].shape
+def experts_backward_fast(where, gates, pieces, stash, weights, spans=None, after=()):
+    n, model = gates.shape[0] // 4, pieces[0].shape[1]
     _, experts, _, share = weights[0].shape
     rows, width = 4 * n, experts * share
     bf, f32 = jnp.bfloat16, jnp.float32
@@ -1013,13 +1043,14 @@
     shapes += [shape_of(rows, model)] + [shape_of(rows, width)] * 3
 
     def body(*refs):
-        experts_backward_kernel(*refs[:17], *refs[17 + len(after) :])
+        used = 9 + WEIGHT_PIECES
+        experts_backward_kernel(spans, *refs[:used], *refs[used + len(after) :])
 
     return pl.pallas_call(
         body,
         name="experts_backward",
         out_shape=shapes,
-        in_specs=[scalar_spec(), whole_spec()] + [any_spec()] * (15 + len(after)),
+        in_specs=[scalar_spec(), whole_spec()] + [any_spec()] * (7 + WEIGHT_PIECES + len(after)),
         out_specs=[any_spec()] * len(shapes),
         scratch_shapes=[
             pltpu.VMEM((rows, model), bf),
@@ -1031,36 +1062,33 @@
             pltpu.VMEM((rows, width), bf),
         ]
         + [pltpu.VMEM((model, width), bf)] * 3
-        + [pltpu.SemaphoreType.DMA((5 + 24 * experts + 13,))],
+        + [pltpu.SemaphoreType.DMA((5 + 24 * experts + 20,))],
         compiler_params=pltpu.CompilerParams(vmem_limit_bytes=52 * MIB),
-        cost_estimate=pl.CostEstimate(
-            flops=6 * rows * model * width, bytes_accessed=12 * rows * model, transcendentals=0
-        ),
+        cost_estimate=cost(6 * rows * model * width),
     )(where, gates, *pieces, *stash, *weights, *after)
 
 
 def weight_grads_kernel(experts, where, *refs):
-    sources, mine, other = refs[:10], refs[10], refs[11]
-    x, r, gg, gu, p, out, semaphores = refs[12:]
+    sources, mine, other = refs[:4], refs[4], refs[5]
+    x, g, out, semaphores = refs[6:]
     copies = Copies(semaphores)
-    for target, near, far in zip((x, r, gg, gu, p), sources[:5], sources[5:]):
+    for target, near, far in zip((x, g), sources[:2], sources[2:]):
         start_rows(copies, (near, far), target)
     copies.wait()
     band = x.shape[1] // 4
     rows = band // CORES
-    share = gg.shape[1] // experts
+    share = g.shape[1] // experts
 
     @pl.loop(0, 4)
     def _(z):
         columns = pl.ds(pl.multiple_of(z * band, band), band)
         k = lax.rem(z - where[0] + 4, 4)
-        for i, (a, b) in enumerate(((x, gg), (x, gu), (r, p))):
-            grads = contract(a[:, columns], b[...], OUTER).astype(jnp.bfloat16)
-            for core in range(CORES):
-                for e in range(experts):
-                    out[core, k, i, e] = grads[
-                        core * rows : (core + 1) * rows, e * share : (e + 1) * share
-                    ]
+        grads = contract(x[:, columns], g[...], OUTER).astype(jnp.bfloat16)
+        for core in range(CORES):
+            for e in range(experts):
+                out[core, k, e] = grads[
+                    core * rows : (core + 1) * rows, e * share : (e + 1) * share
+                ]
 
     copies.start(out.at[1 - where[1]], other)
     copies.start(out.at[where[1]], mine)
@@ -1068,61 +1096,54 @@
 
 
 def weight_grads_fast(where, near, far, experts, after=()):
-    model, width = near[0].shape[1], near[2].shape[1]
+    model, width = near[0].shape[1], near[1].shape[1]
     count = near[0].shape[0] + far[0].shape[0]
     rows, share = model // 8, width // experts
     bf = jnp.bfloat16
 
     def body(*refs):
-        weight_grads_kernel(experts, *refs[:11], *refs[11 + len(after) :])
+        weight_grads_kernel(experts, *refs[:5], *refs[5 + len(after) :])
 
     return pl.pallas_call(
         body,
         name="weight_grads",
-        out_shape=[shape_of(4, 3, experts, rows, share)] * 2,
-        in_specs=[scalar_spec()] + [any_spec()] * (10 + len(after)),
+        out_shape=[shape_of(4, experts, rows, share)] * 2,
+        in_specs=[scalar_spec()] + [any_spec()] * (4 + len(after)),
         out_specs=[any_spec()] * 2,
         scratch_shapes=[
             pltpu.VMEM((count, model), bf),
-            pltpu.VMEM((count, model), bf),
             pltpu.VMEM((count, width), bf),
-            pltpu.VMEM((count, width), bf),
-            pltpu.VMEM((count, width), bf),
-            pltpu.VMEM((CORES, 4, 3, experts, rows, share), bf),
-            pltpu.SemaphoreType.DMA((12,)),
+            pltpu.VMEM((CORES, 4, experts, rows, share), bf),
+            pltpu.SemaphoreType.DMA((6,)),
         ],
-        compiler_params=pltpu.CompilerParams(vmem_limit_bytes=56 * MIB),
-        cost_estimate=pl.CostEstimate(
-            flops=6 * count * model * width, bytes_accessed=8 * count * model, transcendentals=0
-        ),
+        compiler_params=pltpu.CompilerParams(vmem_limit_bytes=40 * MIB),
+        cost_estimate=cost(2 * count * model * width),
     )(where, *near, *far, *after)
 
 
-def cut_kernel(layer, where, w_gate, w_up, w_down, *refs):
-    outs, semaphores = refs[:4], refs[4]
-    copies = Copies(semaphores)
+def cut_kernel(where, w_gate, w_up, w_down, *outs):
     share = outs[0].shape[3]
-    for k, out in enumerate(outs):
+    matrices = (w_gate, w_up, w_down)
+    for (k, first, count), out in zip(SHARES, outs):
         columns = pl.ds(pl.multiple_of(lax.rem(where[0] + k, 4) * share, share), share)
-        for i, w in enumerate((w_gate, w_up, w_down)):
-            copies.start(w.at[layer, :, :, columns], out.at[i])
-    copies.wait()
-
-
-def cut_experts(where, weights, layer, after=()):
+        for i in range(count):
+            out[i, 0] = matrices[first + i][0, 0, :, columns]
+
+
+def cut_experts(where, weights, layer):
     _, experts, rows, hidden = weights[0].shape
-
-    def body(*refs):
-        cut_kernel(layer, *refs[:4], *refs[4 + len(after) :])
-
+    share = hidden // 4
     return pl.pallas_call(
-        body,
+        cut_kernel,
         name="cut_experts",
-        out_shape=[shape_of(3, experts, rows, hidden // 4)] * 4,
-        in_specs=[scalar_spec()] + [any_spec()] * (3 + len(after)),
-        out_specs=[any_spec()] * 4,
-        scratch_shapes=[pltpu.SemaphoreType.DMA((12,))],
-    )(where, *weights, *after)
+        grid=(experts,),
+        out_shape=[shape_of(count, experts, rows, share) for _, _, count in SHARES],
+        in_specs=[scalar_spec()]
+        + [pl.BlockSpec((1, 1, rows, hidden), lambda e: (layer, e, 0, 0))] * 3,
+        out_specs=[
+            pl.BlockSpec((count, 1, rows, share), lambda e: (0, e, 0, 0)) for _, _, count in SHARES
+        ],
+    )(where, *weights)
 
 
 def join_kernel(layer, where, *refs):
@@ -1157,59 +1178,78 @@
     )(where, *pieces, *given)
 
 
-def spread_pieces(place, block, axis=0):
-    half = block.shape[axis] // 2 // 128 * 128 if axis else block.shape[axis] // 2
-    one = place.hop(block, flip=1)
-    two = place.hop(block, flip=2)
-    head = place.hop(lax.slice_in_dim(one, 0, half, axis=axis), flip=2)
-    tail = place.hop(lax.slice_in_dim(two, half, None, axis=axis), flip=1)
+def tie(value, *events):
+    flat, tree = jax.tree.flatten(value)
+    held = lax.optimization_barrier((*flat, *events))
+    return jax.tree.unflatten(tree, held[: len(flat)])
+
+
+def spread_first(place, block):
+    return [block, place.hop(block, flip=1), place.hop(block, flip=2)]
+
+
+def spread_last(place, first, axis=0, cut=None):
+    block, one, two = first
+    cut = cut or block.shape[axis] // 2
+    head = place.hop(lax.slice_in_dim(one, 0, cut, axis=axis), flip=2)
+    tail = place.hop(lax.slice_in_dim(two, cut, None, axis=axis), flip=1)
     return [block, one, two, head, tail]
 
 
+def spread_pieces(place, block):
+    return spread_last(place, spread_first(place, block))
+
+
 def up_hops(place, block):
-    return jnp.concatenate([place.hop(block, up=k) for k in range(1, 4)])
-
-
-def gather_pieces(place, block, axis=0):
-    far = up_hops(place, block)
-    return spread_pieces(place, block, axis), spread_pieces(place, far, axis)
+    return [place.hop(block, up=k) for k in range(1, 4)]
 
 
 def add_low(a, b):
     return (a.astype(jnp.float32) + b.astype(jnp.float32)).astype(a.dtype)
 
 
-def fold_pieces(place, parts):
-    own, one_head, one_tail, two_head, two_tail, last_head, last_tail = parts
-    head = place.hop(last_head, flip=2)
-    tail = place.hop(last_tail, flip=1)
-    one_tail = place.hop(one_tail, flip=1)
-    two_head = place.hop(two_head, flip=2)
-    one_head = place.hop(add_low(one_head, head), flip=1)
-    two_tail = place.hop(add_low(two_tail, tail), flip=2)
-    return own, one_head, one_tail, two_head, two_tail
-
-
-def add_pieces(own, one_head, one_tail, two_head, two_tail, axis=0):
+def fold_first(place, parts):
+    own, one_head, two_tail, to_one, to_two = parts
+    return own, one_head, two_tail, place.hop(to_one, flip=1), place.hop(to_two, flip=2)
+
+
+def fold_sums(first):
+    own, one_head, two_tail, by_one, by_two = first
+    half = one_head.shape[0]
+    return own, add_low(one_head, by_two[half:]), add_low(two_tail, by_one[half:]), by_one, by_two
+
+
+def fold_start(place, parts):
+    return fold_sums(fold_first(place, parts))
+
+
+def fold_end(place, state):
+    own, one_head, two_tail, by_one, by_two = state
+    return own, place.hop(one_head, flip=1), place.hop(two_tail, flip=2), by_one, by_two
+
+
+def add_pieces(own, one_head, two_tail, by_one, by_two, axis=0):
     wide = lambda value: value.astype(jnp.float32)
-    one = jnp.concatenate([one_head, one_tail], axis=axis)
-    two = jnp.concatenate([two_head, two_tail], axis=axis)
+    half = one_head.shape[0]
+    one = jnp.concatenate([one_head, by_one[:half]], axis=axis)
+    two = jnp.concatenate([by_two[:half], two_tail], axis=axis)
     return wide(own) + wide(one) + wide(two)
 
 
-def blocks_kernel(own, one_head, one_tail, two_head, two_tail, *outs):
+def blocks_kernel(own, one_head, two_tail, by_one, by_two, *outs):
     half = one_head.shape[0]
     rows = outs[0].shape[0]
     step = HALF
     for start in range(0, own.shape[0], step):
-        first, second = (one_head, two_head) if start < half else (one_tail, two_tail)
+        terms = (one_head, by_two) if start < half else (two_tail, by_one)
         at = pl.ds(start % half, step)
         total = own[pl.ds(start, step), :].astype(jnp.float32)
-        total = total + first[at, :].astype(jnp.float32) + second[at, :].astype(jnp.float32)
+        for term in terms:
+            total = total + term[at, :].astype(jnp.float32)
         outs[start // rows][pl.ds(start % rows, step), :] = total.astype(jnp.bfloat16)
 
 
-def sum_blocks(own, *halves):
+def sum_blocks(own, *others):
     rows, model = own.shape
     return pl.pallas_call(
         blocks_kernel,
@@ -1217,49 +1257,98 @@
         out_shape=[shape_of(rows // 3, model)] * 3,
         in_specs=[whole_spec()] * 5,
         out_specs=[whole_spec()] * 3,
-    )(own, *halves)
-
-
-def scatter_pieces(place, near, far):
-    blocks = sum_blocks(*fold_pieces(place, far))
-    arrived = [place.hop(blocks[k - 1], up=-k) for k in range(1, 4)]
-    own, one_head, one_tail, two_head, two_tail = fold_pieces(place, near)
-    return [own, *arrived, one_head, one_tail, two_head, two_tail]
+    )(own, *others)
+
+
+def down_hops(place, blocks):
+    return [place.hop(blocks[k - 1], up=-k) for k in range(1, 4)]
 
 
 def total_of(base, extra):
-    total = base.astype(jnp.float32)
-    for block in extra[:4]:
+    *blocks, one_head, two_tail, by_one, by_two = extra
+    total = base.astype(jnp.float32) + add_pieces(blocks[0], one_head, two_tail, by_one, by_two)
+    for block in blocks[1:]:
         total = total + block.astype(jnp.float32)
-    for head, tail in (extra[4:6], extra[6:8]):
-        total = total + jnp.concatenate([head, tail]).astype(jnp.float32)
     return total
 
 
-def gather_matrices(place, pack):
-    near, far = gather_pieces(place, pack, axis=1)
-    own = near + far
-    return own + [place.hop(piece, swap=1) for piece in own]
-
-
-def scatter_matrices(place, mine, other, cut):
-    arrived = place.hop(other, swap=1)
-    total = add_low(mine, arrived)
-    rows = mine.shape[0] // 16
-    chunks = [total[m * 4 * rows : (m + 1) * 4 * rows] for m in range(4)]
-
-    def parts(first, last):
-        piece = [chunk[first * rows : last * rows] for chunk in chunks]
-        found = [piece[0]]
-        for m in range(1, 4):
-            found += [piece[m][:, :cut], piece[m][:, cut:]]
-        return found
-
-    far = add_pieces(*fold_pieces(place, parts(1, 4)), axis=1).astype(jnp.bfloat16)
-    arrived = [
-        place.hop(far[(k - 1) * rows : k * rows], up=-k) for k in range(1, 4)
-    ]
-    final = add_pieces(*fold_pieces(place, parts(0, 1)), axis=1)
+def received(near_ends, arrived):
+    own, one_head, two_tail, by_one, by_two = near_ends
+    return [own, *arrived, one_head, two_tail, by_one, by_two]
+
+
+def merge_kernel(cut, mine, arrived, own, one_head, two_tail, to_one, to_two):
+    m = pl.program_id(0)
+    total = (mine[...].astype(jnp.float32) + arrived[...].astype(jnp.float32)).astype(jnp.bfloat16)
+    rows = total.shape[0]
+
+    @pl.when(m == 0)
+    def _():
+        own[...] = total
+
+    @pl.when(m == 1)
+    def _():
+        one_head[...] = total[:, :cut]
+        to_one[:rows, :] = total[:, cut:]
+
+    @pl.when(m == 2)
+    def _():
+        to_two[:rows, :] = total[:, :cut]
+        two_tail[...] = total[:, cut:]
+
+    @pl.when(m == 3)
+    def _():
+        to_two[rows:, :] = total[:, :cut]
+        to_one[rows:, :] = total[:, cut:]
+
+
+def merge_cores(mine, arrived, cut):
+    rows, width = mine.shape[0] // 4, mine.shape[1]
+    outs = [(rows, width), (rows, cut), (rows, width - cut), (2 * rows, width - cut), (2 * rows, cut)]
+    return pl.pallas_call(
+        functools.partial(merge_kernel, cut),
+        name="merge_cores",
+        grid=(4,),
+        out_shape=[shape_of(*out) for out in outs],
+        in_specs=[pl.BlockSpec((rows, width), lambda m: (m, 0))] * 2,
+        out_specs=[pl.BlockSpec(out, lambda m: (0, 0)) for out in outs],
+        compiler_params=pltpu.CompilerParams(vmem_limit_bytes=40 * MIB),
+    )(mine, arrived)
+
+
+def pack_kernel(*refs):
+    layers = refs[0].shape[0]
+    for l in range(layers):
+        out = refs[l - layers]
+        at = 0
+        for ref in refs[:-layers]:
+            width = ref.shape[2]
+            out[:, at : at + width] = ref[l]
+            at += width
+
+
+def pack_matrices(*arrays):
+    width = sum(a.shape[2] for a in arrays)
+    layers, rows, _ = arrays[0].shape
+    return pl.pallas_call(
+        pack_kernel,
+        name="pack_matrices",
+        out_shape=[shape_of(rows, width)] * layers,
+        in_specs=[whole_spec()] * len(arrays),
+        out_specs=[whole_spec()] * layers,
+    )(*arrays)
+
+
+def scatter_matrices(place, other_far, other_near, mine_far, mine_near, cut, event):
+    rows = mine_near.shape[0] // 4
+    arrived_far = place.hop(other_far, swap=1)
+    arrived_near = place.hop(other_near, swap=1)
+    far = fold_first(place, merge_cores(mine_far, arrived_far, cut))
+    near = fold_start(place, merge_cores(mine_near, arrived_near, cut))
+    far = fold_sums(tie(far, event))
+    far = add_pieces(*fold_end(place, far), axis=1).astype(jnp.bfloat16)
+    arrived = down_hops(place, [far[k * rows : (k + 1) * rows] for k in range(3)])
+    final = add_pieces(*fold_end(place, near), axis=1)
     for block in arrived:
         final = final + block.astype(jnp.float32)
     return final
@@ -1281,18 +1370,10 @@
     )
 
 
-def tie(value, *events):
-    flat, tree = jax.tree.flatten(value)
-    held = lax.optimization_barrier((*flat, *events))
-    return jax.tree.unflatten(tree, held[: len(flat)])
-
-
-def gate_rows_of(place, routes, gates, expert_count):
-    found = gather_gates(place, routes, gates, expert_count)
-    owned = expert_count // place.columns
-    order = jnp.stack(found)
+def gate_rows_of(place, line):
+    order = jnp.stack(spread_gates(place, line))
     order = jnp.transpose(order, (2, 0, 1, 4, 3))
-    order = jnp.pad(order, ((0, 0),) * 4 + ((0, 8 - owned),))
+    order = jnp.pad(order, ((0, 0),) * 4 + ((0, 8 - order.shape[4]),))
     return [
         (layer[:, :1].reshape(-1, 8), layer[:, 1:].reshape(-1, 8)) for layer in order
     ]
@@ -1320,74 +1401,173 @@
     layer_count, _, experts, _ = w_gate.shape
     expert_count = experts * place.columns
     in_width = query.shape[2] + key.shape[2] + value.shape[2]
-    packs = []
-    for l in range(layer_count):
-        gains = jnp.stack([norm_attn[l], norm_ffn[l]], axis=1)
-        gains = jnp.pad(gains, ((0, 0), (0, EXTRA - 2)))
-        packs.append(jnp.concatenate([query[l], key[l], value[l], output[l], gains], axis=1))
+    gains = jnp.stack([norm_attn, norm_ffn], axis=2)
+    gains = jnp.pad(gains, ((0, 0), (0, 0), (0, EXTRA - 2)))
+    packs = pack_matrices(query, key, value, output, gains)
     cut = packs[0].shape[1] // 2 // 128 * 128
     weights = [jnp.transpose(w, (0, 2, 1, 3)) for w in (w_gate, w_up, w_down)]
     tables = tables_of(lengths[0], rows)
 
-    def bring_experts(layer, after):
-        cuts = cut_experts(where, weights, layer, after=after)
-        own = [cuts[0]] + [place.hop(cuts[k], up=k) for k in range(1, 4)]
-        return own + [place.hop(piece, swap=1) for piece in own]
-
-    matrices = [gather_matrices(place, packs[0])]
-    bank = [bring_experts(0, (matrices[0][5],))]
-    gate_rows = gate_rows_of(place, routes, gates, expert_count)
+    def share_cores(shares):
+        return list(shares) + [place.hop(piece, swap=1) for piece in shares]
+
+    def line_of(block):
+        return jnp.concatenate([block] + up_hops(place, block))
+
+    cuts = [cut_experts(where, weights, l) for l in range(layer_count)]
+    gate_line = gates_line(place, routes, gates, expert_count)
+    line = jnp.concatenate([packs[0]] + tie(up_hops(place, packs[0]), cuts[0][0], gate_line))
+    first = spread_first(place, line)
+    gate_rows = gate_rows_of(place, gate_line)
+    cuts[0] = tie(cuts[0], line)
+    shares = [cuts[0][0], place.hop(cuts[0][1], up=1), place.hop(cuts[0][2], up=3)]
+    first = tie(first, shares[1], shares[2], gate_rows[0][0], gate_rows[-1][0], cuts[-1][0])
+    shares.append(place.hop(tie(cuts[0][3], first[0]), up=2))
+    matrices = [share_cores(tie(spread_last(place, first, axis=1, cut=cut), shares[3]))]
+    shares.append(place.hop(tie(cuts[0][4], matrices[0][0]), up=2))
 
     base, extra = tokens.astype(jnp.float32), []
     stored = []
-    last = None
     for l in range(layer_count):
-        outs = attend_forward_fast(where, base, extra, tables, matrices[l], in_width)
+        more = l + 1 < layer_count
+        after = [rows for pair in gate_rows for rows in pair] if l == 0 else []
+        outs = attend_forward_fast(where, base, extra, tables, matrices[l], in_width, after=after)
         h, m, nf = outs[:3]
-        near, far = gather_pieces(place, nf)
-        if l + 1 < layer_count:
-            matrices.append(gather_matrices(place, tie(packs[l + 1], nf)))
-        y_near = experts_forward_fast(where, gate_rows[l][0], near, bank[l])
-        y_far = experts_forward_fast(where, gate_rows[l][1], far, bank[l])
-        if l + 1 < layer_count:
-            bank.append(bring_experts(l + 1, (y_far[0],)))
+        nf, last_share = tie((nf, shares[4]))
+        bank_l = share_cores(shares[:4] + [last_share])
+        ups = up_hops(place, nf)
+        near = spread_pieces(place, nf)
+        far = jnp.concatenate(tie(ups, near[3], near[4]))
+        far = spread_first(place, far)
+        y_near = experts_forward_fast(where, gate_rows[l][0], near, bank_l)
+        near_state = fold_start(place, y_near[:5])
+        line = line_of(tie(packs[l + 1] if more else cotangent, y_near[0]))
+        far = spread_last(place, tie(far, y_near[0]))
+        passing = spread_first(place, tie(line, far[3], far[4]))
+        y_far = experts_forward_fast(
+            where, gate_rows[l][1], far, bank_l, after=(near_state[1], near_state[2])
+        )
+        stored.append((h, outs, y_near[5:], y_far[5:], bank_l))
+        if more:
+            y_far, passing = tie((y_far, passing))
+            far_state = fold_start(place, y_far[:5])
+            ready = tie(cuts[l + 1], far[3])
+            shares = [ready[0], place.hop(ready[1], up=1), None, place.hop(ready[3], up=2)]
+            far_state, one, two = tie((far_state, shares[1], shares[3]), near_state[1])
+            third = place.hop(tie(ready[2], far_state[1]), up=3)
+            far_ends, third = tie((fold_end(place, far_state), third))
+            blocks = sum_blocks(*far_ends)
+            matrices.append(share_cores(spread_last(place, tie(passing, blocks[0]), 1, cut)))
+            arrived = down_hops(place, blocks)
+            shares = [ready[0], one, third, two]
+            shares.append(place.hop(tie(ready[4], blocks[0]), up=2))
+            base, extra = m, received(fold_end(place, near_state), arrived)
         else:
-            last = gather_pieces(place, tie(cotangent, y_far[0]))
-        base, extra = m, scatter_pieces(place, y_near[:7], y_far[:7])
-        stored.append((h, outs, y_near[7:], y_far[7:]))
-    result = total_of(base, extra).astype(jnp.bfloat16)
-
-    upstream = cotangent.astype(jnp.float32)
+            last = spread_last(place, passing)
+
+    upstream = cotangent
     zero = jnp.zeros((rows, model), jnp.bfloat16)
     sums = [None] * layer_count
     joined = None
     for l in reversed(range(layer_count)):
-        h, outs, kept_near, kept_far = stored[l]
-        near, far = last
-        b_near = experts_backward_fast(where, gate_rows[l][0], near, kept_near[1:], bank[l])
-        b_far = experts_backward_fast(where, gate_rows[l][1], far, kept_far[1:], bank[l])
-        extra = scatter_pieces(place, b_near[:7], b_far[:7])
-        mine, other = weight_grads_fast(
-            where, (kept_near[0], *b_near[7:]), (kept_far[0], *b_far[7:]), experts
-        )
-        arrived = place.hop(other, swap=1)
-        total = [add_low(mine[k], arrived[k]) for k in range(4)]
-        pieces = [total[0]] + [place.hop(total[k], up=k) for k in range(1, 4)]
+        h, outs, kept_near, kept_far, bank_l = stored[l]
         m, na, q, k, v, o, lse, gains = outs[1], *outs[3:]
-        upstream, low, mine, other = attend_backward_fast(
+
+        spans = (spans_of(False), spans_of(True)) if l + 1 == layer_count else (None, None)
+
+        def run_near(after=()):
+            return experts_backward_fast(
+                where, gate_rows[l][0], near, kept_near[1:], bank_l, spans[0], after=after
+            )
+
+        def run_far(after=()):
+            return experts_backward_fast(
+                where, gate_rows[l][1], far, kept_far[1:], bank_l, spans[1], after=after
+            )
+
+        if l + 1 == layer_count:
+            near = far = last
+            b_near = run_near(after=(y_far[0],))
+            near_state_b = fold_start(place, b_near[:5])
+            b_far = run_far(after=(b_near[0],))
+            far_first = fold_first(place, b_far[:5])
+        else:
+            ups = up_hops(place, low)
+            near = spread_pieces(place, low)
+            far = jnp.concatenate(tie(ups, near[3], near[4]))
+            far = spread_first(place, far)
+            total = tie(held_total(), far[0])
+            came = [place.hop(total[1], up=1), place.hop(total[3], up=3)]
+            b_near = run_near()
+            near_state_b = fold_start(place, b_near[:5])
+            far, came = tie((far, came), b_near[0])
+            far = spread_last(place, far)
+            came.insert(1, place.hop(tie(total[2], far[0]), up=2))
+            b_far = run_far(after=(near_state_b[1], near_state_b[2]))
+            result_ends = fold_end(place, tie(result_state, far[3], far[4]))
+            b_far, came, result_ends = tie((b_far, came, result_ends))
+            far_first = fold_first(place, b_far[:5])
+            arrived = down_hops(place, sum_blocks(*result_ends))
+            far_first = tie(far_first, *arrived)
+            result = total_of(stored[-1][1][1], received(result_near, arrived)).astype(jnp.bfloat16)
+            joined = join_experts(where, [total[0], *came], l + 1, layer_count, joined)
+
+        def weight_grads(i, after):
+            pick = lambda kept, found: ((kept[0], found[6 + i]) if i < 2 else (found[5], found[8]))
+            return weight_grads_fast(
+                where, pick(kept_near, b_near), pick(kept_far, b_far), experts, after=after
+            )
+
+        near_ends = fold_end(place, near_state_b)
+        grads = [weight_grads(0, (b_far[0],))]
+        grads.append(weight_grads(1, (grads[0][0],)))
+        far_state_b = fold_sums(tie(far_first, grads[1][0]))
+        if l == 0:
+            grads.append(weight_grads(2, (far_state_b[1], far_state_b[2])))
+        far_ends = tie(fold_end(place, far_state_b), grads[-1][0], near_ends[1], near_ends[2])
+        blocks = sum_blocks(*far_ends)
+        arrived = down_hops(place, blocks)
+        if l:
+            grads.append(weight_grads(2, (far_ends[0],)))
+
+        def total_grads():
+            swapped = [place.hop(other, swap=1) for _, other in grads]
+            return [
+                jnp.stack([add_low(grads[i][0][k], swapped[i][k]) for i in range(3)])
+                for k in range(4)
+            ]
+
+        if l == 0:
+            total = total_grads()
+            ready = tie(total, *arrived)
+            came = [place.hop(ready[1], up=1), place.hop(ready[3], up=3)]
+        if l + 1 == layer_count:
+            result_state = fold_start(place, tie(y_far[:5], blocks[0]))
+        upstream, low, *partial = attend_backward_fast(
+            l == 0,
             where,
             zero,
             upstream,
-            extra,
+            received(near_ends, arrived),
             (h, m, na, q, k, v, o, lse, gains),
             tables,
             matrices[l],
             in_width,
+            after=() if l else (*total, joined[0]),
         )
-        if l:
-            last = gather_pieces(place, low)
-        sums[l] = scatter_matrices(place, mine, other, cut)
-        joined = join_experts(where, pieces, l, layer_count, joined)
+        if l + 1 == layer_count:
+            held_total = total_grads
+            result_near = fold_end(place, near_state)
+            low, result_state = tie((low, result_state), *result_near)
+        if l == 0:
+            partial, came = tie((partial, came), sums[-1])
+            came.insert(1, place.hop(tie(total[2], upstream), up=2))
+            sums[l] = scatter_matrices(place, *partial, cut, came[1])
+            joined = join_experts(where, [total[0], *came], l, layer_count, joined)
+        else:
+            sums[l] = lax.psum_scatter(
+                partial[0], AXES, scatter_dimension=0, tiled=True
+            ).astype(jnp.float32)
     sums = jnp.stack(sums)
     gain_sums = sums[:, :, in_width + model :]
     starts = (0, query.shape[2], query.shape[2] + key.shape[2], in_width, in_width + model)

time: 1670 us -> 1260 us (0.75)
  Pallas kernels: 488 us -> 328 us
  starting transfers between devices: 350 us -> 209 us
  waiting for transfers between devices: 679 us -> 593 us
  local copies, waits for them, and re-layouts: 93 us -> 68.4 us
  other arithmetic: 51.3 us -> 31.4 us
    pallas_call x4 -> x11, Pallas kernels: 234 us -> 64.4 us  [the longest x6 48.3 us: weight_grads_fast(): pl.pallas_call(body, name='weight_grads', out_shape=[shape_of(4, experts,...]
    ppermute x206 -> x157, starting transfers between devices: 350 us -> 209 us  [hop(): return lax.ppermute(value, AXES, pairs)]
    ppermute x206 -> x157, waiting for transfers between devices: 679 us -> 593 us  [hop(): return lax.ppermute(value, AXES, pairs)]
    convert_element_type x28 -> x26, other arithmetic: 38.2 us -> 15 us  [add_low(): return (a.astype(jnp.float32) + b.astype(jnp.float32)).astype(a.dtype)]
    unnamed x400 -> x443, local copies, waits for them, and re-layouts: 61.3 us -> 54.3 us
  transfers between devices with their start and end apart: 206 -> 158, of which waited for: 79 -> 65; matrix products, arithmetic and copies ran while one was open for 5% -> 3% of each run, Pallas kernels for 27% -> 23%
where the time goes in v3:
time: 1260 us; the launch traced here: 1250 us
  waiting for transfers between devices  593 us (47%)
  Pallas kernels  328 us (26%)
  starting transfers between devices  209 us (17%)
  local copies, waits for them, and re-layouts  68.4 us (5%)
  other arithmetic  31.4 us (2%)
  between operations  16.9 us (1%)
    ppermute x157, waiting for transfers between devices, hop(): return lax.ppermute(value, AXES, pairs)  593 us
    ppermute x157, starting transfers between devices, hop(): return lax.ppermute(value, AXES, pairs)  209 us
    pallas_call x4, Pallas kernels, experts_backward_fast(): pl.pallas_call(body, name='experts_backward', out_shape=shapes, in_specs=...  78.1 us
    pallas_call x4, Pallas kernels, experts_forward_fast(): pl.pallas_call(body, name='experts_forward', out_shape=shapes, in_specs=[...  70.1 us
    pallas_call x2, Pallas kernels, attend_backward_fast(): pl.pallas_call(body, name='attend_backward', out_shape=shapes, in_specs=[...  60.9 us
    unnamed x443, local copies, waits for them, and re-layouts  54.3 us
    pallas_call x6, Pallas kernels, weight_grads_fast(): pl.pallas_call(body, name='weight_grads', out_shape=[shape_of(4, experts,...  48.3 us
    pallas_call x2, Pallas kernels, attend_forward_fast(): pl.pallas_call(body, name='attend_forward', out_shape=shapes, in_specs=[s...  31.8 us
  transfers between devices with their start and end apart: 158, of which 65 were waited for; matrix products, arithmetic and copies ran while one was open for 3% of the time, Pallas kernels for 23%

profile of v3, /device:TPU:0, one launch (start us, length us, event | category | flops | bytes accessed | tf_op | source)
XLA Modules:
  0.0 1245.7 jit_solution(5971302724559122422)
XLA Ops:
  30.3 16.8 %collective-permute-done.5 = f32[2,20,128]{2,1,0:T(8,128)S(1)} collective-permute-done((f32[2,20,128]{2,1,0:T(8,128)S(1)}, f32[2,20,128]{2,1,0:T(8,128)S(1)}, u32[]{:S(2)}, u32[]{:S(2)}) %collective-permute-start.5) | collective-permute-done | bytes 20512 | tf_op jit(solution)/shard_map/ppermute | solution.py:38
  53.5 8.9 collective-permute-start.8
  63.1 24.4 %collective-permute-done.10 = f32[4,2,5,128]{3,0,2,1:T(4,128)S(1)} collective-permute-done((f32[4,2,5,128]{3,0,2,1:T(4,128)S(1)}, f32[4,2,5,128]{3,0,2,1:T(4,128)S(1)}, u32[]{:S(2)}, u32[]{:S(2)}) %collective-permute-start.10) | collective-permute-done | bytes 20512 | tf_op jit(solution)/shard_map/ppermute | solution.py:38
  105.0 8.1 collective-permute-start.15
  113.1 8.3 collective-permute-done.15.refs_10_.refs_12_
  145.9 16.0 %attend_forward.2 = (f32[128,1536]{1,0:T(8,128)S(1)}, f32[128,1536]{1,0:T(8,128)S(1)}, bf16[128,1536]{1,0:T(8,128)(2,1)S(1)}, bf16[128,1536]{1,0:T(8,128)(2,1)S(...) custom-call(s32[3]{0:T(128)S(1)} %copy-done.101, ...), custom_call_target="tpu_custom_call" | custom-call | flops 103809024 | tf_op jit(solution)/shard_map/attend_forward/pallas_call | solution.py:692
  180.7 15.1 %collective-permute-done.32 = bf16[128,1536]{1,0:T(8,128)(2,1)S(1)} collective-permute-done((bf16[128,1536]{1,0:T(8,128)(2,1)S(1)}, bf16[128,1536]{1,0:T(8,128)(2,1)S(1)}, u32[]{:S(2)}, u32[]{:S(2)}) %collective-permute-start.32) | collective-permute-done | bytes 393248 | tf_op jit(solution)/shard_map/ppermute | solution.py:38
  201.5 13.0 %experts_forward.4 = (bf16[128,1536]{1,0:T(8,128)(2,1)S(1)}, bf16[64,1536]{1,0:T(8,128)(2,1)S(1)}, bf16[64,1536]{1,0:T(8,128)(2,1)S(1)}, bf16[128,1536]{1,0:T(8,...) custom-call(s32[3]{0:T(128)S(1)} %copy-done.101, ...), custom_call_target="tpu_custom_call" | custom-call | flops 188743680 | tf_op jit(solution)/shard_map/experts_forward/pallas_call | solution.py:980
  215.3 8.9 collective-permute-start.40
  225.8 11.0 collective-permute-start.42
  239.0 13.4 %collective-permute-done.41 = bf16[48,4224]{1,0:T(8,128)(2,1)S(1)} collective-permute-done((bf16[48,4224]{1,0:T(8,128)(2,1)S(1)}, bf16[48,4224]{1,0:T(8,128)(2,1)S(1)}, u32[]{:S(2)}, u32[]{:S(2)}) %collective-permute-start.41) | collective-permute-done | bytes 405536 | tf_op jit(solution)/shard_map/ppermute | solution.py:38
  260.9 40.6 %collective-permute-done.39.refs_8_ = bf16[128,1536]{1,0:T(8,128)(2,1)S(1)} collective-permute-done((bf16[128,1536]{1,0:T(8,128)(2,1)S(1)}, bf16[128,1536]{1,0:T(8,128)(2,1)S(1)}, u32[]{:S(2)}, u32[]{:S(2)}) %collective-permute-start.39) | collective-permute-done | bytes 393248 | tf_op jit(solution)/shard_map/ppermute | solution.py:38
  303.5 22.0 %experts_forward.5 = (bf16[384,1536]{1,0:T(8,128)(2,1)}, bf16[192,1536]{1,0:T(8,128)(2,1)S(1)}, bf16[192,1536]{1,0:T(8,128)(2,1)S(1)}, bf16[384,1536]{1,0:T(8,12...) custom-call(s32[3]{0:T(128)S(1)} %copy-done.101, ...), custom_call_target="tpu_custom_call" | custom-call | flops 566231040 | tf_op jit(solution)/shard_map/experts_forward/pallas_call | solution.py:980
  335.6 15.6 %collective-permute-done.46.by_one = bf16[384,1536]{1,0:T(8,128)(2,1)S(1)} collective-permute-done((bf16[384,1536]{1,0:T(8,128)(2,1)}, bf16[384,1536]{1,0:T(8,128)(2,1)S(1)}, u32[]{:S(2)}, u32[]{:S(2)}) %collective-permute-start.46) | collective-permute-done | bytes 1179680 | tf_op jit(solution)/shard_map/ppermute | solution.py:38
  352.4 8.0 collective-permute-done.48.refs_10_.refs_12_
  365.6 10.3 collective-permute-done.49.one_head
  397.7 22.1 %collective-permute-done.53.refs_4_ = bf16[128,1536]{1,0:T(8,128)(2,1)S(1)} collective-permute-done((bf16[128,1536]{1,0:T(8,128)(2,1)}, bf16[128,1536]{1,0:T(8,128)(2,1)S(1)}, u32[]{:S(2)}, u32[]{:S(2)}) %collective-permute-start.53) | collective-permute-done | bytes 393248 | tf_op jit(solution)/shard_map/ppermute | solution.py:38
  429.8 15.8 %attend_forward.3 = (f32[128,1536]{1,0:T(8,128)S(1)}, f32[128,1536]{1,0:T(8,128)S(1)}, bf16[128,1536]{1,0:T(8,128)(2,1)S(1)}, bf16[128,1536]{1,0:T(8,128)(2,1)S(...) custom-call(s32[3]{0:T(128)S(1)} %copy-done.102, ...), custom_call_target="tpu_custom_call" | custom-call | flops 103809024 | tf_op jit(solution)/shard_map/attend_forward/pallas_call | solution.py:692
  464.2 15.4 %collective-permute-done.82 = bf16[128,1536]{1,0:T(8,128)(2,1)S(1)} collective-permute-done((bf16[128,1536]{1,0:T(8,128)(2,1)S(1)}, bf16[128,1536]{1,0:T(8,128)(2,1)S(1)}, u32[]{:S(2)}, u32[]{:S(2)}) %collective-permute-start.82) | collective-permute-done | bytes 393248 | tf_op jit(solution)/shard_map/ppermute | solution.py:38
  489.9 13.0 %experts_forward.6 = (bf16[128,1536]{1,0:T(8,128)(2,1)S(1)}, bf16[64,1536]{1,0:T(8,128)(2,1)S(1)}, bf16[64,1536]{1,0:T(8,128)(2,1)S(1)}, bf16[128,1536]{1,0:T(8,...) custom-call(s32[3]{0:T(128)S(1)} %copy-done.102, ...), custom_call_target="tpu_custom_call" | custom-call | flops 188743680 | tf_op jit(solution)/shard_map/experts_forward/pallas_call | solution.py:980
  502.9 8.0 collective-permute-start.78
  520.3 15.9 %collective-permute-done.79 = bf16[128,1536]{1,0:T(8,128)(2,1)S(1)} collective-permute-done((bf16[128,1536]{1,0:T(8,128)(2,1)S(1)}, bf16[128,1536]{1,0:T(8,128)(2,1)S(1)}, u32[]{:S(2)}, u32[]{:S(2)}) %collective-permute-start.79) | collective-permute-done | bytes 393248 | tf_op jit(solution)/shard_map/ppermute | solution.py:38
  540.7 33.2 %collective-permute-done.88.refs_3_ = bf16[512,1536]{1,0:T(8,128)(2,1)S(1)} collective-permute-done((bf16[512,1536]{1,0:T(8,128)(2,1)S(1)}, bf16[512,1536]{1,0:T(8,128)(2,1)S(1)}, u32[]{:S(2)}, u32[]{:S(2)}) %collective-permute-start.88) | collective-permute-done | bytes 1572896 | tf_op jit(solution)/shard_map/ppermute | solution.py:38
  583.3 22.1 %experts_forward.7 = (bf16[384,1536]{1,0:T(8,128)(2,1)}, bf16[192,1536]{1,0:T(8,128)(2,1)S(1)}, bf16[192,1536]{1,0:T(8,128)(2,1)S(1)}, bf16[384,1536]{1,0:T(8,12...) custom-call(s32[3]{0:T(128)S(1)} %copy-done.102, ...), custom_call_target="tpu_custom_call" | custom-call | flops 566231040 | tf_op jit(solution)/shard_map/experts_forward/pallas_call | solution.py:980
  607.5 12.7 %experts_backward.4 = (bf16[128,1536]{1,0:T(8,128)(2,1)S(1)}, bf16[64,1536]{1,0:T(8,128)(2,1)S(1)}, bf16[64,1536]{1,0:T(8,128)(2,1)S(1)}, bf16[128,1536]{1,0:T(8...) custom-call(s32[3]{0:T(128)S(1)} %copy-done.102, ...), custom_call_target="tpu_custom_call" | custom-call | flops 188743680 | tf_op jit(solution)/shard_map/experts_backward/pallas_call | solution.py:1049
  620.4 26.0 %experts_backward.5 = (bf16[384,1536]{1,0:T(8,128)(2,1)}, bf16[192,1536]{1,0:T(8,128)(2,1)}, bf16[192,1536]{1,0:T(8,128)(2,1)}, bf16[384,1536]{1,0:T(8,128)(2,1)...) custom-call(s32[3]{0:T(128)S(1)} %copy-done.102, ...), custom_call_target="tpu_custom_call" | custom-call | flops 566231040 | tf_op jit(solution)/shard_map/experts_backward/pallas_call | solution.py:1049
  662.3 8.1 weight_grads.7
  670.4 10.0 collective-permute-done.98.refs_9_
  688.3 10.0 collective-permute-done.97.refs_7_
  704.1 11.2 collective-permute-start.100
  732.1 13.5 %collective-permute-done.101.refs_5_ = bf16[128,1536]{1,0:T(8,128)(2,1)S(1)} collective-permute-done((bf16[128,1536]{1,0:T(8,128)(2,1)}, bf16[128,1536]{1,0:T(8,128)(2,1)S(1)}, u32[]{:S(2)}, u32[]{:S(2)}) %collective-permute-start.101) | collective-permute-done | bytes 393248 | tf_op jit(solution)/shard_map/ppermute | solution.py:38
  748.8 30.6 %attend_backward.2 = (f32[128,1536]{1,0:T(8,128)}, bf16[128,1536]{1,0:T(8,128)(2,1)}, bf16[1536,4224]{1,0:T(8,128)(2,1)}) custom-call(s32[3]{0:T(128)} %pad_add_fusion.where.refs_0_, bf16[128,1536]{1,0:T(8,128)(2,1)} %broadcast_in_dim.61.refs_1_, bf16[128,1536]{1,0:T(8,128)(2,1)} %refs_2_.3, bf16[128,1536]{1,0:T(8,128)(2,1)} %copy-done.57, ...), custom_call_target="tpu_custom_call" | custom-call | flops 207618048 | tf_op jit(solution)/shard_map/attend_backward/pallas_call | solution.py:856
  801.8 15.5 %collective-permute-done.106 = bf16[128,1536]{1,0:T(8,128)(2,1)S(1)} collective-permute-done((bf16[128,1536]{1,0:T(8,128)(2,1)S(1)}, bf16[128,1536]{1,0:T(8,128)(2,1)S(1)}, u32[]{:S(2)}, u32[]{:S(2)}) %collective-permute-start.106) | collective-permute-done | bytes 393248 | tf_op jit(solution)/shard_map/ppermute | solution.py:38
  822.3 8.1 collective-permute-start.117
  830.4 13.0 %experts_backward.6 = (bf16[128,1536]{1,0:T(8,128)(2,1)S(1)}, bf16[64,1536]{1,0:T(8,128)(2,1)S(1)}, bf16[64,1536]{1,0:T(8,128)(2,1)S(1)}, bf16[128,1536]{1,0:T(8...) custom-call(s32[3]{0:T(128)S(1)} %copy-done.104, ...), custom_call_target="tpu_custom_call" | custom-call | flops 188743680 | tf_op jit(solution)/shard_map/experts_backward/pallas_call | solution.py:1049
  848.7 12.2 collective-permute-done.118.refs_3_
  868.4 10.9 collective-permute-done.119.refs_5_
  890.2 26.4 %experts_backward.7 = (bf16[384,1536]{1,0:T(8,128)(2,1)}, bf16[192,1536]{1,0:T(8,128)(2,1)}, bf16[192,1536]{1,0:T(8,128)(2,1)}, bf16[384,1536]{1,0:T(8,128)(2,1)...) custom-call(s32[3]{0:T(128)S(1)} %copy-done.104, ...), custom_call_target="tpu_custom_call" | custom-call | flops 566231040 | tf_op jit(solution)/shard_map/experts_backward/pallas_call | solution.py:1049
  932.7 8.2 weight_grads.9
  949.2 42.0 %collective-permute-done.127 = bf16[128,1536]{1,0:T(8,128)(2,1)S(1)} collective-permute-done((bf16[128,1536]{1,0:T(8,128)(2,1)}, bf16[128,1536]{1,0:T(8,128)(2,1)S(1)}, u32[]{:S(2)}, u32[]{:S(2)}) %collective-permute-start.127) | collective-permute-done | bytes 393248 | tf_op jit(solution)/shard_map/ppermute | solution.py:38
  995.2 8.2 weight_grads.11
  1010.2 18.1 %collective-permute-done.134.refs_8_ = bf16[64,1536]{1,0:T(8,128)(2,1)S(1)} collective-permute-done((bf16[64,1536]{1,0:T(8,128)(2,1)S(1)}, bf16[64,1536]{1,0:T(8,128)(2,1)S(1)}, u32[]{:S(2)}, u32[]{:S(2)}) %collective-permute-start.134) | collective-permute-done | bytes 196640 | tf_op jit(solution)/shard_map/ppermute | solution.py:38
  1042.6 10.1 collective-permute-done.135.refs_4_
  1052.6 40.5 %collective-permute-done.136.refs_5_ = bf16[128,1536]{1,0:T(8,128)(2,1)S(1)} collective-permute-done((bf16[128,1536]{1,0:T(8,128)(2,1)}, bf16[128,1536]{1,0:T(8,128)(2,1)S(1)}, u32[]{:S(2)}, u32[]{:S(2)}) %collective-permute-start.136) | collective-permute-done | bytes 393248 | tf_op jit(solution)/shard_map/ppermute | solution.py:38
  1101.2 30.3 %attend_backward.3 = (f32[128,1536]{1,0:T(8,128)}, bf16[128,1536]{1,0:T(8,128)(2,1)}, bf16[576,4224]{1,0:T(8,128)(2,1)}, bf16[192,4224]{1,0:T(8,128)(2,1)}, bf16...) custom-call(s32[3]{0:T(128)} %pad_add_fusion.where.refs_0_, bf16[128,1536]{1,0:T(8,128)(2,1)} %broadcast_in_dim.61.refs_1_, ...), custom_call_target="tpu_custom_call" | custom-call | flops 207618048 | tf_op jit(solution)/shard_map/attend_backward/pallas_call | solution.py:856
  1150.0 31.5 %collective-permute-done.144 = bf16[96,2048]{1,0:T(8,128)(2,1)S(1)} collective-permute-done((bf16[96,2048]{1,0:T(8,128)(2,1)S(1)}, bf16[96,2048]{1,0:T(8,128)(2,1)S(1)}, u32[]{:S(2)}, u32[]{:S(2)}) %collective-permute-start.144) | collective-permute-done | bytes 393248 | tf_op jit(solution)/shard_map/ppermute | solution.py:38
  1186.4 14.0 %collective-permute-done.152 = bf16[144,2048]{1,0:T(8,128)(2,1)S(1)} collective-permute-done((bf16[144,2048]{1,0:T(8,128)(2,1)S(1)}, bf16[144,2048]{1,0:T(8,128)(2,1)S(1)}, u32[]{:S(2)}, u32[]{:S(2)}) %collective-permute-start.152) | collective-permute-done | bytes 589856 | tf_op jit(solution)/shard_map/ppermute | solution.py:38
  1212.5 22.0 %collective-permute-done.155 = bf16[48,4224]{1,0:T(8,128)(2,1)S(1)} collective-permute-done((bf16[48,4224]{1,0:T(8,128)(2,1)S(1)}, bf16[48,4224]{1,0:T(8,128)(2,1)S(1)}, u32[]{:S(2)}, u32[]{:S(2)}) %collective-permute-start.155) | collective-permute-done | bytes 405536 | tf_op jit(solution)/shard_map/ppermute | solution.py:38
  (848 shorter events, 409.8 us)
Async XLA Ops:
  7.2 1227.8 %reduce-scatter.2.cloned.1.call-start = ((), (), s32[]{:S(2)}) async-start(), calls=%async_computation.1 | async-start | bytes 13381632 | tf_op jit(solution)/shard_map/reduce_scatter | solution.py:1568
  50.5 50.3 %collective-permute-start.6 = (bf16[192,4224]{1,0:T(8,128)(2,1)}, bf16[192,4224]{1,0:T(8,128)(2,1)}, u32[]{:S(2)}, u32[]{:S(2)}) collective-permute-start(bf16[192,4224]{1,0:T(8,128)(2,1)} %constant_dynamic-update-slice_fusion.refs_5_.refs_23_), channel_id=1, source_target_pairs={{0,1},{1,0},{2,3},{3,2},{4,5},{5,4},{6,7},{7,6},{8,9},{9,8},{10,11... | collective-permute-start | bytes 4866056 | tf_op jit(solution)/shard_map/ppermute | solution.py:38
  52.0 48.8 %collective-permute-start.7 = (bf16[192,4224]{1,0:T(8,128)(2,1)}, bf16[192,4224]{1,0:T(8,128)(2,1)}, u32[]{:S(2)}, u32[]{:S(2)}) collective-permute-start(bf16[192,4224]{1,0:T(8,128)(2,1)} %constant_dynamic-update-slice_fusion.refs_5_.refs_23_), channel_id=1, source_target_pairs={{0,2},{1,3},{2,0},{3,1},{4,6},{5,7},{6,4},{7,5},{8,10},{9,11},{10,... | collective-permute-start | bytes 4866056 | tf_op jit(solution)/shard_map/ppermute | solution.py:38
  53.5 47.3 %collective-permute-start.8 = (bf16[3,5,192,128]{3,2,1,0:T(8,128)(2,1)}, bf16[3,5,192,128]{3,2,1,0:T(8,128)(2,1)S(1)}, u32[]{:S(2)}, u32[]{:S(2)}) collective-permute-start(bf16[3,5,192,128]{3,2,1,0:T(8,128)(2,1)} %get-tuple-element.322), channel_id=1, source_target_pairs={{0,8},{1,9},{2,10},{3,11},{4,12},{5,13},{6,14},{7,15},{8,16},{9,17... | collective-permute-start | bytes 2211848 | tf_op jit(solution)/shard_map/ppermute | solution.py:38
  62.4 38.4 %collective-permute-start.9 = (bf16[3,5,192,128]{3,2,1,0:T(8,128)(2,1)}, bf16[3,5,192,128]{3,2,1,0:T(8,128)(2,1)S(1)}, u32[]{:S(2)}, u32[]{:S(2)}) collective-permute-start(bf16[3,5,192,128]{3,2,1,0:T(8,128)(2,1)} %get-tuple-element.323), channel_id=1, source_target_pairs={{0,24},{1,25},{2,26},{3,27},{4,28},{5,29},{6,30},{7,31},{8,0},{9,1... | collective-permute-start | bytes 2211848 | tf_op jit(solution)/shard_map/ppermute | solution.py:38
  128.1 36.6 %collective-permute-start.21 = (bf16[2,5,192,128]{3,2,1,0:T(8,128)(2,1)}, bf16[2,5,192,128]{3,2,1,0:T(8,128)(2,1)S(1)}, u32[]{:S(2)}, u32[]{:S(2)}) collective-permute-start(bf16[2,5,192,128]{3,2,1,0:T(8,128)(2,1)} %get-tuple-element.338), channel_id=1, source_target_pairs={{0,16},{1,17},{2,18},{3,19},{4,20},{5,21},{6,22},{7,23},{8,24},{9,... | collective-permute-start | bytes 1474568 | tf_op jit(solution)/shard_map/ppermute | solution.py:38
  196.1 40.7 %collective-permute-start.34 = (bf16[384,1536]{1,0:T(8,128)(2,1)S(1)}, bf16[384,1536]{1,0:T(8,128)(2,1)S(1)}, u32[]{:S(2)}, u32[]{:S(2)}) collective-permute-start(bf16[384,1536]{1,0:T(8,128)(2,1)S(1)} %constant_dynamic-update-slice_fusion.4.refs_2_), channel_id=1, source_target_pairs={{0,1},{1,0},{2,3},{3,2},{4,5},{5,4},{6,7},{7,6},{8,9},{9,8},{10,11... | collective-permute-start | bytes 3538952 | tf_op jit(solution)/shard_map/ppermute | solution.py:38
  196.7 40.1 %collective-permute-start.35 = (bf16[384,1536]{1,0:T(8,128)(2,1)S(1)}, bf16[384,1536]{1,0:T(8,128)(2,1)S(1)}, u32[]{:S(2)}, u32[]{:S(2)}) collective-permute-start(bf16[384,1536]{1,0:T(8,128)(2,1)S(1)} %constant_dynamic-update-slice_fusion.4.refs_2_), channel_id=1, source_target_pairs={{0,2},{1,3},{2,0},{3,1},{4,6},{5,7},{6,4},{7,5},{8,10},{9,11},{10,... | collective-permute-start | bytes 3538952 | tf_op jit(solution)/shard_map/ppermute | solution.py:38
  256.8 68.8 %collective-permute-start.43 = (bf16[192,4224]{1,0:T(8,128)(2,1)}, bf16[192,4224]{1,0:T(8,128)(2,1)S(1)}, u32[]{:S(2)}, u32[]{:S(2)}) collective-permute-start(bf16[192,4224]{1,0:T(8,128)(2,1)} %pad_maximum_fusion.refs_13_.refs_23_), channel_id=1, source_target_pairs={{0,1},{1,0},{2,3},{3,2},{4,5},{5,4},{6,7},{7,6},{8,9},{9,8},{10,11... | collective-permute-start | bytes 4866056 | tf_op jit(solution)/shard_map/ppermute | solution.py:38
  258.3 67.3 %collective-permute-start.44 = (bf16[192,4224]{1,0:T(8,128)(2,1)}, bf16[192,4224]{1,0:T(8,128)(2,1)S(1)}, u32[]{:S(2)}, u32[]{:S(2)}) collective-permute-start(bf16[192,4224]{1,0:T(8,128)(2,1)} %pad_maximum_fusion.refs_13_.refs_23_), channel_id=1, source_target_pairs={{0,2},{1,3},{2,0},{3,1},{4,6},{5,7},{6,4},{7,5},{8,10},{9,11},{10,... | collective-permute-start | bytes 4866056 | tf_op jit(solution)/shard_map/ppermute | solution.py:38
  258.8 42.7 %collective-permute-start.39 = (bf16[128,1536]{1,0:T(8,128)(2,1)S(1)}, bf16[128,1536]{1,0:T(8,128)(2,1)S(1)}, u32[]{:S(2)}, u32[]{:S(2)}) collective-permute-start(bf16[128,1536]{1,0:T(8,128)(2,1)S(1)} %get-tuple-element.352), channel_id=1, source_target_pairs={{0,1},{1,0},{2,3},{3,2},{4,5},{5,4},{6,7},{7,6},{8,9},{9,8},{10,11... | collective-permute-start | bytes 1179656 | tf_op jit(solution)/shard_map/ppermute | solution.py:38
  259.4 43.3 %collective-permute-start.38 = (bf16[128,1536]{1,0:T(8,128)(2,1)S(1)}, bf16[128,1536]{1,0:T(8,128)(2,1)S(1)}, u32[]{:S(2)}, u32[]{:S(2)}) collective-permute-start(bf16[128,1536]{1,0:T(8,128)(2,1)S(1)} %get-tuple-element.350), channel_id=1, source_target_pairs={{0,2},{1,3},{2,0},{3,1},{4,6},{5,7},{6,4},{7,5},{8,10},{9,11},{10,... | collective-permute-start | bytes 1179656 | tf_op jit(solution)/shard_map/ppermute | solution.py:38
  327.3 33.2 %collective-permute-start.47 = (bf16[3,5,192,128]{3,2,1,0:T(8,128)(2,1)S(1)}, bf16[3,5,192,128]{3,2,1,0:T(8,128)(2,1)S(1)}, u32[]{:S(2)}, u32[]{:S(2)}) collective-permute-start(bf16[3,5,192,128]{3,2,1,0:T(8,128)(2,1)S(1)} %copy-done.208), channel_id=1, source_target_pairs={{0,8},{1,9},{2,10},{3,11},{4,12},{5,13},{6,14},{7,15},{8,16},{9,17... | collective-permute-start | bytes 2211848 | tf_op jit(solution)/shard_map/ppermute | solution.py:38
  384.1 36.2 %collective-permute-start.57 = (bf16[192,2048]{1,0:T(8,128)(2,1)S(1)}, bf16[192,2048]{1,0:T(8,128)(2,1)S(1)}, u32[]{:S(2)}, u32[]{:S(2)}) collective-permute-start(bf16[192,2048]{1,0:T(8,128)(2,1)S(1)} %slice.332), channel_id=1, source_target_pairs={{0,2},{1,3},{2,0},{3,1},{4,6},{5,7},{6,4},{7,5},{8,10},{9,11},{10,... | collective-permute-start | bytes 2359304 | tf_op jit(solution)/shard_map/ppermute | solution.py:38
  536.6 37.4 %collective-permute-start.88 = (bf16[512,1536]{1,0:T(8,128)(2,1)S(1)}, bf16[512,1536]{1,0:T(8,128)(2,1)S(1)}, u32[]{:S(2)}, u32[]{:S(2)}) collective-permute-start(bf16[512,1536]{1,0:T(8,128)(2,1)S(1)} %pad_maximum_fusion.1.refs_2_), channel_id=1, source_target_pairs={{0,1},{1,0},{2,3},{3,2},{4,5},{5,4},{6,7},{7,6},{8,9},{9,8},{10,11... | collective-permute-start | bytes 4718600 | tf_op jit(solution)/shard_map/ppermute | solution.py:38
  537.5 37.3 %collective-permute-start.89 = (bf16[512,1536]{1,0:T(8,128)(2,1)S(1)}, bf16[512,1536]{1,0:T(8,128)(2,1)S(1)}, u32[]{:S(2)}, u32[]{:S(2)}) collective-permute-start(bf16[512,1536]{1,0:T(8,128)(2,1)S(1)} %pad_maximum_fusion.1.refs_2_), channel_id=1, source_target_pairs={{0,2},{1,3},{2,0},{3,1},{4,6},{5,7},{6,4},{7,5},{8,10},{9,11},{10,... | collective-permute-start | bytes 4718600 | tf_op jit(solution)/shard_map/ppermute | solution.py:38
  537.7 44.6 %collective-permute-start.76 = (bf16[128,1536]{1,0:T(8,128)(2,1)S(1)}, bf16[128,1536]{1,0:T(8,128)(2,1)S(1)}, u32[]{:S(2)}, u32[]{:S(2)}) collective-permute-start(bf16[128,1536]{1,0:T(8,128)(2,1)S(1)} %get-tuple-element.409), channel_id=1, source_target_pairs={{0,1},{1,0},{2,3},{3,2},{4,5},{5,4},{6,7},{7,6},{8,9},{9,8},{10,11... | collective-permute-start | bytes 1179656 | tf_op jit(solution)/shard_map/ppermute | solution.py:38
  539.1 44.1 %collective-permute-start.74 = (bf16[128,1536]{1,0:T(8,128)(2,1)S(1)}, bf16[128,1536]{1,0:T(8,128)(2,1)S(1)}, u32[]{:S(2)}, u32[]{:S(2)}) collective-permute-start(bf16[128,1536]{1,0:T(8,128)(2,1)S(1)} %get-tuple-element.408), channel_id=1, source_target_pairs={{0,2},{1,3},{2,0},{3,1},{4,6},{5,7},{6,4},{7,5},{8,10},{9,11},{10,... | collective-permute-start | bytes 1179656 | tf_op jit(solution)/shard_map/ppermute | solution.py:38
  646.4 34.5 %collective-permute-start.92 = (bf16[384,1536]{1,0:T(8,128)(2,1)}, bf16[384,1536]{1,0:T(8,128)(2,1)S(1)}, u32[]{:S(2)}, u32[]{:S(2)}) collective-permute-start(bf16[384,1536]{1,0:T(8,128)(2,1)} %get-tuple-element.428), channel_id=1, source_target_pairs={{0,1},{1,0},{2,3},{3,2},{4,5},{5,4},{6,7},{7,6},{8,9},{9,8},{10,11... | collective-permute-start | bytes 3538952 | tf_op jit(solution)/shard_map/ppermute | solution.py:38
  647.7 33.2 %collective-permute-start.93 = (bf16[384,1536]{1,0:T(8,128)(2,1)}, bf16[384,1536]{1,0:T(8,128)(2,1)S(1)}, u32[]{:S(2)}, u32[]{:S(2)}) collective-permute-start(bf16[384,1536]{1,0:T(8,128)(2,1)} %get-tuple-element.429), channel_id=1, source_target_pairs={{0,2},{1,3},{2,0},{3,1},{4,6},{5,7},{6,4},{7,5},{8,10},{9,11},{10,... | collective-permute-start | bytes 3538952 | tf_op jit(solution)/shard_map/ppermute | solution.py:38
  648.8 35.0 %collective-permute-start.96 = (bf16[128,1536]{1,0:T(8,128)(2,1)}, bf16[128,1536]{1,0:T(8,128)(2,1)S(1)}, u32[]{:S(2)}, u32[]{:S(2)}) collective-permute-start(bf16[128,1536]{1,0:T(8,128)(2,1)} %get-tuple-element.444), channel_id=1, source_target_pairs={{0,2},{1,3},{2,0},{3,1},{4,6},{5,7},{6,4},{7,5},{8,10},{9,11},{10,... | collective-permute-start | bytes 1179656 | tf_op jit(solution)/shard_map/ppermute | solution.py:38
  702.6 76.8 %collective-permute-start.104 = (bf16[384,1536]{1,0:T(8,128)(2,1)}, bf16[384,1536]{1,0:T(8,128)(2,1)}, u32[]{:S(2)}, u32[]{:S(2)}) collective-permute-start(bf16[384,1536]{1,0:T(8,128)(2,1)} %get-tuple-element.472), channel_id=1, source_target_pairs={{0,1},{1,0},{2,3},{3,2},{4,5},{5,4},{6,7},{7,6},{8,9},{9,8},{10,11... | collective-permute-start | bytes 3538952 | tf_op jit(solution)/shard_map/ppermute | solution.py:38
  703.0 78.7 %collective-permute-start.103 = (bf16[384,1536]{1,0:T(8,128)(2,1)}, bf16[384,1536]{1,0:T(8,128)(2,1)}, u32[]{:S(2)}, u32[]{:S(2)}) collective-permute-start(bf16[384,1536]{1,0:T(8,128)(2,1)} %get-tuple-element.470), channel_id=1, source_target_pairs={{0,2},{1,3},{2,0},{3,1},{4,6},{5,7},{6,4},{7,5},{8,10},{9,11},{10,... | collective-permute-start | bytes 3538952 | tf_op jit(solution)/shard_map/ppermute | solution.py:38
  731.1 53.0 %collective-permute-start.77 = (bf16[64,1536]{1,0:T(8,128)(2,1)S(1)}, bf16[64,1536]{1,0:T(8,128)(2,1)S(1)}, u32[]{:S(2)}, u32[]{:S(2)}) collective-permute-start(bf16[64,1536]{1,0:T(8,128)(2,1)S(1)} %copy-done.68), channel_id=1, source_target_pairs={{0,2},{1,3},{2,0},{3,1},{4,6},{5,7},{6,4},{7,5},{8,10},{9,11},{10,... | collective-permute-start | bytes 589832 | tf_op jit(solution)/shard_map/ppermute | solution.py:38
  745.5 38.6 %collective-permute-start.75 = (bf16[64,1536]{1,0:T(8,128)(2,1)S(1)}, bf16[64,1536]{1,0:T(8,128)(2,1)S(1)}, u32[]{:S(2)}, u32[]{:S(2)}) collective-permute-start(bf16[64,1536]{1,0:T(8,128)(2,1)S(1)} %copy-done.70), channel_id=1, source_target_pairs={{0,1},{1,0},{2,3},{3,2},{4,5},{5,4},{6,7},{7,6},{8,9},{9,8},{10,11... | collective-permute-start | bytes 589832 | tf_op jit(solution)/shard_map/ppermute | solution.py:38
  747.3 39.0 %collective-permute-start.114 = (bf16[4,5,192,128]{3,2,1,0:T(8,128)(2,1)S(1)}, bf16[4,5,192,128]{3,2,1,0:T(8,128)(2,1)}, u32[]{:S(2)}, u32[]{:S(2)}) collective-permute-start(bf16[4,5,192,128]{3,2,1,0:T(8,128)(2,1)S(1)} %copy-done.119), channel_id=1, source_target_pairs={{0,4},{1,5},{2,6},{3,7},{4,0},{5,1},{6,2},{7,3},{8,12},{9,13},{10,... | collective-permute-start | bytes 2949128 | tf_op jit(solution)/shard_map/ppermute | solution.py:38
  817.4 44.4 %collective-permute-start.112 = (bf16[384,1536]{1,0:T(8,128)(2,1)S(1)}, bf16[384,1536]{1,0:T(8,128)(2,1)S(1)}, u32[]{:S(2)}, u32[]{:S(2)}) collective-permute-start(bf16[384,1536]{1,0:T(8,128)(2,1)S(1)} %constant_dynamic-update-slice_fusion.10.refs_2_), channel_id=1, source_target_pairs={{0,1},{1,0},{2,3},{3,2},{4,5},{5,4},{6,7},{7,6},{8,9},{9,8},{10,11... | collective-permute-start | bytes 3538952 | tf_op jit(solution)/shard_map/ppermute | solution.py:38
  818.7 43.1 %collective-permute-start.113 = (bf16[384,1536]{1,0:T(8,128)(2,1)S(1)}, bf16[384,1536]{1,0:T(8,128)(2,1)S(1)}, u32[]{:S(2)}, u32[]{:S(2)}) collective-permute-start(bf16[384,1536]{1,0:T(8,128)(2,1)S(1)} %constant_dynamic-update-slice_fusion.10.refs_2_), channel_id=1, source_target_pairs={{0,2},{1,3},{2,0},{3,1},{4,6},{5,7},{6,4},{7,5},{8,10},{9,11},{10,... | collective-permute-start | bytes 3538952 | tf_op jit(solution)/shard_map/ppermute | solution.py:38
  867.8 48.8 %collective-permute-start.123 = (bf16[3,5,192,128]{3,2,1,0:T(8,128)(2,1)}, bf16[3,5,192,128]{3,2,1,0:T(8,128)(2,1)S(1)}, u32[]{:S(2)}, u32[]{:S(2)}) collective-permute-start(bf16[3,5,192,128]{3,2,1,0:T(8,128)(2,1)} %pad_maximum_fusion.4), channel_id=1, source_target_pairs={{0,16},{1,17},{2,18},{3,19},{4,20},{5,21},{6,22},{7,23},{8,24},{9,... | collective-permute-start | bytes 2211848 | tf_op jit(solution)/shard_map/ppermute | solution.py:38
  881.7 35.9 %collective-permute-start.124 = (bf16[192,1536]{1,0:T(8,128)(2,1)}, bf16[192,1536]{1,0:T(8,128)(2,1)S(1)}, u32[]{:S(2)}, u32[]{:S(2)}) collective-permute-start(bf16[192,1536]{1,0:T(8,128)(2,1)} %add_convert_fusion.6), channel_id=1, source_target_pairs={{0,1},{1,0},{2,3},{3,2},{4,5},{5,4},{6,7},{7,6},{8,9},{9,8},{10,11... | collective-permute-start | bytes 1769480 | tf_op jit(solution)/shard_map/ppermute | solution.py:38
  882.1 35.5 %collective-permute-start.125 = (bf16[192,1536]{1,0:T(8,128)(2,1)}, bf16[192,1536]{1,0:T(8,128)(2,1)S(1)}, u32[]{:S(2)}, u32[]{:S(2)}) collective-permute-start(bf16[192,1536]{1,0:T(8,128)(2,1)} %add_convert_fusion.5), channel_id=1, source_target_pairs={{0,2},{1,3},{2,0},{3,1},{4,6},{5,7},{6,4},{7,5},{8,10},{9,11},{10,... | collective-permute-start | bytes 1769480 | tf_op jit(solution)/shard_map/ppermute | solution.py:38
  918.6 72.7 %collective-permute-start.129 = (bf16[384,1536]{1,0:T(8,128)(2,1)}, bf16[384,1536]{1,0:T(8,128)(2,1)}, u32[]{:S(2)}, u32[]{:S(2)}) collective-permute-start(bf16[384,1536]{1,0:T(8,128)(2,1)} %get-tuple-element.532), channel_id=1, source_target_pairs={{0,1},{1,0},{2,3},{3,2},{4,5},{5,4},{6,7},{7,6},{8,9},{9,8},{10,11... | collective-permute-start | bytes 3538952 | tf_op jit(solution)/shard_map/ppermute | solution.py:38
  919.0 72.3 %collective-permute-start.130 = (bf16[384,1536]{1,0:T(8,128)(2,1)}, bf16[384,1536]{1,0:T(8,128)(2,1)}, u32[]{:S(2)}, u32[]{:S(2)}) collective-permute-start(bf16[384,1536]{1,0:T(8,128)(2,1)} %get-tuple-element.533), channel_id=1, source_target_pairs={{0,2},{1,3},{2,0},{3,1},{4,6},{5,7},{6,4},{7,5},{8,10},{9,11},{10,... | collective-permute-start | bytes 3538952 | tf_op jit(solution)/shard_map/ppermute | solution.py:38
  927.2 64.0 %collective-permute-start.127 = (bf16[128,1536]{1,0:T(8,128)(2,1)}, bf16[128,1536]{1,0:T(8,128)(2,1)S(1)}, u32[]{:S(2)}, u32[]{:S(2)}) collective-permute-start(bf16[128,1536]{1,0:T(8,128)(2,1)} %get-tuple-element.526), channel_id=1, source_target_pairs={{0,16},{1,17},{2,18},{3,19},{4,20},{5,21},{6,22},{7,23},{8,24},{9,... | collective-permute-start | bytes 1179656 | tf_op jit(solution)/shard_map/ppermute | solution.py:38
  927.2 64.1 %collective-permute-start.128 = (bf16[128,1536]{1,0:T(8,128)(2,1)}, bf16[128,1536]{1,0:T(8,128)(2,1)S(1)}, u32[]{:S(2)}, u32[]{:S(2)}) collective-permute-start(bf16[128,1536]{1,0:T(8,128)(2,1)} %get-tuple-element.527), channel_id=1, source_target_pairs={{0,8},{1,9},{2,10},{3,11},{4,12},{5,13},{6,14},{7,15},{8,16},{9,17... | collective-permute-start | bytes 1179656 | tf_op jit(solution)/shard_map/ppermute | solution.py:38
  949.2 57.4 %collective-permute-start.138 = (bf16[4,5,192,128]{3,2,1,0:T(8,128)(2,1)}, bf16[4,5,192,128]{3,2,1,0:T(8,128)(2,1)S(1)}, u32[]{:S(2)}, u32[]{:S(2)}) collective-permute-start(bf16[4,5,192,128]{3,2,1,0:T(8,128)(2,1)} %get-tuple-element.572), channel_id=1, source_target_pairs={{0,4},{1,5},{2,6},{3,7},{4,0},{5,1},{6,2},{7,3},{8,12},{9,13},{10,... | collective-permute-start | bytes 2949128 | tf_op jit(solution)/shard_map/ppermute | solution.py:38
  1003.4 34.2 %collective-permute-start.140 = (bf16[4,5,192,128]{3,2,1,0:T(8,128)(2,1)}, bf16[4,5,192,128]{3,2,1,0:T(8,128)(2,1)}, u32[]{:S(2)}, u32[]{:S(2)}) collective-permute-start(bf16[4,5,192,128]{3,2,1,0:T(8,128)(2,1)} %get-tuple-element.574), channel_id=1, source_target_pairs={{0,4},{1,5},{2,6},{3,7},{4,0},{5,1},{6,2},{7,3},{8,12},{9,13},{10,... | collective-permute-start | bytes 2949128 | tf_op jit(solution)/shard_map/ppermute | solution.py:38
  1035.3 57.9 %collective-permute-start.136 = (bf16[128,1536]{1,0:T(8,128)(2,1)}, bf16[128,1536]{1,0:T(8,128)(2,1)S(1)}, u32[]{:S(2)}, u32[]{:S(2)}) collective-permute-start(bf16[128,1536]{1,0:T(8,128)(2,1)} %get-tuple-element.562), channel_id=1, source_target_pairs={{0,16},{1,17},{2,18},{3,19},{4,20},{5,21},{6,22},{7,23},{8,24},{9,... | collective-permute-start | bytes 1179656 | tf_op jit(solution)/shard_map/ppermute | solution.py:38
  1035.6 57.6 %collective-permute-start.137 = (bf16[128,1536]{1,0:T(8,128)(2,1)}, bf16[128,1536]{1,0:T(8,128)(2,1)S(1)}, u32[]{:S(2)}, u32[]{:S(2)}) collective-permute-start(bf16[128,1536]{1,0:T(8,128)(2,1)} %get-tuple-element.563), channel_id=1, source_target_pairs={{0,8},{1,9},{2,10},{3,11},{4,12},{5,13},{6,14},{7,15},{8,16},{9,17... | collective-permute-start | bytes 1179656 | tf_op jit(solution)/shard_map/ppermute | solution.py:38
  1093.2 38.4 %collective-permute-start.141 = (bf16[3,5,192,128]{3,2,1,0:T(8,128)(2,1)S(1)}, bf16[3,5,192,128]{3,2,1,0:T(8,128)(2,1)S(1)}, u32[]{:S(2)}, u32[]{:S(2)}) collective-permute-start(bf16[3,5,192,128]{3,2,1,0:T(8,128)(2,1)S(1)} %pad_maximum_fusion.7.refs_34_), channel_id=1, source_target_pairs={{0,8},{1,9},{2,10},{3,11},{4,12},{5,13},{6,14},{7,15},{8,16},{9,17... | collective-permute-start | bytes 2211848 | tf_op jit(solution)/shard_map/ppermute | solution.py:38
  1093.3 38.4 %collective-permute-start.142 = (bf16[3,5,192,128]{3,2,1,0:T(8,128)(2,1)S(1)}, bf16[3,5,192,128]{3,2,1,0:T(8,128)(2,1)S(1)}, u32[]{:S(2)}, u32[]{:S(2)}) collective-permute-start(bf16[3,5,192,128]{3,2,1,0:T(8,128)(2,1)S(1)} %pad_maximum_fusion.9.refs_36_), channel_id=1, source_target_pairs={{0,24},{1,25},{2,26},{3,27},{4,28},{5,29},{6,30},{7,31},{8,0},{9,1... | collective-permute-start | bytes 2211848 | tf_op jit(solution)/shard_map/ppermute | solution.py:38
  1145.0 38.4 %collective-permute-start.149 = (bf16[288,2176]{1,0:T(8,128)(2,1)S(1)}, bf16[288,2176]{1,0:T(8,128)(2,1)S(1)}, u32[]{:S(2)}, u32[]{:S(2)}) collective-permute-start(bf16[288,2176]{1,0:T(8,128)(2,1)S(1)} %get-tuple-element.600), channel_id=1, source_target_pairs={{0,1},{1,0},{2,3},{3,2},{4,5},{5,4},{6,7},{7,6},{8,9},{9,8},{10,11... | collective-permute-start | bytes 3760136 | tf_op jit(solution)/shard_map/ppermute | solution.py:38
  1145.1 38.3 %collective-permute-start.150 = (bf16[288,2048]{1,0:T(8,128)(2,1)S(1)}, bf16[288,2048]{1,0:T(8,128)(2,1)S(1)}, u32[]{:S(2)}, u32[]{:S(2)}) collective-permute-start(bf16[288,2048]{1,0:T(8,128)(2,1)S(1)} %get-tuple-element.601), channel_id=1, source_target_pairs={{0,2},{1,3},{2,0},{3,1},{4,6},{5,7},{6,4},{7,5},{8,10},{9,11},{10,... | collective-permute-start | bytes 3538952 | tf_op jit(solution)/shard_map/ppermute | solution.py:38
  1146.2 35.4 %collective-permute-start.144 = (bf16[96,2048]{1,0:T(8,128)(2,1)S(1)}, bf16[96,2048]{1,0:T(8,128)(2,1)S(1)}, u32[]{:S(2)}, u32[]{:S(2)}) collective-permute-start(bf16[96,2048]{1,0:T(8,128)(2,1)S(1)} %get-tuple-element.592), channel_id=1, source_target_pairs={{0,2},{1,3},{2,0},{3,1},{4,6},{5,7},{6,4},{7,5},{8,10},{9,11},{10,... | collective-permute-start | bytes 1179656 | tf_op jit(solution)/shard_map/ppermute | solution.py:38
  1148.1 35.3 %collective-permute-start.151 = (bf16[3,5,192,128]{3,2,1,0:T(8,128)(2,1)S(1)}, bf16[3,5,192,128]{3,2,1,0:T(8,128)(2,1)S(1)}, u32[]{:S(2)}, u32[]{:S(2)}) collective-permute-start(bf16[3,5,192,128]{3,2,1,0:T(8,128)(2,1)S(1)} %copy-done.141), channel_id=1, source_target_pairs={{0,16},{1,17},{2,18},{3,19},{4,20},{5,21},{6,22},{7,23},{8,24},{9,... | collective-permute-start | bytes 2211848 | tf_op jit(solution)/shard_map/ppermute | solution.py:38
  1148.1 36.4 %collective-permute-start.146 = (bf16[96,2176]{1,0:T(8,128)(2,1)S(1)}, bf16[96,2176]{1,0:T(8,128)(2,1)S(1)}, u32[]{:S(2)}, u32[]{:S(2)}) collective-permute-start(bf16[96,2176]{1,0:T(8,128)(2,1)S(1)} %get-tuple-element.593), channel_id=1, source_target_pairs={{0,1},{1,0},{2,3},{3,2},{4,5},{5,4},{6,7},{7,6},{8,9},{9,8},{10,11... | collective-permute-start | bytes 1253384 | tf_op jit(solution)/shard_map/ppermute | solution.py:38
  1201.3 33.3 %collective-permute-start.155 = (bf16[48,4224]{1,0:T(8,128)(2,1)S(1)}, bf16[48,4224]{1,0:T(8,128)(2,1)S(1)}, u32[]{:S(2)}, u32[]{:S(2)}) collective-permute-start(bf16[48,4224]{1,0:T(8,128)(2,1)S(1)} %get-tuple-element.649), channel_id=1, source_target_pairs={{0,16},{1,17},{2,18},{3,19},{4,20},{5,21},{6,22},{7,23},{8,24},{9,... | collective-permute-start | bytes 1216520 | tf_op jit(solution)/shard_map/ppermute | solution.py:38
  1201.4 33.2 %collective-permute-start.156 = (bf16[48,4224]{1,0:T(8,128)(2,1)S(1)}, bf16[48,4224]{1,0:T(8,128)(2,1)S(1)}, u32[]{:S(2)}, u32[]{:S(2)}) collective-permute-start(bf16[48,4224]{1,0:T(8,128)(2,1)S(1)} %get-tuple-element.648), channel_id=1, source_target_pairs={{0,8},{1,9},{2,10},{3,11},{4,12},{5,13},{6,14},{7,15},{8,16},{9,17... | collective-permute-start | bytes 1216520 | tf_op jit(solution)/shard_map/ppermute | solution.py:38
  (330 other events, 6090.4 us)
Sparse Core Ops, SparseCore 0:
  867.3 227.0 reduce-scatter.1

commit v4 on v3

--- a/solution.py
+++ b/solution.py
@@ -85,25 +85,27 @@
     return total
 
 
-def gates_line(place, routes, gates, expert_count):
+def gate_table(routes, gates, expert_count):
     names = jnp.arange(expert_count, dtype=jnp.int32)
     chosen = routes[:, None, :, :] == names[None, :, None, None]
-    table = jnp.sum(jnp.where(chosen, gates[:, None, :, :], 0.0), axis=3)
-    return jnp.stack([table] + [place.hop(table, up=k) for k in range(1, place.planes)])
-
-
-def spread_gates(place, line):
-    owned = line.shape[2] // place.columns
+    return jnp.sum(jnp.where(chosen, gates[:, None, :, :], 0.0), axis=3)
+
+
+def spread_gates(place, table):
+    axis = table.ndim - 2
+    owned = table.shape[axis] // place.columns
     found = []
     for m in range(place.columns):
         start = (place.column ^ m) * owned
-        piece = lax.dynamic_slice_in_dim(line, start, owned, axis=2)
+        piece = lax.dynamic_slice_in_dim(table, start, owned, axis=axis)
         found.append(place.hop(piece, flip=m) if m else piece)
     return found
 
 
 def gather_gates(place, routes, gates, expert_count):
-    return spread_gates(place, gates_line(place, routes, gates, expert_count))
+    table = gate_table(routes, gates, expert_count)
+    line = jnp.stack([table] + [place.hop(table, up=k) for k in range(1, place.planes)])
+    return spread_gates(place, line)
 
 
 def gather_experts(place, weights):
@@ -568,20 +570,10 @@
 
 
 def read_sum(base, extra):
-    if not extra:
-        return base[...].astype(jnp.float32)
-    *blocks, one_head, two_tail, by_one, by_two = extra
-    top = pl.ds(0, HALF)
-    halves = []
-    for side, terms in enumerate(((one_head, by_two), (two_tail, by_one))):
-        rows = pl.ds(side * HALF, HALF)
-        total = base[rows, :].astype(jnp.float32)
-        for block in blocks:
-            total = total + block[rows, :].astype(jnp.float32)
-        for term in terms:
-            total = total + term[top, :].astype(jnp.float32)
-        halves.append(total)
-    return jnp.concatenate(halves, axis=0)
+    total = base[...].astype(jnp.float32)
+    for term in extra:
+        total = total + term[pl.ds(0, total.shape[0]), :].astype(jnp.float32)
+    return total
 
 
 def attend_forward_kernel(terms, width, where, base, *refs):
@@ -708,7 +700,7 @@
     )(where, base, *extra, *tables, *pieces, *after)
 
 
-def attend_backward_kernel(terms, width, where, base, upstream, *refs):
+def attend_backward_kernel(groups, terms, width, where, base, upstream, *refs):
     refs = list(refs)
     extra = [refs.pop(0) for _ in range(terms)]
     h_in, m_in, na, q, k, v, o, lse_in, gains, cosine, sine, allowed = refs[:12]
@@ -815,19 +807,17 @@
 
     both = jnp.concatenate([gain_attn, gain_ffn, jnp.zeros((EXTRA - 2, model), jnp.float32)], axis=0)
     sums[:, pl.ds(in_width + model, EXTRA)] = both.T.astype(jnp.bfloat16)
-    if len(outs) == 3:
-        copies.start(sums, outs[2])
-    else:
-        for swapped in (1, 0):
-            for first, count in ((1, 3), (0, 1)):
-                target = outs[2 + 2 * (1 - swapped) + (1 - first)]
-                for m_index in range(4):
-                    for n in range(count):
-                        row = shard_row(where, swapped, m_index, first + n, shard)
-                        copies.start(
-                            sums.at[pl.ds(row, shard), :],
-                            target.at[pl.ds((m_index * count + n) * shard, shard), :],
-                        )
+    at = 2
+    for swapped in (1, 0):
+        for first, count in groups:
+            for m_index in range(4):
+                for n in range(count):
+                    row = shard_row(where, swapped, m_index, first + n, shard)
+                    copies.start(
+                        sums.at[pl.ds(row, shard), :],
+                        outs[at].at[pl.ds((m_index * count + n) * shard, shard), :],
+                    )
+            at += 1
     gh = gh_out[...] + inverse * scaled - h * (inverse * inverse * inverse) * inner
     gh_out[...] = gh
     gh_low[...] = gh.astype(jnp.bfloat16)
@@ -835,7 +825,7 @@
 
 
 def attend_backward_fast(
-    split, where, base, upstream, extra, stash, tables, pieces, in_width, after=()
+    groups, where, base, upstream, extra, stash, tables, pieces, in_width, after=()
 ):
     rows, model = upstream.shape
     bf, f32 = jnp.bfloat16, jnp.float32
@@ -844,14 +834,13 @@
         shape_of(rows, model, dtype=f32),
         shape_of(rows, model),
     ]
-    if split:
-        shapes += [shape_of(model // 8 * part, total) for part in (3, 1, 3, 1)]
-    else:
-        shapes += [shape_of(model, total)]
+    shapes += [shape_of(model // 8 * count, total) for _, count in groups] * CORES
 
     def body(*refs):
         used = 3 + len(extra) + 12 + MATRIX_PIECES
-        attend_backward_kernel(len(extra), in_width, *refs[:used], *refs[used + len(after) :])
+        attend_backward_kernel(
+            groups, len(extra), in_width, *refs[:used], *refs[used + len(after) :]
+        )
 
     return pl.pallas_call(
         body,
@@ -874,7 +863,7 @@
     )(where, base, upstream, *extra, *stash, *tables, *pieces, *after)
 
 
-SHARES = ((0, 0, 3), (1, 0, 3), (3, 0, 3), (2, 0, 1), (2, 1, 2))
+SHARES = ((0, 0, 3), (1, 0, 3), (2, 0, 3), (3, 0, 3))
 WEIGHT_PIECES = CORES * len(SHARES)
 
 
@@ -900,19 +889,12 @@
     return wide
 
 
-def start_rows(copies, pieces, rows_ref, spans=None):
+def start_rows(copies, pieces, rows_ref):
     at = 0
-    for index, piece in enumerate(pieces):
-        first, rows = spans[index] if spans else (0, piece.shape[0])
-        if rows:
-            copies.start(piece.at[pl.ds(first, rows), :], rows_ref.at[pl.ds(at, rows), :])
+    for piece in pieces:
+        rows = piece.shape[0]
+        copies.start(piece, rows_ref.at[pl.ds(at, rows), :])
         at += rows
-
-
-def spans_of(far):
-    if far:
-        return ((HALF * 2, HALF * 6),) * 3 + ((HALF * 2, HALF * 2), (0, HALF * 4))
-    return ((0, HALF * 2),) * 4 + ((0, 0),)
 
 
 def part_rows(n):
@@ -996,13 +978,13 @@
     )(where, gates, *pieces, *weights, *after)
 
 
-def experts_backward_kernel(spans, where, gates, *refs):
+def experts_backward_kernel(where, gates, *refs):
     pieces, g_in, u_in = refs[:5], refs[5], refs[6]
     weights, refs = refs[7 : 7 + WEIGHT_PIECES], refs[7 + WEIGHT_PIECES :]
     parts, r_out, gg_out, gu_out, p_out = refs[:5], *refs[5:9]
     x, y, g, u, gg, gu, p, w_gate, w_up, w_down, semaphores = refs[9:]
     copies = Copies(semaphores)
-    start_rows(copies, pieces, x, spans)
+    start_rows(copies, pieces, x)
     load_experts(copies, where, weights, (w_gate, w_up, w_down))
     copies.start(g_in, g)
     copies.start(u_in, u)
@@ -1034,7 +1016,7 @@
     copies.wait()
 
 
-def experts_backward_fast(where, gates, pieces, stash, weights, spans=None, after=()):
+def experts_backward_fast(where, gates, pieces, stash, weights, after=()):
     n, model = gates.shape[0] // 4, pieces[0].shape[1]
     _, experts, _, share = weights[0].shape
     rows, width = 4 * n, experts * share
@@ -1044,7 +1026,7 @@
 
     def body(*refs):
         used = 9 + WEIGHT_PIECES
-        experts_backward_kernel(spans, *refs[:used], *refs[used + len(after) :])
+        experts_backward_kernel(*refs[:used], *refs[used + len(after) :])
 
     return pl.pallas_call(
         body,
@@ -1146,6 +1128,26 @@
     )(where, *weights)
 
 
+def merge_grads_kernel(*refs):
+    mine, arrived, outs = refs[:3], refs[3:6], refs[6:]
+    for i in range(3):
+        for k, out in enumerate(outs):
+            total = mine[i][k, 0].astype(jnp.float32) + arrived[i][k, 0].astype(jnp.float32)
+            out[i, 0] = total.astype(jnp.bfloat16)
+
+
+def merge_grads(mine, arrived):
+    planes, experts, rows, share = mine[0].shape
+    return pl.pallas_call(
+        merge_grads_kernel,
+        name="merge_grads",
+        grid=(experts,),
+        out_shape=[shape_of(3, experts, rows, share)] * planes,
+        in_specs=[pl.BlockSpec((planes, 1, rows, share), lambda e: (0, e, 0, 0))] * 6,
+        out_specs=[pl.BlockSpec((3, 1, rows, share), lambda e: (0, e, 0, 0))] * planes,
+    )(*mine, *arrived)
+
+
 def join_kernel(layer, where, *refs):
     pieces, outs = refs[:4], refs[-3:]
     i = pl.program_id(0)
@@ -1236,45 +1238,41 @@
     return wide(own) + wide(one) + wide(two)
 
 
-def blocks_kernel(own, one_head, two_tail, by_one, by_two, *outs):
+def blocks_kernel(sides, own, one_head, two_tail, by_one, by_two, *outs):
     half = one_head.shape[0]
-    rows = outs[0].shape[0]
-    step = HALF
-    for start in range(0, own.shape[0], step):
-        terms = (one_head, by_two) if start < half else (two_tail, by_one)
-        at = pl.ds(start % half, step)
-        total = own[pl.ds(start, step), :].astype(jnp.float32)
+    for side, out in zip(sides, outs):
+        terms = (two_tail, by_one) if side else (one_head, by_two)
+        total = own[side * half : (side + 1) * half, :].astype(jnp.float32)
         for term in terms:
-            total = total + term[at, :].astype(jnp.float32)
-        outs[start // rows][pl.ds(start % rows, step), :] = total.astype(jnp.bfloat16)
-
-
-def sum_blocks(own, *others):
-    rows, model = own.shape
+            total = total + term[:half, :].astype(jnp.float32)
+        out[...] = total.astype(jnp.bfloat16)
+
+
+def sum_blocks(ends, sides):
+    half, model = ends[1].shape
     return pl.pallas_call(
-        blocks_kernel,
+        functools.partial(blocks_kernel, sides),
         name="sum_blocks",
-        out_shape=[shape_of(rows // 3, model)] * 3,
+        out_shape=[shape_of(half, model)] * len(sides),
         in_specs=[whole_spec()] * 5,
-        out_specs=[whole_spec()] * 3,
-    )(own, *others)
-
-
-def down_hops(place, blocks):
-    return [place.hop(blocks[k - 1], up=-k) for k in range(1, 4)]
+        out_specs=[whole_spec()] * len(sides),
+    )(*ends)
+
+
+def down_hops(place, blocks, first=1):
+    return [place.hop(block, up=-first - n) for n, block in enumerate(blocks)]
 
 
 def total_of(base, extra):
-    *blocks, one_head, two_tail, by_one, by_two = extra
-    total = base.astype(jnp.float32) + add_pieces(blocks[0], one_head, two_tail, by_one, by_two)
-    for block in blocks[1:]:
-        total = total + block.astype(jnp.float32)
+    total = base.astype(jnp.float32)
+    for term in extra:
+        total = total + term[: base.shape[0]].astype(jnp.float32)
     return total
 
 
 def received(near_ends, arrived):
-    own, one_head, two_tail, by_one, by_two = near_ends
-    return [own, *arrived, one_head, two_tail, by_one, by_two]
+    own, one_head, _, _, by_two = near_ends
+    return [own, *arrived, one_head, by_two]
 
 
 def merge_kernel(cut, mine, arrived, own, one_head, two_tail, to_one, to_two):
@@ -1339,19 +1337,12 @@
     )(*arrays)
 
 
-def scatter_matrices(place, other_far, other_near, mine_far, mine_near, cut, event):
-    rows = mine_near.shape[0] // 4
-    arrived_far = place.hop(other_far, swap=1)
-    arrived_near = place.hop(other_near, swap=1)
-    far = fold_first(place, merge_cores(mine_far, arrived_far, cut))
-    near = fold_start(place, merge_cores(mine_near, arrived_near, cut))
-    far = fold_sums(tie(far, event))
-    far = add_pieces(*fold_end(place, far), axis=1).astype(jnp.bfloat16)
-    arrived = down_hops(place, [far[k * rows : (k + 1) * rows] for k in range(3)])
-    final = add_pieces(*fold_end(place, near), axis=1)
-    for block in arrived:
-        final = final + block.astype(jnp.float32)
-    return final
+def sum_down(place, total, own):
+    rows = own.shape[0]
+    total = total.astype(jnp.bfloat16)
+    for block in down_hops(place, [total[k * rows : (k + 1) * rows] for k in range(3)]):
+        own = own + block.astype(jnp.float32)
+    return own
 
 
 def tables_of(length_row, rows):
@@ -1370,12 +1361,11 @@
     )
 
 
-def gate_rows_of(place, line):
-    order = jnp.stack(spread_gates(place, line))
-    order = jnp.transpose(order, (2, 0, 1, 4, 3))
+def gate_rows_of(found):
+    order = jnp.transpose(jnp.stack(found), (2, 1, 0, 4, 3))
     order = jnp.pad(order, ((0, 0),) * 4 + ((0, 8 - order.shape[4]),))
     return [
-        (layer[:, :1].reshape(-1, 8), layer[:, 1:].reshape(-1, 8)) for layer in order
+        (layer[:, :2].reshape(-1, 8), layer[:, 2:].reshape(-1, 8)) for layer in order
     ]
 
 
@@ -1408,62 +1398,93 @@
     weights = [jnp.transpose(w, (0, 2, 1, 3)) for w in (w_gate, w_up, w_down)]
     tables = tables_of(lengths[0], rows)
 
-    def share_cores(shares):
-        return list(shares) + [place.hop(piece, swap=1) for piece in shares]
-
     def line_of(block):
         return jnp.concatenate([block] + up_hops(place, block))
 
     cuts = [cut_experts(where, weights, l) for l in range(layer_count)]
-    gate_line = gates_line(place, routes, gates, expert_count)
-    line = jnp.concatenate([packs[0]] + tie(up_hops(place, packs[0]), cuts[0][0], gate_line))
+    table = gate_table(*tie((routes, gates), packs[0]), expert_count)
+    found = jnp.stack(spread_gates(place, table))
+    found = [found] + up_hops(place, found)
+    line = jnp.concatenate([packs[0]] + tie(up_hops(place, packs[0]), *[cut[0] for cut in cuts], found[0]))
     first = spread_first(place, line)
-    gate_rows = gate_rows_of(place, gate_line)
+    gate_rows = gate_rows_of(found)
     cuts[0] = tie(cuts[0], line)
-    shares = [cuts[0][0], place.hop(cuts[0][1], up=1), place.hop(cuts[0][2], up=3)]
-    first = tie(first, shares[1], shares[2], gate_rows[0][0], gate_rows[-1][0], cuts[-1][0])
-    shares.append(place.hop(tie(cuts[0][3], first[0]), up=2))
-    matrices = [share_cores(tie(spread_last(place, first, axis=1, cut=cut), shares[3]))]
-    shares.append(place.hop(tie(cuts[0][4], matrices[0][0]), up=2))
+    own_swaps = [place.hop(tie(cut[0], line), swap=1) for cut in cuts]
+    two = place.hop(cuts[0][2], up=2)
+    swapped = [place.hop(line, swap=1)]
+    events = (gate_rows[0][0], gate_rows[-1][0], swapped[0], *own_swaps)
+    first = tie(first, two, *events)
+    one = place.hop(tie(cuts[0][1], first[0]), up=1)
+    swapped += [place.hop(piece, swap=1) for piece in first[1:]]
+    last_two = tie(spread_last(place, first, axis=1, cut=cut)[3:], one, *swapped[1:])
+    matrices = [[*first, *last_two, *swapped, *[place.hop(p, swap=1) for p in last_two]]]
+    shares = [cuts[0][0], one, two, place.hop(tie(cuts[0][3], last_two[0]), up=3)]
+    share_swaps = [own_swaps[0], place.hop(one, swap=1), place.hop(two, swap=1)]
+
+    def run_forward(l, which, pieces, bank, after=()):
+        return experts_forward_fast(where, gate_rows[l][which], pieces, bank, after=after)
+
+    def run_backward(l, which, pieces, stash, bank, after=()):
+        return experts_backward_fast(where, gate_rows[l][which], pieces, stash, bank, after=after)
+
+    def pairs_of(block, *events):
+        ups = up_hops(place, block)
+        near = spread_first(place, jnp.concatenate([block, ups[0]]))
+        return near, ups[1:]
 
     base, extra = tokens.astype(jnp.float32), []
     stored = []
     for l in range(layer_count):
         more = l + 1 < layer_count
         after = [rows for pair in gate_rows for rows in pair] if l == 0 else []
+        after += share_swaps
         outs = attend_forward_fast(where, base, extra, tables, matrices[l], in_width, after=after)
         h, m, nf = outs[:3]
-        nf, last_share = tie((nf, shares[4]))
-        bank_l = share_cores(shares[:4] + [last_share])
-        ups = up_hops(place, nf)
-        near = spread_pieces(place, nf)
-        far = jnp.concatenate(tie(ups, near[3], near[4]))
-        far = spread_first(place, far)
-        y_near = experts_forward_fast(where, gate_rows[l][0], near, bank_l)
-        near_state = fold_start(place, y_near[:5])
-        line = line_of(tie(packs[l + 1] if more else cotangent, y_near[0]))
-        far = spread_last(place, tie(far, y_near[0]))
-        passing = spread_first(place, tie(line, far[3], far[4]))
-        y_far = experts_forward_fast(
-            where, gate_rows[l][1], far, bank_l, after=(near_state[1], near_state[2])
-        )
-        stored.append((h, outs, y_near[5:], y_far[5:], bank_l))
+        nf, late = tie((nf, shares[4 - len(shares) + len(share_swaps) :]))
+        share_swaps += [place.hop(piece, swap=1) for piece in late]
+        bank_l = [*shares[: 4 - len(late)], *late, *share_swaps]
+        near, far = pairs_of(nf)
+        near = spread_last(place, near)
+        far = spread_first(place, jnp.concatenate(tie(far, near[3], near[4])))
+        line = up_hops(place, tie(packs[l + 1] if more else cotangent, far[0]))
+        y_near = run_forward(l, 0, near, bank_l)
+        y_near, far, line[0], line[2] = tie((y_near, far, line[0], line[2]))
+        far = spread_last(place, far)
         if more:
-            y_far, passing = tie((y_far, passing))
-            far_state = fold_start(place, y_far[:5])
-            ready = tie(cuts[l + 1], far[3])
-            shares = [ready[0], place.hop(ready[1], up=1), None, place.hop(ready[3], up=2)]
-            far_state, one, two = tie((far_state, shares[1], shares[3]), near_state[1])
-            third = place.hop(tie(ready[2], far_state[1]), up=3)
-            far_ends, third = tie((fold_end(place, far_state), third))
-            blocks = sum_blocks(*far_ends)
-            matrices.append(share_cores(spread_last(place, tie(passing, blocks[0]), 1, cut)))
-            arrived = down_hops(place, blocks)
-            shares = [ready[0], one, third, two]
-            shares.append(place.hop(tie(ready[4], blocks[0]), up=2))
-            base, extra = m, received(fold_end(place, near_state), arrived)
+            near_first = fold_first(place, tie(y_near[:5], far[3]))
+            y_far = run_forward(l, 1, far, bank_l, after=(y_near[0],))
+            y_far, near_first, line[1] = tie((y_far, near_first, line[1]))
+            one = place.hop(tie(cuts[l + 1][1], line[1]), up=1)
+            far_first = fold_first(place, y_far[:5])
+            near_ends = fold_end(place, fold_sums(near_first))
+            far_first, one = tie((far_first, one))
+            far_state = fold_sums(far_first)
+            one_swap = place.hop(one, swap=1)
+            far_ends, one_swap = tie((fold_end(place, far_state), one_swap), *near_ends[1:3])
+            line = jnp.concatenate([packs[l + 1], *line])
+            passing = spread_first(place, tie(line, far_ends[1], far_ends[2]))
+            line_swap = place.hop(line, swap=1)
+            arrived = down_hops(place, sum_blocks(near_ends, (1,)))
+            blocks = sum_blocks(far_ends, (0, 1))
+            arrived += down_hops(place, blocks, 2)
+            passing = tie(passing, *arrived)
+            two = place.hop(tie(cuts[l + 1][2], arrived[0], arrived[1], arrived[2]), up=2)
+            swapped = [line_swap] + [place.hop(piece, swap=1) for piece in passing[1:]]
+            last_two = tie(spread_last(place, passing, 1, cut)[3:], *swapped[1:])
+            share_swaps = [own_swaps[l + 1], one_swap]
+            ends = [place.hop(p, swap=1) for p in last_two]
+            matrices.append([*passing, *last_two, *swapped, *ends])
+            shares = [cuts[l + 1][0], one, two]
+            shares.append(place.hop(tie(cuts[l + 1][3], last_two[0]), up=3))
+            base, extra = m, received(near_ends, arrived)
         else:
-            last = spread_last(place, passing)
+            last_near = jnp.concatenate(tie([cotangent, line[0]], far[3], far[4]))
+            last_near = spread_first(place, last_near)
+            y_far = run_forward(l, 1, far, bank_l, after=(y_near[0],))
+            y_far, last_near, line = tie((y_far, last_near, line))
+            last_near = spread_last(place, last_near)
+            last_far = spread_first(place, jnp.concatenate(tie(line[1:], *last_near[3:])))
+        stored.append((h, outs, y_near, y_far, bank_l))
 
     upstream = cotangent
     zero = jnp.zeros((rows, model), jnp.bfloat16)
@@ -1472,79 +1493,77 @@
     for l in reversed(range(layer_count)):
         h, outs, kept_near, kept_far, bank_l = stored[l]
         m, na, q, k, v, o, lse, gains = outs[1], *outs[3:]
-
-        spans = (spans_of(False), spans_of(True)) if l + 1 == layer_count else (None, None)
-
-        def run_near(after=()):
-            return experts_backward_fast(
-                where, gate_rows[l][0], near, kept_near[1:], bank_l, spans[0], after=after
-            )
-
-        def run_far(after=()):
-            return experts_backward_fast(
-                where, gate_rows[l][1], far, kept_far[1:], bank_l, spans[1], after=after
-            )
-
-        if l + 1 == layer_count:
-            near = far = last
-            b_near = run_near(after=(y_far[0],))
-            near_state_b = fold_start(place, b_near[:5])
-            b_far = run_far(after=(b_near[0],))
+        top = l + 1 == layer_count
+
+        if top:
+            b_near = run_backward(l, 0, last_near, kept_near[6:], bank_l, (y_far[0],))
+            b_near, last_far = tie((b_near, last_far))
+            far = spread_last(place, last_far)
+            near_first = fold_first(place, tie(b_near[:5], far[3], far[4]))
+            b_far = run_backward(l, 1, far, kept_far[6:], bank_l, (b_near[0],))
+            b_far, near_first = tie((b_far, near_first))
             far_first = fold_first(place, b_far[:5])
         else:
-            ups = up_hops(place, low)
-            near = spread_pieces(place, low)
-            far = jnp.concatenate(tie(ups, near[3], near[4]))
-            far = spread_first(place, far)
-            total = tie(held_total(), far[0])
-            came = [place.hop(total[1], up=1), place.hop(total[3], up=3)]
-            b_near = run_near()
-            near_state_b = fold_start(place, b_near[:5])
-            far, came = tie((far, came), b_near[0])
+            near, far = pairs_of(low)
+            near = spread_last(place, near)
+            far = spread_first(place, jnp.concatenate(tie(far, near[3], near[4])))
+            b_near = run_backward(l, 0, near, kept_near[6:], bank_l)
+            b_near, far = tie((b_near, far))
             far = spread_last(place, far)
-            came.insert(1, place.hop(tie(total[2], far[0]), up=2))
-            b_far = run_far(after=(near_state_b[1], near_state_b[2]))
-            result_ends = fold_end(place, tie(result_state, far[3], far[4]))
-            b_far, came, result_ends = tie((b_far, came, result_ends))
+            result_blocks = sum_blocks(tie(result_ends, b_near[0]), (0, 1))
+            result_arrived = down_hops(place, result_blocks, 2)
+            other_sum = place.hop(tie(other_one, b_near[0]), swap=1)
+            merged = merge_cores(mine_one, other_sum, cut)
+            held, merged = tie((held, merged), far[3], far[4])
+            came = [place.hop(tie(held[1], result_blocks[0]), up=1), came[0]]
+            merged_first = fold_first(place, merged)
+            b_far = run_backward(l, 1, far, kept_far[6:], bank_l, (b_near[0],))
+            b_far, merged_first, came[0] = tie((b_far, merged_first, came[0]))
             far_first = fold_first(place, b_far[:5])
-            arrived = down_hops(place, sum_blocks(*result_ends))
-            far_first = tie(far_first, *arrived)
-            result = total_of(stored[-1][1][1], received(result_near, arrived)).astype(jnp.bfloat16)
-            joined = join_experts(where, [total[0], *came], l + 1, layer_count, joined)
-
-        def weight_grads(i, after):
-            pick = lambda kept, found: ((kept[0], found[6 + i]) if i < 2 else (found[5], found[8]))
-            return weight_grads_fast(
-                where, pick(kept_near, b_near), pick(kept_far, b_far), experts, after=after
-            )
-
-        near_ends = fold_end(place, near_state_b)
+            near_first = fold_first(place, tie(b_near[:5], b_far[0]))
+            came.append(place.hop(tie(held[3], came[0]), up=3))
+
+        def weight_grads(i, after, near=(kept_near, b_near), far=(kept_far, b_far)):
+            pick = lambda kept, found: ((kept[5], found[6 + i]) if i < 2 else (found[5], found[8]))
+            return weight_grads_fast(where, pick(*near), pick(*far), experts, after=after)
+
         grads = [weight_grads(0, (b_far[0],))]
-        grads.append(weight_grads(1, (grads[0][0],)))
-        far_state_b = fold_sums(tie(far_first, grads[1][0]))
-        if l == 0:
-            grads.append(weight_grads(2, (far_state_b[1], far_state_b[2])))
-        far_ends = tie(fold_end(place, far_state_b), grads[-1][0], near_ends[1], near_ends[2])
-        blocks = sum_blocks(*far_ends)
-        arrived = down_hops(place, blocks)
-        if l:
-            grads.append(weight_grads(2, (far_ends[0],)))
-
-        def total_grads():
-            swapped = [place.hop(other, swap=1) for _, other in grads]
-            return [
-                jnp.stack([add_low(grads[i][0][k], swapped[i][k]) for i in range(3)])
-                for k in range(4)
-            ]
-
-        if l == 0:
-            total = total_grads()
-            ready = tie(total, *arrived)
-            came = [place.hop(ready[1], up=1), place.hop(ready[3], up=3)]
-        if l + 1 == layer_count:
-            result_state = fold_start(place, tie(y_far[:5], blocks[0]))
+        far_state = fold_sums(tie(far_first, grads[0][0]))
+        near_ends = fold_end(place, fold_sums(near_first))
+        grads.append(weight_grads(1, (far_state[1], far_state[2])))
+        swapped = [place.hop(grads[0][1], swap=1)]
+        far_ends = fold_end(place, far_state)
+        far_ends, swapped = tie((far_ends, swapped), grads[1][0], *near_ends[1:3])
+        swapped.append(place.hop(grads[1][1], swap=1))
+        if not top:
+            far_ends, came, result_arrived = tie((far_ends, came, result_arrived))
+        arrived = down_hops(place, sum_blocks(near_ends, (1,)))
+        blocks = sum_blocks(far_ends, (0, 1))
+        arrived += down_hops(place, blocks, 2)
+        grads.append(weight_grads(2, (blocks[0],)))
+        arrived, swapped = tie((arrived, swapped), grads[2][0])
+        swapped.append(place.hop(tie(grads[2][1], *arrived), swap=1))
+        total = merge_grads([mine for mine, _ in grads], swapped)
+        if top:
+            held = total
+            came = [place.hop(held[2], up=2)]
+            result_state = fold_start(place, tie(kept_far[:5], blocks[0]))
+            result_ends = fold_end(place, tie(result_state, *arrived))
+            result_first = fold_first(place, tie(kept_near[:5], *arrived))
+            after = ()
+            groups = ((0, 4),)
+        else:
+            held_came = [held[0], *came]
+            merged_ends = fold_end(place, fold_sums(tie(merged_first, blocks[0])))
+            one_total = add_pieces(*merged_ends, axis=1)
+            shard = mine_one.shape[0] // 16
+            low_total = tie(one_total[shard:].astype(jnp.bfloat16), *arrived)
+            one_arrived = down_hops(place, [low_total[n * shard :][:shard] for n in range(3)])
+            result_near = fold_end(place, fold_sums(tie(result_first, *arrived)))
+            after = (low_total, total[0])
+            groups = ((1, 3), (0, 1))
         upstream, low, *partial = attend_backward_fast(
-            l == 0,
+            groups,
             where,
             zero,
             upstream,
@@ -1553,21 +1572,34 @@
             tables,
             matrices[l],
             in_width,
-            after=() if l else (*total, joined[0]),
+            after=after,
         )
-        if l + 1 == layer_count:
-            held_total = total_grads
-            result_near = fold_end(place, near_state)
-            low, result_state = tie((low, result_state), *result_near)
-        if l == 0:
-            partial, came = tie((partial, came), sums[-1])
-            came.insert(1, place.hop(tie(total[2], upstream), up=2))
-            sums[l] = scatter_matrices(place, *partial, cut, came[1])
-            joined = join_experts(where, [total[0], *came], l, layer_count, joined)
+        if top:
+            low, result_ends, result_first, came = tie((low, result_ends, result_first, came))
+            other_one, mine_one = partial
         else:
-            sums[l] = lax.psum_scatter(
-                partial[0], AXES, scatter_dimension=0, tiled=True
-            ).astype(jnp.float32)
+            partial, result_near = tie((partial, result_near))
+    partial, one_arrived = tie((partial, one_arrived))
+    sums[1] = one_total[:shard]
+    for block in one_arrived:
+        sums[1] = sums[1] + block.astype(jnp.float32)
+    other_far, other_near, mine_far, mine_near = partial
+    other_far, other_near = place.hop(other_far, swap=1), place.hop(other_near, swap=1)
+    merged_far = merge_cores(mine_far, other_far, cut)
+    merged_near = merge_cores(mine_near, other_near, cut)
+    came = [place.hop(tie(total[k], upstream), up=k) for k in (1, 3)]
+    far_first = fold_first(place, merged_far)
+    near_first = fold_first(place, tie(merged_near, merged_far[0]))
+    far_state, near_state = fold_sums(tie(far_first, *came)), fold_sums(near_first)
+    came.insert(1, place.hop(tie(total[2], far_state[1]), up=2))
+    far_ends, near_ends = fold_end(place, far_state), fold_end(place, near_state)
+    far_total = add_pieces(*far_ends, axis=1)
+    sums[0] = sum_down(place, far_total, add_pieces(*near_ends, axis=1))
+    joined = join_experts(where, tie(held_came, far_state[1]), 1, layer_count, None)
+    joined = join_experts(where, [total[0], *came], 0, layer_count, joined)
+    last_block = down_hops(place, sum_blocks(tie(result_near, far_state[1]), (1,)))
+    result = total_of(stored[-1][1][1], received(result_near, last_block + result_arrived))
+    result = result.astype(jnp.bfloat16)
     sums = jnp.stack(sums)
     gain_sums = sums[:, :, in_width + model :]
     starts = (0, query.shape[2], query.shape[2] + key.shape[2], in_width, in_width + model)

time: 1260 us -> 1160 us (0.921)
  waiting for transfers between devices: 593 us -> 494 us
  Pallas kernels: 328 us -> 346 us
  between operations: 16.9 us -> 3.5 us
    ppermute x157 -> x165, waiting for transfers between devices: 593 us -> 494 us  [hop(): return lax.ppermute(value, AXES, pairs)]
    pallas_call x4 -> x10, Pallas kernels: 14.1 us -> 34.7 us  [the longest x8 22.6 us: sum_blocks(): pl.pallas_call(functools.partial(blocks_kernel, sides), name='sum_blocks'...]
    ppermute x157 -> x165, starting transfers between devices: 209 us -> 204 us  [hop(): return lax.ppermute(value, AXES, pairs)]
    unnamed x443 -> x434, local copies, waits for them, and re-layouts: 54.3 us -> 56.3 us
  transfers between devices with their start and end apart: 158 -> 165, of which waited for: 65 -> 62; matrix products, arithmetic and copies ran while one was open for 3% -> 4% of each run, Pallas kernels for 23% -> 30%
where the time goes in v4:
time: 1160 us; the launch traced here: 1150 us
  waiting for transfers between devices  494 us (43%)
  Pallas kernels  346 us (30%)
  starting transfers between devices  204 us (18%)
  local copies, waits for them, and re-layouts  76.4 us (7%)
  other arithmetic  27.8 us (2%)
    ppermute x165, waiting for transfers between devices, hop(): return lax.ppermute(value, AXES, pairs)  494 us
    ppermute x165, starting transfers between devices, hop(): return lax.ppermute(value, AXES, pairs)  204 us
    pallas_call x4, Pallas kernels, experts_backward_fast(): pl.pallas_call(body, name='experts_backward', out_shape=shapes, in_specs=...  76.1 us
    pallas_call x4, Pallas kernels, experts_forward_fast(): pl.pallas_call(body, name='experts_forward', out_shape=shapes, in_specs=[...  64.4 us
    pallas_call x2, Pallas kernels, attend_backward_fast(): pl.pallas_call(body, name='attend_backward', out_shape=shapes, in_specs=[...  60.9 us
    unnamed x434, local copies, waits for them, and re-layouts  56.3 us
    pallas_call x6, Pallas kernels, weight_grads_fast(): pl.pallas_call(body, name='weight_grads', out_shape=[shape_of(4, experts,...  46.5 us
    pallas_call x2, Pallas kernels, attend_forward_fast(): pl.pallas_call(body, name='attend_forward', out_shape=shapes, in_specs=[s...  32.3 us
  transfers between devices with their start and end apart: 165, of which 62 were waited for; matrix products, arithmetic and copies ran while one was open for 4% of the time, Pallas kernels for 30%

profile of v4, /device:TPU:0, one launch (start us, length us, event | category | flops | bytes accessed | tf_op | source)
XLA Modules:
  0.0 1152.7 jit_solution(17290105994391322261)
XLA Ops:
  42.5 9.2 collective-permute-start.9
  65.5 30.6 %collective-permute-done.8.refs_9_.refs_11_ = bf16[3,5,192,128]{3,2,1,0:T(8,128)(2,1)} collective-permute-done((bf16[3,5,192,128]{3,2,1,0:T(8,128)(2,1)S(1)}, bf16[3,5,192,128]{3,2,1,0:T(8,128)(2,1)}, u32[]{:S(2)}, u32[]{:S(2)}) %collective-permute-start.8) | collective-permute-done | bytes 737312 | tf_op jit(solution)/shard_map/ppermute | solution.py:38
  100.6 19.6 %collective-permute-done.17.refs_8_.refs_10_ = bf16[3,5,192,128]{3,2,1,0:T(8,128)(2,1)} collective-permute-done((bf16[3,5,192,128]{3,2,1,0:T(8,128)(2,1)S(1)}, bf16[3,5,192,128]{3,2,1,0:T(8,128)(2,1)}, u32[]{:S(2)}, u32[]{:S(2)}) %collective-permute-start.17) | collective-permute-done | bytes 737312 | tf_op jit(solution)/shard_map/ppermute | solution.py:38
  134.4 16.2 %attend_forward.2 = (f32[128,1536]{1,0:T(8,128)S(1)}, f32[128,1536]{1,0:T(8,128)S(1)}, bf16[128,1536]{1,0:T(8,128)(2,1)S(1)}, bf16[128,1536]{1,0:T(8,128)(2,1)S(...) custom-call(s32[3]{0:T(128)S(1)} %copy-done.104, ...), custom_call_target="tpu_custom_call" | custom-call | flops 103809024 | tf_op jit(solution)/shard_map/attend_forward/pallas_call | solution.py:684
  154.1 11.8 %collective-permute-done.25 = bf16[128,1536]{1,0:T(8,128)(2,1)S(1)} collective-permute-done((bf16[128,1536]{1,0:T(8,128)(2,1)S(1)}, bf16[128,1536]{1,0:T(8,128)(2,1)S(1)}, u32[]{:S(2)}, u32[]{:S(2)}) %collective-permute-start.25) | collective-permute-done | bytes 393248 | tf_op jit(solution)/shard_map/ppermute | solution.py:38
  170.9 14.2 %collective-permute-done.26.refs_3_ = bf16[256,1536]{1,0:T(8,128)(2,1)S(1)} collective-permute-done((bf16[256,1536]{1,0:T(8,128)(2,1)S(1)}, bf16[256,1536]{1,0:T(8,128)(2,1)S(1)}, u32[]{:S(2)}, u32[]{:S(2)}) %collective-permute-start.26) | collective-permute-done | bytes 786464 | tf_op jit(solution)/shard_map/ppermute | solution.py:38
  203.5 16.2 %experts_forward.4 = (bf16[256,1536]{1,0:T(8,128)(2,1)}, bf16[128,1536]{1,0:T(8,128)(2,1)S(1)}, bf16[128,1536]{1,0:T(8,128)(2,1)S(1)}, bf16[256,1536]{1,0:T(8,12...) custom-call(s32[3]{0:T(128)S(1)} %copy-done.104, ...), custom_call_target="tpu_custom_call" | custom-call | flops 377487360 | tf_op jit(solution)/shard_map/experts_forward/pallas_call | solution.py:962
  220.2 10.7 collective-permute-done.37.refs_5_
  236.3 21.7 %collective-permute-done.38.refs_6_ = bf16[128,1536]{1,0:T(8,128)(2,1)S(1)} collective-permute-done((bf16[128,1536]{1,0:T(8,128)(2,1)S(1)}, bf16[128,1536]{1,0:T(8,128)(2,1)S(1)}, u32[]{:S(2)}, u32[]{:S(2)}) %collective-permute-start.38) | collective-permute-done | bytes 393248 | tf_op jit(solution)/shard_map/ppermute | solution.py:38
  258.0 16.1 %experts_forward.5 = (bf16[256,1536]{1,0:T(8,128)(2,1)}, bf16[128,1536]{1,0:T(8,128)(2,1)S(1)}, bf16[128,1536]{1,0:T(8,128)(2,1)S(1)}, bf16[256,1536]{1,0:T(8,12...) custom-call(s32[3]{0:T(128)S(1)} %copy-done.104, ...), custom_call_target="tpu_custom_call" | custom-call | flops 377487360 | tf_op jit(solution)/shard_map/experts_forward/pallas_call | solution.py:962
  279.5 13.1 %collective-permute-done.47.refs_8_.refs_10_ = bf16[3,5,192,128]{3,2,1,0:T(8,128)(2,1)S(1)} collective-permute-done((bf16[3,5,192,128]{3,2,1,0:T(8,128)(2,1)S(1)}, bf16[3,5,192,128]{3,2,1,0:T(8,128)(2,1)S(1)}, u32[]{:S(2)}, u32[]{:S(2)}) %collective-permute-start.47) | collective-permute-done | bytes 737312 | tf_op jit(solution)/shard_map/ppermute | solution.py:38
  327.6 23.1 %collective-permute-done.51.refs_4_ = bf16[128,1536]{1,0:T(8,128)(2,1)S(1)} collective-permute-done((bf16[128,1536]{1,0:T(8,128)(2,1)}, bf16[128,1536]{1,0:T(8,128)(2,1)S(1)}, u32[]{:S(2)}, u32[]{:S(2)}) %collective-permute-start.51) | collective-permute-done | bytes 393248 | tf_op jit(solution)/shard_map/ppermute | solution.py:38
  355.5 18.2 %collective-permute-done.55.refs_14_.refs_24_ = bf16[192,2048]{1,0:T(8,128)(2,1)S(1)} collective-permute-done((bf16[192,2048]{1,0:T(8,128)(2,1)S(1)}, bf16[192,2048]{1,0:T(8,128)(2,1)S(1)}, u32[]{:S(2)}, u32[]{:S(2)}) %collective-permute-start.55) | collective-permute-done | bytes 786464 | tf_op jit(solution)/shard_map/ppermute | solution.py:38
  380.0 16.1 %attend_forward.3 = (f32[128,1536]{1,0:T(8,128)S(1)}, f32[128,1536]{1,0:T(8,128)S(1)}, bf16[128,1536]{1,0:T(8,128)(2,1)S(1)}, bf16[128,1536]{1,0:T(8,128)(2,1)S(...) custom-call(s32[3]{0:T(128)S(1)} %copy-done.104, ...), custom_call_target="tpu_custom_call" | custom-call | flops 103809024 | tf_op jit(solution)/shard_map/attend_forward/pallas_call | solution.py:684
  397.1 13.7 %collective-permute-done.62.refs_9_.refs_11_ = bf16[3,5,192,128]{3,2,1,0:T(8,128)(2,1)S(1)} collective-permute-done((bf16[3,5,192,128]{3,2,1,0:T(8,128)(2,1)}, bf16[3,5,192,128]{3,2,1,0:T(8,128)(2,1)S(1)}, u32[]{:S(2)}, u32[]{:S(2)}) %collective-permute-start.62) | collective-permute-done | bytes 737312 | tf_op jit(solution)/shard_map/ppermute | solution.py:38
  411.5 15.3 %collective-permute-start.64 = (bf16[128,1536]{1,0:T(8,128)(2,1)S(1)}, bf16[128,1536]{1,0:T(8,128)(2,1)S(1)}, u32[]{:S(2)}, u32[]{:S(2)}) collective-permute-start(bf16[128,1536]{1,0:T(8,128)(2,1)S(1)} %get-tuple-element.582), channel_id=1, source_target_pairs={{0,8},{1,9},{2,10},{3,11},{4,12},{5,13},{6,14},{7,15},{8,16},{9,17... | collective-permute-start | bytes 1179656 | tf_op jit(solution)/shard_map/ppermute | solution.py:38
  426.9 8.8 collective-permute-done.64
  442.0 12.2 %collective-permute-done.65.refs_3_ = bf16[256,1536]{1,0:T(8,128)(2,1)S(1)} collective-permute-done((bf16[256,1536]{1,0:T(8,128)(2,1)S(1)}, bf16[256,1536]{1,0:T(8,128)(2,1)S(1)}, u32[]{:S(2)}, u32[]{:S(2)}) %collective-permute-start.65) | collective-permute-done | bytes 786464 | tf_op jit(solution)/shard_map/ppermute | solution.py:38
  472.1 16.3 %experts_forward.6 = (bf16[256,1536]{1,0:T(8,128)(2,1)}, bf16[128,1536]{1,0:T(8,128)(2,1)S(1)}, bf16[128,1536]{1,0:T(8,128)(2,1)S(1)}, bf16[256,1536]{1,0:T(8,12...) custom-call(s32[3]{0:T(128)S(1)} %copy-done.104, ...), custom_call_target="tpu_custom_call" | custom-call | flops 377487360 | tf_op jit(solution)/shard_map/experts_forward/pallas_call | solution.py:962
  492.0 8.9 collective-permute-done.77.refs_5_
  504.0 15.8 %experts_forward.7 = (bf16[256,1536]{1,0:T(8,128)(2,1)}, bf16[128,1536]{1,0:T(8,128)(2,1)S(1)}, bf16[128,1536]{1,0:T(8,128)(2,1)S(1)}, bf16[256,1536]{1,0:T(8,12...) custom-call(s32[3]{0:T(128)S(1)} %copy-done.104, ...), custom_call_target="tpu_custom_call" | custom-call | flops 377487360 | tf_op jit(solution)/shard_map/experts_forward/pallas_call | solution.py:962
  524.0 8.9 collective-permute-done.82.refs_5_
  536.4 18.7 %experts_backward.4 = (bf16[256,1536]{1,0:T(8,128)(2,1)}, bf16[128,1536]{1,0:T(8,128)(2,1)S(1)}, bf16[128,1536]{1,0:T(8,128)(2,1)S(1)}, bf16[256,1536]{1,0:T(8,1...) custom-call(s32[3]{0:T(128)S(1)} %copy-done.104, ...), custom_call_target="tpu_custom_call" | custom-call | flops 377487360 | tf_op jit(solution)/shard_map/experts_backward/pallas_call | solution.py:1031
  567.1 19.5 %experts_backward.5 = (bf16[256,1536]{1,0:T(8,128)(2,1)}, bf16[128,1536]{1,0:T(8,128)(2,1)S(1)}, bf16[128,1536]{1,0:T(8,128)(2,1)S(1)}, bf16[256,1536]{1,0:T(8,1...) custom-call(s32[3]{0:T(128)S(1)} %copy-done.104, ...), custom_call_target="tpu_custom_call" | custom-call | flops 377487360 | tf_op jit(solution)/shard_map/experts_backward/pallas_call | solution.py:1031
  591.1 7.9 weight_grads.6
  605.0 7.9 weight_grads.7
  615.8 9.4 collective-permute-done.90.one_head.refs_7_
  643.8 7.6 weight_grads.8
  652.3 11.8 %collective-permute-done.98.refs_5_ = bf16[128,1536]{1,0:T(8,128)(2,1)S(1)} collective-permute-done((bf16[128,1536]{1,0:T(8,128)(2,1)}, bf16[128,1536]{1,0:T(8,128)(2,1)S(1)}, u32[]{:S(2)}, u32[]{:S(2)}) %collective-permute-start.98) | collective-permute-done | bytes 393248 | tf_op jit(solution)/shard_map/ppermute | solution.py:38
  676.1 8.7 collective-permute-done.101.by_two
  687.7 30.3 %attend_backward.2 = (f32[128,1536]{1,0:T(8,128)}, bf16[128,1536]{1,0:T(8,128)(2,1)}, bf16[768,4224]{1,0:T(8,128)(2,1)}, bf16[768,4224]{1,0:T(8,128)(2,1)}) custom-call(s32[3]{0:T(128)} %pad_add_fusion.where.refs_0_, bf16[128,1536]{1,0:T(8,128)(2,1)} %broadcast_in_dim.61.refs_1_, bf16[128,1536]{1,0:T(8,128)(2,1)} %refs_2_.3, ...), custom_call_target="tpu_custom_call" | custom-call | flops 207618048 | tf_op jit(solution)/shard_map/attend_backward/pallas_call | solution.py:845
  720.0 9.9 collective-permute-done.109
  733.2 14.0 %collective-permute-done.110.refs_3_ = bf16[256,1536]{1,0:T(8,128)(2,1)S(1)} collective-permute-done((bf16[256,1536]{1,0:T(8,128)(2,1)S(1)}, bf16[256,1536]{1,0:T(8,128)(2,1)S(1)}, u32[]{:S(2)}, u32[]{:S(2)}) %collective-permute-start.110) | collective-permute-done | bytes 786464 | tf_op jit(solution)/shard_map/ppermute | solution.py:38
  760.2 18.6 %experts_backward.6 = (bf16[256,1536]{1,0:T(8,128)(2,1)}, bf16[128,1536]{1,0:T(8,128)(2,1)S(1)}, bf16[128,1536]{1,0:T(8,128)(2,1)S(1)}, bf16[256,1536]{1,0:T(8,1...) custom-call(s32[3]{0:T(128)S(1)} %copy-done.105, ...), custom_call_target="tpu_custom_call" | custom-call | flops 377487360 | tf_op jit(solution)/shard_map/experts_backward/pallas_call | solution.py:1031
  781.1 8.5 collective-permute-done.120.arrived
  808.8 19.3 %experts_backward.7 = (bf16[256,1536]{1,0:T(8,128)(2,1)}, bf16[128,1536]{1,0:T(8,128)(2,1)S(1)}, bf16[128,1536]{1,0:T(8,128)(2,1)S(1)}, bf16[256,1536]{1,0:T(8,1...) custom-call(s32[3]{0:T(128)S(1)} %copy-done.105, ...), custom_call_target="tpu_custom_call" | custom-call | flops 377487360 | tf_op jit(solution)/shard_map/experts_backward/pallas_call | solution.py:1031
  829.6 10.2 collective-permute-done.122
  846.9 7.6 weight_grads.9
  863.9 12.6 %collective-permute-done.126.by_one = bf16[256,1536]{1,0:T(8,128)(2,1)S(1)} collective-permute-done((bf16[256,1536]{1,0:T(8,128)(2,1)S(1)}, bf16[256,1536]{1,0:T(8,128)(2,1)S(1)}, u32[]{:S(2)}, u32[]{:S(2)}) %collective-permute-start.126) | collective-permute-done | bytes 786464 | tf_op jit(solution)/shard_map/ppermute | solution.py:38
  892.4 7.9 weight_grads.10
  901.3 9.2 collective-permute-done.135
  927.7 11.5 collective-permute-done.137.refs_5_
  970.9 30.6 %attend_backward.3 = (f32[128,1536]{1,0:T(8,128)}, bf16[128,1536]{1,0:T(8,128)(2,1)}, bf16[576,4224]{1,0:T(8,128)(2,1)}, bf16[192,4224]{1,0:T(8,128)(2,1)}, bf16...) custom-call(s32[3]{0:T(128)} %pad_add_fusion.where.refs_0_, bf16[128,1536]{1,0:T(8,128)(2,1)} %broadcast_in_dim.61.refs_1_, ...), custom_call_target="tpu_custom_call" | custom-call | flops 207618048 | tf_op jit(solution)/shard_map/attend_backward/pallas_call | solution.py:845
  1004.6 7.6 collective-permute-done.154.arrived
  1026.1 31.6 %collective-permute-done.155 = bf16[96,2048]{1,0:T(8,128)(2,1)S(1)} collective-permute-done((bf16[96,2048]{1,0:T(8,128)(2,1)S(1)}, bf16[96,2048]{1,0:T(8,128)(2,1)S(1)}, u32[]{:S(2)}, u32[]{:S(2)}) %collective-permute-start.155) | collective-permute-done | bytes 393248 | tf_op jit(solution)/shard_map/ppermute | solution.py:38
  1091.9 20.4 %collective-permute-done.153 = bf16[128,1536]{1,0:T(8,128)(2,1)S(1)} collective-permute-done((bf16[128,1536]{1,0:T(8,128)(2,1)}, bf16[128,1536]{1,0:T(8,128)(2,1)S(1)}, u32[]{:S(2)}, u32[]{:S(2)}) %collective-permute-start.153) | collective-permute-done | bytes 393248 | tf_op jit(solution)/shard_map/ppermute | solution.py:38
  1114.1 17.9 %collective-permute-start.163 = (bf16[48,4224]{1,0:T(8,128)(2,1)S(1)}, bf16[48,4224]{1,0:T(8,128)(2,1)S(1)}, u32[]{:S(2)}, u32[]{:S(2)}) collective-permute-start(bf16[48,4224]{1,0:T(8,128)(2,1)S(1)} %get-tuple-element.958), channel_id=1, source_target_pairs={{0,8},{1,9},{2,10},{3,11},{4,12},{5,13},{6,14},{7,15},{8,16},{9,17... | collective-permute-start | bytes 1216520 | tf_op jit(solution)/shard_map/ppermute | solution.py:38
  1137.2 11.2 collective-permute-done.162
  (851 shorter events, 442.1 us)
Async XLA Ops:
  7.9 29.1 %collective-permute-start.1 = (bf16[48,4224]{1,0:T(8,128)(2,1)}, bf16[48,4224]{1,0:T(8,128)(2,1)S(1)}, u32[]{:S(2)}, u32[]{:S(2)}) collective-permute-start(bf16[48,4224]{1,0:T(8,128)(2,1)} %get-tuple-element.480), channel_id=1, source_target_pairs={{0,16},{1,17},{2,18},{3,19},{4,20},{5,21},{6,22},{7,23},{8,24},{9,... | collective-permute-start | bytes 1216520 | tf_op jit(solution)/shard_map/ppermute | solution.py:38
  39.4 56.7 %collective-permute-start.12 = (bf16[192,4224]{1,0:T(8,128)(2,1)}, bf16[192,4224]{1,0:T(8,128)(2,1)}, u32[]{:S(2)}, u32[]{:S(2)}) collective-permute-start(bf16[192,4224]{1,0:T(8,128)(2,1)} %constant_dynamic-update-slice_fusion.refs_5_.refs_21_), channel_id=1, source_target_pairs={{0,4},{1,5},{2,6},{3,7},{4,0},{5,1},{6,2},{7,3},{8,12},{9,13},{10,... | collective-permute-start | bytes 4866056 | tf_op jit(solution)/shard_map/ppermute | solution.py:38
  39.4 56.7 %collective-permute-start.6 = (bf16[192,4224]{1,0:T(8,128)(2,1)}, bf16[192,4224]{1,0:T(8,128)(2,1)}, u32[]{:S(2)}, u32[]{:S(2)}) collective-permute-start(bf16[192,4224]{1,0:T(8,128)(2,1)} %constant_dynamic-update-slice_fusion.refs_5_.refs_21_), channel_id=1, source_target_pairs={{0,1},{1,0},{2,3},{3,2},{4,5},{5,4},{6,7},{7,6},{8,9},{9,8},{10,11... | collective-permute-start | bytes 4866056 | tf_op jit(solution)/shard_map/ppermute | solution.py:38
  40.9 55.2 %collective-permute-start.7 = (bf16[192,4224]{1,0:T(8,128)(2,1)}, bf16[192,4224]{1,0:T(8,128)(2,1)}, u32[]{:S(2)}, u32[]{:S(2)}) collective-permute-start(bf16[192,4224]{1,0:T(8,128)(2,1)} %constant_dynamic-update-slice_fusion.refs_5_.refs_21_), channel_id=1, source_target_pairs={{0,2},{1,3},{2,0},{3,1},{4,6},{5,7},{6,4},{7,5},{8,10},{9,11},{10,... | collective-permute-start | bytes 4866056 | tf_op jit(solution)/shard_map/ppermute | solution.py:38
  62.9 33.2 %collective-permute-start.8 = (bf16[3,5,192,128]{3,2,1,0:T(8,128)(2,1)S(1)}, bf16[3,5,192,128]{3,2,1,0:T(8,128)(2,1)}, u32[]{:S(2)}, u32[]{:S(2)}) collective-permute-start(bf16[3,5,192,128]{3,2,1,0:T(8,128)(2,1)S(1)} %copy-done.205), channel_id=1, source_target_pairs={{0,16},{1,17},{2,18},{3,19},{4,20},{5,21},{6,22},{7,23},{8,24},{9,... | collective-permute-start | bytes 2211848 | tf_op jit(solution)/shard_map/ppermute | solution.py:38
  63.5 32.7 %collective-permute-start.14 = (bf16[3,5,192,128]{3,2,1,0:T(8,128)(2,1)S(1)}, bf16[3,5,192,128]{3,2,1,0:T(8,128)(2,1)S(1)}, u32[]{:S(2)}, u32[]{:S(2)}) collective-permute-start(bf16[3,5,192,128]{3,2,1,0:T(8,128)(2,1)S(1)} %copy-done.9), channel_id=1, source_target_pairs={{0,4},{1,5},{2,6},{3,7},{4,0},{5,1},{6,2},{7,3},{8,12},{9,13},{10,... | collective-permute-start | bytes 2211848 | tf_op jit(solution)/shard_map/ppermute | solution.py:38
  120.8 31.8 %collective-permute-start.24 = (bf16[3,5,192,128]{3,2,1,0:T(8,128)(2,1)}, bf16[3,5,192,128]{3,2,1,0:T(8,128)(2,1)}, u32[]{:S(2)}, u32[]{:S(2)}) collective-permute-start(bf16[3,5,192,128]{3,2,1,0:T(8,128)(2,1)} %get-tuple-element.505), channel_id=1, source_target_pairs={{0,24},{1,25},{2,26},{3,27},{4,28},{5,29},{6,30},{7,31},{8,0},{9,1... | collective-permute-start | bytes 2211848 | tf_op jit(solution)/shard_map/ppermute | solution.py:38
  230.8 43.4 %collective-permute-start.39 = (bf16[256,1536]{1,0:T(8,128)(2,1)}, bf16[256,1536]{1,0:T(8,128)(2,1)S(1)}, u32[]{:S(2)}, u32[]{:S(2)}) collective-permute-start(bf16[256,1536]{1,0:T(8,128)(2,1)} %get-tuple-element.539), channel_id=1, source_target_pairs={{0,1},{1,0},{2,3},{3,2},{4,5},{5,4},{6,7},{7,6},{8,9},{9,8},{10,11... | collective-permute-start | bytes 2359304 | tf_op jit(solution)/shard_map/ppermute | solution.py:38
  231.4 42.8 %collective-permute-start.40 = (bf16[256,1536]{1,0:T(8,128)(2,1)}, bf16[256,1536]{1,0:T(8,128)(2,1)S(1)}, u32[]{:S(2)}, u32[]{:S(2)}) collective-permute-start(bf16[256,1536]{1,0:T(8,128)(2,1)} %get-tuple-element.540), channel_id=1, source_target_pairs={{0,2},{1,3},{2,0},{3,1},{4,6},{5,7},{6,4},{7,5},{8,10},{9,11},{10,... | collective-permute-start | bytes 2359304 | tf_op jit(solution)/shard_map/ppermute | solution.py:38
  233.2 41.0 %collective-permute-start.41 = (bf16[48,4224]{1,0:T(8,128)(2,1)S(1)}, bf16[48,4224]{1,0:T(8,128)(2,1)S(1)}, u32[]{:S(2)}, u32[]{:S(2)}) collective-permute-start(bf16[48,4224]{1,0:T(8,128)(2,1)S(1)} %copy-done.180), channel_id=1, source_target_pairs={{0,16},{1,17},{2,18},{3,19},{4,20},{5,21},{6,22},{7,23},{8,24},{9,... | collective-permute-start | bytes 1216520 | tf_op jit(solution)/shard_map/ppermute | solution.py:38
  309.3 41.4 %collective-permute-start.53 = (bf16[192,4224]{1,0:T(8,128)(2,1)}, bf16[192,4224]{1,0:T(8,128)(2,1)}, u32[]{:S(2)}, u32[]{:S(2)}) collective-permute-start(bf16[192,4224]{1,0:T(8,128)(2,1)} %constant_dynamic-update-slice_fusion.8.refs_11_.refs_21_), channel_id=1, source_target_pairs={{0,1},{1,0},{2,3},{3,2},{4,5},{5,4},{6,7},{7,6},{8,9},{9,8},{10,11... | collective-permute-start | bytes 4866056 | tf_op jit(solution)/shard_map/ppermute | solution.py:38
  310.9 39.8 %collective-permute-start.54 = (bf16[192,4224]{1,0:T(8,128)(2,1)}, bf16[192,4224]{1,0:T(8,128)(2,1)}, u32[]{:S(2)}, u32[]{:S(2)}) collective-permute-start(bf16[192,4224]{1,0:T(8,128)(2,1)} %constant_dynamic-update-slice_fusion.8.refs_11_.refs_21_), channel_id=1, source_target_pairs={{0,2},{1,3},{2,0},{3,1},{4,6},{5,7},{6,4},{7,5},{8,10},{9,11},{10,... | collective-permute-start | bytes 4866056 | tf_op jit(solution)/shard_map/ppermute | solution.py:38
  320.5 30.2 %collective-permute-start.51 = (bf16[128,1536]{1,0:T(8,128)(2,1)}, bf16[128,1536]{1,0:T(8,128)(2,1)S(1)}, u32[]{:S(2)}, u32[]{:S(2)}) collective-permute-start(bf16[128,1536]{1,0:T(8,128)(2,1)} %get-tuple-element.565), channel_id=1, source_target_pairs={{0,16},{1,17},{2,18},{3,19},{4,20},{5,21},{6,22},{7,23},{8,24},{9,... | collective-permute-start | bytes 1179656 | tf_op jit(solution)/shard_map/ppermute | solution.py:38
  320.6 30.1 %collective-permute-start.52 = (bf16[128,1536]{1,0:T(8,128)(2,1)}, bf16[128,1536]{1,0:T(8,128)(2,1)S(1)}, u32[]{:S(2)}, u32[]{:S(2)}) collective-permute-start(bf16[128,1536]{1,0:T(8,128)(2,1)} %get-tuple-element.566), channel_id=1, source_target_pairs={{0,8},{1,9},{2,10},{3,11},{4,12},{5,13},{6,14},{7,15},{8,16},{9,17... | collective-permute-start | bytes 1179656 | tf_op jit(solution)/shard_map/ppermute | solution.py:38
  374.2 36.5 %collective-permute-start.62 = (bf16[3,5,192,128]{3,2,1,0:T(8,128)(2,1)}, bf16[3,5,192,128]{3,2,1,0:T(8,128)(2,1)S(1)}, u32[]{:S(2)}, u32[]{:S(2)}) collective-permute-start(bf16[3,5,192,128]{3,2,1,0:T(8,128)(2,1)} %get-tuple-element.579), channel_id=1, source_target_pairs={{0,16},{1,17},{2,18},{3,19},{4,20},{5,21},{6,22},{7,23},{8,24},{9,... | collective-permute-start | bytes 2211848 | tf_op jit(solution)/shard_map/ppermute | solution.py:38
  377.7 33.8 %collective-permute-start.63 = (bf16[3,5,192,128]{3,2,1,0:T(8,128)(2,1)}, bf16[3,5,192,128]{3,2,1,0:T(8,128)(2,1)S(1)}, u32[]{:S(2)}, u32[]{:S(2)}) collective-permute-start(bf16[3,5,192,128]{3,2,1,0:T(8,128)(2,1)} %get-tuple-element.581), channel_id=1, source_target_pairs={{0,24},{1,25},{2,26},{3,27},{4,28},{5,29},{6,30},{7,31},{8,0},{9,1... | collective-permute-start | bytes 2211848 | tf_op jit(solution)/shard_map/ppermute | solution.py:38
  600.0 29.7 %collective-permute-start.97 = (bf16[4,5,192,128]{3,2,1,0:T(8,128)(2,1)}, bf16[4,5,192,128]{3,2,1,0:T(8,128)(2,1)}, u32[]{:S(2)}, u32[]{:S(2)}) collective-permute-start(bf16[4,5,192,128]{3,2,1,0:T(8,128)(2,1)} %get-tuple-element.675), channel_id=1, source_target_pairs={{0,4},{1,5},{2,6},{3,7},{4,0},{5,1},{6,2},{7,3},{8,12},{9,13},{10,... | collective-permute-start | bytes 2949128 | tf_op jit(solution)/shard_map/ppermute | solution.py:38
  613.0 51.1 %collective-permute-start.100 = (bf16[4,5,192,128]{3,2,1,0:T(8,128)(2,1)}, bf16[4,5,192,128]{3,2,1,0:T(8,128)(2,1)}, u32[]{:S(2)}, u32[]{:S(2)}) collective-permute-start(bf16[4,5,192,128]{3,2,1,0:T(8,128)(2,1)} %get-tuple-element.687), channel_id=1, source_target_pairs={{0,4},{1,5},{2,6},{3,7},{4,0},{5,1},{6,2},{7,3},{8,12},{9,13},{10,... | collective-permute-start | bytes 2949128 | tf_op jit(solution)/shard_map/ppermute | solution.py:38
  636.2 27.9 %collective-permute-start.98 = (bf16[128,1536]{1,0:T(8,128)(2,1)}, bf16[128,1536]{1,0:T(8,128)(2,1)S(1)}, u32[]{:S(2)}, u32[]{:S(2)}) collective-permute-start(bf16[128,1536]{1,0:T(8,128)(2,1)} %get-tuple-element.684.refs_5_), channel_id=1, source_target_pairs={{0,16},{1,17},{2,18},{3,19},{4,20},{5,21},{6,22},{7,23},{8,24},{9,... | collective-permute-start | bytes 1179656 | tf_op jit(solution)/shard_map/ppermute | solution.py:38
  637.8 29.1 %collective-permute-start.102 = (bf16[256,1536]{1,0:T(8,128)(2,1)}, bf16[256,1536]{1,0:T(8,128)(2,1)S(1)}, u32[]{:S(2)}, u32[]{:S(2)}) collective-permute-start(bf16[256,1536]{1,0:T(8,128)(2,1)} %get-tuple-element.714), channel_id=1, source_target_pairs={{0,1},{1,0},{2,3},{3,2},{4,5},{5,4},{6,7},{7,6},{8,9},{9,8},{10,11... | collective-permute-start | bytes 2359304 | tf_op jit(solution)/shard_map/ppermute | solution.py:38
  664.8 53.3 %collective-permute-start.105 = (bf16[256,1536]{1,0:T(8,128)(2,1)}, bf16[256,1536]{1,0:T(8,128)(2,1)S(1)}, u32[]{:S(2)}, u32[]{:S(2)}) collective-permute-start(bf16[256,1536]{1,0:T(8,128)(2,1)} %get-tuple-element.727), channel_id=1, source_target_pairs={{0,1},{1,0},{2,3},{3,2},{4,5},{5,4},{6,7},{7,6},{8,9},{9,8},{10,11... | collective-permute-start | bytes 2359304 | tf_op jit(solution)/shard_map/ppermute | solution.py:38
  666.2 51.9 %collective-permute-start.106 = (bf16[256,1536]{1,0:T(8,128)(2,1)}, bf16[256,1536]{1,0:T(8,128)(2,1)S(1)}, u32[]{:S(2)}, u32[]{:S(2)}) collective-permute-start(bf16[256,1536]{1,0:T(8,128)(2,1)} %get-tuple-element.728), channel_id=1, source_target_pairs={{0,2},{1,3},{2,0},{3,1},{4,6},{5,7},{6,4},{7,5},{8,10},{9,11},{10,... | collective-permute-start | bytes 2359304 | tf_op jit(solution)/shard_map/ppermute | solution.py:38
  673.8 44.3 %collective-permute-start.108 = (bf16[3,5,192,128]{3,2,1,0:T(8,128)(2,1)}, bf16[3,5,192,128]{3,2,1,0:T(8,128)(2,1)S(1)}, u32[]{:S(2)}, u32[]{:S(2)}) collective-permute-start(bf16[3,5,192,128]{3,2,1,0:T(8,128)(2,1)} %get-tuple-element.733), channel_id=1, source_target_pairs={{0,16},{1,17},{2,18},{3,19},{4,20},{5,21},{6,22},{7,23},{8,24},{9,... | collective-permute-start | bytes 2211848 | tf_op jit(solution)/shard_map/ppermute | solution.py:38
  684.9 33.2 %collective-permute-start.103 = (bf16[128,1536]{1,0:T(8,128)(2,1)S(1)}, bf16[128,1536]{1,0:T(8,128)(2,1)S(1)}, u32[]{:S(2)}, u32[]{:S(2)}) collective-permute-start(bf16[128,1536]{1,0:T(8,128)(2,1)S(1)} %add_convert_fusion.13), channel_id=1, source_target_pairs={{0,1},{1,0},{2,3},{3,2},{4,5},{5,4},{6,7},{7,6},{8,9},{9,8},{10,11... | collective-permute-start | bytes 1179656 | tf_op jit(solution)/shard_map/ppermute | solution.py:38
  685.5 32.6 %collective-permute-start.104 = (bf16[128,1536]{1,0:T(8,128)(2,1)S(1)}, bf16[128,1536]{1,0:T(8,128)(2,1)S(1)}, u32[]{:S(2)}, u32[]{:S(2)}) collective-permute-start(bf16[128,1536]{1,0:T(8,128)(2,1)S(1)} %add_convert_fusion.12), channel_id=1, source_target_pairs={{0,2},{1,3},{2,0},{3,1},{4,6},{5,7},{6,4},{7,5},{8,10},{9,11},{10,... | collective-permute-start | bytes 1179656 | tf_op jit(solution)/shard_map/ppermute | solution.py:38
  801.3 39.1 %collective-permute-start.121 = (bf16[384,2176]{1,0:T(8,128)(2,1)}, bf16[384,2176]{1,0:T(8,128)(2,1)}, u32[]{:S(2)}, u32[]{:S(2)}) collective-permute-start(bf16[384,2176]{1,0:T(8,128)(2,1)} %get-tuple-element.781), channel_id=1, source_target_pairs={{0,1},{1,0},{2,3},{3,2},{4,5},{5,4},{6,7},{7,6},{8,9},{9,8},{10,11... | collective-permute-start | bytes 5013512 | tf_op jit(solution)/shard_map/ppermute | solution.py:38
  803.3 36.5 %collective-permute-start.122 = (bf16[384,2048]{1,0:T(8,128)(2,1)}, bf16[384,2048]{1,0:T(8,128)(2,1)}, u32[]{:S(2)}, u32[]{:S(2)}) collective-permute-start(bf16[384,2048]{1,0:T(8,128)(2,1)} %get-tuple-element.782), channel_id=1, source_target_pairs={{0,2},{1,3},{2,0},{3,1},{4,6},{5,7},{6,4},{7,5},{8,10},{9,11},{10,... | collective-permute-start | bytes 4718600 | tf_op jit(solution)/shard_map/ppermute | solution.py:38
  842.3 69.7 %collective-permute-start.134 = (bf16[3,5,192,128]{3,2,1,0:T(8,128)(2,1)}, bf16[3,5,192,128]{3,2,1,0:T(8,128)(2,1)S(1)}, u32[]{:S(2)}, u32[]{:S(2)}) collective-permute-start(bf16[3,5,192,128]{3,2,1,0:T(8,128)(2,1)} %get-tuple-element.828), channel_id=1, source_target_pairs={{0,24},{1,25},{2,26},{3,27},{4,28},{5,29},{6,30},{7,31},{8,0},{9,1... | collective-permute-start | bytes 2211848 | tf_op jit(solution)/shard_map/ppermute | solution.py:38
  901.3 48.9 %collective-permute-start.139 = (bf16[4,5,192,128]{3,2,1,0:T(8,128)(2,1)}, bf16[4,5,192,128]{3,2,1,0:T(8,128)(2,1)}, u32[]{:S(2)}, u32[]{:S(2)}) collective-permute-start(bf16[4,5,192,128]{3,2,1,0:T(8,128)(2,1)} %get-tuple-element.838), channel_id=1, source_target_pairs={{0,4},{1,5},{2,6},{3,7},{4,0},{5,1},{6,2},{7,3},{8,12},{9,13},{10,... | collective-permute-start | bytes 2949128 | tf_op jit(solution)/shard_map/ppermute | solution.py:38
  915.8 34.4 %collective-permute-start.138 = (bf16[128,1536]{1,0:T(8,128)(2,1)}, bf16[128,1536]{1,0:T(8,128)(2,1)}, u32[]{:S(2)}, u32[]{:S(2)}) collective-permute-start(bf16[128,1536]{1,0:T(8,128)(2,1)} %get-tuple-element.836), channel_id=1, source_target_pairs={{0,8},{1,9},{2,10},{3,11},{4,12},{5,13},{6,14},{7,15},{8,16},{9,17... | collective-permute-start | bytes 1179656 | tf_op jit(solution)/shard_map/ppermute | solution.py:38
  919.1 31.1 %collective-permute-start.128 = (bf16[128,1536]{1,0:T(8,128)(2,1)}, bf16[128,1536]{1,0:T(8,128)(2,1)S(1)}, u32[]{:S(2)}, u32[]{:S(2)}) collective-permute-start(bf16[128,1536]{1,0:T(8,128)(2,1)} %sum_blocks.13), channel_id=1, source_target_pairs={{0,24},{1,25},{2,26},{3,27},{4,28},{5,29},{6,30},{7,31},{8,0},{9,1... | collective-permute-start | bytes 1179656 | tf_op jit(solution)/shard_map/ppermute | solution.py:38
  924.6 34.0 %collective-permute-start.141 = (bf16[192,2176]{1,0:T(8,128)(2,1)S(1)}, bf16[192,2176]{1,0:T(8,128)(2,1)S(1)}, u32[]{:S(2)}, u32[]{:S(2)}) collective-permute-start(bf16[192,2176]{1,0:T(8,128)(2,1)S(1)} %add_convert_fusion.1), channel_id=1, source_target_pairs={{0,2},{1,3},{2,0},{3,1},{4,6},{5,7},{6,4},{7,5},{8,10},{9,11},{10,... | collective-permute-start | bytes 2506760 | tf_op jit(solution)/shard_map/ppermute | solution.py:38
  951.3 50.1 %collective-permute-start.144 = (bf16[128,1536]{1,0:T(8,128)(2,1)}, bf16[128,1536]{1,0:T(8,128)(2,1)}, u32[]{:S(2)}, u32[]{:S(2)}) collective-permute-start(bf16[128,1536]{1,0:T(8,128)(2,1)} %add_convert_fusion.6), channel_id=1, source_target_pairs={{0,2},{1,3},{2,0},{3,1},{4,6},{5,7},{6,4},{7,5},{8,10},{9,11},{10,... | collective-permute-start | bytes 1179656 | tf_op jit(solution)/shard_map/ppermute | solution.py:38
  961.0 40.5 %collective-permute-start.145 = (bf16[48,4224]{1,0:T(8,128)(2,1)S(1)}, bf16[48,4224]{1,0:T(8,128)(2,1)}, u32[]{:S(2)}, u32[]{:S(2)}) collective-permute-start(bf16[48,4224]{1,0:T(8,128)(2,1)S(1)} %get-tuple-element.962), channel_id=1, source_target_pairs={{0,24},{1,25},{2,26},{3,27},{4,28},{5,29},{6,30},{7,31},{8,0},{9,1... | collective-permute-start | bytes 1216520 | tf_op jit(solution)/shard_map/ppermute | solution.py:38
  961.0 40.5 %collective-permute-start.146 = (bf16[48,4224]{1,0:T(8,128)(2,1)S(1)}, bf16[48,4224]{1,0:T(8,128)(2,1)}, u32[]{:S(2)}, u32[]{:S(2)}) collective-permute-start(bf16[48,4224]{1,0:T(8,128)(2,1)S(1)} %get-tuple-element.961), channel_id=1, source_target_pairs={{0,16},{1,17},{2,18},{3,19},{4,20},{5,21},{6,22},{7,23},{8,24},{9,... | collective-permute-start | bytes 1216520 | tf_op jit(solution)/shard_map/ppermute | solution.py:38
  961.0 40.5 %collective-permute-start.147 = (bf16[48,4224]{1,0:T(8,128)(2,1)S(1)}, bf16[48,4224]{1,0:T(8,128)(2,1)}, u32[]{:S(2)}, u32[]{:S(2)}) collective-permute-start(bf16[48,4224]{1,0:T(8,128)(2,1)S(1)} %get-tuple-element.960), channel_id=1, source_target_pairs={{0,8},{1,9},{2,10},{3,11},{4,12},{5,13},{6,14},{7,15},{8,16},{9,17... | collective-permute-start | bytes 1216520 | tf_op jit(solution)/shard_map/ppermute | solution.py:38
  963.9 37.6 %collective-permute-start.143 = (bf16[128,1536]{1,0:T(8,128)(2,1)}, bf16[128,1536]{1,0:T(8,128)(2,1)S(1)}, u32[]{:S(2)}, u32[]{:S(2)}) collective-permute-start(bf16[128,1536]{1,0:T(8,128)(2,1)} %add_convert_fusion.7), channel_id=1, source_target_pairs={{0,1},{1,0},{2,3},{3,2},{4,5},{5,4},{6,7},{7,6},{8,9},{9,8},{10,11... | collective-permute-start | bytes 1179656 | tf_op jit(solution)/shard_map/ppermute | solution.py:38
  1002.1 57.1 %collective-permute-start.152 = (bf16[3,5,192,128]{3,2,1,0:T(8,128)(2,1)S(1)}, bf16[3,5,192,128]{3,2,1,0:T(8,128)(2,1)S(1)}, u32[]{:S(2)}, u32[]{:S(2)}) collective-permute-start(bf16[3,5,192,128]{3,2,1,0:T(8,128)(2,1)S(1)} %copy-done.204), channel_id=1, source_target_pairs={{0,24},{1,25},{2,26},{3,27},{4,28},{5,29},{6,30},{7,31},{8,0},{9,1... | collective-permute-start | bytes 2211848 | tf_op jit(solution)/shard_map/ppermute | solution.py:38
  1004.5 55.9 %collective-permute-start.151 = (bf16[3,5,192,128]{3,2,1,0:T(8,128)(2,1)S(1)}, bf16[3,5,192,128]{3,2,1,0:T(8,128)(2,1)S(1)}, u32[]{:S(2)}, u32[]{:S(2)}) collective-permute-start(bf16[3,5,192,128]{3,2,1,0:T(8,128)(2,1)S(1)} %copy-done.203), channel_id=1, source_target_pairs={{0,8},{1,9},{2,10},{3,11},{4,12},{5,13},{6,14},{7,15},{8,16},{9,17... | collective-permute-start | bytes 2211848 | tf_op jit(solution)/shard_map/ppermute | solution.py:38
  1020.3 40.1 %collective-permute-start.149 = (bf16[288,2176]{1,0:T(8,128)(2,1)S(1)}, bf16[288,2176]{1,0:T(8,128)(2,1)S(1)}, u32[]{:S(2)}, u32[]{:S(2)}) collective-permute-start(bf16[288,2176]{1,0:T(8,128)(2,1)S(1)} %get-tuple-element.899), channel_id=1, source_target_pairs={{0,1},{1,0},{2,3},{3,2},{4,5},{5,4},{6,7},{7,6},{8,9},{9,8},{10,11... | collective-permute-start | bytes 3760136 | tf_op jit(solution)/shard_map/ppermute | solution.py:38
  1021.5 38.9 %collective-permute-start.150 = (bf16[288,2048]{1,0:T(8,128)(2,1)S(1)}, bf16[288,2048]{1,0:T(8,128)(2,1)S(1)}, u32[]{:S(2)}, u32[]{:S(2)}) collective-permute-start(bf16[288,2048]{1,0:T(8,128)(2,1)S(1)} %get-tuple-element.900), channel_id=1, source_target_pairs={{0,2},{1,3},{2,0},{3,1},{4,6},{5,7},{6,4},{7,5},{8,10},{9,11},{10,... | collective-permute-start | bytes 3538952 | tf_op jit(solution)/shard_map/ppermute | solution.py:38
  1022.5 35.1 %collective-permute-start.155 = (bf16[96,2048]{1,0:T(8,128)(2,1)S(1)}, bf16[96,2048]{1,0:T(8,128)(2,1)S(1)}, u32[]{:S(2)}, u32[]{:S(2)}) collective-permute-start(bf16[96,2048]{1,0:T(8,128)(2,1)S(1)} %get-tuple-element.924), channel_id=1, source_target_pairs={{0,2},{1,3},{2,0},{3,1},{4,6},{5,7},{6,4},{7,5},{8,10},{9,11},{10,... | collective-permute-start | bytes 1179656 | tf_op jit(solution)/shard_map/ppermute | solution.py:38
  1059.2 77.9 %collective-permute-start.156 = (bf16[48,2048]{1,0:T(8,128)(2,1)}, bf16[48,2048]{1,0:T(8,128)(2,1)}, u32[]{:S(2)}, u32[]{:S(2)}) collective-permute-start(bf16[48,2048]{1,0:T(8,128)(2,1)} %add_convert_fusion.23), channel_id=1, source_target_pairs={{0,1},{1,0},{2,3},{3,2},{4,5},{5,4},{6,7},{7,6},{8,9},{9,8},{10,11... | collective-permute-start | bytes 589832 | tf_op jit(solution)/shard_map/ppermute | solution.py:38
  1071.0 66.1 %collective-permute-start.158 = (bf16[48,2176]{1,0:T(8,128)(2,1)}, bf16[48,2176]{1,0:T(8,128)(2,1)}, u32[]{:S(2)}, u32[]{:S(2)}) collective-permute-start(bf16[48,2176]{1,0:T(8,128)(2,1)} %add_convert_fusion.22), channel_id=1, source_target_pairs={{0,2},{1,3},{2,0},{3,1},{4,6},{5,7},{6,4},{7,5},{8,10},{9,11},{10,... | collective-permute-start | bytes 626696 | tf_op jit(solution)/shard_map/ppermute | solution.py:38
  1073.8 40.3 %collective-permute-start.164 = (bf16[3,5,192,128]{3,2,1,0:T(8,128)(2,1)}, bf16[3,5,192,128]{3,2,1,0:T(8,128)(2,1)S(1)}, u32[]{:S(2)}, u32[]{:S(2)}) collective-permute-start(bf16[3,5,192,128]{3,2,1,0:T(8,128)(2,1)} %get-tuple-element.934), channel_id=1, source_target_pairs={{0,16},{1,17},{2,18},{3,19},{4,20},{5,21},{6,22},{7,23},{8,24},{9,... | collective-permute-start | bytes 2211848 | tf_op jit(solution)/shard_map/ppermute | solution.py:38
  1089.8 47.4 %collective-permute-start.161 = (bf16[48,4224]{1,0:T(8,128)(2,1)S(1)}, bf16[48,4224]{1,0:T(8,128)(2,1)S(1)}, u32[]{:S(2)}, u32[]{:S(2)}) collective-permute-start(bf16[48,4224]{1,0:T(8,128)(2,1)S(1)} %get-tuple-element.957), channel_id=1, source_target_pairs={{0,24},{1,25},{2,26},{3,27},{4,28},{5,29},{6,30},{7,31},{8,0},{9,1... | collective-permute-start | bytes 1216520 | tf_op jit(solution)/shard_map/ppermute | solution.py:38
  1112.3 36.2 %collective-permute-start.162 = (bf16[48,4224]{1,0:T(8,128)(2,1)S(1)}, bf16[48,4224]{1,0:T(8,128)(2,1)S(1)}, u32[]{:S(2)}, u32[]{:S(2)}) collective-permute-start(bf16[48,4224]{1,0:T(8,128)(2,1)S(1)} %get-tuple-element.959), channel_id=1, source_target_pairs={{0,16},{1,17},{2,18},{3,19},{4,20},{5,21},{6,22},{7,23},{8,24},{9,... | collective-permute-start | bytes 1216520 | tf_op jit(solution)/shard_map/ppermute | solution.py:38
  1114.1 34.3 %collective-permute-start.163 = (bf16[48,4224]{1,0:T(8,128)(2,1)S(1)}, bf16[48,4224]{1,0:T(8,128)(2,1)S(1)}, u32[]{:S(2)}, u32[]{:S(2)}) collective-permute-start(bf16[48,4224]{1,0:T(8,128)(2,1)S(1)} %get-tuple-element.958), channel_id=1, source_target_pairs={{0,8},{1,9},{2,10},{3,11},{4,12},{5,13},{6,14},{7,15},{8,16},{9,17... | collective-permute-start | bytes 1216520 | tf_op jit(solution)/shard_map/ppermute | solution.py:38
  (329 other events, 7059.9 us)

commit v5 on v4

--- a/solution.py
+++ b/solution.py
@@ -473,7 +473,6 @@
 LANES = 128
 EXTRA = 128
 HALF = 64
-TILE = 256
 MIB = 1 << 20
 COST_PART = 16
 
@@ -897,42 +896,97 @@
         at += rows
 
 
+class Pool:
+    def __init__(self, semaphores, used=0):
+        self.semaphores = semaphores
+        self.used = used
+
+    def copy(self, source, target):
+        self.used += 1
+        return pltpu.make_async_copy(source, target, self.semaphores.at[self.used - 1])
+
+
+def rows_at(ref, first, count):
+    return ref.at[pl.ds(first, count), :]
+
+
+def tile_loads(pool, pieces, x):
+    n = pieces[0].shape[0]
+    found = [[pool.copy(pieces[m], rows_at(x, m * n, n))] for m in range(3)]
+    half = n // 2
+    last = [pool.copy(pieces[3 + i], rows_at(x, 3 * n + i * half, half)) for i in range(2)]
+    return found + [last]
+
+
+def tile_slices(pool, source, target, n):
+    return [[pool.copy(rows_at(source, m * n, n), rows_at(target, m * n, n))] for m in range(4)]
+
+
+def tile_parts(pool, y, parts):
+    n = parts[0].shape[0]
+    half = n // 2
+    own, one_head, two_tail, to_one, to_two = parts
+
+    def copy(first, count, part, at=0):
+        return pool.copy(rows_at(y, first, count), rows_at(part, at, count))
+
+    return [
+        [copy(0, n, own)],
+        [copy(n, half, one_head), copy(n + half, half, to_one)],
+        [copy(2 * n, half, to_two), copy(2 * n + half, half, two_tail)],
+        [copy(3 * n, half, to_two, half), copy(3 * n + half, half, to_one, half)],
+    ]
+
+
+def for_tile(i, groups, act):
+    for m in range(4):
+
+        @pl.when(i == m)
+        def _():
+            for group in groups:
+                for copy in group[m]:
+                    act(copy)
+
+
+def finish(groups):
+    for group in groups:
+        for copies in group:
+            for copy in copies:
+                copy.wait()
+
+
 def part_rows(n):
     return [n, n // 2, n // 2, n, n]
-
-
-def start_parts(copies, y, parts):
-    n = parts[0].shape[0]
-    half = n // 2
-
-    def start(first, count, part, at=0):
-        copies.start(y.at[pl.ds(first, count), :], part.at[pl.ds(at, count), :])
-
-    own, one_head, two_tail, to_one, to_two = parts
-    start(0, n, own)
-    start(n, half, one_head)
-    start(2 * n + half, half, two_tail)
-    start(n + half, half, to_one)
-    start(3 * n + half, half, to_one, half)
-    start(2 * n, half, to_two)
-    start(3 * n, half, to_two, half)
 
 
 def experts_forward_kernel(where, gates, *refs):
     pieces, weights, refs = refs[:5], refs[5 : 5 + WEIGHT_PIECES], refs[5 + WEIGHT_PIECES :]
     parts, x_out, g_out, u_out = refs[:5], *refs[5:8]
     x, y, g, u, w_gate, w_up, w_down, semaphores = refs[8:]
-    copies = Copies(semaphores)
-    start_rows(copies, pieces, x)
+    n = pieces[0].shape[0]
+    pool = Pool(semaphores)
+    loads = tile_loads(pool, pieces, x)
+    for group in loads:
+        for copy in group:
+            copy.start()
+    copies = Copies(semaphores, pool.used)
     load_experts(copies, where, weights, (w_gate, w_up, w_down))
+    pool.used = copies.used
+    kept = tile_slices(pool, x, x_out, n)
+    stores = [
+        tile_parts(pool, y, parts),
+        tile_slices(pool, g, g_out, n),
+        tile_slices(pool, u, u_out, n),
+    ]
     share = weights[0].shape[3]
     width = w_gate.shape[1]
     copies.wait()
-    copies.start(x, x_out)
-
-    @pl.loop(0, x.shape[0] // TILE)
+
+    @pl.loop(0, 4)
     def _(i):
-        row = pl.ds(pl.multiple_of(i * TILE, TILE), TILE)
+        for_tile(i, [loads], lambda copy: copy.wait())
+        for_tile(i, [kept], lambda copy: copy.start())
+        row = pl.ds(pl.multiple_of(i * n, n), n)
         gate_pre = contract(x[row, :], w_gate[...], PLAIN)
         up_pre = contract(x[row, :], w_up[...], PLAIN)
         g[row, :] = gate_pre
@@ -940,11 +994,9 @@
         wide = widen_tile(gates[row, :], share, width)
         weighed = (gate_pre * jax.nn.sigmoid(gate_pre) * up_pre * wide).astype(jnp.bfloat16)
         y[row, :] = contract(weighed, w_down[...], ACROSS).astype(jnp.bfloat16)
-
-    start_parts(copies, y, parts)
-    copies.start(g, g_out)
-    copies.start(u, u_out)
-    copies.wait()
+        for_tile(i, stores, lambda copy: copy.start())
+
+    finish([kept, *stores])
 
 
 def experts_forward_fast(where, gates, pieces, weights, after=()):
@@ -972,7 +1024,7 @@
             pltpu.VMEM((rows, width), f32),
         ]
         + [pltpu.VMEM((model, width), bf)] * 3
-        + [pltpu.SemaphoreType.DMA((5 + 24 * experts + 20,))],
+        + [pltpu.SemaphoreType.DMA((24 * experts + 48,))],
         compiler_params=pltpu.CompilerParams(vmem_limit_bytes=48 * MIB),
         cost_estimate=cost(6 * rows * model * width),
     )(where, gates, *pieces, *weights, *after)
@@ -983,19 +1035,39 @@
     weights, refs = refs[7 : 7 + WEIGHT_PIECES], refs[7 + WEIGHT_PIECES :]
     parts, r_out, gg_out, gu_out, p_out = refs[:5], *refs[5:9]
     x, y, g, u, gg, gu, p, w_gate, w_up, w_down, semaphores = refs[9:]
-    copies = Copies(semaphores)
-    start_rows(copies, pieces, x)
+    n = pieces[0].shape[0]
+    pool = Pool(semaphores)
+    loads = [
+        tile_loads(pool, pieces, x),
+        tile_slices(pool, g_in, g, n),
+        tile_slices(pool, u_in, u, n),
+    ]
+    for group in loads[0]:
+        for copy in group:
+            copy.start()
+    copies = Copies(semaphores, pool.used)
     load_experts(copies, where, weights, (w_gate, w_up, w_down))
-    copies.start(g_in, g)
-    copies.start(u_in, u)
+    for loaded in loads[1:]:
+        for group in loaded:
+            for copy in group:
+                copy.start()
+    pool.used = copies.used
+    kept = tile_slices(pool, x, r_out, n)
+    stores = [
+        tile_parts(pool, y, parts),
+        tile_slices(pool, gg, gg_out, n),
+        tile_slices(pool, gu, gu_out, n),
+        tile_slices(pool, p, p_out, n),
+    ]
     share = weights[0].shape[3]
     width = w_gate.shape[1]
     copies.wait()
-    copies.start(x, r_out)
-
-    @pl.loop(0, x.shape[0] // TILE)
+
+    @pl.loop(0, 4)
     def _(i):
-        row = pl.ds(pl.multiple_of(i * TILE, TILE), TILE)
+        for_tile(i, loads, lambda copy: copy.wait())
+        for_tile(i, [kept], lambda copy: copy.start())
+        row = pl.ds(pl.multiple_of(i * n, n), n)
         wide = widen_tile(gates[row, :], share, width)
         hidden_grad = contract(x[row, :], w_down[...], PLAIN) * wide
         gate_pre, up_pre = g[row, :], u[row, :]
@@ -1008,12 +1080,9 @@
         back = contract(gg[row, :], w_gate[...], ACROSS)
         back = back + contract(gu[row, :], w_up[...], ACROSS)
         y[row, :] = back.astype(jnp.bfloat16)
-
-    start_parts(copies, y, parts)
-    copies.start(gg, gg_out)
-    copies.start(gu, gu_out)
-    copies.start(p, p_out)
-    copies.wait()
+        for_tile(i, stores, lambda copy: copy.start())
+
+    finish([kept, *stores])
 
 
 def experts_backward_fast(where, gates, pieces, stash, weights, after=()):
@@ -1044,7 +1113,7 @@
             pltpu.VMEM((rows, width), bf),
         ]
         + [pltpu.VMEM((model, width), bf)] * 3
-        + [pltpu.SemaphoreType.DMA((5 + 24 * experts + 20,))],
+        + [pltpu.SemaphoreType.DMA((24 * experts + 48,))],
         compiler_params=pltpu.CompilerParams(vmem_limit_bytes=52 * MIB),
         cost_estimate=cost(6 * rows * model * width),
     )(where, gates, *pieces, *stash, *weights, *after)
@@ -1407,18 +1476,17 @@
     found = [found] + up_hops(place, found)
     line = jnp.concatenate([packs[0]] + tie(up_hops(place, packs[0]), *[cut[0] for cut in cuts], found[0]))
     first = spread_first(place, line)
-    gate_rows = gate_rows_of(found)
     cuts[0] = tie(cuts[0], line)
     own_swaps = [place.hop(tie(cut[0], line), swap=1) for cut in cuts]
-    two = place.hop(cuts[0][2], up=2)
+    one = place.hop(cuts[0][1], up=1)
     swapped = [place.hop(line, swap=1)]
-    events = (gate_rows[0][0], gate_rows[-1][0], swapped[0], *own_swaps)
-    first = tie(first, two, *events)
-    one = place.hop(tie(cuts[0][1], first[0]), up=1)
+    two = place.hop(tie(cuts[0][2], line), up=2)
+    first = tie(first, one, two, swapped[0], *own_swaps)
+    three = place.hop(tie(cuts[0][3], first[0]), up=3)
     swapped += [place.hop(piece, swap=1) for piece in first[1:]]
-    last_two = tie(spread_last(place, first, axis=1, cut=cut)[3:], one, *swapped[1:])
+    last_two = tie(spread_last(place, first, axis=1, cut=cut)[3:], three, *swapped[1:])
     matrices = [[*first, *last_two, *swapped, *[place.hop(p, swap=1) for p in last_two]]]
-    shares = [cuts[0][0], one, two, place.hop(tie(cuts[0][3], last_two[0]), up=3)]
+    shares = [cuts[0][0], one, two, three]
     share_swaps = [own_swaps[0], place.hop(one, swap=1), place.hop(two, swap=1)]
 
     def run_forward(l, which, pieces, bank, after=()):
@@ -1436,11 +1504,12 @@
     stored = []
     for l in range(layer_count):
         more = l + 1 < layer_count
-        after = [rows for pair in gate_rows for rows in pair] if l == 0 else []
-        after += share_swaps
+        after = list(share_swaps)
         outs = attend_forward_fast(where, base, extra, tables, matrices[l], in_width, after=after)
         h, m, nf = outs[:3]
-        nf, late = tie((nf, shares[4 - len(shares) + len(share_swaps) :]))
+        nf, late, found = tie((nf, shares[len(share_swaps) :], found))
+        if l == 0:
+            gate_rows = gate_rows_of(found)
         share_swaps += [place.hop(piece, swap=1) for piece in late]
         bank_l = [*shares[: 4 - len(late)], *late, *share_swaps]
         near, far = pairs_of(nf)
@@ -1451,7 +1520,7 @@
         y_near, far, line[0], line[2] = tie((y_near, far, line[0], line[2]))
         far = spread_last(place, far)
         if more:
-            near_first = fold_first(place, tie(y_near[:5], far[3]))
+            near_first = fold_first(place, tie(y_near[:5], far[3], far[4]))
             y_far = run_forward(l, 1, far, bank_l, after=(y_near[0],))
             y_far, near_first, line[1] = tie((y_far, near_first, line[1]))
             one = place.hop(tie(cuts[l + 1][1], line[1]), up=1)
@@ -1468,9 +1537,9 @@
             blocks = sum_blocks(far_ends, (0, 1))
             arrived += down_hops(place, blocks, 2)
             passing = tie(passing, *arrived)
-            two = place.hop(tie(cuts[l + 1][2], arrived[0], arrived[1], arrived[2]), up=2)
+            two = place.hop(tie(cuts[l + 1][2], *arrived), up=2)
             swapped = [line_swap] + [place.hop(piece, swap=1) for piece in passing[1:]]
-            last_two = tie(spread_last(place, passing, 1, cut)[3:], *swapped[1:])
+            last_two, two = tie((spread_last(place, passing, 1, cut)[3:], two), *swapped[1:])
             share_swaps = [own_swaps[l + 1], one_swap]
             ends = [place.hop(p, swap=1) for p in last_two]
             matrices.append([*passing, *last_two, *swapped, *ends])
@@ -1504,62 +1573,71 @@
             b_far, near_first = tie((b_far, near_first))
             far_first = fold_first(place, b_far[:5])
         else:
-            near, far = pairs_of(low)
-            near = spread_last(place, near)
-            far = spread_first(place, jnp.concatenate(tie(far, near[3], near[4])))
-            b_near = run_backward(l, 0, near, kept_near[6:], bank_l)
-            b_near, far = tie((b_near, far))
+            ups = up_hops(place, low)
+            held = merge_grads(*held_parts)
+            result_ends = fold_end(place, fold_sums(result_first))
+            ups[0], held = tie((ups[0], held), *result_ends[1:3])
+            near = jnp.concatenate([low, ups[0]])
+            other_sum = place.hop(tie(other_one, near), swap=1)
+            near = spread_last(place, spread_first(place, near))
+            far = spread_first(place, jnp.concatenate(tie(ups[1:], near[3], near[4])))
+            result_blocks = sum_blocks(result_ends, (0, 1))
+            result_arrived = down_hops(place, tie(result_blocks, far[0]), 2)
+            b_near = run_backward(l, 0, near, kept_near[6:], bank_l, (held[0],))
+            b_near, far, result_arrived = tie((b_near, far, result_arrived))
+            merged = merge_cores(mine_one, tie(other_sum, b_near[0]), cut)
             far = spread_last(place, far)
-            result_blocks = sum_blocks(tie(result_ends, b_near[0]), (0, 1))
-            result_arrived = down_hops(place, result_blocks, 2)
-            other_sum = place.hop(tie(other_one, b_near[0]), swap=1)
-            merged = merge_cores(mine_one, other_sum, cut)
-            held, merged = tie((held, merged), far[3], far[4])
-            came = [place.hop(tie(held[1], result_blocks[0]), up=1), came[0]]
-            merged_first = fold_first(place, merged)
+            came = [place.hop(tie(held[2], b_near[0]), up=2)]
+            merged_first = fold_first(place, tie(merged, far[3], far[4]))
             b_far = run_backward(l, 1, far, kept_far[6:], bank_l, (b_near[0],))
             b_far, merged_first, came[0] = tie((b_far, merged_first, came[0]))
             far_first = fold_first(place, b_far[:5])
-            near_first = fold_first(place, tie(b_near[:5], b_far[0]))
-            came.append(place.hop(tie(held[3], came[0]), up=3))
+            came.insert(0, place.hop(tie(held[1], b_far[0]), up=1))
+            came.append(place.hop(tie(held[3], b_far[0]), up=3))
 
         def weight_grads(i, after, near=(kept_near, b_near), far=(kept_far, b_far)):
             pick = lambda kept, found: ((kept[5], found[6 + i]) if i < 2 else (found[5], found[8]))
             return weight_grads_fast(where, pick(*near), pick(*far), experts, after=after)
 
         grads = [weight_grads(0, (b_far[0],))]
-        far_state = fold_sums(tie(far_first, grads[0][0]))
-        near_ends = fold_end(place, fold_sums(near_first))
-        grads.append(weight_grads(1, (far_state[1], far_state[2])))
-        swapped = [place.hop(grads[0][1], swap=1)]
+        if not top:
+            grads.append(weight_grads(1, (grads[0][0], came[0])))
+        far_state = fold_sums(tie(far_first, grads[-1][0]))
+        if not top:
+            near_first = fold_first(place, tie(b_near[:5], far_state[1], far_state[2]))
+        grads.append(weight_grads(len(grads), (far_state[1], far_state[2])))
+        swapped = [place.hop(other, swap=1) for _, other in grads[:-1]]
         far_ends = fold_end(place, far_state)
-        far_ends, swapped = tie((far_ends, swapped), grads[1][0], *near_ends[1:3])
-        swapped.append(place.hop(grads[1][1], swap=1))
+        far_ends, swapped = tie((far_ends, swapped), grads[-1][0])
+        swapped.append(place.hop(grads[-1][1], swap=1))
         if not top:
-            far_ends, came, result_arrived = tie((far_ends, came, result_arrived))
+            far_ends, came = tie((far_ends, came))
+        event = far_state if top else far_ends
+        near_state = fold_sums(tie(near_first, event[1], event[2]))
+        near_ends = fold_end(place, near_state)
         arrived = down_hops(place, sum_blocks(near_ends, (1,)))
         blocks = sum_blocks(far_ends, (0, 1))
         arrived += down_hops(place, blocks, 2)
-        grads.append(weight_grads(2, (blocks[0],)))
-        arrived, swapped = tie((arrived, swapped), grads[2][0])
-        swapped.append(place.hop(tie(grads[2][1], *arrived), swap=1))
-        total = merge_grads([mine for mine, _ in grads], swapped)
         if top:
-            held = total
-            came = [place.hop(held[2], up=2)]
-            result_state = fold_start(place, tie(kept_far[:5], blocks[0]))
-            result_ends = fold_end(place, tie(result_state, *arrived))
-            result_first = fold_first(place, tie(kept_near[:5], *arrived))
+            grads.append(weight_grads(2, (blocks[0],)))
+            arrived, swapped = tie((arrived, swapped), grads[2][0])
+            swapped.append(place.hop(tie(grads[2][1], *arrived), swap=1))
+        if top:
+            result_first = fold_first(place, tie(kept_far[:5], *arrived))
+            result_near_first = fold_first(place, tie(kept_near[:5], *arrived))
             after = ()
             groups = ((0, 4),)
         else:
             held_came = [held[0], *came]
-            merged_ends = fold_end(place, fold_sums(tie(merged_first, blocks[0])))
+            total = merge_grads([mine for mine, _ in grads], swapped)
+            merged_ends = fold_end(place, fold_sums(tie(merged_first, blocks[0], *near_ends[1:3])))
             one_total = add_pieces(*merged_ends, axis=1)
             shard = mine_one.shape[0] // 16
-            low_total = tie(one_total[shard:].astype(jnp.bfloat16), *arrived)
+            low_total = one_total[shard:].astype(jnp.bfloat16)
+            arrived = tie(arrived, total[0], low_total)
+            low_total = tie(low_total, *arrived)
             one_arrived = down_hops(place, [low_total[n * shard :][:shard] for n in range(3)])
-            result_near = fold_end(place, fold_sums(tie(result_first, *arrived)))
+            result_near = fold_end(place, fold_sums(tie(result_near_first, *arrived)))
             after = (low_total, total[0])
             groups = ((1, 3), (0, 1))
         upstream, low, *partial = attend_backward_fast(
@@ -1575,7 +1653,8 @@
             after=after,
         )
         if top:
-            low, result_ends, result_first, came = tie((low, result_ends, result_first, came))
+            low, result_first, result_near_first = tie((low, result_first, result_near_first))
+            held_parts = ([mine for mine, _ in grads], swapped)
             other_one, mine_one = partial
         else:
             partial, result_near = tie((partial, result_near))
@@ -1586,16 +1665,17 @@
     other_far, other_near, mine_far, mine_near = partial
     other_far, other_near = place.hop(other_far, swap=1), place.hop(other_near, swap=1)
     merged_far = merge_cores(mine_far, other_far, cut)
+    came = [place.hop(tie(total[k], upstream), up=k) for k in (1, 2, 3)]
+    merged_far, came[0] = tie((merged_far, came[0]))
     merged_near = merge_cores(mine_near, other_near, cut)
-    came = [place.hop(tie(total[k], upstream), up=k) for k in (1, 3)]
     far_first = fold_first(place, merged_far)
-    near_first = fold_first(place, tie(merged_near, merged_far[0]))
-    far_state, near_state = fold_sums(tie(far_first, *came)), fold_sums(near_first)
-    came.insert(1, place.hop(tie(total[2], far_state[1]), up=2))
-    far_ends, near_ends = fold_end(place, far_state), fold_end(place, near_state)
+    joined = join_experts(where, tie(held_came, merged_far[0]), 1, layer_count, None)
+    far_state = fold_sums(tie(far_first, joined[0]))
+    near_first = fold_first(place, tie(merged_near, far_state[1], far_state[2]))
+    near_ends = fold_end(place, fold_sums(near_first))
+    far_ends = tie(fold_end(place, far_state), *came)
     far_total = add_pieces(*far_ends, axis=1)
     sums[0] = sum_down(place, far_total, add_pieces(*near_ends, axis=1))
-    joined = join_experts(where, tie(held_came, far_state[1]), 1, layer_count, None)
     joined = join_experts(where, [total[0], *came], 0, layer_count, joined)
     last_block = down_hops(place, sum_blocks(tie(result_near, far_state[1]), (1,)))
     result = total_of(stored[-1][1][1], received(result_near, last_block + result_arrived))

time: 1160 us -> 1080 us (0.931)
  starting transfers between devices: 204 us -> 163 us
  waiting for transfers between devices: 494 us -> 455 us
    ppermute x165, starting transfers between devices: 204 us -> 163 us  [hop(): return lax.ppermute(value, AXES, pairs)]
    ppermute x165, waiting for transfers between devices: 494 us -> 455 us  [hop(): return lax.ppermute(value, AXES, pairs)]
    unnamed x434 -> x454, local copies, waits for them, and re-layouts: 56.3 us -> 51.1 us
  transfers between devices with their start and end apart: 165 -> 165, of which waited for: 62 -> 66; matrix products, arithmetic and copies ran while one was open for 4% -> 5% of each run, Pallas kernels for 30% -> 31%
where the time goes in v5:
time: 1080 us; the launch traced here: 1070 us
  waiting for transfers between devices  455 us (42%)
  Pallas kernels  337 us (31%)
  starting transfers between devices  163 us (15%)
  local copies, waits for them, and re-layouts  79.6 us (7%)
  other arithmetic  32 us (3%)
    ppermute x165, waiting for transfers between devices, hop(): return lax.ppermute(value, AXES, pairs)  455 us
    ppermute x165, starting transfers between devices, hop(): return lax.ppermute(value, AXES, pairs)  163 us
    pallas_call x4, Pallas kernels, experts_backward_fast(): pl.pallas_call(body, name='experts_backward', out_shape=shapes, in_specs=...  69.9 us
    pallas_call x2, Pallas kernels, attend_backward_fast(): pl.pallas_call(body, name='attend_backward', out_shape=shapes, in_specs=[...  61 us
    pallas_call x4, Pallas kernels, experts_forward_fast(): pl.pallas_call(body, name='experts_forward', out_shape=shapes, in_specs=[...  58.7 us
    unnamed x454, local copies, waits for them, and re-layouts  51.1 us
    pallas_call x6, Pallas kernels, weight_grads_fast(): pl.pallas_call(body, name='weight_grads', out_shape=[shape_of(4, experts,...  47.2 us
    pallas_call x2, Pallas kernels, attend_forward_fast(): pl.pallas_call(body, name='attend_forward', out_shape=shapes, in_specs=[s...  32.2 us
  transfers between devices with their start and end apart: 165, of which 66 were waited for; matrix products, arithmetic and copies ran while one was open for 5% of the time, Pallas kernels for 31%

profile of v5, /device:TPU:0, one launch (start us, length us, event | category | flops | bytes accessed | tf_op | source)
XLA Modules:
  0.0 1071.3 jit_solution(12443632176577528741)
XLA Ops:
  30.2 6.9 collective-permute-done.1
  40.4 8.3 collective-permute-start.9
  51.8 45.8 %collective-permute-done.9.refs_9_.refs_11_ = bf16[3,5,192,128]{3,2,1,0:T(8,128)(2,1)S(1)} collective-permute-done((bf16[3,5,192,128]{3,2,1,0:T(8,128)(2,1)}, bf16[3,5,192,128]{3,2,1,0:T(8,128)(2,1)S(1)}, u32[]{:S(2)}, u32[]{:S(2)}) %collective-permute-start.9) | collective-permute-done | bytes 737312 | tf_op jit(solution)/shard_map/ppermute | solution.py:38
  102.0 17.9 %collective-permute-done.15.refs_10_.refs_12_ = bf16[3,5,192,128]{3,2,1,0:T(8,128)(2,1)} collective-permute-done((bf16[3,5,192,128]{3,2,1,0:T(8,128)(2,1)S(1)}, bf16[3,5,192,128]{3,2,1,0:T(8,128)(2,1)}, u32[]{:S(2)}, u32[]{:S(2)}) %collective-permute-start.15) | collective-permute-done | bytes 737312 | tf_op jit(solution)/shard_map/ppermute | solution.py:38
  126.6 15.4 %attend_forward.2 = (f32[128,1536]{1,0:T(8,128)S(1)}, f32[128,1536]{1,0:T(8,128)S(1)}, bf16[128,1536]{1,0:T(8,128)(2,1)S(1)}, bf16[128,1536]{1,0:T(8,128)(2,1)S(...) custom-call(s32[3]{0:T(128)S(1)} %copy-done.124, ...), custom_call_target="tpu_custom_call" | custom-call | flops 103809024 | tf_op jit(solution)/shard_map/attend_forward/pallas_call | solution.py:683
  143.6 11.8 %collective-permute-done.25 = bf16[128,1536]{1,0:T(8,128)(2,1)S(1)} collective-permute-done((bf16[128,1536]{1,0:T(8,128)(2,1)S(1)}, bf16[128,1536]{1,0:T(8,128)(2,1)S(1)}, u32[]{:S(2)}, u32[]{:S(2)}) %collective-permute-start.25) | collective-permute-done | bytes 393248 | tf_op jit(solution)/shard_map/ppermute | solution.py:38
  158.9 14.6 %collective-permute-done.26.refs_3_ = bf16[256,1536]{1,0:T(8,128)(2,1)S(1)} collective-permute-done((bf16[256,1536]{1,0:T(8,128)(2,1)S(1)}, bf16[256,1536]{1,0:T(8,128)(2,1)S(1)}, u32[]{:S(2)}, u32[]{:S(2)}) %collective-permute-start.26) | collective-permute-done | bytes 786464 | tf_op jit(solution)/shard_map/ppermute | solution.py:38
  176.6 6.8 collective-permute-done.28.refs_5_
  198.0 14.7 %experts_forward.4 = (bf16[256,1536]{1,0:T(8,128)(2,1)}, bf16[128,1536]{1,0:T(8,128)(2,1)S(1)}, bf16[128,1536]{1,0:T(8,128)(2,1)S(1)}, bf16[256,1536]{1,0:T(8,12...) custom-call(s32[3]{0:T(128)S(1)} %copy-done.124, ...), custom_call_target="tpu_custom_call" | custom-call | flops 377487360 | tf_op jit(solution)/shard_map/experts_forward/pallas_call | solution.py:1014
  216.7 8.3 collective-permute-done.37.refs_5_
  236.3 14.7 %experts_forward.5 = (bf16[256,1536]{1,0:T(8,128)(2,1)}, bf16[128,1536]{1,0:T(8,128)(2,1)S(1)}, bf16[128,1536]{1,0:T(8,128)(2,1)S(1)}, bf16[256,1536]{1,0:T(8,12...) custom-call(s32[3]{0:T(128)S(1)} %copy-done.124, ...), custom_call_target="tpu_custom_call" | custom-call | flops 377487360 | tf_op jit(solution)/shard_map/experts_forward/pallas_call | solution.py:1014
  259.0 10.5 collective-permute-done.47.refs_8_.refs_10_
  305.1 24.2 %collective-permute-done.51.refs_4_ = bf16[128,1536]{1,0:T(8,128)(2,1)S(1)} collective-permute-done((bf16[128,1536]{1,0:T(8,128)(2,1)}, bf16[128,1536]{1,0:T(8,128)(2,1)S(1)}, u32[]{:S(2)}, u32[]{:S(2)}) %collective-permute-start.51) | collective-permute-done | bytes 393248 | tf_op jit(solution)/shard_map/ppermute | solution.py:38
  336.6 28.5 %collective-permute-done.57.refs_9_.refs_11_ = bf16[3,5,192,128]{3,2,1,0:T(8,128)(2,1)S(1)} collective-permute-done((bf16[3,5,192,128]{3,2,1,0:T(8,128)(2,1)}, bf16[3,5,192,128]{3,2,1,0:T(8,128)(2,1)S(1)}, u32[]{:S(2)}, u32[]{:S(2)}) %collective-permute-start.57) | collective-permute-done | bytes 737312 | tf_op jit(solution)/shard_map/ppermute | solution.py:38
  372.1 16.7 %attend_forward.3 = (f32[128,1536]{1,0:T(8,128)S(1)}, f32[128,1536]{1,0:T(8,128)S(1)}, bf16[128,1536]{1,0:T(8,128)(2,1)S(1)}, bf16[128,1536]{1,0:T(8,128)(2,1)S(...) custom-call(s32[3]{0:T(128)S(1)} %copy-done.124, ...), custom_call_target="tpu_custom_call" | custom-call | flops 103809024 | tf_op jit(solution)/shard_map/attend_forward/pallas_call | solution.py:683
  389.0 12.9 %collective-permute-done.64 = bf16[128,1536]{1,0:T(8,128)(2,1)S(1)} collective-permute-done((bf16[128,1536]{1,0:T(8,128)(2,1)S(1)}, bf16[128,1536]{1,0:T(8,128)(2,1)S(1)}, u32[]{:S(2)}, u32[]{:S(2)}) %collective-permute-start.64) | collective-permute-done | bytes 393248 | tf_op jit(solution)/shard_map/ppermute | solution.py:38
  404.9 15.9 %collective-permute-done.65.refs_3_ = bf16[256,1536]{1,0:T(8,128)(2,1)S(1)} collective-permute-done((bf16[256,1536]{1,0:T(8,128)(2,1)S(1)}, bf16[256,1536]{1,0:T(8,128)(2,1)S(1)}, u32[]{:S(2)}, u32[]{:S(2)}) %collective-permute-start.65) | collective-permute-done | bytes 786464 | tf_op jit(solution)/shard_map/ppermute | solution.py:38
  424.7 6.5 collective-permute-done.67.refs_5_
  444.3 14.7 %experts_forward.6 = (bf16[256,1536]{1,0:T(8,128)(2,1)}, bf16[128,1536]{1,0:T(8,128)(2,1)S(1)}, bf16[128,1536]{1,0:T(8,128)(2,1)S(1)}, bf16[256,1536]{1,0:T(8,12...) custom-call(s32[3]{0:T(128)S(1)} %copy-done.124, ...), custom_call_target="tpu_custom_call" | custom-call | flops 377487360 | tf_op jit(solution)/shard_map/experts_forward/pallas_call | solution.py:1014
  463.5 7.9 collective-permute-done.77.refs_5_
  481.4 14.7 %experts_forward.7 = (bf16[256,1536]{1,0:T(8,128)(2,1)}, bf16[128,1536]{1,0:T(8,128)(2,1)S(1)}, bf16[128,1536]{1,0:T(8,128)(2,1)S(1)}, bf16[256,1536]{1,0:T(8,12...) custom-call(s32[3]{0:T(128)S(1)} %copy-done.124, ...), custom_call_target="tpu_custom_call" | custom-call | flops 377487360 | tf_op jit(solution)/shard_map/experts_forward/pallas_call | solution.py:1014
  501.9 6.4 collective-permute-done.82.refs_5_
  514.2 17.1 %experts_backward.4 = (bf16[256,1536]{1,0:T(8,128)(2,1)}, bf16[128,1536]{1,0:T(8,128)(2,1)S(1)}, bf16[128,1536]{1,0:T(8,128)(2,1)S(1)}, bf16[256,1536]{1,0:T(8,1...) custom-call(s32[3]{0:T(128)S(1)} %copy-done.124, ...), custom_call_target="tpu_custom_call" | custom-call | flops 377487360 | tf_op jit(solution)/shard_map/experts_backward/pallas_call | solution.py:1100
  544.1 17.9 %experts_backward.5 = (bf16[256,1536]{1,0:T(8,128)(2,1)}, bf16[128,1536]{1,0:T(8,128)(2,1)S(1)}, bf16[128,1536]{1,0:T(8,128)(2,1)S(1)}, bf16[256,1536]{1,0:T(8,1...) custom-call(s32[3]{0:T(128)S(1)} %copy-done.124, ...), custom_call_target="tpu_custom_call" | custom-call | flops 377487360 | tf_op jit(solution)/shard_map/experts_backward/pallas_call | solution.py:1100
  566.4 7.6 weight_grads.6
  578.3 8.0 weight_grads.7
  612.0 8.0 weight_grads.8
  635.4 30.6 %attend_backward.2 = (f32[128,1536]{1,0:T(8,128)}, bf16[128,1536]{1,0:T(8,128)(2,1)}, bf16[768,4224]{1,0:T(8,128)(2,1)}, bf16[768,4224]{1,0:T(8,128)(2,1)}) custom-call(s32[3]{0:T(128)} %pad_add_fusion.where.refs_0_, bf16[128,1536]{1,0:T(8,128)(2,1)} %broadcast_in_dim.61.refs_1_, bf16[128,1536]{1,0:T(8,128)(2,1)} %refs_2_.3, ...), custom_call_target="tpu_custom_call" | custom-call | flops 207618048 | tf_op jit(solution)/shard_map/attend_backward/pallas_call | solution.py:844
  689.2 14.4 %collective-permute-done.109.refs_3_ = bf16[256,1536]{1,0:T(8,128)(2,1)S(1)} collective-permute-done((bf16[256,1536]{1,0:T(8,128)(2,1)S(1)}, bf16[256,1536]{1,0:T(8,128)(2,1)S(1)}, u32[]{:S(2)}, u32[]{:S(2)}) %collective-permute-start.109) | collective-permute-done | bytes 786464 | tf_op jit(solution)/shard_map/ppermute | solution.py:38
  706.8 7.6 collective-permute-done.111.refs_5_
  722.9 17.1 %experts_backward.6 = (bf16[256,1536]{1,0:T(8,128)(2,1)}, bf16[128,1536]{1,0:T(8,128)(2,1)S(1)}, bf16[128,1536]{1,0:T(8,128)(2,1)S(1)}, bf16[256,1536]{1,0:T(8,1...) custom-call(s32[3]{0:T(128)S(1)} %copy-done.125, ...), custom_call_target="tpu_custom_call" | custom-call | flops 377487360 | tf_op jit(solution)/shard_map/experts_backward/pallas_call | solution.py:1100
  740.0 7.3 collective-permute-done.117
  750.6 7.3 merge_cores.3
  762.4 17.8 %experts_backward.7 = (bf16[256,1536]{1,0:T(8,128)(2,1)}, bf16[128,1536]{1,0:T(8,128)(2,1)S(1)}, bf16[128,1536]{1,0:T(8,128)(2,1)S(1)}, bf16[256,1536]{1,0:T(8,1...) custom-call(s32[3]{0:T(128)S(1)} %copy-done.125, ...), custom_call_target="tpu_custom_call" | custom-call | flops 377487360 | tf_op jit(solution)/shard_map/experts_backward/pallas_call | solution.py:1100
  780.2 12.8 %collective-permute-done.124.refs_2_ = bf16[3,5,192,128]{3,2,1,0:T(8,128)(2,1)S(1)} collective-permute-done((bf16[3,5,192,128]{3,2,1,0:T(8,128)(2,1)}, bf16[3,5,192,128]{3,2,1,0:T(8,128)(2,1)S(1)}, u32[]{:S(2)}, u32[]{:S(2)}) %collective-permute-start.124) | collective-permute-done | bytes 737312 | tf_op jit(solution)/shard_map/ppermute | solution.py:38
  803.2 7.6 weight_grads.9
  811.0 6.6 collective-permute-done.127.refs_6_.refs_1_
  817.6 7.9 weight_grads.10
  829.7 8.0 collective-permute-done.131.two_tail
  840.7 8.1 weight_grads.11
  901.0 8.2 collective-permute-done.137.refs_4_
  916.9 30.4 %attend_backward.3 = (f32[128,1536]{1,0:T(8,128)}, bf16[128,1536]{1,0:T(8,128)(2,1)}, bf16[576,4224]{1,0:T(8,128)(2,1)}, bf16[192,4224]{1,0:T(8,128)(2,1)}, bf16...) custom-call(s32[3]{0:T(128)} %pad_add_fusion.where.refs_0_, bf16[128,1536]{1,0:T(8,128)(2,1)} %broadcast_in_dim.61.refs_1_, ...), custom_call_target="tpu_custom_call" | custom-call | flops 207618048 | tf_op jit(solution)/shard_map/attend_backward/pallas_call | solution.py:844
  949.5 7.6 collective-permute-done.148.arrived
  962.0 7.6 collective-permute-done.149.refs_1_
  978.6 20.6 %collective-permute-done.151 = bf16[288,2048]{1,0:T(8,128)(2,1)S(1)} collective-permute-done((bf16[288,2048]{1,0:T(8,128)(2,1)S(1)}, bf16[288,2048]{1,0:T(8,128)(2,1)S(1)}, u32[]{:S(2)}, u32[]{:S(2)}) %collective-permute-start.151) | collective-permute-done | bytes 1179680 | tf_op jit(solution)/shard_map/ppermute | solution.py:38
  1009.4 10.7 collective-permute-done.160.refs_2_
  1038.7 8.4 collective-permute-done.162
  1047.2 20.9 %collective-permute-done.163 = bf16[48,4224]{1,0:T(8,128)(2,1)S(1)} collective-permute-done((bf16[48,4224]{1,0:T(8,128)(2,1)S(1)}, bf16[48,4224]{1,0:T(8,128)(2,1)S(1)}, u32[]{:S(2)}, u32[]{:S(2)}) %collective-permute-start.163) | collective-permute-done | bytes 405536 | tf_op jit(solution)/shard_map/ppermute | solution.py:38
  (872 shorter events, 417.4 us)
Async XLA Ops:
  7.9 29.1 %collective-permute-start.1 = (bf16[48,4224]{1,0:T(8,128)(2,1)}, bf16[48,4224]{1,0:T(8,128)(2,1)S(1)}, u32[]{:S(2)}, u32[]{:S(2)}) collective-permute-start(bf16[48,4224]{1,0:T(8,128)(2,1)} %get-tuple-element.499), channel_id=1, source_target_pairs={{0,16},{1,17},{2,18},{3,19},{4,20},{5,21},{6,22},{7,23},{8,24},{9,... | collective-permute-start | bytes 1216520 | tf_op jit(solution)/shard_map/ppermute | solution.py:38
  37.2 62.7 %collective-permute-start.10 = (bf16[192,4224]{1,0:T(8,128)(2,1)S(1)}, bf16[192,4224]{1,0:T(8,128)(2,1)S(1)}, u32[]{:S(2)}, u32[]{:S(2)}) collective-permute-start(bf16[192,4224]{1,0:T(8,128)(2,1)S(1)} %constant_dynamic-update-slice_fusion.refs_5_.refs_21_), channel_id=1, source_target_pairs={{0,4},{1,5},{2,6},{3,7},{4,0},{5,1},{6,2},{7,3},{8,12},{9,13},{10,... | collective-permute-start | bytes 4866056 | tf_op jit(solution)/shard_map/ppermute | solution.py:38
  37.3 62.6 %collective-permute-start.6 = (bf16[192,4224]{1,0:T(8,128)(2,1)S(1)}, bf16[192,4224]{1,0:T(8,128)(2,1)S(1)}, u32[]{:S(2)}, u32[]{:S(2)}) collective-permute-start(bf16[192,4224]{1,0:T(8,128)(2,1)S(1)} %constant_dynamic-update-slice_fusion.refs_5_.refs_21_), channel_id=1, source_target_pairs={{0,1},{1,0},{2,3},{3,2},{4,5},{5,4},{6,7},{7,6},{8,9},{9,8},{10,11... | collective-permute-start | bytes 4866056 | tf_op jit(solution)/shard_map/ppermute | solution.py:38
  38.8 61.1 %collective-permute-start.7 = (bf16[192,4224]{1,0:T(8,128)(2,1)S(1)}, bf16[192,4224]{1,0:T(8,128)(2,1)S(1)}, u32[]{:S(2)}, u32[]{:S(2)}) collective-permute-start(bf16[192,4224]{1,0:T(8,128)(2,1)S(1)} %constant_dynamic-update-slice_fusion.refs_5_.refs_21_), channel_id=1, source_target_pairs={{0,2},{1,3},{2,0},{3,1},{4,6},{5,7},{6,4},{7,5},{8,10},{9,11},{10,... | collective-permute-start | bytes 4866056 | tf_op jit(solution)/shard_map/ppermute | solution.py:38
  40.4 57.2 %collective-permute-start.9 = (bf16[3,5,192,128]{3,2,1,0:T(8,128)(2,1)}, bf16[3,5,192,128]{3,2,1,0:T(8,128)(2,1)S(1)}, u32[]{:S(2)}, u32[]{:S(2)}) collective-permute-start(bf16[3,5,192,128]{3,2,1,0:T(8,128)(2,1)} %get-tuple-element.512), channel_id=1, source_target_pairs={{0,16},{1,17},{2,18},{3,19},{4,20},{5,21},{6,22},{7,23},{8,24},{9,... | collective-permute-start | bytes 2211848 | tf_op jit(solution)/shard_map/ppermute | solution.py:38
  48.7 48.9 %collective-permute-start.8 = (bf16[3,5,192,128]{3,2,1,0:T(8,128)(2,1)S(1)}, bf16[3,5,192,128]{3,2,1,0:T(8,128)(2,1)S(1)}, u32[]{:S(2)}, u32[]{:S(2)}) collective-permute-start(bf16[3,5,192,128]{3,2,1,0:T(8,128)(2,1)S(1)} %copy-done.217), channel_id=1, source_target_pairs={{0,8},{1,9},{2,10},{3,11},{4,12},{5,13},{6,14},{7,15},{8,16},{9,17... | collective-permute-start | bytes 2211848 | tf_op jit(solution)/shard_map/ppermute | solution.py:38
  185.6 27.1 %collective-permute-start.33 = (bf16[256,1536]{1,0:T(8,128)(2,1)}, bf16[256,1536]{1,0:T(8,128)(2,1)}, u32[]{:S(2)}, u32[]{:S(2)}) collective-permute-start(bf16[256,1536]{1,0:T(8,128)(2,1)} %constant_dynamic-update-slice_fusion.6.refs_2_), channel_id=1, source_target_pairs={{0,1},{1,0},{2,3},{3,2},{4,5},{5,4},{6,7},{7,6},{8,9},{9,8},{10,11... | collective-permute-start | bytes 2359304 | tf_op jit(solution)/shard_map/ppermute | solution.py:38
  287.5 41.9 %collective-permute-start.53 = (bf16[192,4224]{1,0:T(8,128)(2,1)}, bf16[192,4224]{1,0:T(8,128)(2,1)}, u32[]{:S(2)}, u32[]{:S(2)}) collective-permute-start(bf16[192,4224]{1,0:T(8,128)(2,1)} %constant_dynamic-update-slice_fusion.8.refs_11_.refs_21_), channel_id=1, source_target_pairs={{0,1},{1,0},{2,3},{3,2},{4,5},{5,4},{6,7},{7,6},{8,9},{9,8},{10,11... | collective-permute-start | bytes 4866056 | tf_op jit(solution)/shard_map/ppermute | solution.py:38
  288.4 41.0 %collective-permute-start.54 = (bf16[192,4224]{1,0:T(8,128)(2,1)}, bf16[192,4224]{1,0:T(8,128)(2,1)}, u32[]{:S(2)}, u32[]{:S(2)}) collective-permute-start(bf16[192,4224]{1,0:T(8,128)(2,1)} %constant_dynamic-update-slice_fusion.8.refs_11_.refs_21_), channel_id=1, source_target_pairs={{0,2},{1,3},{2,0},{3,1},{4,6},{5,7},{6,4},{7,5},{8,10},{9,11},{10,... | collective-permute-start | bytes 4866056 | tf_op jit(solution)/shard_map/ppermute | solution.py:38
  298.1 31.3 %collective-permute-start.51 = (bf16[128,1536]{1,0:T(8,128)(2,1)}, bf16[128,1536]{1,0:T(8,128)(2,1)S(1)}, u32[]{:S(2)}, u32[]{:S(2)}) collective-permute-start(bf16[128,1536]{1,0:T(8,128)(2,1)} %get-tuple-element.588), channel_id=1, source_target_pairs={{0,16},{1,17},{2,18},{3,19},{4,20},{5,21},{6,22},{7,23},{8,24},{9,... | collective-permute-start | bytes 1179656 | tf_op jit(solution)/shard_map/ppermute | solution.py:38
  298.8 30.6 %collective-permute-start.52 = (bf16[128,1536]{1,0:T(8,128)(2,1)}, bf16[128,1536]{1,0:T(8,128)(2,1)S(1)}, u32[]{:S(2)}, u32[]{:S(2)}) collective-permute-start(bf16[128,1536]{1,0:T(8,128)(2,1)} %get-tuple-element.589), channel_id=1, source_target_pairs={{0,8},{1,9},{2,10},{3,11},{4,12},{5,13},{6,14},{7,15},{8,16},{9,17... | collective-permute-start | bytes 1179656 | tf_op jit(solution)/shard_map/ppermute | solution.py:38
  329.4 35.8 %collective-permute-start.58 = (bf16[192,4224]{1,0:T(8,128)(2,1)}, bf16[192,4224]{1,0:T(8,128)(2,1)S(1)}, u32[]{:S(2)}, u32[]{:S(2)}) collective-permute-start(bf16[192,4224]{1,0:T(8,128)(2,1)} %collective-permute-done.53.refs_12_.refs_22_), channel_id=1, source_target_pairs={{0,4},{1,5},{2,6},{3,7},{4,0},{5,1},{6,2},{7,3},{8,12},{9,13},{10,... | collective-permute-start | bytes 4866056 | tf_op jit(solution)/shard_map/ppermute | solution.py:38
  329.4 35.7 %collective-permute-start.59 = (bf16[192,4224]{1,0:T(8,128)(2,1)}, bf16[192,4224]{1,0:T(8,128)(2,1)S(1)}, u32[]{:S(2)}, u32[]{:S(2)}) collective-permute-start(bf16[192,4224]{1,0:T(8,128)(2,1)} %collective-permute-done.54.refs_13_.refs_23_), channel_id=1, source_target_pairs={{0,4},{1,5},{2,6},{3,7},{4,0},{5,1},{6,2},{7,3},{8,12},{9,13},{10,... | collective-permute-start | bytes 4866056 | tf_op jit(solution)/shard_map/ppermute | solution.py:38
  330.0 35.1 %collective-permute-start.57 = (bf16[3,5,192,128]{3,2,1,0:T(8,128)(2,1)}, bf16[3,5,192,128]{3,2,1,0:T(8,128)(2,1)S(1)}, u32[]{:S(2)}, u32[]{:S(2)}) collective-permute-start(bf16[3,5,192,128]{3,2,1,0:T(8,128)(2,1)} %get-tuple-element.597), channel_id=1, source_target_pairs={{0,16},{1,17},{2,18},{3,19},{4,20},{5,21},{6,22},{7,23},{8,24},{9,... | collective-permute-start | bytes 2211848 | tf_op jit(solution)/shard_map/ppermute | solution.py:38
  333.3 31.8 %collective-permute-start.56 = (bf16[192,2176]{1,0:T(8,128)(2,1)S(1)}, bf16[192,2176]{1,0:T(8,128)(2,1)S(1)}, u32[]{:S(2)}, u32[]{:S(2)}) collective-permute-start(bf16[192,2176]{1,0:T(8,128)(2,1)S(1)} %slice.223), channel_id=1, source_target_pairs={{0,1},{1,0},{2,3},{3,2},{4,5},{5,4},{6,7},{7,6},{8,9},{9,8},{10,11... | collective-permute-start | bytes 2506760 | tf_op jit(solution)/shard_map/ppermute | solution.py:38
  335.5 29.6 %collective-permute-start.55 = (bf16[192,2048]{1,0:T(8,128)(2,1)S(1)}, bf16[192,2048]{1,0:T(8,128)(2,1)S(1)}, u32[]{:S(2)}, u32[]{:S(2)}) collective-permute-start(bf16[192,2048]{1,0:T(8,128)(2,1)S(1)} %slice.222), channel_id=1, source_target_pairs={{0,2},{1,3},{2,0},{3,1},{4,6},{5,7},{6,4},{7,5},{8,10},{9,11},{10,... | collective-permute-start | bytes 2359304 | tf_op jit(solution)/shard_map/ppermute | solution.py:38
  586.3 44.3 %collective-permute-start.100 = (bf16[4,5,192,128]{3,2,1,0:T(8,128)(2,1)}, bf16[4,5,192,128]{3,2,1,0:T(8,128)(2,1)}, u32[]{:S(2)}, u32[]{:S(2)}) collective-permute-start(bf16[4,5,192,128]{3,2,1,0:T(8,128)(2,1)} %get-tuple-element.716), channel_id=1, source_target_pairs={{0,4},{1,5},{2,6},{3,7},{4,0},{5,1},{6,2},{7,3},{8,12},{9,13},{10,... | collective-permute-start | bytes 2949128 | tf_op jit(solution)/shard_map/ppermute | solution.py:38
  595.1 29.6 %collective-permute-start.98 = (bf16[128,1536]{1,0:T(8,128)(2,1)}, bf16[128,1536]{1,0:T(8,128)(2,1)}, u32[]{:S(2)}, u32[]{:S(2)}) collective-permute-start(bf16[128,1536]{1,0:T(8,128)(2,1)} %get-tuple-element.713.refs_5_), channel_id=1, source_target_pairs={{0,16},{1,17},{2,18},{3,19},{4,20},{5,21},{6,22},{7,23},{8,24},{9,... | collective-permute-start | bytes 1179656 | tf_op jit(solution)/shard_map/ppermute | solution.py:38
  597.3 27.4 %collective-permute-start.99 = (bf16[128,1536]{1,0:T(8,128)(2,1)}, bf16[128,1536]{1,0:T(8,128)(2,1)}, u32[]{:S(2)}, u32[]{:S(2)}) collective-permute-start(bf16[128,1536]{1,0:T(8,128)(2,1)} %get-tuple-element.714), channel_id=1, source_target_pairs={{0,8},{1,9},{2,10},{3,11},{4,12},{5,13},{6,14},{7,15},{8,16},{9,17... | collective-permute-start | bytes 1179656 | tf_op jit(solution)/shard_map/ppermute | solution.py:38
  630.6 35.4 %collective-permute-start.103 = (bf16[256,1536]{1,0:T(8,128)(2,1)}, bf16[256,1536]{1,0:T(8,128)(2,1)S(1)}, u32[]{:S(2)}, u32[]{:S(2)}) collective-permute-start(bf16[256,1536]{1,0:T(8,128)(2,1)} %get-tuple-element.751), channel_id=1, source_target_pairs={{0,1},{1,0},{2,3},{3,2},{4,5},{5,4},{6,7},{7,6},{8,9},{9,8},{10,11... | collective-permute-start | bytes 2359304 | tf_op jit(solution)/shard_map/ppermute | solution.py:38
  631.8 34.3 %collective-permute-start.104 = (bf16[256,1536]{1,0:T(8,128)(2,1)}, bf16[256,1536]{1,0:T(8,128)(2,1)S(1)}, u32[]{:S(2)}, u32[]{:S(2)}) collective-permute-start(bf16[256,1536]{1,0:T(8,128)(2,1)} %get-tuple-element.752), channel_id=1, source_target_pairs={{0,2},{1,3},{2,0},{3,1},{4,6},{5,7},{6,4},{7,5},{8,10},{9,11},{10,... | collective-permute-start | bytes 2359304 | tf_op jit(solution)/shard_map/ppermute | solution.py:38
  632.5 33.6 %collective-permute-start.101 = (bf16[256,1536]{1,0:T(8,128)(2,1)}, bf16[256,1536]{1,0:T(8,128)(2,1)S(1)}, u32[]{:S(2)}, u32[]{:S(2)}) collective-permute-start(bf16[256,1536]{1,0:T(8,128)(2,1)} %get-tuple-element.742), channel_id=1, source_target_pairs={{0,1},{1,0},{2,3},{3,2},{4,5},{5,4},{6,7},{7,6},{8,9},{9,8},{10,11... | collective-permute-start | bytes 2359304 | tf_op jit(solution)/shard_map/ppermute | solution.py:38
  633.6 33.3 %collective-permute-start.102 = (bf16[256,1536]{1,0:T(8,128)(2,1)}, bf16[256,1536]{1,0:T(8,128)(2,1)S(1)}, u32[]{:S(2)}, u32[]{:S(2)}) collective-permute-start(bf16[256,1536]{1,0:T(8,128)(2,1)} %get-tuple-element.743), channel_id=1, source_target_pairs={{0,2},{1,3},{2,0},{3,1},{4,6},{5,7},{6,4},{7,5},{8,10},{9,11},{10,... | collective-permute-start | bytes 2359304 | tf_op jit(solution)/shard_map/ppermute | solution.py:38
  634.7 39.0 %collective-permute-start.106 = (bf16[4,5,192,128]{3,2,1,0:T(8,128)(2,1)S(1)}, bf16[4,5,192,128]{3,2,1,0:T(8,128)(2,1)S(1)}, u32[]{:S(2)}, u32[]{:S(2)}) collective-permute-start(bf16[4,5,192,128]{3,2,1,0:T(8,128)(2,1)S(1)} %get-tuple-element.757), channel_id=1, source_target_pairs={{0,4},{1,5},{2,6},{3,7},{4,0},{5,1},{6,2},{7,3},{8,12},{9,13},{10,... | collective-permute-start | bytes 2949128 | tf_op jit(solution)/shard_map/ppermute | solution.py:38
  683.6 67.0 %collective-permute-start.121 = (bf16[768,4224]{1,0:T(8,128)(2,1)}, bf16[768,4224]{1,0:T(8,128)(2,1)}, u32[]{:S(2)}, u32[]{:S(2)}) collective-permute-start(bf16[768,4224]{1,0:T(8,128)(2,1)} %get-tuple-element.807), channel_id=1, source_target_pairs={{0,4},{1,5},{2,6},{3,7},{4,0},{5,1},{6,2},{7,3},{8,12},{9,13},{10,... | collective-permute-start | bytes 19464200 | tf_op jit(solution)/shard_map/ppermute | solution.py:38
  715.6 31.8 %collective-permute-start.115 = (bf16[256,1536]{1,0:T(8,128)(2,1)S(1)}, bf16[256,1536]{1,0:T(8,128)(2,1)S(1)}, u32[]{:S(2)}, u32[]{:S(2)}) collective-permute-start(bf16[256,1536]{1,0:T(8,128)(2,1)S(1)} %constant_dynamic-update-slice_fusion.22.refs_2_), channel_id=1, source_target_pairs={{0,1},{1,0},{2,3},{3,2},{4,5},{5,4},{6,7},{7,6},{8,9},{9,8},{10,11... | collective-permute-start | bytes 2359304 | tf_op jit(solution)/shard_map/ppermute | solution.py:38
  716.6 30.8 %collective-permute-start.116 = (bf16[256,1536]{1,0:T(8,128)(2,1)S(1)}, bf16[256,1536]{1,0:T(8,128)(2,1)S(1)}, u32[]{:S(2)}, u32[]{:S(2)}) collective-permute-start(bf16[256,1536]{1,0:T(8,128)(2,1)S(1)} %constant_dynamic-update-slice_fusion.22.refs_2_), channel_id=1, source_target_pairs={{0,2},{1,3},{2,0},{3,1},{4,6},{5,7},{6,4},{7,5},{8,10},{9,11},{10,... | collective-permute-start | bytes 2359304 | tf_op jit(solution)/shard_map/ppermute | solution.py:38
  759.6 37.8 %collective-permute-start.122 = (bf16[384,2176]{1,0:T(8,128)(2,1)}, bf16[384,2176]{1,0:T(8,128)(2,1)}, u32[]{:S(2)}, u32[]{:S(2)}) collective-permute-start(bf16[384,2176]{1,0:T(8,128)(2,1)} %get-tuple-element.817), channel_id=1, source_target_pairs={{0,1},{1,0},{2,3},{3,2},{4,5},{5,4},{6,7},{7,6},{8,9},{9,8},{10,11... | collective-permute-start | bytes 5013512 | tf_op jit(solution)/shard_map/ppermute | solution.py:38
  760.9 34.8 %collective-permute-start.123 = (bf16[384,2048]{1,0:T(8,128)(2,1)}, bf16[384,2048]{1,0:T(8,128)(2,1)}, u32[]{:S(2)}, u32[]{:S(2)}) collective-permute-start(bf16[384,2048]{1,0:T(8,128)(2,1)} %get-tuple-element.818), channel_id=1, source_target_pairs={{0,2},{1,3},{2,0},{3,1},{4,6},{5,7},{6,4},{7,5},{8,10},{9,11},{10,... | collective-permute-start | bytes 4718600 | tf_op jit(solution)/shard_map/ppermute | solution.py:38
  761.5 31.5 %collective-permute-start.124 = (bf16[3,5,192,128]{3,2,1,0:T(8,128)(2,1)}, bf16[3,5,192,128]{3,2,1,0:T(8,128)(2,1)S(1)}, u32[]{:S(2)}, u32[]{:S(2)}) collective-permute-start(bf16[3,5,192,128]{3,2,1,0:T(8,128)(2,1)} %get-tuple-element.820), channel_id=1, source_target_pairs={{0,16},{1,17},{2,18},{3,19},{4,20},{5,21},{6,22},{7,23},{8,24},{9,... | collective-permute-start | bytes 2211848 | tf_op jit(solution)/shard_map/ppermute | solution.py:38
  797.5 28.2 %collective-permute-start.125 = (bf16[256,1536]{1,0:T(8,128)(2,1)}, bf16[256,1536]{1,0:T(8,128)(2,1)S(1)}, u32[]{:S(2)}, u32[]{:S(2)}) collective-permute-start(bf16[256,1536]{1,0:T(8,128)(2,1)} %get-tuple-element.824), channel_id=1, source_target_pairs={{0,1},{1,0},{2,3},{3,2},{4,5},{5,4},{6,7},{7,6},{8,9},{9,8},{10,11... | collective-permute-start | bytes 2359304 | tf_op jit(solution)/shard_map/ppermute | solution.py:38
  798.1 27.6 %collective-permute-start.126 = (bf16[256,1536]{1,0:T(8,128)(2,1)}, bf16[256,1536]{1,0:T(8,128)(2,1)}, u32[]{:S(2)}, u32[]{:S(2)}) collective-permute-start(bf16[256,1536]{1,0:T(8,128)(2,1)} %get-tuple-element.825), channel_id=1, source_target_pairs={{0,2},{1,3},{2,0},{3,1},{4,6},{5,7},{6,4},{7,5},{8,10},{9,11},{10,... | collective-permute-start | bytes 2359304 | tf_op jit(solution)/shard_map/ppermute | solution.py:38
  825.6 30.1 %collective-permute-start.133 = (bf16[4,5,192,128]{3,2,1,0:T(8,128)(2,1)}, bf16[4,5,192,128]{3,2,1,0:T(8,128)(2,1)S(1)}, u32[]{:S(2)}, u32[]{:S(2)}) collective-permute-start(bf16[4,5,192,128]{3,2,1,0:T(8,128)(2,1)} %get-tuple-element.847), channel_id=1, source_target_pairs={{0,4},{1,5},{2,6},{3,7},{4,0},{5,1},{6,2},{7,3},{8,12},{9,13},{10,... | collective-permute-start | bytes 2949128 | tf_op jit(solution)/shard_map/ppermute | solution.py:38
  827.7 28.0 %collective-permute-start.128 = (bf16[256,1536]{1,0:T(8,128)(2,1)}, bf16[256,1536]{1,0:T(8,128)(2,1)S(1)}, u32[]{:S(2)}, u32[]{:S(2)}) collective-permute-start(bf16[256,1536]{1,0:T(8,128)(2,1)} %get-tuple-element.843), channel_id=1, source_target_pairs={{0,1},{1,0},{2,3},{3,2},{4,5},{5,4},{6,7},{7,6},{8,9},{9,8},{10,11... | collective-permute-start | bytes 2359304 | tf_op jit(solution)/shard_map/ppermute | solution.py:38
  910.8 36.5 %collective-permute-start.144 = (bf16[128,1536]{1,0:T(8,128)(2,1)}, bf16[128,1536]{1,0:T(8,128)(2,1)}, u32[]{:S(2)}, u32[]{:S(2)}) collective-permute-start(bf16[128,1536]{1,0:T(8,128)(2,1)} %add_convert_fusion.6), channel_id=1, source_target_pairs={{0,2},{1,3},{2,0},{3,1},{4,6},{5,7},{6,4},{7,5},{8,10},{9,11},{10,... | collective-permute-start | bytes 1179656 | tf_op jit(solution)/shard_map/ppermute | solution.py:38
  911.5 35.9 %collective-permute-start.145 = (bf16[48,4224]{1,0:T(8,128)(2,1)S(1)}, bf16[48,4224]{1,0:T(8,128)(2,1)S(1)}, u32[]{:S(2)}, u32[]{:S(2)}) collective-permute-start(bf16[48,4224]{1,0:T(8,128)(2,1)S(1)} %get-tuple-element.1000), channel_id=1, source_target_pairs={{0,24},{1,25},{2,26},{3,27},{4,28},{5,29},{6,30},{7,31},{8,0},{9,1... | collective-permute-start | bytes 1216520 | tf_op jit(solution)/shard_map/ppermute | solution.py:38
  911.6 37.1 %collective-permute-start.146 = (bf16[48,4224]{1,0:T(8,128)(2,1)S(1)}, bf16[48,4224]{1,0:T(8,128)(2,1)S(1)}, u32[]{:S(2)}, u32[]{:S(2)}) collective-permute-start(bf16[48,4224]{1,0:T(8,128)(2,1)S(1)} %get-tuple-element.999), channel_id=1, source_target_pairs={{0,16},{1,17},{2,18},{3,19},{4,20},{5,21},{6,22},{7,23},{8,24},{9,... | collective-permute-start | bytes 1216520 | tf_op jit(solution)/shard_map/ppermute | solution.py:38
  913.6 35.1 %collective-permute-start.147 = (bf16[48,4224]{1,0:T(8,128)(2,1)S(1)}, bf16[48,4224]{1,0:T(8,128)(2,1)S(1)}, u32[]{:S(2)}, u32[]{:S(2)}) collective-permute-start(bf16[48,4224]{1,0:T(8,128)(2,1)S(1)} %get-tuple-element.998), channel_id=1, source_target_pairs={{0,8},{1,9},{2,10},{3,11},{4,12},{5,13},{6,14},{7,15},{8,16},{9,17... | collective-permute-start | bytes 1216520 | tf_op jit(solution)/shard_map/ppermute | solution.py:38
  915.4 32.0 %collective-permute-start.143 = (bf16[128,1536]{1,0:T(8,128)(2,1)}, bf16[128,1536]{1,0:T(8,128)(2,1)S(1)}, u32[]{:S(2)}, u32[]{:S(2)}) collective-permute-start(bf16[128,1536]{1,0:T(8,128)(2,1)} %add_convert_fusion.7), channel_id=1, source_target_pairs={{0,1},{1,0},{2,3},{3,2},{4,5},{5,4},{6,7},{7,6},{8,9},{9,8},{10,11... | collective-permute-start | bytes 1179656 | tf_op jit(solution)/shard_map/ppermute | solution.py:38
  970.5 29.1 %collective-permute-start.150 = (bf16[288,2176]{1,0:T(8,128)(2,1)S(1)}, bf16[288,2176]{1,0:T(8,128)(2,1)S(1)}, u32[]{:S(2)}, u32[]{:S(2)}) collective-permute-start(bf16[288,2176]{1,0:T(8,128)(2,1)S(1)} %get-tuple-element.935), channel_id=1, source_target_pairs={{0,1},{1,0},{2,3},{3,2},{4,5},{5,4},{6,7},{7,6},{8,9},{9,8},{10,11... | collective-permute-start | bytes 3760136 | tf_op jit(solution)/shard_map/ppermute | solution.py:38
  972.0 27.3 %collective-permute-start.151 = (bf16[288,2048]{1,0:T(8,128)(2,1)S(1)}, bf16[288,2048]{1,0:T(8,128)(2,1)S(1)}, u32[]{:S(2)}, u32[]{:S(2)}) collective-permute-start(bf16[288,2048]{1,0:T(8,128)(2,1)S(1)} %get-tuple-element.936), channel_id=1, source_target_pairs={{0,2},{1,3},{2,0},{3,1},{4,6},{5,7},{6,4},{7,5},{8,10},{9,11},{10,... | collective-permute-start | bytes 3538952 | tf_op jit(solution)/shard_map/ppermute | solution.py:38
  972.6 36.3 %collective-permute-start.161 = (bf16[3,5,192,128]{3,2,1,0:T(8,128)(2,1)}, bf16[3,5,192,128]{3,2,1,0:T(8,128)(2,1)}, u32[]{:S(2)}, u32[]{:S(2)}) collective-permute-start(bf16[3,5,192,128]{3,2,1,0:T(8,128)(2,1)} %get-tuple-element.973), channel_id=1, source_target_pairs={{0,24},{1,25},{2,26},{3,27},{4,28},{5,29},{6,30},{7,31},{8,0},{9,1... | collective-permute-start | bytes 2211848 | tf_op jit(solution)/shard_map/ppermute | solution.py:38
  972.6 47.5 %collective-permute-start.160 = (bf16[3,5,192,128]{3,2,1,0:T(8,128)(2,1)}, bf16[3,5,192,128]{3,2,1,0:T(8,128)(2,1)}, u32[]{:S(2)}, u32[]{:S(2)}) collective-permute-start(bf16[3,5,192,128]{3,2,1,0:T(8,128)(2,1)} %get-tuple-element.971), channel_id=1, source_target_pairs={{0,16},{1,17},{2,18},{3,19},{4,20},{5,21},{6,22},{7,23},{8,24},{9,... | collective-permute-start | bytes 2211848 | tf_op jit(solution)/shard_map/ppermute | solution.py:38
  1001.6 27.8 %collective-permute-start.154 = (bf16[96,2048]{1,0:T(8,128)(2,1)}, bf16[96,2048]{1,0:T(8,128)(2,1)}, u32[]{:S(2)}, u32[]{:S(2)}) collective-permute-start(bf16[96,2048]{1,0:T(8,128)(2,1)} %get-tuple-element.965), channel_id=1, source_target_pairs={{0,2},{1,3},{2,0},{3,1},{4,6},{5,7},{6,4},{7,5},{8,10},{9,11},{10,... | collective-permute-start | bytes 1179656 | tf_op jit(solution)/shard_map/ppermute | solution.py:38
  1004.1 28.5 %collective-permute-start.159 = (bf16[144,2176]{1,0:T(8,128)(2,1)}, bf16[144,2176]{1,0:T(8,128)(2,1)}, u32[]{:S(2)}, u32[]{:S(2)}) collective-permute-start(bf16[144,2176]{1,0:T(8,128)(2,1)} %add_convert_fusion.3), channel_id=1, source_target_pairs={{0,2},{1,3},{2,0},{3,1},{4,6},{5,7},{6,4},{7,5},{8,10},{9,11},{10,... | collective-permute-start | bytes 1880072 | tf_op jit(solution)/shard_map/ppermute | solution.py:38
  1004.7 27.9 %collective-permute-start.158 = (bf16[144,2048]{1,0:T(8,128)(2,1)}, bf16[144,2048]{1,0:T(8,128)(2,1)}, u32[]{:S(2)}, u32[]{:S(2)}) collective-permute-start(bf16[144,2048]{1,0:T(8,128)(2,1)} %add_convert_fusion.4), channel_id=1, source_target_pairs={{0,1},{1,0},{2,3},{3,2},{4,5},{5,4},{6,7},{7,6},{8,9},{9,8},{10,11... | collective-permute-start | bytes 1769480 | tf_op jit(solution)/shard_map/ppermute | solution.py:38
  1034.6 33.4 %collective-permute-start.163 = (bf16[48,4224]{1,0:T(8,128)(2,1)S(1)}, bf16[48,4224]{1,0:T(8,128)(2,1)S(1)}, u32[]{:S(2)}, u32[]{:S(2)}) collective-permute-start(bf16[48,4224]{1,0:T(8,128)(2,1)S(1)} %get-tuple-element.997), channel_id=1, source_target_pairs={{0,16},{1,17},{2,18},{3,19},{4,20},{5,21},{6,22},{7,23},{8,24},{9,... | collective-permute-start | bytes 1216520 | tf_op jit(solution)/shard_map/ppermute | solution.py:38
  1034.7 33.3 %collective-permute-start.164 = (bf16[48,4224]{1,0:T(8,128)(2,1)S(1)}, bf16[48,4224]{1,0:T(8,128)(2,1)S(1)}, u32[]{:S(2)}, u32[]{:S(2)}) collective-permute-start(bf16[48,4224]{1,0:T(8,128)(2,1)S(1)} %get-tuple-element.996), channel_id=1, source_target_pairs={{0,8},{1,9},{2,10},{3,11},{4,12},{5,13},{6,14},{7,15},{8,16},{9,17... | collective-permute-start | bytes 1216520 | tf_op jit(solution)/shard_map/ppermute | solution.py:38
  (339 other events, 6606.0 us)

commit v6 on v5

--- a/solution.py
+++ b/solution.py
@@ -525,16 +525,22 @@
 MATRIX_COPIES = 40
 
 
-def load_matrices(copies, where, pieces, full):
+def load_columns(copies, where, pieces, full, low, high):
     rows, cut = pieces[0].shape[0] // 4, pieces[3].shape[1]
-    spans = ((0, 0, full.shape[1]),) * 3 + ((3, 0, cut), (3, cut, full.shape[1] - cut))
+    spans = ((0, 0, full.shape[1]), (1, 0, full.shape[1]), (2, 0, full.shape[1]), (3, 0, cut))
+    spans += ((3, cut, full.shape[1]),)
     for swapped in range(CORES):
-        for index, (m, low, width) in enumerate(spans):
-            piece = pieces[swapped * 5 + index]
+        for index, (m, first, last) in enumerate(spans):
+            begin, end = max(low, first), min(high, last)
+            if begin >= end:
+                continue
             for k in range(4):
-                row = shard_row(where, swapped, m or index, k, rows)
+                row = shard_row(where, swapped, m, k, rows)
                 copies.start(
-                    piece.at[pl.ds(k * rows, rows), :], full.at[pl.ds(row, rows), pl.ds(low, width)]
+                    pieces[swapped * 5 + index].at[
+                        pl.ds(k * rows, rows), pl.ds(begin - first, end - begin)
+                    ],
+                    full.at[pl.ds(row, rows), pl.ds(begin, end - begin)],
                 )
 
 
@@ -583,13 +589,16 @@
     refs = refs[3 + MATRIX_PIECES :]
     h_out, m_out, nf_out, na_out, q_out, k_out, v_out, o_out, lse_out, gain_out = refs[:10]
     full, proj, mixed, semaphores = refs[10:]
+    model = full.shape[0]
+    in_width = width
     copies = Copies(semaphores)
-    load_matrices(copies, where, pieces, full)
+    load_columns(copies, where, pieces, full, 0, in_width)
+    load_columns(copies, where, pieces, full, in_width + model, full.shape[1])
+    later = Copies(semaphores, copies.used)
+    load_columns(later, where, pieces, full, in_width, in_width + model)
     h = read_sum(base, extra)
     h_out[...] = h
     inverse = lax.rsqrt(jnp.mean(h * h, axis=1, keepdims=True) + NORM_EPS)
-    model = h.shape[1]
-    in_width = width
     key_start = model
     value_start = model + (in_width - model) // 2
     copies.wait()
@@ -646,6 +655,8 @@
             o_out[:, columns] = total.astype(jnp.bfloat16)
         lse_out[...] = lse
 
+    later.wait()
+
     @pl.loop(0, model // step)
     def _(i):
         columns = pl.ds(pl.multiple_of(i * step, step), step)
@@ -692,7 +703,7 @@
             pltpu.VMEM((model, total), bf),
             pltpu.VMEM((rows, in_width), f32),
             pltpu.VMEM((rows, model), f32),
-            pltpu.SemaphoreType.DMA((MATRIX_COPIES,)),
+            pltpu.SemaphoreType.DMA((3 * MATRIX_COPIES,)),
         ],
         compiler_params=pltpu.CompilerParams(vmem_limit_bytes=44 * MIB),
         cost_estimate=cost(2 * rows * model * total),
@@ -713,7 +724,9 @@
     value_start = model + (in_width - model) // 2
     shard = full.shape[0] // 32
     copies = Copies(semaphores)
-    load_matrices(copies, where, pieces, full)
+    load_columns(copies, where, pieces, full, in_width, in_width + model)
+    later = Copies(semaphores, copies.used)
+    load_columns(later, where, pieces, full, 0, in_width)
     gnf = read_sum(base, extra)
     m = m_in[...]
     inverse = lax.rsqrt(jnp.mean(m * m, axis=1, keepdims=True) + NORM_EPS)
@@ -780,19 +793,6 @@
         grad_in[:, pl.ds(key_start + start, LANES)] = key_grad.astype(jnp.bfloat16)
         grad_in[:, pl.ds(value_start + start, LANES)] = value_grad.astype(jnp.bfloat16)
 
-    turned[...] = jnp.zeros_like(turned)
-
-    @pl.loop(0, in_width // step)
-    def _(i):
-        columns = pl.ds(pl.multiple_of(i * step, step), step)
-        turned[...] += contract(grad_in[:, columns], full[:, columns], ACROSS)
-
-    grad_na = turned[...]
-    h = h_in[...]
-    inverse = lax.rsqrt(jnp.mean(h * h, axis=1, keepdims=True) + NORM_EPS)
-    gain_attn = jnp.sum(grad_na * h * inverse, axis=0, keepdims=True)
-    scaled = grad_na * gains[0:1]
-    inner = jnp.mean(scaled * h, axis=1, keepdims=True)
     band = 384
 
     @pl.loop(0, model // band)
@@ -804,23 +804,42 @@
         )
         sums[row, :in_width] = contract(na[:, row], grad_in[...], OUTER).astype(jnp.bfloat16)
 
+    def store_sums(low, width):
+        at = 2
+        for swapped in (1, 0):
+            for first, count in groups:
+                for m_index in range(4):
+                    for n in range(count):
+                        row = shard_row(where, swapped, m_index, first + n, shard)
+                        place = pl.ds((m_index * count + n) * shard, shard)
+                        columns = pl.ds(low, width)
+                        later.start(
+                            sums.at[pl.ds(row, shard), columns], outs[at].at[place, columns]
+                        )
+                at += 1
+
+    later.wait()
+    store_sums(0, in_width + model)
+    turned[...] = jnp.zeros_like(turned)
+
+    @pl.loop(0, in_width // step)
+    def _(i):
+        columns = pl.ds(pl.multiple_of(i * step, step), step)
+        turned[...] += contract(grad_in[:, columns], full[:, columns], ACROSS)
+
+    grad_na = turned[...]
+    h = h_in[...]
+    inverse = lax.rsqrt(jnp.mean(h * h, axis=1, keepdims=True) + NORM_EPS)
+    gain_attn = jnp.sum(grad_na * h * inverse, axis=0, keepdims=True)
+    scaled = grad_na * gains[0:1]
+    inner = jnp.mean(scaled * h, axis=1, keepdims=True)
     both = jnp.concatenate([gain_attn, gain_ffn, jnp.zeros((EXTRA - 2, model), jnp.float32)], axis=0)
     sums[:, pl.ds(in_width + model, EXTRA)] = both.T.astype(jnp.bfloat16)
-    at = 2
-    for swapped in (1, 0):
-        for first, count in groups:
-            for m_index in range(4):
-                for n in range(count):
-                    row = shard_row(where, swapped, m_index, first + n, shard)
-                    copies.start(
-                        sums.at[pl.ds(row, shard), :],
-                        outs[at].at[pl.ds((m_index * count + n) * shard, shard), :],
-                    )
-            at += 1
+    store_sums(in_width + model, EXTRA)
     gh = gh_out[...] + inverse * scaled - h * (inverse * inverse * inverse) * inner
     gh_out[...] = gh
     gh_low[...] = gh.astype(jnp.bfloat16)
-    copies.wait()
+    later.wait()
 
 
 def attend_backward_fast(
@@ -855,7 +874,7 @@
             pltpu.VMEM((rows, model), bf),
             pltpu.VMEM((rows, in_width), bf),
             pltpu.VMEM((rows, model), f32),
-            pltpu.SemaphoreType.DMA((MATRIX_COPIES + 32,)),
+            pltpu.SemaphoreType.DMA((2 * MATRIX_COPIES + 64,)),
         ],
         compiler_params=pltpu.CompilerParams(vmem_limit_bytes=56 * MIB),
         cost_estimate=cost(4 * rows * model * total),
@@ -880,6 +899,17 @@
                     copies.start(piece.at[i, e], target.at[row, pl.ds(e * share, share)])
 
 
+def load_weights(copies, where, weights, targets):
+    if len(weights) > 1:
+        load_experts(copies, where, weights, targets)
+    else:
+        rows = targets[0].shape[0] // 8
+        for i, target in enumerate(targets):
+            for n in range(8):
+                row = pl.ds(n * rows, rows)
+                copies.start(weights[0].at[i, row, :], target.at[row, :])
+
+
 def widen_tile(columns, share, width):
     lane = lax.broadcasted_iota(jnp.int32, (columns.shape[0], width), 1)
     wide = jnp.broadcast_to(columns[:, 0:1], lane.shape)
@@ -959,10 +989,11 @@
     return [n, n // 2, n // 2, n, n]
 
 
-def experts_forward_kernel(where, gates, *refs):
-    pieces, weights, refs = refs[:5], refs[5 : 5 + WEIGHT_PIECES], refs[5 + WEIGHT_PIECES :]
+def experts_forward_kernel(share, count, where, gates, *refs):
+    pieces, weights, refs = refs[:5], refs[5 : 5 + count], refs[5 + count :]
     parts, x_out, g_out, u_out = refs[:5], *refs[5:8]
-    x, y, g, u, w_gate, w_up, w_down, semaphores = refs[8:]
+    x, y, g, u, w_gate, w_up, w_down, semaphores = refs[-8:]
+    laid = refs[8:-8]
     n = pieces[0].shape[0]
     pool = Pool(semaphores)
     loads = tile_loads(pool, pieces, x)
@@ -970,17 +1001,20 @@
         for copy in group:
             copy.start()
     copies = Copies(semaphores, pool.used)
-    load_experts(copies, where, weights, (w_gate, w_up, w_down))
+    load_weights(copies, where, weights, (w_gate, w_up, w_down))
     pool.used = copies.used
+    pool.used = copies.used + 3
     kept = tile_slices(pool, x, x_out, n)
     stores = [
         tile_parts(pool, y, parts),
         tile_slices(pool, g, g_out, n),
         tile_slices(pool, u, u_out, n),
     ]
-    share = weights[0].shape[3]
     width = w_gate.shape[1]
     copies.wait()
+    for i, w in enumerate((w_gate, w_up, w_down)):
+        if laid:
+            copies.start(w, laid[0].at[i])
 
     @pl.loop(0, 4)
     def _(i):
@@ -997,25 +1031,29 @@
         for_tile(i, stores, lambda copy: copy.start())
 
     finish([kept, *stores])
-
-
-def experts_forward_fast(where, gates, pieces, weights, after=()):
+    copies.wait()
+
+
+def experts_forward_fast(experts, where, gates, pieces, weights, after=()):
     n, model = pieces[0].shape
-    _, experts, _, share = weights[0].shape
-    rows, width = 4 * n, experts * share
+    rows, count = 4 * n, len(weights)
+    width = experts * weights[0].shape[3] if count > 1 else weights[0].shape[2]
+    share = width // experts
     bf, f32 = jnp.bfloat16, jnp.float32
     shapes = [shape_of(r, model) for r in part_rows(n)]
     shapes += [shape_of(rows, model)] + [shape_of(rows, width, dtype=f32)] * 2
+    if count > 1:
+        shapes += [shape_of(3, model, width)]
 
     def body(*refs):
-        used = 7 + WEIGHT_PIECES
-        experts_forward_kernel(*refs[:used], *refs[used + len(after) :])
+        used = 7 + count
+        experts_forward_kernel(share, count, *refs[:used], *refs[used + len(after) :])
 
     return pl.pallas_call(
         body,
         name="experts_forward",
         out_shape=shapes,
-        in_specs=[scalar_spec(), whole_spec()] + [any_spec()] * (5 + WEIGHT_PIECES + len(after)),
+        in_specs=[scalar_spec(), whole_spec()] + [any_spec()] * (5 + count + len(after)),
         out_specs=[any_spec()] * len(shapes),
         scratch_shapes=[
             pltpu.VMEM((rows, model), bf),
@@ -1030,9 +1068,9 @@
     )(where, gates, *pieces, *weights, *after)
 
 
-def experts_backward_kernel(where, gates, *refs):
+def experts_backward_kernel(share, where, gates, *refs):
     pieces, g_in, u_in = refs[:5], refs[5], refs[6]
-    weights, refs = refs[7 : 7 + WEIGHT_PIECES], refs[7 + WEIGHT_PIECES :]
+    weights, refs = refs[7:8], refs[8:]
     parts, r_out, gg_out, gu_out, p_out = refs[:5], *refs[5:9]
     x, y, g, u, gg, gu, p, w_gate, w_up, w_down, semaphores = refs[9:]
     n = pieces[0].shape[0]
@@ -1046,7 +1084,7 @@
         for copy in group:
             copy.start()
     copies = Copies(semaphores, pool.used)
-    load_experts(copies, where, weights, (w_gate, w_up, w_down))
+    load_weights(copies, where, weights, (w_gate, w_up, w_down))
     for loaded in loads[1:]:
         for group in loaded:
             for copy in group:
@@ -1059,7 +1097,6 @@
         tile_slices(pool, gu, gu_out, n),
         tile_slices(pool, p, p_out, n),
     ]
-    share = weights[0].shape[3]
     width = w_gate.shape[1]
     copies.wait()
 
@@ -1085,23 +1122,22 @@
     finish([kept, *stores])
 
 
-def experts_backward_fast(where, gates, pieces, stash, weights, after=()):
+def experts_backward_fast(experts, where, gates, pieces, stash, weights, after=()):
     n, model = gates.shape[0] // 4, pieces[0].shape[1]
-    _, experts, _, share = weights[0].shape
-    rows, width = 4 * n, experts * share
+    rows, width = 4 * n, weights[0].shape[2]
+    share = width // experts
     bf, f32 = jnp.bfloat16, jnp.float32
     shapes = [shape_of(r, model) for r in part_rows(n)]
     shapes += [shape_of(rows, model)] + [shape_of(rows, width)] * 3
 
     def body(*refs):
-        used = 9 + WEIGHT_PIECES
-        experts_backward_kernel(*refs[:used], *refs[used + len(after) :])
+        experts_backward_kernel(share, *refs[:10], *refs[10 + len(after) :])
 
     return pl.pallas_call(
         body,
         name="experts_backward",
         out_shape=shapes,
-        in_specs=[scalar_spec(), whole_spec()] + [any_spec()] * (7 + WEIGHT_PIECES + len(after)),
+        in_specs=[scalar_spec(), whole_spec()] + [any_spec()] * (8 + len(after)),
         out_specs=[any_spec()] * len(shapes),
         scratch_shapes=[
             pltpu.VMEM((rows, model), bf),
@@ -1490,10 +1526,12 @@
     share_swaps = [own_swaps[0], place.hop(one, swap=1), place.hop(two, swap=1)]
 
     def run_forward(l, which, pieces, bank, after=()):
-        return experts_forward_fast(where, gate_rows[l][which], pieces, bank, after=after)
+        return experts_forward_fast(experts, where, gate_rows[l][which], pieces, bank, after=after)
 
     def run_backward(l, which, pieces, stash, bank, after=()):
-        return experts_backward_fast(where, gate_rows[l][which], pieces, stash, bank, after=after)
+        return experts_backward_fast(
+            experts, where, gate_rows[l][which], pieces, stash, bank, after=after
+        )
 
     def pairs_of(block, *events):
         ups = up_hops(place, block)
@@ -1516,7 +1554,8 @@
         near = spread_last(place, near)
         far = spread_first(place, jnp.concatenate(tie(far, near[3], near[4])))
         line = up_hops(place, tie(packs[l + 1] if more else cotangent, far[0]))
-        y_near = run_forward(l, 0, near, bank_l)
+        *y_near, laid = run_forward(l, 0, near, bank_l)
+        bank_l = [laid]
         y_near, far, line[0], line[2] = tie((y_near, far, line[0], line[2]))
         far = spread_last(place, far)
         if more:
@@ -1587,7 +1626,7 @@
             b_near, far, result_arrived = tie((b_near, far, result_arrived))
             merged = merge_cores(mine_one, tie(other_sum, b_near[0]), cut)
             far = spread_last(place, far)
-            came = [place.hop(tie(held[2], b_near[0]), up=2)]
+            came = [place.hop(tie(held[2][2:], b_near[0]), up=2)]
             merged_first = fold_first(place, tie(merged, far[3], far[4]))
             b_far = run_backward(l, 1, far, kept_far[6:], bank_l, (b_near[0],))
             b_far, merged_first, came[0] = tie((b_far, merged_first, came[0]))
@@ -1620,7 +1659,9 @@
         arrived += down_hops(place, blocks, 2)
         if top:
             grads.append(weight_grads(2, (blocks[0],)))
-            arrived, swapped = tie((arrived, swapped), grads[2][0])
+            early = jnp.stack([add_low(grads[n][0][2], swapped[n][2]) for n in range(2)])
+            arrived, swapped, early = tie((arrived, swapped, early), grads[2][0])
+            early = place.hop(tie(early, *arrived), up=2)
             swapped.append(place.hop(tie(grads[2][1], *arrived), swap=1))
         if top:
             result_first = fold_first(place, tie(kept_far[:5], *arrived))
@@ -1628,7 +1669,7 @@
             after = ()
             groups = ((0, 4),)
         else:
-            held_came = [held[0], *came]
+            held_came = [held[0], came[0], jnp.concatenate([early, came[1]]), came[2]]
             total = merge_grads([mine for mine, _ in grads], swapped)
             merged_ends = fold_end(place, fold_sums(tie(merged_first, blocks[0], *near_ends[1:3])))
             one_total = add_pieces(*merged_ends, axis=1)
@@ -1653,7 +1694,9 @@
             after=after,
         )
         if top:
-            low, result_first, result_near_first = tie((low, result_first, result_near_first))
+            low, result_first, result_near_first, early = tie(
+                (low, result_first, result_near_first, early)
+            )
             held_parts = ([mine for mine, _ in grads], swapped)
             other_one, mine_one = partial
         else:

time: 1080 us -> 1070 us (level)
  starting transfers between devices: 163 us -> 184 us
  waiting for transfers between devices: 455 us -> 434 us
    ppermute x165 -> x166, waiting for transfers between devices: 455 us -> 434 us  [hop(): return lax.ppermute(value, AXES, pairs)]
    ppermute x165 -> x166, starting transfers between devices: 163 us -> 184 us  [hop(): return lax.ppermute(value, AXES, pairs)]
    unnamed x454 -> x460, local copies, waits for them, and re-layouts: 51.1 us -> 58.3 us
  transfers between devices with their start and end apart: 165 -> 166, of which waited for: 66 -> 58; matrix products, arithmetic and copies ran while one was open for 5% -> 5% of each run, Pallas kernels for 31% -> 31%
where the time goes in v6:
time: 1070 us; the launch traced here: 1060 us
  waiting for transfers between devices  434 us (41%)
  Pallas kernels  327 us (31%)
  starting transfers between devices  184 us (17%)
  local copies, waits for them, and re-layouts  81.4 us (8%)
  other arithmetic  31.6 us (3%)
    ppermute x166, waiting for transfers between devices, hop(): return lax.ppermute(value, AXES, pairs)  434 us
    ppermute x166, starting transfers between devices, hop(): return lax.ppermute(value, AXES, pairs)  184 us
    pallas_call x4, Pallas kernels, experts_backward_fast(): pl.pallas_call(body, name='experts_backward', out_shape=shapes, in_specs=...  69.4 us
    pallas_call x4, Pallas kernels, experts_forward_fast(): pl.pallas_call(body, name='experts_forward', out_shape=shapes, in_specs=[...  60.5 us
    unnamed x460, local copies, waits for them, and re-layouts  58.3 us
    pallas_call x2, Pallas kernels, attend_backward_fast(): pl.pallas_call(body, name='attend_backward', out_shape=shapes, in_specs=[...  50.5 us
    pallas_call x6, Pallas kernels, weight_grads_fast(): pl.pallas_call(body, name='weight_grads', out_shape=[shape_of(4, experts,...  47.1 us
    pallas_call x2, Pallas kernels, attend_forward_fast(): pl.pallas_call(body, name='attend_forward', out_shape=shapes, in_specs=[s...  30.8 us
  transfers between devices with their start and end apart: 166, of which 58 were waited for; matrix products, arithmetic and copies ran while one was open for 5% of the time, Pallas kernels for 31%

profile of v6, /device:TPU:0, one launch (start us, length us, event | category | flops | bytes accessed | tf_op | source)
XLA Modules:
  0.0 1061.3 jit_solution(8715677253936140565)
XLA Ops:
  30.2 6.9 collective-permute-done.1
  42.5 8.3 collective-permute-start.9
  53.9 45.8 %collective-permute-done.9.refs_9_ = bf16[3,5,192,128]{3,2,1,0:T(8,128)(2,1)S(1)} collective-permute-done((bf16[3,5,192,128]{3,2,1,0:T(8,128)(2,1)}, bf16[3,5,192,128]{3,2,1,0:T(8,128)(2,1)S(1)}, u32[]{:S(2)}, u32[]{:S(2)}) %collective-permute-start.9) | collective-permute-done | bytes 737312 | tf_op jit(solution)/shard_map/ppermute | solution.py:38
  105.3 18.1 %collective-permute-done.15.refs_10_ = bf16[3,5,192,128]{3,2,1,0:T(8,128)(2,1)} collective-permute-done((bf16[3,5,192,128]{3,2,1,0:T(8,128)(2,1)S(1)}, bf16[3,5,192,128]{3,2,1,0:T(8,128)(2,1)}, u32[]{:S(2)}, u32[]{:S(2)}) %collective-permute-start.15) | collective-permute-done | bytes 737312 | tf_op jit(solution)/shard_map/ppermute | solution.py:38
  131.0 15.2 %attend_forward.2 = (f32[128,1536]{1,0:T(8,128)S(1)}, f32[128,1536]{1,0:T(8,128)S(1)}, bf16[128,1536]{1,0:T(8,128)(2,1)S(1)}, bf16[128,1536]{1,0:T(8,128)(2,1)S(...) custom-call(s32[3]{0:T(128)S(1)} %copy-done.117, ...), custom_call_target="tpu_custom_call" | custom-call | flops 103809024 | tf_op jit(solution)/shard_map/attend_forward/pallas_call | solution.py:694
  147.9 11.5 %collective-permute-done.25 = bf16[128,1536]{1,0:T(8,128)(2,1)S(1)} collective-permute-done((bf16[128,1536]{1,0:T(8,128)(2,1)S(1)}, bf16[128,1536]{1,0:T(8,128)(2,1)S(1)}, u32[]{:S(2)}, u32[]{:S(2)}) %collective-permute-start.25) | collective-permute-done | bytes 393248 | tf_op jit(solution)/shard_map/ppermute | solution.py:38
  163.1 14.5 %collective-permute-done.26.refs_3_ = bf16[256,1536]{1,0:T(8,128)(2,1)S(1)} collective-permute-done((bf16[256,1536]{1,0:T(8,128)(2,1)S(1)}, bf16[256,1536]{1,0:T(8,128)(2,1)S(1)}, u32[]{:S(2)}, u32[]{:S(2)}) %collective-permute-start.26) | collective-permute-done | bytes 786464 | tf_op jit(solution)/shard_map/ppermute | solution.py:38
  180.3 6.4 collective-permute-done.28.refs_5_
  199.8 14.6 %experts_forward.4 = (bf16[256,1536]{1,0:T(8,128)(2,1)}, bf16[128,1536]{1,0:T(8,128)(2,1)S(1)}, bf16[128,1536]{1,0:T(8,128)(2,1)S(1)}, bf16[256,1536]{1,0:T(8,12...) custom-call(s32[3]{0:T(128)S(1)} %copy-done.117, ...), custom_call_target="tpu_custom_call" | custom-call | flops 377487360 | tf_op jit(solution)/shard_map/experts_forward/pallas_call | solution.py:1052
  218.1 7.5 collective-permute-done.37.refs_5_
  235.4 15.6 %experts_forward.5 = (bf16[256,1536]{1,0:T(8,128)(2,1)S(1)}, bf16[128,1536]{1,0:T(8,128)(2,1)S(1)}, bf16[128,1536]{1,0:T(8,128)(2,1)S(1)}, bf16[256,1536]{1,0:T(...) custom-call(s32[3]{0:T(128)S(1)} %copy-done.117, ...), custom_call_target="tpu_custom_call" | custom-call | flops 377487360 | tf_op jit(solution)/shard_map/experts_forward/pallas_call | solution.py:1052
  258.1 11.5 %collective-permute-done.47.refs_8_ = bf16[3,5,192,128]{3,2,1,0:T(8,128)(2,1)S(1)} collective-permute-done((bf16[3,5,192,128]{3,2,1,0:T(8,128)(2,1)S(1)}, bf16[3,5,192,128]{3,2,1,0:T(8,128)(2,1)S(1)}, u32[]{:S(2)}, u32[]{:S(2)}) %collective-permute-start.47) | collective-permute-done | bytes 737312 | tf_op jit(solution)/shard_map/ppermute | solution.py:38
  305.3 23.6 %collective-permute-done.51.refs_4_ = bf16[128,1536]{1,0:T(8,128)(2,1)S(1)} collective-permute-done((bf16[128,1536]{1,0:T(8,128)(2,1)}, bf16[128,1536]{1,0:T(8,128)(2,1)S(1)}, u32[]{:S(2)}, u32[]{:S(2)}) %collective-permute-start.51) | collective-permute-done | bytes 393248 | tf_op jit(solution)/shard_map/ppermute | solution.py:38
  336.5 28.2 %collective-permute-done.57.refs_9_ = bf16[3,5,192,128]{3,2,1,0:T(8,128)(2,1)S(1)} collective-permute-done((bf16[3,5,192,128]{3,2,1,0:T(8,128)(2,1)S(1)}, bf16[3,5,192,128]{3,2,1,0:T(8,128)(2,1)S(1)}, u32[]{:S(2)}, u32[]{:S(2)}) %collective-permute-start.57) | collective-permute-done | bytes 737312 | tf_op jit(solution)/shard_map/ppermute | solution.py:38
  372.7 15.5 %attend_forward.3 = (f32[128,1536]{1,0:T(8,128)S(1)}, f32[128,1536]{1,0:T(8,128)S(1)}, bf16[128,1536]{1,0:T(8,128)(2,1)S(1)}, bf16[128,1536]{1,0:T(8,128)(2,1)S(...) custom-call(s32[3]{0:T(128)S(1)} %copy-done.117, ...), custom_call_target="tpu_custom_call" | custom-call | flops 103809024 | tf_op jit(solution)/shard_map/attend_forward/pallas_call | solution.py:694
  388.4 12.9 %collective-permute-done.64 = bf16[128,1536]{1,0:T(8,128)(2,1)S(1)} collective-permute-done((bf16[128,1536]{1,0:T(8,128)(2,1)S(1)}, bf16[128,1536]{1,0:T(8,128)(2,1)S(1)}, u32[]{:S(2)}, u32[]{:S(2)}) %collective-permute-start.64) | collective-permute-done | bytes 393248 | tf_op jit(solution)/shard_map/ppermute | solution.py:38
  404.3 15.9 %collective-permute-done.65.refs_3_ = bf16[256,1536]{1,0:T(8,128)(2,1)S(1)} collective-permute-done((bf16[256,1536]{1,0:T(8,128)(2,1)S(1)}, bf16[256,1536]{1,0:T(8,128)(2,1)S(1)}, u32[]{:S(2)}, u32[]{:S(2)}) %collective-permute-start.65) | collective-permute-done | bytes 786464 | tf_op jit(solution)/shard_map/ppermute | solution.py:38
  423.4 6.3 collective-permute-done.67.refs_5_
  443.6 14.6 %experts_forward.6 = (bf16[256,1536]{1,0:T(8,128)(2,1)}, bf16[128,1536]{1,0:T(8,128)(2,1)S(1)}, bf16[128,1536]{1,0:T(8,128)(2,1)S(1)}, bf16[256,1536]{1,0:T(8,12...) custom-call(s32[3]{0:T(128)S(1)} %copy-done.117, ...), custom_call_target="tpu_custom_call" | custom-call | flops 377487360 | tf_op jit(solution)/shard_map/experts_forward/pallas_call | solution.py:1052
  461.5 7.9 collective-permute-done.77.refs_5_
  476.9 15.6 %experts_forward.7 = (bf16[256,1536]{1,0:T(8,128)(2,1)S(1)}, bf16[128,1536]{1,0:T(8,128)(2,1)S(1)}, bf16[128,1536]{1,0:T(8,128)(2,1)S(1)}, bf16[256,1536]{1,0:T(...) custom-call(s32[3]{0:T(128)S(1)} %copy-done.117, ...), custom_call_target="tpu_custom_call" | custom-call | flops 377487360 | tf_op jit(solution)/shard_map/experts_forward/pallas_call | solution.py:1052
  499.5 6.5 collective-permute-done.82.refs_5_
  511.1 17.0 %experts_backward.4 = (bf16[256,1536]{1,0:T(8,128)(2,1)}, bf16[128,1536]{1,0:T(8,128)(2,1)S(1)}, bf16[128,1536]{1,0:T(8,128)(2,1)S(1)}, bf16[256,1536]{1,0:T(8,1...) custom-call(s32[3]{0:T(128)S(1)} %copy-done.117, ...), custom_call_target="tpu_custom_call" | custom-call | flops 377487360 | tf_op jit(solution)/shard_map/experts_backward/pallas_call | solution.py:1136
  540.5 17.7 %experts_backward.5 = (bf16[256,1536]{1,0:T(8,128)(2,1)}, bf16[128,1536]{1,0:T(8,128)(2,1)S(1)}, bf16[128,1536]{1,0:T(8,128)(2,1)S(1)}, bf16[256,1536]{1,0:T(8,1...) custom-call(s32[3]{0:T(128)S(1)} %copy-done.117, ...), custom_call_target="tpu_custom_call" | custom-call | flops 377487360 | tf_op jit(solution)/shard_map/experts_backward/pallas_call | solution.py:1136
  562.8 7.8 weight_grads.6
  574.8 7.9 weight_grads.7
  612.1 7.6 weight_grads.8
  636.5 25.3 %attend_backward.2 = (f32[128,1536]{1,0:T(8,128)}, bf16[128,1536]{1,0:T(8,128)(2,1)}, bf16[768,4224]{1,0:T(8,128)(2,1)}, bf16[768,4224]{1,0:T(8,128)(2,1)}) custom-call(s32[3]{0:T(128)} %pad_add_fusion.where.refs_0_, bf16[128,1536]{1,0:T(8,128)(2,1)} %broadcast_in_dim.61.refs_1_, bf16[128,1536]{1,0:T(8,128)(2,1)} %refs_2_.3, ...), custom_call_target="tpu_custom_call" | custom-call | flops 207618048 | tf_op jit(solution)/shard_map/attend_backward/pallas_call | solution.py:863
  687.2 13.0 %collective-permute-done.110.refs_3_ = bf16[256,1536]{1,0:T(8,128)(2,1)S(1)} collective-permute-done((bf16[256,1536]{1,0:T(8,128)(2,1)S(1)}, bf16[256,1536]{1,0:T(8,128)(2,1)S(1)}, u32[]{:S(2)}, u32[]{:S(2)}) %collective-permute-start.110) | collective-permute-done | bytes 786464 | tf_op jit(solution)/shard_map/ppermute | solution.py:38
  704.2 6.8 collective-permute-done.112.refs_5_
  720.4 17.0 %experts_backward.6 = (bf16[256,1536]{1,0:T(8,128)(2,1)}, bf16[128,1536]{1,0:T(8,128)(2,1)S(1)}, bf16[128,1536]{1,0:T(8,128)(2,1)S(1)}, bf16[256,1536]{1,0:T(8,1...) custom-call(s32[3]{0:T(128)S(1)} %copy-done.118, ...), custom_call_target="tpu_custom_call" | custom-call | flops 377487360 | tf_op jit(solution)/shard_map/experts_backward/pallas_call | solution.py:1136
  737.4 6.9 collective-permute-done.118
  746.7 7.3 merge_cores.3
  761.5 17.7 %experts_backward.7 = (bf16[256,1536]{1,0:T(8,128)(2,1)}, bf16[128,1536]{1,0:T(8,128)(2,1)S(1)}, bf16[128,1536]{1,0:T(8,128)(2,1)S(1)}, bf16[256,1536]{1,0:T(8,1...) custom-call(s32[3]{0:T(128)S(1)} %copy-done.118, ...), custom_call_target="tpu_custom_call" | custom-call | flops 377487360 | tf_op jit(solution)/shard_map/experts_backward/pallas_call | solution.py:1136
  780.7 9.9 collective-permute-done.124
  798.3 7.6 weight_grads.9
  810.4 7.9 weight_grads.10
  821.9 8.7 collective-permute-done.132.two_tail
  834.3 8.3 weight_grads.11
  893.8 8.2 collective-permute-done.138.refs_4_
  908.0 25.2 %attend_backward.3 = (f32[128,1536]{1,0:T(8,128)}, bf16[128,1536]{1,0:T(8,128)(2,1)}, bf16[576,4224]{1,0:T(8,128)(2,1)}, bf16[192,4224]{1,0:T(8,128)(2,1)}, bf16...) custom-call(s32[3]{0:T(128)} %pad_add_fusion.where.refs_0_, bf16[128,1536]{1,0:T(8,128)(2,1)} %broadcast_in_dim.61.refs_1_, ...), custom_call_target="tpu_custom_call" | custom-call | flops 207618048 | tf_op jit(solution)/shard_map/attend_backward/pallas_call | solution.py:863
  933.2 7.3 collective-permute-done.147
  941.3 7.5 collective-permute-done.149.arrived
  953.8 7.6 collective-permute-done.150.refs_1_
  969.6 19.3 %collective-permute-done.152 = bf16[288,2048]{1,0:T(8,128)(2,1)S(1)} collective-permute-done((bf16[288,2048]{1,0:T(8,128)(2,1)S(1)}, bf16[288,2048]{1,0:T(8,128)(2,1)S(1)}, u32[]{:S(2)}, u32[]{:S(2)}) %collective-permute-start.152) | collective-permute-done | bytes 1179680 | tf_op jit(solution)/shard_map/ppermute | solution.py:38
  999.6 10.8 %collective-permute-done.161.refs_2_ = bf16[3,5,192,128]{3,2,1,0:T(8,128)(2,1)} collective-permute-done((bf16[3,5,192,128]{3,2,1,0:T(8,128)(2,1)}, bf16[3,5,192,128]{3,2,1,0:T(8,128)(2,1)}, u32[]{:S(2)}, u32[]{:S(2)}) %collective-permute-start.161) | collective-permute-done | bytes 737312 | tf_op jit(solution)/shard_map/ppermute | solution.py:38
  1028.9 8.4 collective-permute-done.163
  1037.2 20.8 %collective-permute-done.164 = bf16[48,4224]{1,0:T(8,128)(2,1)S(1)} collective-permute-done((bf16[48,4224]{1,0:T(8,128)(2,1)S(1)}, bf16[48,4224]{1,0:T(8,128)(2,1)S(1)}, u32[]{:S(2)}, u32[]{:S(2)}) %collective-permute-start.164) | collective-permute-done | bytes 405536 | tf_op jit(solution)/shard_map/ppermute | solution.py:38
  (885 shorter events, 424.8 us)
Async XLA Ops:
  7.9 29.1 %collective-permute-start.1 = (bf16[48,4224]{1,0:T(8,128)(2,1)}, bf16[48,4224]{1,0:T(8,128)(2,1)S(1)}, u32[]{:S(2)}, u32[]{:S(2)}) collective-permute-start(bf16[48,4224]{1,0:T(8,128)(2,1)} %get-tuple-element.504), channel_id=1, source_target_pairs={{0,16},{1,17},{2,18},{3,19},{4,20},{5,21},{6,22},{7,23},{8,24},{9,... | collective-permute-start | bytes 1216520 | tf_op jit(solution)/shard_map/ppermute | solution.py:38
  10.5 26.5 %collective-permute-start.2 = (bf16[48,4224]{1,0:T(8,128)(2,1)}, bf16[48,4224]{1,0:T(8,128)(2,1)S(1)}, u32[]{:S(2)}, u32[]{:S(2)}) collective-permute-start(bf16[48,4224]{1,0:T(8,128)(2,1)} %get-tuple-element.504), channel_id=1, source_target_pairs={{0,24},{1,25},{2,26},{3,27},{4,28},{5,29},{6,30},{7,31},{8,0},{9,1... | collective-permute-start | bytes 1216520 | tf_op jit(solution)/shard_map/ppermute | solution.py:38
  39.4 63.4 %collective-permute-start.10 = (bf16[192,4224]{1,0:T(8,128)(2,1)}, bf16[192,4224]{1,0:T(8,128)(2,1)S(1)}, u32[]{:S(2)}, u32[]{:S(2)}) collective-permute-start(bf16[192,4224]{1,0:T(8,128)(2,1)} %constant_dynamic-update-slice_fusion.refs_5_.refs_21_), channel_id=1, source_target_pairs={{0,4},{1,5},{2,6},{3,7},{4,0},{5,1},{6,2},{7,3},{8,12},{9,13},{10,... | collective-permute-start | bytes 4866056 | tf_op jit(solution)/shard_map/ppermute | solution.py:38
  39.4 63.4 %collective-permute-start.6 = (bf16[192,4224]{1,0:T(8,128)(2,1)}, bf16[192,4224]{1,0:T(8,128)(2,1)S(1)}, u32[]{:S(2)}, u32[]{:S(2)}) collective-permute-start(bf16[192,4224]{1,0:T(8,128)(2,1)} %constant_dynamic-update-slice_fusion.refs_5_.refs_21_), channel_id=1, source_target_pairs={{0,1},{1,0},{2,3},{3,2},{4,5},{5,4},{6,7},{7,6},{8,9},{9,8},{10,11... | collective-permute-start | bytes 4866056 | tf_op jit(solution)/shard_map/ppermute | solution.py:38
  40.9 61.9 %collective-permute-start.7 = (bf16[192,4224]{1,0:T(8,128)(2,1)}, bf16[192,4224]{1,0:T(8,128)(2,1)S(1)}, u32[]{:S(2)}, u32[]{:S(2)}) collective-permute-start(bf16[192,4224]{1,0:T(8,128)(2,1)} %constant_dynamic-update-slice_fusion.refs_5_.refs_21_), channel_id=1, source_target_pairs={{0,2},{1,3},{2,0},{3,1},{4,6},{5,7},{6,4},{7,5},{8,10},{9,11},{10,... | collective-permute-start | bytes 4866056 | tf_op jit(solution)/shard_map/ppermute | solution.py:38
  42.5 57.2 %collective-permute-start.9 = (bf16[3,5,192,128]{3,2,1,0:T(8,128)(2,1)}, bf16[3,5,192,128]{3,2,1,0:T(8,128)(2,1)S(1)}, u32[]{:S(2)}, u32[]{:S(2)}) collective-permute-start(bf16[3,5,192,128]{3,2,1,0:T(8,128)(2,1)} %get-tuple-element.517), channel_id=1, source_target_pairs={{0,16},{1,17},{2,18},{3,19},{4,20},{5,21},{6,22},{7,23},{8,24},{9,... | collective-permute-start | bytes 2211848 | tf_op jit(solution)/shard_map/ppermute | solution.py:38
  50.8 48.9 %collective-permute-start.8 = (bf16[3,5,192,128]{3,2,1,0:T(8,128)(2,1)S(1)}, bf16[3,5,192,128]{3,2,1,0:T(8,128)(2,1)S(1)}, u32[]{:S(2)}, u32[]{:S(2)}) collective-permute-start(bf16[3,5,192,128]{3,2,1,0:T(8,128)(2,1)S(1)} %copy-done.220), channel_id=1, source_target_pairs={{0,8},{1,9},{2,10},{3,11},{4,12},{5,13},{6,14},{7,15},{8,16},{9,17... | collective-permute-start | bytes 2211848 | tf_op jit(solution)/shard_map/ppermute | solution.py:38
  255.4 26.5 %collective-permute-start.43 = (bf16[128,1536]{1,0:T(8,128)(2,1)S(1)}, bf16[128,1536]{1,0:T(8,128)(2,1)S(1)}, u32[]{:S(2)}, u32[]{:S(2)}) collective-permute-start(bf16[128,1536]{1,0:T(8,128)(2,1)S(1)} %add_convert_fusion.20), channel_id=1, source_target_pairs={{0,2},{1,3},{2,0},{3,1},{4,6},{5,7},{6,4},{7,5},{8,10},{9,11},{10,... | collective-permute-start | bytes 1179656 | tf_op jit(solution)/shard_map/ppermute | solution.py:38
  287.0 41.9 %collective-permute-start.53 = (bf16[192,4224]{1,0:T(8,128)(2,1)}, bf16[192,4224]{1,0:T(8,128)(2,1)}, u32[]{:S(2)}, u32[]{:S(2)}) collective-permute-start(bf16[192,4224]{1,0:T(8,128)(2,1)} %constant_dynamic-update-slice_fusion.8.refs_11_.refs_21_), channel_id=1, source_target_pairs={{0,1},{1,0},{2,3},{3,2},{4,5},{5,4},{6,7},{7,6},{8,9},{9,8},{10,11... | collective-permute-start | bytes 4866056 | tf_op jit(solution)/shard_map/ppermute | solution.py:38
  288.0 40.9 %collective-permute-start.54 = (bf16[192,4224]{1,0:T(8,128)(2,1)}, bf16[192,4224]{1,0:T(8,128)(2,1)}, u32[]{:S(2)}, u32[]{:S(2)}) collective-permute-start(bf16[192,4224]{1,0:T(8,128)(2,1)} %constant_dynamic-update-slice_fusion.8.refs_11_.refs_21_), channel_id=1, source_target_pairs={{0,2},{1,3},{2,0},{3,1},{4,6},{5,7},{6,4},{7,5},{8,10},{9,11},{10,... | collective-permute-start | bytes 4866056 | tf_op jit(solution)/shard_map/ppermute | solution.py:38
  298.3 30.6 %collective-permute-start.51 = (bf16[128,1536]{1,0:T(8,128)(2,1)}, bf16[128,1536]{1,0:T(8,128)(2,1)S(1)}, u32[]{:S(2)}, u32[]{:S(2)}) collective-permute-start(bf16[128,1536]{1,0:T(8,128)(2,1)} %get-tuple-element.594), channel_id=1, source_target_pairs={{0,16},{1,17},{2,18},{3,19},{4,20},{5,21},{6,22},{7,23},{8,24},{9,... | collective-permute-start | bytes 1179656 | tf_op jit(solution)/shard_map/ppermute | solution.py:38
  299.0 29.9 %collective-permute-start.52 = (bf16[128,1536]{1,0:T(8,128)(2,1)}, bf16[128,1536]{1,0:T(8,128)(2,1)S(1)}, u32[]{:S(2)}, u32[]{:S(2)}) collective-permute-start(bf16[128,1536]{1,0:T(8,128)(2,1)} %get-tuple-element.595), channel_id=1, source_target_pairs={{0,8},{1,9},{2,10},{3,11},{4,12},{5,13},{6,14},{7,15},{8,16},{9,17... | collective-permute-start | bytes 1179656 | tf_op jit(solution)/shard_map/ppermute | solution.py:38
  328.9 35.8 %collective-permute-start.58 = (bf16[192,4224]{1,0:T(8,128)(2,1)}, bf16[192,4224]{1,0:T(8,128)(2,1)S(1)}, u32[]{:S(2)}, u32[]{:S(2)}) collective-permute-start(bf16[192,4224]{1,0:T(8,128)(2,1)} %collective-permute-done.53.refs_12_.refs_22_), channel_id=1, source_target_pairs={{0,4},{1,5},{2,6},{3,7},{4,0},{5,1},{6,2},{7,3},{8,12},{9,13},{10,... | collective-permute-start | bytes 4866056 | tf_op jit(solution)/shard_map/ppermute | solution.py:38
  329.0 35.7 %collective-permute-start.59 = (bf16[192,4224]{1,0:T(8,128)(2,1)}, bf16[192,4224]{1,0:T(8,128)(2,1)S(1)}, u32[]{:S(2)}, u32[]{:S(2)}) collective-permute-start(bf16[192,4224]{1,0:T(8,128)(2,1)} %collective-permute-done.54.refs_13_.refs_23_), channel_id=1, source_target_pairs={{0,4},{1,5},{2,6},{3,7},{4,0},{5,1},{6,2},{7,3},{8,12},{9,13},{10,... | collective-permute-start | bytes 4866056 | tf_op jit(solution)/shard_map/ppermute | solution.py:38
  329.5 35.1 %collective-permute-start.57 = (bf16[3,5,192,128]{3,2,1,0:T(8,128)(2,1)S(1)}, bf16[3,5,192,128]{3,2,1,0:T(8,128)(2,1)S(1)}, u32[]{:S(2)}, u32[]{:S(2)}) collective-permute-start(bf16[3,5,192,128]{3,2,1,0:T(8,128)(2,1)S(1)} %copy-done.217), channel_id=1, source_target_pairs={{0,16},{1,17},{2,18},{3,19},{4,20},{5,21},{6,22},{7,23},{8,24},{9,... | collective-permute-start | bytes 2211848 | tf_op jit(solution)/shard_map/ppermute | solution.py:38
  333.1 31.6 %collective-permute-start.56 = (bf16[192,2176]{1,0:T(8,128)(2,1)S(1)}, bf16[192,2176]{1,0:T(8,128)(2,1)S(1)}, u32[]{:S(2)}, u32[]{:S(2)}) collective-permute-start(bf16[192,2176]{1,0:T(8,128)(2,1)S(1)} %slice.238), channel_id=1, source_target_pairs={{0,1},{1,0},{2,3},{3,2},{4,5},{5,4},{6,7},{7,6},{8,9},{9,8},{10,11... | collective-permute-start | bytes 2506760 | tf_op jit(solution)/shard_map/ppermute | solution.py:38
  335.5 29.2 %collective-permute-start.55 = (bf16[192,2048]{1,0:T(8,128)(2,1)S(1)}, bf16[192,2048]{1,0:T(8,128)(2,1)S(1)}, u32[]{:S(2)}, u32[]{:S(2)}) collective-permute-start(bf16[192,2048]{1,0:T(8,128)(2,1)S(1)} %slice.237), channel_id=1, source_target_pairs={{0,2},{1,3},{2,0},{3,1},{4,6},{5,7},{6,4},{7,5},{8,10},{9,11},{10,... | collective-permute-start | bytes 2359304 | tf_op jit(solution)/shard_map/ppermute | solution.py:38
  582.8 37.9 %collective-permute-start.100 = (bf16[4,5,192,128]{3,2,1,0:T(8,128)(2,1)}, bf16[4,5,192,128]{3,2,1,0:T(8,128)(2,1)}, u32[]{:S(2)}, u32[]{:S(2)}) collective-permute-start(bf16[4,5,192,128]{3,2,1,0:T(8,128)(2,1)} %get-tuple-element.723), channel_id=1, source_target_pairs={{0,4},{1,5},{2,6},{3,7},{4,0},{5,1},{6,2},{7,3},{8,12},{9,13},{10,... | collective-permute-start | bytes 2949128 | tf_op jit(solution)/shard_map/ppermute | solution.py:38
  591.6 30.4 %collective-permute-start.98 = (bf16[128,1536]{1,0:T(8,128)(2,1)}, bf16[128,1536]{1,0:T(8,128)(2,1)}, u32[]{:S(2)}, u32[]{:S(2)}) collective-permute-start(bf16[128,1536]{1,0:T(8,128)(2,1)} %get-tuple-element.720.refs_5_), channel_id=1, source_target_pairs={{0,16},{1,17},{2,18},{3,19},{4,20},{5,21},{6,22},{7,23},{8,24},{9,... | collective-permute-start | bytes 1179656 | tf_op jit(solution)/shard_map/ppermute | solution.py:38
  593.7 28.3 %collective-permute-start.99 = (bf16[128,1536]{1,0:T(8,128)(2,1)}, bf16[128,1536]{1,0:T(8,128)(2,1)}, u32[]{:S(2)}, u32[]{:S(2)}) collective-permute-start(bf16[128,1536]{1,0:T(8,128)(2,1)} %get-tuple-element.721), channel_id=1, source_target_pairs={{0,8},{1,9},{2,10},{3,11},{4,12},{5,13},{6,14},{7,15},{8,16},{9,17... | collective-permute-start | bytes 1179656 | tf_op jit(solution)/shard_map/ppermute | solution.py:38
  625.4 36.5 %collective-permute-start.103 = (bf16[256,1536]{1,0:T(8,128)(2,1)}, bf16[256,1536]{1,0:T(8,128)(2,1)S(1)}, u32[]{:S(2)}, u32[]{:S(2)}) collective-permute-start(bf16[256,1536]{1,0:T(8,128)(2,1)} %get-tuple-element.758), channel_id=1, source_target_pairs={{0,1},{1,0},{2,3},{3,2},{4,5},{5,4},{6,7},{7,6},{8,9},{9,8},{10,11... | collective-permute-start | bytes 2359304 | tf_op jit(solution)/shard_map/ppermute | solution.py:38
  626.5 35.5 %collective-permute-start.104 = (bf16[256,1536]{1,0:T(8,128)(2,1)}, bf16[256,1536]{1,0:T(8,128)(2,1)S(1)}, u32[]{:S(2)}, u32[]{:S(2)}) collective-permute-start(bf16[256,1536]{1,0:T(8,128)(2,1)} %get-tuple-element.759), channel_id=1, source_target_pairs={{0,2},{1,3},{2,0},{3,1},{4,6},{5,7},{6,4},{7,5},{8,10},{9,11},{10,... | collective-permute-start | bytes 2359304 | tf_op jit(solution)/shard_map/ppermute | solution.py:38
  627.4 34.5 %collective-permute-start.101 = (bf16[256,1536]{1,0:T(8,128)(2,1)S(1)}, bf16[256,1536]{1,0:T(8,128)(2,1)S(1)}, u32[]{:S(2)}, u32[]{:S(2)}) collective-permute-start(bf16[256,1536]{1,0:T(8,128)(2,1)S(1)} %copy-done.135), channel_id=1, source_target_pairs={{0,1},{1,0},{2,3},{3,2},{4,5},{5,4},{6,7},{7,6},{8,9},{9,8},{10,11... | collective-permute-start | bytes 2359304 | tf_op jit(solution)/shard_map/ppermute | solution.py:38
  628.5 33.5 %collective-permute-start.102 = (bf16[256,1536]{1,0:T(8,128)(2,1)S(1)}, bf16[256,1536]{1,0:T(8,128)(2,1)S(1)}, u32[]{:S(2)}, u32[]{:S(2)}) collective-permute-start(bf16[256,1536]{1,0:T(8,128)(2,1)S(1)} %copy-done.133), channel_id=1, source_target_pairs={{0,2},{1,3},{2,0},{3,1},{4,6},{5,7},{6,4},{7,5},{8,10},{9,11},{10,... | collective-permute-start | bytes 2359304 | tf_op jit(solution)/shard_map/ppermute | solution.py:38
  629.5 32.4 %collective-permute-start.105 = (bf16[2,5,192,128]{3,2,1,0:T(8,128)(2,1)S(1)}, bf16[2,5,192,128]{3,2,1,0:T(8,128)(2,1)S(1)}, u32[]{:S(2)}, u32[]{:S(2)}) collective-permute-start(bf16[2,5,192,128]{3,2,1,0:T(8,128)(2,1)S(1)} %pad_maximum_fusion.2), channel_id=1, source_target_pairs={{0,16},{1,17},{2,18},{3,19},{4,20},{5,21},{6,22},{7,23},{8,24},{9,... | collective-permute-start | bytes 1474568 | tf_op jit(solution)/shard_map/ppermute | solution.py:38
  680.2 66.4 %collective-permute-start.122 = (bf16[768,4224]{1,0:T(8,128)(2,1)}, bf16[768,4224]{1,0:T(8,128)(2,1)}, u32[]{:S(2)}, u32[]{:S(2)}) collective-permute-start(bf16[768,4224]{1,0:T(8,128)(2,1)} %get-tuple-element.816), channel_id=1, source_target_pairs={{0,4},{1,5},{2,6},{3,7},{4,0},{5,1},{6,2},{7,3},{8,12},{9,13},{10,... | collective-permute-start | bytes 19464200 | tf_op jit(solution)/shard_map/ppermute | solution.py:38
  711.9 32.5 %collective-permute-start.116 = (bf16[256,1536]{1,0:T(8,128)(2,1)S(1)}, bf16[256,1536]{1,0:T(8,128)(2,1)S(1)}, u32[]{:S(2)}, u32[]{:S(2)}) collective-permute-start(bf16[256,1536]{1,0:T(8,128)(2,1)S(1)} %constant_dynamic-update-slice_fusion.22.refs_2_), channel_id=1, source_target_pairs={{0,1},{1,0},{2,3},{3,2},{4,5},{5,4},{6,7},{7,6},{8,9},{9,8},{10,11... | collective-permute-start | bytes 2359304 | tf_op jit(solution)/shard_map/ppermute | solution.py:38
  713.1 31.3 %collective-permute-start.117 = (bf16[256,1536]{1,0:T(8,128)(2,1)S(1)}, bf16[256,1536]{1,0:T(8,128)(2,1)S(1)}, u32[]{:S(2)}, u32[]{:S(2)}) collective-permute-start(bf16[256,1536]{1,0:T(8,128)(2,1)S(1)} %constant_dynamic-update-slice_fusion.22.refs_2_), channel_id=1, source_target_pairs={{0,2},{1,3},{2,0},{3,1},{4,6},{5,7},{6,4},{7,5},{8,10},{9,11},{10,... | collective-permute-start | bytes 2359304 | tf_op jit(solution)/shard_map/ppermute | solution.py:38
  716.9 27.5 %collective-permute-start.118 = (bf16[128,1536]{1,0:T(8,128)(2,1)}, bf16[128,1536]{1,0:T(8,128)(2,1)S(1)}, u32[]{:S(2)}, u32[]{:S(2)}) collective-permute-start(bf16[128,1536]{1,0:T(8,128)(2,1)} %get-tuple-element.793), channel_id=1, source_target_pairs={{0,16},{1,17},{2,18},{3,19},{4,20},{5,21},{6,22},{7,23},{8,24},{9,... | collective-permute-start | bytes 1179656 | tf_op jit(solution)/shard_map/ppermute | solution.py:38
  755.8 36.7 %collective-permute-start.123 = (bf16[384,2176]{1,0:T(8,128)(2,1)}, bf16[384,2176]{1,0:T(8,128)(2,1)}, u32[]{:S(2)}, u32[]{:S(2)}) collective-permute-start(bf16[384,2176]{1,0:T(8,128)(2,1)} %get-tuple-element.826), channel_id=1, source_target_pairs={{0,1},{1,0},{2,3},{3,2},{4,5},{5,4},{6,7},{7,6},{8,9},{9,8},{10,11... | collective-permute-start | bytes 5013512 | tf_op jit(solution)/shard_map/ppermute | solution.py:38
  756.8 33.8 %collective-permute-start.124 = (bf16[384,2048]{1,0:T(8,128)(2,1)}, bf16[384,2048]{1,0:T(8,128)(2,1)}, u32[]{:S(2)}, u32[]{:S(2)}) collective-permute-start(bf16[384,2048]{1,0:T(8,128)(2,1)} %get-tuple-element.827), channel_id=1, source_target_pairs={{0,2},{1,3},{2,0},{3,1},{4,6},{5,7},{6,4},{7,5},{8,10},{9,11},{10,... | collective-permute-start | bytes 4718600 | tf_op jit(solution)/shard_map/ppermute | solution.py:38
  818.4 29.8 %collective-permute-start.134 = (bf16[4,5,192,128]{3,2,1,0:T(8,128)(2,1)}, bf16[4,5,192,128]{3,2,1,0:T(8,128)(2,1)S(1)}, u32[]{:S(2)}, u32[]{:S(2)}) collective-permute-start(bf16[4,5,192,128]{3,2,1,0:T(8,128)(2,1)} %get-tuple-element.856), channel_id=1, source_target_pairs={{0,4},{1,5},{2,6},{3,7},{4,0},{5,1},{6,2},{7,3},{8,12},{9,13},{10,... | collective-permute-start | bytes 2949128 | tf_op jit(solution)/shard_map/ppermute | solution.py:38
  819.8 29.3 %collective-permute-start.129 = (bf16[256,1536]{1,0:T(8,128)(2,1)}, bf16[256,1536]{1,0:T(8,128)(2,1)S(1)}, u32[]{:S(2)}, u32[]{:S(2)}) collective-permute-start(bf16[256,1536]{1,0:T(8,128)(2,1)} %get-tuple-element.852), channel_id=1, source_target_pairs={{0,1},{1,0},{2,3},{3,2},{4,5},{5,4},{6,7},{7,6},{8,9},{9,8},{10,11... | collective-permute-start | bytes 2359304 | tf_op jit(solution)/shard_map/ppermute | solution.py:38
  820.9 28.2 %collective-permute-start.130 = (bf16[256,1536]{1,0:T(8,128)(2,1)S(1)}, bf16[256,1536]{1,0:T(8,128)(2,1)S(1)}, u32[]{:S(2)}, u32[]{:S(2)}) collective-permute-start(bf16[256,1536]{1,0:T(8,128)(2,1)S(1)} %copy-done.215), channel_id=1, source_target_pairs={{0,2},{1,3},{2,0},{3,1},{4,6},{5,7},{6,4},{7,5},{8,10},{9,11},{10,... | collective-permute-start | bytes 2359304 | tf_op jit(solution)/shard_map/ppermute | solution.py:38
  821.9 26.3 %collective-permute-start.135 = (bf16[3,5,192,128]{3,2,1,0:T(8,128)(2,1)}, bf16[3,5,192,128]{3,2,1,0:T(8,128)(2,1)S(1)}, u32[]{:S(2)}, u32[]{:S(2)}) collective-permute-start(bf16[3,5,192,128]{3,2,1,0:T(8,128)(2,1)} %get-tuple-element.869), channel_id=1, source_target_pairs={{0,24},{1,25},{2,26},{3,27},{4,28},{5,29},{6,30},{7,31},{8,0},{9,1... | collective-permute-start | bytes 2211848 | tf_op jit(solution)/shard_map/ppermute | solution.py:38
  902.1 31.0 %collective-permute-start.145 = (bf16[128,1536]{1,0:T(8,128)(2,1)S(1)}, bf16[128,1536]{1,0:T(8,128)(2,1)S(1)}, u32[]{:S(2)}, u32[]{:S(2)}) collective-permute-start(bf16[128,1536]{1,0:T(8,128)(2,1)S(1)} %add_convert_fusion.6), channel_id=1, source_target_pairs={{0,2},{1,3},{2,0},{3,1},{4,6},{5,7},{6,4},{7,5},{8,10},{9,11},{10,... | collective-permute-start | bytes 1179656 | tf_op jit(solution)/shard_map/ppermute | solution.py:38
  903.3 29.9 %collective-permute-start.146 = (bf16[48,4224]{1,0:T(8,128)(2,1)S(1)}, bf16[48,4224]{1,0:T(8,128)(2,1)S(1)}, u32[]{:S(2)}, u32[]{:S(2)}) collective-permute-start(bf16[48,4224]{1,0:T(8,128)(2,1)S(1)} %get-tuple-element.1010), channel_id=1, source_target_pairs={{0,24},{1,25},{2,26},{3,27},{4,28},{5,29},{6,30},{7,31},{8,0},{9,1... | collective-permute-start | bytes 1216520 | tf_op jit(solution)/shard_map/ppermute | solution.py:38
  903.3 37.1 %collective-permute-start.147 = (bf16[48,4224]{1,0:T(8,128)(2,1)S(1)}, bf16[48,4224]{1,0:T(8,128)(2,1)S(1)}, u32[]{:S(2)}, u32[]{:S(2)}) collective-permute-start(bf16[48,4224]{1,0:T(8,128)(2,1)S(1)} %get-tuple-element.1009), channel_id=1, source_target_pairs={{0,16},{1,17},{2,18},{3,19},{4,20},{5,21},{6,22},{7,23},{8,24},{9,... | collective-permute-start | bytes 1216520 | tf_op jit(solution)/shard_map/ppermute | solution.py:38
  905.4 35.1 %collective-permute-start.148 = (bf16[48,4224]{1,0:T(8,128)(2,1)S(1)}, bf16[48,4224]{1,0:T(8,128)(2,1)S(1)}, u32[]{:S(2)}, u32[]{:S(2)}) collective-permute-start(bf16[48,4224]{1,0:T(8,128)(2,1)S(1)} %get-tuple-element.1008), channel_id=1, source_target_pairs={{0,8},{1,9},{2,10},{3,11},{4,12},{5,13},{6,14},{7,15},{8,16},{9,17... | collective-permute-start | bytes 1216520 | tf_op jit(solution)/shard_map/ppermute | solution.py:38
  961.5 28.3 %collective-permute-start.151 = (bf16[288,2176]{1,0:T(8,128)(2,1)S(1)}, bf16[288,2176]{1,0:T(8,128)(2,1)S(1)}, u32[]{:S(2)}, u32[]{:S(2)}) collective-permute-start(bf16[288,2176]{1,0:T(8,128)(2,1)S(1)} %get-tuple-element.944), channel_id=1, source_target_pairs={{0,1},{1,0},{2,3},{3,2},{4,5},{5,4},{6,7},{7,6},{8,9},{9,8},{10,11... | collective-permute-start | bytes 3760136 | tf_op jit(solution)/shard_map/ppermute | solution.py:38
  962.5 26.4 %collective-permute-start.152 = (bf16[288,2048]{1,0:T(8,128)(2,1)S(1)}, bf16[288,2048]{1,0:T(8,128)(2,1)S(1)}, u32[]{:S(2)}, u32[]{:S(2)}) collective-permute-start(bf16[288,2048]{1,0:T(8,128)(2,1)S(1)} %get-tuple-element.945), channel_id=1, source_target_pairs={{0,2},{1,3},{2,0},{3,1},{4,6},{5,7},{6,4},{7,5},{8,10},{9,11},{10,... | collective-permute-start | bytes 3538952 | tf_op jit(solution)/shard_map/ppermute | solution.py:38
  963.6 35.0 %collective-permute-start.162 = (bf16[3,5,192,128]{3,2,1,0:T(8,128)(2,1)}, bf16[3,5,192,128]{3,2,1,0:T(8,128)(2,1)S(1)}, u32[]{:S(2)}, u32[]{:S(2)}) collective-permute-start(bf16[3,5,192,128]{3,2,1,0:T(8,128)(2,1)} %get-tuple-element.983), channel_id=1, source_target_pairs={{0,24},{1,25},{2,26},{3,27},{4,28},{5,29},{6,30},{7,31},{8,0},{9,1... | collective-permute-start | bytes 2211848 | tf_op jit(solution)/shard_map/ppermute | solution.py:38
  963.7 46.8 %collective-permute-start.161 = (bf16[3,5,192,128]{3,2,1,0:T(8,128)(2,1)}, bf16[3,5,192,128]{3,2,1,0:T(8,128)(2,1)}, u32[]{:S(2)}, u32[]{:S(2)}) collective-permute-start(bf16[3,5,192,128]{3,2,1,0:T(8,128)(2,1)} %get-tuple-element.981), channel_id=1, source_target_pairs={{0,16},{1,17},{2,18},{3,19},{4,20},{5,21},{6,22},{7,23},{8,24},{9,... | collective-permute-start | bytes 2211848 | tf_op jit(solution)/shard_map/ppermute | solution.py:38
  991.7 27.7 %collective-permute-start.155 = (bf16[96,2048]{1,0:T(8,128)(2,1)}, bf16[96,2048]{1,0:T(8,128)(2,1)}, u32[]{:S(2)}, u32[]{:S(2)}) collective-permute-start(bf16[96,2048]{1,0:T(8,128)(2,1)} %get-tuple-element.975), channel_id=1, source_target_pairs={{0,2},{1,3},{2,0},{3,1},{4,6},{5,7},{6,4},{7,5},{8,10},{9,11},{10,... | collective-permute-start | bytes 1179656 | tf_op jit(solution)/shard_map/ppermute | solution.py:38
  993.8 28.8 %collective-permute-start.160 = (bf16[144,2176]{1,0:T(8,128)(2,1)}, bf16[144,2176]{1,0:T(8,128)(2,1)}, u32[]{:S(2)}, u32[]{:S(2)}) collective-permute-start(bf16[144,2176]{1,0:T(8,128)(2,1)} %add_convert_fusion.3), channel_id=1, source_target_pairs={{0,2},{1,3},{2,0},{3,1},{4,6},{5,7},{6,4},{7,5},{8,10},{9,11},{10,... | collective-permute-start | bytes 1880072 | tf_op jit(solution)/shard_map/ppermute | solution.py:38
  994.8 27.8 %collective-permute-start.159 = (bf16[144,2048]{1,0:T(8,128)(2,1)}, bf16[144,2048]{1,0:T(8,128)(2,1)}, u32[]{:S(2)}, u32[]{:S(2)}) collective-permute-start(bf16[144,2048]{1,0:T(8,128)(2,1)} %add_convert_fusion.4), channel_id=1, source_target_pairs={{0,1},{1,0},{2,3},{3,2},{4,5},{5,4},{6,7},{7,6},{8,9},{9,8},{10,11... | collective-permute-start | bytes 1769480 | tf_op jit(solution)/shard_map/ppermute | solution.py:38
  1024.6 33.4 %collective-permute-start.164 = (bf16[48,4224]{1,0:T(8,128)(2,1)S(1)}, bf16[48,4224]{1,0:T(8,128)(2,1)S(1)}, u32[]{:S(2)}, u32[]{:S(2)}) collective-permute-start(bf16[48,4224]{1,0:T(8,128)(2,1)S(1)} %get-tuple-element.1007), channel_id=1, source_target_pairs={{0,16},{1,17},{2,18},{3,19},{4,20},{5,21},{6,22},{7,23},{8,24},{9,... | collective-permute-start | bytes 1216520 | tf_op jit(solution)/shard_map/ppermute | solution.py:38
  1024.7 33.3 %collective-permute-start.165 = (bf16[48,4224]{1,0:T(8,128)(2,1)S(1)}, bf16[48,4224]{1,0:T(8,128)(2,1)S(1)}, u32[]{:S(2)}, u32[]{:S(2)}) collective-permute-start(bf16[48,4224]{1,0:T(8,128)(2,1)S(1)} %get-tuple-element.1006), channel_id=1, source_target_pairs={{0,8},{1,9},{2,10},{3,11},{4,12},{5,13},{6,14},{7,15},{8,16},{9,17... | collective-permute-start | bytes 1216520 | tf_op jit(solution)/shard_map/ppermute | solution.py:38
  (343 other events, 6052.8 us)

commit v7 on v6

--- a/solution.py
+++ b/solution.py
@@ -1440,14 +1440,6 @@
         in_specs=[whole_spec()] * len(arrays),
         out_specs=[whole_spec()] * layers,
     )(*arrays)
-
-
-def sum_down(place, total, own):
-    rows = own.shape[0]
-    total = total.astype(jnp.bfloat16)
-    for block in down_hops(place, [total[k * rows : (k + 1) * rows] for k in range(3)]):
-        own = own + block.astype(jnp.float32)
-    return own
 
 
 def tables_of(length_row, rows):
@@ -1715,11 +1707,15 @@
     joined = join_experts(where, tie(held_came, merged_far[0]), 1, layer_count, None)
     far_state = fold_sums(tie(far_first, joined[0]))
     near_first = fold_first(place, tie(merged_near, far_state[1], far_state[2]))
-    near_ends = fold_end(place, fold_sums(near_first))
     far_ends = tie(fold_end(place, far_state), *came)
-    far_total = add_pieces(*far_ends, axis=1)
-    sums[0] = sum_down(place, far_total, add_pieces(*near_ends, axis=1))
-    joined = join_experts(where, [total[0], *came], 0, layer_count, joined)
+    near_ends = fold_end(place, fold_sums(tie(near_first, *far_ends[1:3])))
+    far_total = add_pieces(*far_ends, axis=1).astype(jnp.bfloat16)
+    far_blocks = down_hops(place, [far_total[n * shard :][:shard] for n in range(3)])
+    sums[0] = add_pieces(*near_ends, axis=1)
+    for block in far_blocks:
+        sums[0] = sums[0] + block.astype(jnp.float32)
+    held_came = tie([total[0], *came], near_ends[1], near_ends[2])
+    joined = join_experts(where, held_came, 0, layer_count, joined)
     last_block = down_hops(place, sum_blocks(tie(result_near, far_state[1]), (1,)))
     result = total_of(stored[-1][1][1], received(result_near, last_block + result_arrived))
     result = result.astype(jnp.bfloat16)

time: 1070 us -> 1070 us (level)
    unnamed x460 -> x458, local copies, waits for them, and re-layouts: 58.3 us -> 58.5 us
  transfers between devices with their start and end apart: 166 -> 166, of which waited for: 58 -> 60; matrix products, arithmetic and copies ran while one was open for 5% -> 5% of each run, Pallas kernels for 31% -> 31%
where the time goes in v7:
time: 1070 us; the launch traced here: 1060 us
  waiting for transfers between devices  432 us (40%)
  Pallas kernels  327 us (31%)
  starting transfers between devices  183 us (17%)
  local copies, waits for them, and re-layouts  82.6 us (8%)
  other arithmetic  32.4 us (3%)
    ppermute x166, waiting for transfers between devices, hop(): return lax.ppermute(value, AXES, pairs)  432 us
    ppermute x166, starting transfers between devices, hop(): return lax.ppermute(value, AXES, pairs)  183 us
    pallas_call x4, Pallas kernels, experts_backward_fast(): pl.pallas_call(body, name='experts_backward', out_shape=shapes, in_specs=...  69.4 us
    pallas_call x4, Pallas kernels, experts_forward_fast(): pl.pallas_call(body, name='experts_forward', out_shape=shapes, in_specs=[...  60.5 us
    unnamed x458, local copies, waits for them, and re-layouts  58.5 us
    pallas_call x2, Pallas kernels, attend_backward_fast(): pl.pallas_call(body, name='attend_backward', out_shape=shapes, in_specs=[...  50.5 us
    pallas_call x6, Pallas kernels, weight_grads_fast(): pl.pallas_call(body, name='weight_grads', out_shape=[shape_of(4, experts,...  47.1 us
    pallas_call x2, Pallas kernels, attend_forward_fast(): pl.pallas_call(body, name='attend_forward', out_shape=shapes, in_specs=[s...  30.8 us
  transfers between devices with their start and end apart: 166, of which 60 were waited for; matrix products, arithmetic and copies ran while one was open for 5% of the time, Pallas kernels for 31%

profile of v7, /device:TPU:0, one launch (start us, length us, event | category | flops | bytes accessed | tf_op | source)
XLA Modules:
  0.0 1060.1 jit_solution(1668025036516737552)
XLA Ops:
  30.3 6.8 collective-permute-done.1
  42.5 8.3 collective-permute-start.9
  53.9 45.8 %collective-permute-done.9.refs_9_ = bf16[3,5,192,128]{3,2,1,0:T(8,128)(2,1)S(1)} collective-permute-done((bf16[3,5,192,128]{3,2,1,0:T(8,128)(2,1)}, bf16[3,5,192,128]{3,2,1,0:T(8,128)(2,1)S(1)}, u32[]{:S(2)}, u32[]{:S(2)}) %collective-permute-start.9) | collective-permute-done | bytes 737312 | tf_op jit(solution)/shard_map/ppermute | solution.py:38
  105.4 18.1 %collective-permute-done.15.refs_10_ = bf16[3,5,192,128]{3,2,1,0:T(8,128)(2,1)} collective-permute-done((bf16[3,5,192,128]{3,2,1,0:T(8,128)(2,1)S(1)}, bf16[3,5,192,128]{3,2,1,0:T(8,128)(2,1)}, u32[]{:S(2)}, u32[]{:S(2)}) %collective-permute-start.15) | collective-permute-done | bytes 737312 | tf_op jit(solution)/shard_map/ppermute | solution.py:38
  131.1 15.2 %attend_forward.2 = (f32[128,1536]{1,0:T(8,128)S(1)}, f32[128,1536]{1,0:T(8,128)S(1)}, bf16[128,1536]{1,0:T(8,128)(2,1)S(1)}, bf16[128,1536]{1,0:T(8,128)(2,1)S(...) custom-call(s32[3]{0:T(128)S(1)} %copy-done.117, ...), custom_call_target="tpu_custom_call" | custom-call | flops 103809024 | tf_op jit(solution)/shard_map/attend_forward/pallas_call | solution.py:694
  147.9 11.5 %collective-permute-done.25 = bf16[128,1536]{1,0:T(8,128)(2,1)S(1)} collective-permute-done((bf16[128,1536]{1,0:T(8,128)(2,1)S(1)}, bf16[128,1536]{1,0:T(8,128)(2,1)S(1)}, u32[]{:S(2)}, u32[]{:S(2)}) %collective-permute-start.25) | collective-permute-done | bytes 393248 | tf_op jit(solution)/shard_map/ppermute | solution.py:38
  163.1 14.5 %collective-permute-done.26.refs_3_ = bf16[256,1536]{1,0:T(8,128)(2,1)S(1)} collective-permute-done((bf16[256,1536]{1,0:T(8,128)(2,1)S(1)}, bf16[256,1536]{1,0:T(8,128)(2,1)S(1)}, u32[]{:S(2)}, u32[]{:S(2)}) %collective-permute-start.26) | collective-permute-done | bytes 786464 | tf_op jit(solution)/shard_map/ppermute | solution.py:38
  180.3 6.4 collective-permute-done.28.refs_5_
  199.8 14.6 %experts_forward.4 = (bf16[256,1536]{1,0:T(8,128)(2,1)}, bf16[128,1536]{1,0:T(8,128)(2,1)S(1)}, bf16[128,1536]{1,0:T(8,128)(2,1)S(1)}, bf16[256,1536]{1,0:T(8,12...) custom-call(s32[3]{0:T(128)S(1)} %copy-done.117, ...), custom_call_target="tpu_custom_call" | custom-call | flops 377487360 | tf_op jit(solution)/shard_map/experts_forward/pallas_call | solution.py:1052
  218.1 7.5 collective-permute-done.37.refs_5_
  235.4 15.6 %experts_forward.5 = (bf16[256,1536]{1,0:T(8,128)(2,1)S(1)}, bf16[128,1536]{1,0:T(8,128)(2,1)S(1)}, bf16[128,1536]{1,0:T(8,128)(2,1)S(1)}, bf16[256,1536]{1,0:T(...) custom-call(s32[3]{0:T(128)S(1)} %copy-done.117, ...), custom_call_target="tpu_custom_call" | custom-call | flops 377487360 | tf_op jit(solution)/shard_map/experts_forward/pallas_call | solution.py:1052
  258.1 11.5 %collective-permute-done.47.refs_8_ = bf16[3,5,192,128]{3,2,1,0:T(8,128)(2,1)S(1)} collective-permute-done((bf16[3,5,192,128]{3,2,1,0:T(8,128)(2,1)S(1)}, bf16[3,5,192,128]{3,2,1,0:T(8,128)(2,1)S(1)}, u32[]{:S(2)}, u32[]{:S(2)}) %collective-permute-start.47) | collective-permute-done | bytes 737312 | tf_op jit(solution)/shard_map/ppermute | solution.py:38
  305.3 23.6 %collective-permute-done.51.refs_4_ = bf16[128,1536]{1,0:T(8,128)(2,1)S(1)} collective-permute-done((bf16[128,1536]{1,0:T(8,128)(2,1)}, bf16[128,1536]{1,0:T(8,128)(2,1)S(1)}, u32[]{:S(2)}, u32[]{:S(2)}) %collective-permute-start.51) | collective-permute-done | bytes 393248 | tf_op jit(solution)/shard_map/ppermute | solution.py:38
  336.5 28.2 %collective-permute-done.57.refs_9_ = bf16[3,5,192,128]{3,2,1,0:T(8,128)(2,1)S(1)} collective-permute-done((bf16[3,5,192,128]{3,2,1,0:T(8,128)(2,1)S(1)}, bf16[3,5,192,128]{3,2,1,0:T(8,128)(2,1)S(1)}, u32[]{:S(2)}, u32[]{:S(2)}) %collective-permute-start.57) | collective-permute-done | bytes 737312 | tf_op jit(solution)/shard_map/ppermute | solution.py:38
  372.7 15.5 %attend_forward.3 = (f32[128,1536]{1,0:T(8,128)S(1)}, f32[128,1536]{1,0:T(8,128)S(1)}, bf16[128,1536]{1,0:T(8,128)(2,1)S(1)}, bf16[128,1536]{1,0:T(8,128)(2,1)S(...) custom-call(s32[3]{0:T(128)S(1)} %copy-done.117, ...), custom_call_target="tpu_custom_call" | custom-call | flops 103809024 | tf_op jit(solution)/shard_map/attend_forward/pallas_call | solution.py:694
  388.5 12.9 %collective-permute-done.64 = bf16[128,1536]{1,0:T(8,128)(2,1)S(1)} collective-permute-done((bf16[128,1536]{1,0:T(8,128)(2,1)S(1)}, bf16[128,1536]{1,0:T(8,128)(2,1)S(1)}, u32[]{:S(2)}, u32[]{:S(2)}) %collective-permute-start.64) | collective-permute-done | bytes 393248 | tf_op jit(solution)/shard_map/ppermute | solution.py:38
  404.4 15.9 %collective-permute-done.65.refs_3_ = bf16[256,1536]{1,0:T(8,128)(2,1)S(1)} collective-permute-done((bf16[256,1536]{1,0:T(8,128)(2,1)S(1)}, bf16[256,1536]{1,0:T(8,128)(2,1)S(1)}, u32[]{:S(2)}, u32[]{:S(2)}) %collective-permute-start.65) | collective-permute-done | bytes 786464 | tf_op jit(solution)/shard_map/ppermute | solution.py:38
  423.4 6.3 collective-permute-done.67.refs_5_
  443.6 14.7 %experts_forward.6 = (bf16[256,1536]{1,0:T(8,128)(2,1)}, bf16[128,1536]{1,0:T(8,128)(2,1)S(1)}, bf16[128,1536]{1,0:T(8,128)(2,1)S(1)}, bf16[256,1536]{1,0:T(8,12...) custom-call(s32[3]{0:T(128)S(1)} %copy-done.117, ...), custom_call_target="tpu_custom_call" | custom-call | flops 377487360 | tf_op jit(solution)/shard_map/experts_forward/pallas_call | solution.py:1052
  461.5 7.9 collective-permute-done.77.refs_5_
  477.0 15.6 %experts_forward.7 = (bf16[256,1536]{1,0:T(8,128)(2,1)S(1)}, bf16[128,1536]{1,0:T(8,128)(2,1)S(1)}, bf16[128,1536]{1,0:T(8,128)(2,1)S(1)}, bf16[256,1536]{1,0:T(...) custom-call(s32[3]{0:T(128)S(1)} %copy-done.117, ...), custom_call_target="tpu_custom_call" | custom-call | flops 377487360 | tf_op jit(solution)/shard_map/experts_forward/pallas_call | solution.py:1052
  499.6 6.4 collective-permute-done.82.refs_5_
  511.1 17.0 %experts_backward.4 = (bf16[256,1536]{1,0:T(8,128)(2,1)}, bf16[128,1536]{1,0:T(8,128)(2,1)S(1)}, bf16[128,1536]{1,0:T(8,128)(2,1)S(1)}, bf16[256,1536]{1,0:T(8,1...) custom-call(s32[3]{0:T(128)S(1)} %copy-done.117, ...), custom_call_target="tpu_custom_call" | custom-call | flops 377487360 | tf_op jit(solution)/shard_map/experts_backward/pallas_call | solution.py:1136
  540.6 17.7 %experts_backward.5 = (bf16[256,1536]{1,0:T(8,128)(2,1)}, bf16[128,1536]{1,0:T(8,128)(2,1)S(1)}, bf16[128,1536]{1,0:T(8,128)(2,1)S(1)}, bf16[256,1536]{1,0:T(8,1...) custom-call(s32[3]{0:T(128)S(1)} %copy-done.117, ...), custom_call_target="tpu_custom_call" | custom-call | flops 377487360 | tf_op jit(solution)/shard_map/experts_backward/pallas_call | solution.py:1136
  562.9 7.8 weight_grads.6
  574.8 7.9 weight_grads.7
  612.2 7.6 weight_grads.8
  629.5 6.3 collective-permute-start.105
  636.6 25.3 %attend_backward.2 = (f32[128,1536]{1,0:T(8,128)}, bf16[128,1536]{1,0:T(8,128)(2,1)}, bf16[768,4224]{1,0:T(8,128)(2,1)}, bf16[768,4224]{1,0:T(8,128)(2,1)}) custom-call(s32[3]{0:T(128)} %pad_add_fusion.where.refs_0_, bf16[128,1536]{1,0:T(8,128)(2,1)} %broadcast_in_dim.61.refs_1_, bf16[128,1536]{1,0:T(8,128)(2,1)} %refs_2_.3, ...), custom_call_target="tpu_custom_call" | custom-call | flops 207618048 | tf_op jit(solution)/shard_map/attend_backward/pallas_call | solution.py:863
  687.3 13.0 %collective-permute-done.110.refs_3_ = bf16[256,1536]{1,0:T(8,128)(2,1)S(1)} collective-permute-done((bf16[256,1536]{1,0:T(8,128)(2,1)S(1)}, bf16[256,1536]{1,0:T(8,128)(2,1)S(1)}, u32[]{:S(2)}, u32[]{:S(2)}) %collective-permute-start.110) | collective-permute-done | bytes 786464 | tf_op jit(solution)/shard_map/ppermute | solution.py:38
  704.3 6.8 collective-permute-done.112.refs_5_
  720.5 17.0 %experts_backward.6 = (bf16[256,1536]{1,0:T(8,128)(2,1)}, bf16[128,1536]{1,0:T(8,128)(2,1)S(1)}, bf16[128,1536]{1,0:T(8,128)(2,1)S(1)}, bf16[256,1536]{1,0:T(8,1...) custom-call(s32[3]{0:T(128)S(1)} %copy-done.118, ...), custom_call_target="tpu_custom_call" | custom-call | flops 377487360 | tf_op jit(solution)/shard_map/experts_backward/pallas_call | solution.py:1136
  737.5 7.0 collective-permute-done.118
  746.8 7.4 merge_cores.3
  761.5 17.7 %experts_backward.7 = (bf16[256,1536]{1,0:T(8,128)(2,1)}, bf16[128,1536]{1,0:T(8,128)(2,1)S(1)}, bf16[128,1536]{1,0:T(8,128)(2,1)S(1)}, bf16[256,1536]{1,0:T(8,1...) custom-call(s32[3]{0:T(128)S(1)} %copy-done.118, ...), custom_call_target="tpu_custom_call" | custom-call | flops 377487360 | tf_op jit(solution)/shard_map/experts_backward/pallas_call | solution.py:1136
  780.8 9.8 collective-permute-done.124
  798.3 7.6 weight_grads.9
  810.4 7.9 weight_grads.10
  821.9 8.7 collective-permute-done.132.two_tail
  834.3 8.3 weight_grads.11
  893.8 8.2 collective-permute-done.138.refs_4_
  908.1 25.2 %attend_backward.3 = (f32[128,1536]{1,0:T(8,128)}, bf16[128,1536]{1,0:T(8,128)(2,1)}, bf16[576,4224]{1,0:T(8,128)(2,1)}, bf16[192,4224]{1,0:T(8,128)(2,1)}, bf16...) custom-call(s32[3]{0:T(128)} %pad_add_fusion.where.refs_0_, bf16[128,1536]{1,0:T(8,128)(2,1)} %broadcast_in_dim.61.refs_1_, ...), custom_call_target="tpu_custom_call" | custom-call | flops 207618048 | tf_op jit(solution)/shard_map/attend_backward/pallas_call | solution.py:863
  933.4 7.1 collective-permute-done.147
  941.5 7.5 collective-permute-done.149.arrived
  953.9 7.6 collective-permute-done.150.refs_1_
  969.8 19.1 %collective-permute-done.152 = bf16[288,2048]{1,0:T(8,128)(2,1)S(1)} collective-permute-done((bf16[288,2048]{1,0:T(8,128)(2,1)S(1)}, bf16[288,2048]{1,0:T(8,128)(2,1)S(1)}, u32[]{:S(2)}, u32[]{:S(2)}) %collective-permute-start.152) | collective-permute-done | bytes 1179680 | tf_op jit(solution)/shard_map/ppermute | solution.py:38
  999.7 10.7 %collective-permute-done.159.refs_2_ = bf16[3,5,192,128]{3,2,1,0:T(8,128)(2,1)} collective-permute-done((bf16[3,5,192,128]{3,2,1,0:T(8,128)(2,1)}, bf16[3,5,192,128]{3,2,1,0:T(8,128)(2,1)}, u32[]{:S(2)}, u32[]{:S(2)}) %collective-permute-start.159) | collective-permute-done | bytes 737312 | tf_op jit(solution)/shard_map/ppermute | solution.py:38
  1032.8 24.1 %collective-permute-done.164 = bf16[48,4224]{1,0:T(8,128)(2,1)S(1)} collective-permute-done((bf16[48,4224]{1,0:T(8,128)(2,1)S(1)}, bf16[48,4224]{1,0:T(8,128)(2,1)S(1)}, u32[]{:S(2)}, u32[]{:S(2)}) %collective-permute-start.164) | collective-permute-done | bytes 405536 | tf_op jit(solution)/shard_map/ppermute | solution.py:38
  (883 shorter events, 422.9 us)
Async XLA Ops:
  7.9 29.1 %collective-permute-start.1 = (bf16[48,4224]{1,0:T(8,128)(2,1)}, bf16[48,4224]{1,0:T(8,128)(2,1)S(1)}, u32[]{:S(2)}, u32[]{:S(2)}) collective-permute-start(bf16[48,4224]{1,0:T(8,128)(2,1)} %get-tuple-element.513), channel_id=1, source_target_pairs={{0,16},{1,17},{2,18},{3,19},{4,20},{5,21},{6,22},{7,23},{8,24},{9,... | collective-permute-start | bytes 1216520 | tf_op jit(solution)/shard_map/ppermute | solution.py:38
  10.5 26.5 %collective-permute-start.2 = (bf16[48,4224]{1,0:T(8,128)(2,1)}, bf16[48,4224]{1,0:T(8,128)(2,1)S(1)}, u32[]{:S(2)}, u32[]{:S(2)}) collective-permute-start(bf16[48,4224]{1,0:T(8,128)(2,1)} %get-tuple-element.513), channel_id=1, source_target_pairs={{0,24},{1,25},{2,26},{3,27},{4,28},{5,29},{6,30},{7,31},{8,0},{9,1... | collective-permute-start | bytes 1216520 | tf_op jit(solution)/shard_map/ppermute | solution.py:38
  39.4 63.4 %collective-permute-start.10 = (bf16[192,4224]{1,0:T(8,128)(2,1)}, bf16[192,4224]{1,0:T(8,128)(2,1)S(1)}, u32[]{:S(2)}, u32[]{:S(2)}) collective-permute-start(bf16[192,4224]{1,0:T(8,128)(2,1)} %constant_dynamic-update-slice_fusion.refs_5_.refs_21_), channel_id=1, source_target_pairs={{0,4},{1,5},{2,6},{3,7},{4,0},{5,1},{6,2},{7,3},{8,12},{9,13},{10,... | collective-permute-start | bytes 4866056 | tf_op jit(solution)/shard_map/ppermute | solution.py:38
  39.4 63.4 %collective-permute-start.6 = (bf16[192,4224]{1,0:T(8,128)(2,1)}, bf16[192,4224]{1,0:T(8,128)(2,1)S(1)}, u32[]{:S(2)}, u32[]{:S(2)}) collective-permute-start(bf16[192,4224]{1,0:T(8,128)(2,1)} %constant_dynamic-update-slice_fusion.refs_5_.refs_21_), channel_id=1, source_target_pairs={{0,1},{1,0},{2,3},{3,2},{4,5},{5,4},{6,7},{7,6},{8,9},{9,8},{10,11... | collective-permute-start | bytes 4866056 | tf_op jit(solution)/shard_map/ppermute | solution.py:38
  40.9 62.0 %collective-permute-start.7 = (bf16[192,4224]{1,0:T(8,128)(2,1)}, bf16[192,4224]{1,0:T(8,128)(2,1)S(1)}, u32[]{:S(2)}, u32[]{:S(2)}) collective-permute-start(bf16[192,4224]{1,0:T(8,128)(2,1)} %constant_dynamic-update-slice_fusion.refs_5_.refs_21_), channel_id=1, source_target_pairs={{0,2},{1,3},{2,0},{3,1},{4,6},{5,7},{6,4},{7,5},{8,10},{9,11},{10,... | collective-permute-start | bytes 4866056 | tf_op jit(solution)/shard_map/ppermute | solution.py:38
  42.5 57.2 %collective-permute-start.9 = (bf16[3,5,192,128]{3,2,1,0:T(8,128)(2,1)}, bf16[3,5,192,128]{3,2,1,0:T(8,128)(2,1)S(1)}, u32[]{:S(2)}, u32[]{:S(2)}) collective-permute-start(bf16[3,5,192,128]{3,2,1,0:T(8,128)(2,1)} %get-tuple-element.526), channel_id=1, source_target_pairs={{0,16},{1,17},{2,18},{3,19},{4,20},{5,21},{6,22},{7,23},{8,24},{9,... | collective-permute-start | bytes 2211848 | tf_op jit(solution)/shard_map/ppermute | solution.py:38
  50.9 48.9 %collective-permute-start.8 = (bf16[3,5,192,128]{3,2,1,0:T(8,128)(2,1)S(1)}, bf16[3,5,192,128]{3,2,1,0:T(8,128)(2,1)S(1)}, u32[]{:S(2)}, u32[]{:S(2)}) collective-permute-start(bf16[3,5,192,128]{3,2,1,0:T(8,128)(2,1)S(1)} %copy-done.219), channel_id=1, source_target_pairs={{0,8},{1,9},{2,10},{3,11},{4,12},{5,13},{6,14},{7,15},{8,16},{9,17... | collective-permute-start | bytes 2211848 | tf_op jit(solution)/shard_map/ppermute | solution.py:38
  255.4 26.5 %collective-permute-start.43 = (bf16[128,1536]{1,0:T(8,128)(2,1)S(1)}, bf16[128,1536]{1,0:T(8,128)(2,1)S(1)}, u32[]{:S(2)}, u32[]{:S(2)}) collective-permute-start(bf16[128,1536]{1,0:T(8,128)(2,1)S(1)} %add_convert_fusion.20), channel_id=1, source_target_pairs={{0,2},{1,3},{2,0},{3,1},{4,6},{5,7},{6,4},{7,5},{8,10},{9,11},{10,... | collective-permute-start | bytes 1179656 | tf_op jit(solution)/shard_map/ppermute | solution.py:38
  287.0 42.0 %collective-permute-start.53 = (bf16[192,4224]{1,0:T(8,128)(2,1)}, bf16[192,4224]{1,0:T(8,128)(2,1)}, u32[]{:S(2)}, u32[]{:S(2)}) collective-permute-start(bf16[192,4224]{1,0:T(8,128)(2,1)} %constant_dynamic-update-slice_fusion.8.refs_11_.refs_21_), channel_id=1, source_target_pairs={{0,1},{1,0},{2,3},{3,2},{4,5},{5,4},{6,7},{7,6},{8,9},{9,8},{10,11... | collective-permute-start | bytes 4866056 | tf_op jit(solution)/shard_map/ppermute | solution.py:38
  288.0 40.9 %collective-permute-start.54 = (bf16[192,4224]{1,0:T(8,128)(2,1)}, bf16[192,4224]{1,0:T(8,128)(2,1)}, u32[]{:S(2)}, u32[]{:S(2)}) collective-permute-start(bf16[192,4224]{1,0:T(8,128)(2,1)} %constant_dynamic-update-slice_fusion.8.refs_11_.refs_21_), channel_id=1, source_target_pairs={{0,2},{1,3},{2,0},{3,1},{4,6},{5,7},{6,4},{7,5},{8,10},{9,11},{10,... | collective-permute-start | bytes 4866056 | tf_op jit(solution)/shard_map/ppermute | solution.py:38
  298.3 30.6 %collective-permute-start.51 = (bf16[128,1536]{1,0:T(8,128)(2,1)}, bf16[128,1536]{1,0:T(8,128)(2,1)S(1)}, u32[]{:S(2)}, u32[]{:S(2)}) collective-permute-start(bf16[128,1536]{1,0:T(8,128)(2,1)} %get-tuple-element.603), channel_id=1, source_target_pairs={{0,16},{1,17},{2,18},{3,19},{4,20},{5,21},{6,22},{7,23},{8,24},{9,... | collective-permute-start | bytes 1179656 | tf_op jit(solution)/shard_map/ppermute | solution.py:38
  299.0 29.9 %collective-permute-start.52 = (bf16[128,1536]{1,0:T(8,128)(2,1)}, bf16[128,1536]{1,0:T(8,128)(2,1)S(1)}, u32[]{:S(2)}, u32[]{:S(2)}) collective-permute-start(bf16[128,1536]{1,0:T(8,128)(2,1)} %get-tuple-element.604), channel_id=1, source_target_pairs={{0,8},{1,9},{2,10},{3,11},{4,12},{5,13},{6,14},{7,15},{8,16},{9,17... | collective-permute-start | bytes 1179656 | tf_op jit(solution)/shard_map/ppermute | solution.py:38
  329.0 35.8 %collective-permute-start.58 = (bf16[192,4224]{1,0:T(8,128)(2,1)}, bf16[192,4224]{1,0:T(8,128)(2,1)S(1)}, u32[]{:S(2)}, u32[]{:S(2)}) collective-permute-start(bf16[192,4224]{1,0:T(8,128)(2,1)} %collective-permute-done.53.refs_12_.refs_22_), channel_id=1, source_target_pairs={{0,4},{1,5},{2,6},{3,7},{4,0},{5,1},{6,2},{7,3},{8,12},{9,13},{10,... | collective-permute-start | bytes 4866056 | tf_op jit(solution)/shard_map/ppermute | solution.py:38
  329.0 35.7 %collective-permute-start.59 = (bf16[192,4224]{1,0:T(8,128)(2,1)}, bf16[192,4224]{1,0:T(8,128)(2,1)S(1)}, u32[]{:S(2)}, u32[]{:S(2)}) collective-permute-start(bf16[192,4224]{1,0:T(8,128)(2,1)} %collective-permute-done.54.refs_13_.refs_23_), channel_id=1, source_target_pairs={{0,4},{1,5},{2,6},{3,7},{4,0},{5,1},{6,2},{7,3},{8,12},{9,13},{10,... | collective-permute-start | bytes 4866056 | tf_op jit(solution)/shard_map/ppermute | solution.py:38
  329.6 35.1 %collective-permute-start.57 = (bf16[3,5,192,128]{3,2,1,0:T(8,128)(2,1)S(1)}, bf16[3,5,192,128]{3,2,1,0:T(8,128)(2,1)S(1)}, u32[]{:S(2)}, u32[]{:S(2)}) collective-permute-start(bf16[3,5,192,128]{3,2,1,0:T(8,128)(2,1)S(1)} %copy-done.216), channel_id=1, source_target_pairs={{0,16},{1,17},{2,18},{3,19},{4,20},{5,21},{6,22},{7,23},{8,24},{9,... | collective-permute-start | bytes 2211848 | tf_op jit(solution)/shard_map/ppermute | solution.py:38
  333.1 31.6 %collective-permute-start.56 = (bf16[192,2176]{1,0:T(8,128)(2,1)S(1)}, bf16[192,2176]{1,0:T(8,128)(2,1)S(1)}, u32[]{:S(2)}, u32[]{:S(2)}) collective-permute-start(bf16[192,2176]{1,0:T(8,128)(2,1)S(1)} %slice.240), channel_id=1, source_target_pairs={{0,1},{1,0},{2,3},{3,2},{4,5},{5,4},{6,7},{7,6},{8,9},{9,8},{10,11... | collective-permute-start | bytes 2506760 | tf_op jit(solution)/shard_map/ppermute | solution.py:38
  335.5 29.3 %collective-permute-start.55 = (bf16[192,2048]{1,0:T(8,128)(2,1)S(1)}, bf16[192,2048]{1,0:T(8,128)(2,1)S(1)}, u32[]{:S(2)}, u32[]{:S(2)}) collective-permute-start(bf16[192,2048]{1,0:T(8,128)(2,1)S(1)} %slice.239), channel_id=1, source_target_pairs={{0,2},{1,3},{2,0},{3,1},{4,6},{5,7},{6,4},{7,5},{8,10},{9,11},{10,... | collective-permute-start | bytes 2359304 | tf_op jit(solution)/shard_map/ppermute | solution.py:38
  432.5 25.8 %collective-permute-start.73 = (bf16[256,1536]{1,0:T(8,128)(2,1)S(1)}, bf16[256,1536]{1,0:T(8,128)(2,1)S(1)}, u32[]{:S(2)}, u32[]{:S(2)}) collective-permute-start(bf16[256,1536]{1,0:T(8,128)(2,1)S(1)} %constant_dynamic-update-slice_fusion.14.refs_2_), channel_id=1, source_target_pairs={{0,1},{1,0},{2,3},{3,2},{4,5},{5,4},{6,7},{7,6},{8,9},{9,8},{10,11... | collective-permute-start | bytes 2359304 | tf_op jit(solution)/shard_map/ppermute | solution.py:38
  582.8 38.0 %collective-permute-start.100 = (bf16[4,5,192,128]{3,2,1,0:T(8,128)(2,1)}, bf16[4,5,192,128]{3,2,1,0:T(8,128)(2,1)}, u32[]{:S(2)}, u32[]{:S(2)}) collective-permute-start(bf16[4,5,192,128]{3,2,1,0:T(8,128)(2,1)} %get-tuple-element.732), channel_id=1, source_target_pairs={{0,4},{1,5},{2,6},{3,7},{4,0},{5,1},{6,2},{7,3},{8,12},{9,13},{10,... | collective-permute-start | bytes 2949128 | tf_op jit(solution)/shard_map/ppermute | solution.py:38
  591.6 30.5 %collective-permute-start.98 = (bf16[128,1536]{1,0:T(8,128)(2,1)}, bf16[128,1536]{1,0:T(8,128)(2,1)}, u32[]{:S(2)}, u32[]{:S(2)}) collective-permute-start(bf16[128,1536]{1,0:T(8,128)(2,1)} %get-tuple-element.729.refs_5_), channel_id=1, source_target_pairs={{0,16},{1,17},{2,18},{3,19},{4,20},{5,21},{6,22},{7,23},{8,24},{9,... | collective-permute-start | bytes 1179656 | tf_op jit(solution)/shard_map/ppermute | solution.py:38
  593.8 28.3 %collective-permute-start.99 = (bf16[128,1536]{1,0:T(8,128)(2,1)}, bf16[128,1536]{1,0:T(8,128)(2,1)}, u32[]{:S(2)}, u32[]{:S(2)}) collective-permute-start(bf16[128,1536]{1,0:T(8,128)(2,1)} %get-tuple-element.730), channel_id=1, source_target_pairs={{0,8},{1,9},{2,10},{3,11},{4,12},{5,13},{6,14},{7,15},{8,16},{9,17... | collective-permute-start | bytes 1179656 | tf_op jit(solution)/shard_map/ppermute | solution.py:38
  625.4 36.5 %collective-permute-start.103 = (bf16[256,1536]{1,0:T(8,128)(2,1)}, bf16[256,1536]{1,0:T(8,128)(2,1)S(1)}, u32[]{:S(2)}, u32[]{:S(2)}) collective-permute-start(bf16[256,1536]{1,0:T(8,128)(2,1)} %get-tuple-element.767), channel_id=1, source_target_pairs={{0,1},{1,0},{2,3},{3,2},{4,5},{5,4},{6,7},{7,6},{8,9},{9,8},{10,11... | collective-permute-start | bytes 2359304 | tf_op jit(solution)/shard_map/ppermute | solution.py:38
  626.5 35.5 %collective-permute-start.104 = (bf16[256,1536]{1,0:T(8,128)(2,1)}, bf16[256,1536]{1,0:T(8,128)(2,1)S(1)}, u32[]{:S(2)}, u32[]{:S(2)}) collective-permute-start(bf16[256,1536]{1,0:T(8,128)(2,1)} %get-tuple-element.768), channel_id=1, source_target_pairs={{0,2},{1,3},{2,0},{3,1},{4,6},{5,7},{6,4},{7,5},{8,10},{9,11},{10,... | collective-permute-start | bytes 2359304 | tf_op jit(solution)/shard_map/ppermute | solution.py:38
  627.5 34.5 %collective-permute-start.101 = (bf16[256,1536]{1,0:T(8,128)(2,1)S(1)}, bf16[256,1536]{1,0:T(8,128)(2,1)S(1)}, u32[]{:S(2)}, u32[]{:S(2)}) collective-permute-start(bf16[256,1536]{1,0:T(8,128)(2,1)S(1)} %copy-done.135), channel_id=1, source_target_pairs={{0,1},{1,0},{2,3},{3,2},{4,5},{5,4},{6,7},{7,6},{8,9},{9,8},{10,11... | collective-permute-start | bytes 2359304 | tf_op jit(solution)/shard_map/ppermute | solution.py:38
  628.5 33.5 %collective-permute-start.102 = (bf16[256,1536]{1,0:T(8,128)(2,1)S(1)}, bf16[256,1536]{1,0:T(8,128)(2,1)S(1)}, u32[]{:S(2)}, u32[]{:S(2)}) collective-permute-start(bf16[256,1536]{1,0:T(8,128)(2,1)S(1)} %copy-done.133), channel_id=1, source_target_pairs={{0,2},{1,3},{2,0},{3,1},{4,6},{5,7},{6,4},{7,5},{8,10},{9,11},{10,... | collective-permute-start | bytes 2359304 | tf_op jit(solution)/shard_map/ppermute | solution.py:38
  629.5 32.4 %collective-permute-start.105 = (bf16[2,5,192,128]{3,2,1,0:T(8,128)(2,1)S(1)}, bf16[2,5,192,128]{3,2,1,0:T(8,128)(2,1)S(1)}, u32[]{:S(2)}, u32[]{:S(2)}) collective-permute-start(bf16[2,5,192,128]{3,2,1,0:T(8,128)(2,1)S(1)} %pad_maximum_fusion.2), channel_id=1, source_target_pairs={{0,16},{1,17},{2,18},{3,19},{4,20},{5,21},{6,22},{7,23},{8,24},{9,... | collective-permute-start | bytes 1474568 | tf_op jit(solution)/shard_map/ppermute | solution.py:38
  680.3 66.4 %collective-permute-start.122 = (bf16[768,4224]{1,0:T(8,128)(2,1)}, bf16[768,4224]{1,0:T(8,128)(2,1)}, u32[]{:S(2)}, u32[]{:S(2)}) collective-permute-start(bf16[768,4224]{1,0:T(8,128)(2,1)} %get-tuple-element.825), channel_id=1, source_target_pairs={{0,4},{1,5},{2,6},{3,7},{4,0},{5,1},{6,2},{7,3},{8,12},{9,13},{10,... | collective-permute-start | bytes 19464200 | tf_op jit(solution)/shard_map/ppermute | solution.py:38
  712.0 32.5 %collective-permute-start.116 = (bf16[256,1536]{1,0:T(8,128)(2,1)S(1)}, bf16[256,1536]{1,0:T(8,128)(2,1)S(1)}, u32[]{:S(2)}, u32[]{:S(2)}) collective-permute-start(bf16[256,1536]{1,0:T(8,128)(2,1)S(1)} %constant_dynamic-update-slice_fusion.22.refs_2_), channel_id=1, source_target_pairs={{0,1},{1,0},{2,3},{3,2},{4,5},{5,4},{6,7},{7,6},{8,9},{9,8},{10,11... | collective-permute-start | bytes 2359304 | tf_op jit(solution)/shard_map/ppermute | solution.py:38
  713.1 31.3 %collective-permute-start.117 = (bf16[256,1536]{1,0:T(8,128)(2,1)S(1)}, bf16[256,1536]{1,0:T(8,128)(2,1)S(1)}, u32[]{:S(2)}, u32[]{:S(2)}) collective-permute-start(bf16[256,1536]{1,0:T(8,128)(2,1)S(1)} %constant_dynamic-update-slice_fusion.22.refs_2_), channel_id=1, source_target_pairs={{0,2},{1,3},{2,0},{3,1},{4,6},{5,7},{6,4},{7,5},{8,10},{9,11},{10,... | collective-permute-start | bytes 2359304 | tf_op jit(solution)/shard_map/ppermute | solution.py:38
  717.0 27.5 %collective-permute-start.118 = (bf16[128,1536]{1,0:T(8,128)(2,1)}, bf16[128,1536]{1,0:T(8,128)(2,1)S(1)}, u32[]{:S(2)}, u32[]{:S(2)}) collective-permute-start(bf16[128,1536]{1,0:T(8,128)(2,1)} %get-tuple-element.802), channel_id=1, source_target_pairs={{0,16},{1,17},{2,18},{3,19},{4,20},{5,21},{6,22},{7,23},{8,24},{9,... | collective-permute-start | bytes 1179656 | tf_op jit(solution)/shard_map/ppermute | solution.py:38
  755.9 36.7 %collective-permute-start.123 = (bf16[384,2176]{1,0:T(8,128)(2,1)}, bf16[384,2176]{1,0:T(8,128)(2,1)}, u32[]{:S(2)}, u32[]{:S(2)}) collective-permute-start(bf16[384,2176]{1,0:T(8,128)(2,1)} %get-tuple-element.835), channel_id=1, source_target_pairs={{0,1},{1,0},{2,3},{3,2},{4,5},{5,4},{6,7},{7,6},{8,9},{9,8},{10,11... | collective-permute-start | bytes 5013512 | tf_op jit(solution)/shard_map/ppermute | solution.py:38
  756.8 33.8 %collective-permute-start.124 = (bf16[384,2048]{1,0:T(8,128)(2,1)}, bf16[384,2048]{1,0:T(8,128)(2,1)}, u32[]{:S(2)}, u32[]{:S(2)}) collective-permute-start(bf16[384,2048]{1,0:T(8,128)(2,1)} %get-tuple-element.836), channel_id=1, source_target_pairs={{0,2},{1,3},{2,0},{3,1},{4,6},{5,7},{6,4},{7,5},{8,10},{9,11},{10,... | collective-permute-start | bytes 4718600 | tf_op jit(solution)/shard_map/ppermute | solution.py:38
  792.5 25.9 %collective-permute-start.126 = (bf16[256,1536]{1,0:T(8,128)(2,1)}, bf16[256,1536]{1,0:T(8,128)(2,1)S(1)}, u32[]{:S(2)}, u32[]{:S(2)}) collective-permute-start(bf16[256,1536]{1,0:T(8,128)(2,1)} %get-tuple-element.842), channel_id=1, source_target_pairs={{0,1},{1,0},{2,3},{3,2},{4,5},{5,4},{6,7},{7,6},{8,9},{9,8},{10,11... | collective-permute-start | bytes 2359304 | tf_op jit(solution)/shard_map/ppermute | solution.py:38
  818.4 29.8 %collective-permute-start.134 = (bf16[4,5,192,128]{3,2,1,0:T(8,128)(2,1)}, bf16[4,5,192,128]{3,2,1,0:T(8,128)(2,1)S(1)}, u32[]{:S(2)}, u32[]{:S(2)}) collective-permute-start(bf16[4,5,192,128]{3,2,1,0:T(8,128)(2,1)} %get-tuple-element.865), channel_id=1, source_target_pairs={{0,4},{1,5},{2,6},{3,7},{4,0},{5,1},{6,2},{7,3},{8,12},{9,13},{10,... | collective-permute-start | bytes 2949128 | tf_op jit(solution)/shard_map/ppermute | solution.py:38
  819.8 29.4 %collective-permute-start.129 = (bf16[256,1536]{1,0:T(8,128)(2,1)}, bf16[256,1536]{1,0:T(8,128)(2,1)S(1)}, u32[]{:S(2)}, u32[]{:S(2)}) collective-permute-start(bf16[256,1536]{1,0:T(8,128)(2,1)} %get-tuple-element.861), channel_id=1, source_target_pairs={{0,1},{1,0},{2,3},{3,2},{4,5},{5,4},{6,7},{7,6},{8,9},{9,8},{10,11... | collective-permute-start | bytes 2359304 | tf_op jit(solution)/shard_map/ppermute | solution.py:38
  820.9 28.3 %collective-permute-start.130 = (bf16[256,1536]{1,0:T(8,128)(2,1)S(1)}, bf16[256,1536]{1,0:T(8,128)(2,1)S(1)}, u32[]{:S(2)}, u32[]{:S(2)}) collective-permute-start(bf16[256,1536]{1,0:T(8,128)(2,1)S(1)} %copy-done.214), channel_id=1, source_target_pairs={{0,2},{1,3},{2,0},{3,1},{4,6},{5,7},{6,4},{7,5},{8,10},{9,11},{10,... | collective-permute-start | bytes 2359304 | tf_op jit(solution)/shard_map/ppermute | solution.py:38
  821.9 26.3 %collective-permute-start.135 = (bf16[3,5,192,128]{3,2,1,0:T(8,128)(2,1)}, bf16[3,5,192,128]{3,2,1,0:T(8,128)(2,1)S(1)}, u32[]{:S(2)}, u32[]{:S(2)}) collective-permute-start(bf16[3,5,192,128]{3,2,1,0:T(8,128)(2,1)} %get-tuple-element.878), channel_id=1, source_target_pairs={{0,24},{1,25},{2,26},{3,27},{4,28},{5,29},{6,30},{7,31},{8,0},{9,1... | collective-permute-start | bytes 2211848 | tf_op jit(solution)/shard_map/ppermute | solution.py:38
  902.1 31.2 %collective-permute-start.145 = (bf16[128,1536]{1,0:T(8,128)(2,1)S(1)}, bf16[128,1536]{1,0:T(8,128)(2,1)S(1)}, u32[]{:S(2)}, u32[]{:S(2)}) collective-permute-start(bf16[128,1536]{1,0:T(8,128)(2,1)S(1)} %add_convert_fusion.6), channel_id=1, source_target_pairs={{0,2},{1,3},{2,0},{3,1},{4,6},{5,7},{6,4},{7,5},{8,10},{9,11},{10,... | collective-permute-start | bytes 1179656 | tf_op jit(solution)/shard_map/ppermute | solution.py:38
  903.3 30.0 %collective-permute-start.146 = (bf16[48,4224]{1,0:T(8,128)(2,1)S(1)}, bf16[48,4224]{1,0:T(8,128)(2,1)S(1)}, u32[]{:S(2)}, u32[]{:S(2)}) collective-permute-start(bf16[48,4224]{1,0:T(8,128)(2,1)S(1)} %get-tuple-element.1028), channel_id=1, source_target_pairs={{0,24},{1,25},{2,26},{3,27},{4,28},{5,29},{6,30},{7,31},{8,0},{9,1... | collective-permute-start | bytes 1216520 | tf_op jit(solution)/shard_map/ppermute | solution.py:38
  903.4 37.1 %collective-permute-start.147 = (bf16[48,4224]{1,0:T(8,128)(2,1)S(1)}, bf16[48,4224]{1,0:T(8,128)(2,1)S(1)}, u32[]{:S(2)}, u32[]{:S(2)}) collective-permute-start(bf16[48,4224]{1,0:T(8,128)(2,1)S(1)} %get-tuple-element.1027), channel_id=1, source_target_pairs={{0,16},{1,17},{2,18},{3,19},{4,20},{5,21},{6,22},{7,23},{8,24},{9,... | collective-permute-start | bytes 1216520 | tf_op jit(solution)/shard_map/ppermute | solution.py:38
  905.5 35.1 %collective-permute-start.148 = (bf16[48,4224]{1,0:T(8,128)(2,1)S(1)}, bf16[48,4224]{1,0:T(8,128)(2,1)S(1)}, u32[]{:S(2)}, u32[]{:S(2)}) collective-permute-start(bf16[48,4224]{1,0:T(8,128)(2,1)S(1)} %get-tuple-element.1026), channel_id=1, source_target_pairs={{0,8},{1,9},{2,10},{3,11},{4,12},{5,13},{6,14},{7,15},{8,16},{9,17... | collective-permute-start | bytes 1216520 | tf_op jit(solution)/shard_map/ppermute | solution.py:38
  907.4 26.0 %collective-permute-start.144 = (bf16[128,1536]{1,0:T(8,128)(2,1)}, bf16[128,1536]{1,0:T(8,128)(2,1)S(1)}, u32[]{:S(2)}, u32[]{:S(2)}) collective-permute-start(bf16[128,1536]{1,0:T(8,128)(2,1)} %add_convert_fusion.7), channel_id=1, source_target_pairs={{0,1},{1,0},{2,3},{3,2},{4,5},{5,4},{6,7},{7,6},{8,9},{9,8},{10,11... | collective-permute-start | bytes 1179656 | tf_op jit(solution)/shard_map/ppermute | solution.py:38
  961.5 28.2 %collective-permute-start.151 = (bf16[288,2176]{1,0:T(8,128)(2,1)S(1)}, bf16[288,2176]{1,0:T(8,128)(2,1)S(1)}, u32[]{:S(2)}, u32[]{:S(2)}) collective-permute-start(bf16[288,2176]{1,0:T(8,128)(2,1)S(1)} %get-tuple-element.953), channel_id=1, source_target_pairs={{0,1},{1,0},{2,3},{3,2},{4,5},{5,4},{6,7},{7,6},{8,9},{9,8},{10,11... | collective-permute-start | bytes 3760136 | tf_op jit(solution)/shard_map/ppermute | solution.py:38
  962.5 26.4 %collective-permute-start.152 = (bf16[288,2048]{1,0:T(8,128)(2,1)S(1)}, bf16[288,2048]{1,0:T(8,128)(2,1)S(1)}, u32[]{:S(2)}, u32[]{:S(2)}) collective-permute-start(bf16[288,2048]{1,0:T(8,128)(2,1)S(1)} %get-tuple-element.954), channel_id=1, source_target_pairs={{0,2},{1,3},{2,0},{3,1},{4,6},{5,7},{6,4},{7,5},{8,10},{9,11},{10,... | collective-permute-start | bytes 3538952 | tf_op jit(solution)/shard_map/ppermute | solution.py:38
  963.6 31.2 %collective-permute-start.160 = (bf16[3,5,192,128]{3,2,1,0:T(8,128)(2,1)}, bf16[3,5,192,128]{3,2,1,0:T(8,128)(2,1)S(1)}, u32[]{:S(2)}, u32[]{:S(2)}) collective-permute-start(bf16[3,5,192,128]{3,2,1,0:T(8,128)(2,1)} %get-tuple-element.992), channel_id=1, source_target_pairs={{0,24},{1,25},{2,26},{3,27},{4,28},{5,29},{6,30},{7,31},{8,0},{9,1... | collective-permute-start | bytes 2211848 | tf_op jit(solution)/shard_map/ppermute | solution.py:38
  963.7 46.7 %collective-permute-start.159 = (bf16[3,5,192,128]{3,2,1,0:T(8,128)(2,1)}, bf16[3,5,192,128]{3,2,1,0:T(8,128)(2,1)}, u32[]{:S(2)}, u32[]{:S(2)}) collective-permute-start(bf16[3,5,192,128]{3,2,1,0:T(8,128)(2,1)} %get-tuple-element.990), channel_id=1, source_target_pairs={{0,16},{1,17},{2,18},{3,19},{4,20},{5,21},{6,22},{7,23},{8,24},{9,... | collective-permute-start | bytes 2211848 | tf_op jit(solution)/shard_map/ppermute | solution.py:38
  1021.3 35.6 %collective-permute-start.164 = (bf16[48,4224]{1,0:T(8,128)(2,1)S(1)}, bf16[48,4224]{1,0:T(8,128)(2,1)S(1)}, u32[]{:S(2)}, u32[]{:S(2)}) collective-permute-start(bf16[48,4224]{1,0:T(8,128)(2,1)S(1)} %get-tuple-element.1025), channel_id=1, source_target_pairs={{0,16},{1,17},{2,18},{3,19},{4,20},{5,21},{6,22},{7,23},{8,24},{9,... | collective-permute-start | bytes 1216520 | tf_op jit(solution)/shard_map/ppermute | solution.py:38
  1024.1 32.8 %collective-permute-start.165 = (bf16[48,4224]{1,0:T(8,128)(2,1)S(1)}, bf16[48,4224]{1,0:T(8,128)(2,1)S(1)}, u32[]{:S(2)}, u32[]{:S(2)}) collective-permute-start(bf16[48,4224]{1,0:T(8,128)(2,1)S(1)} %get-tuple-element.1024), channel_id=1, source_target_pairs={{0,8},{1,9},{2,10},{3,11},{4,12},{5,13},{6,14},{7,15},{8,16},{9,17... | collective-permute-start | bytes 1216520 | tf_op jit(solution)/shard_map/ppermute | solution.py:38
  (342 other events, 6030.1 us)
